TPU v7x, 128 devices: a whole 4x4x4 slice. The times are simulated.
128 devices in a mesh: req: 4 (over x), seq: 32 (over z, y, core).
Axes of the slice: x: 4, y: 4, z: 4, core: 2. Of those that a mesh axis runs over, the one named last changes fastest.
Arguments:
- new_tokens: bfloat16 [32, 4, 2048], P('req'), may hold values from -6 to 6
- norm_gain: float32 [2048], replicated, may hold values from 0.5 to 1.5
- w_query: bfloat16 [2048, 2048], P(None, 'req'), may hold values from -0.25 to 0.25
- w_key: bfloat16 [2048, 1024], P(None, 'req'), may hold values from -0.125 to 0.125
- w_value: bfloat16 [2048, 1024], P(None, 'req'), may hold values from -0.125 to 0.125
- w_out: bfloat16 [2048, 2048], P('req'), may hold values from -0.125 to 0.125
- pool_keys: bfloat16 [16384, 16, 1024], P(('req', 'seq')), may hold values from -1000 to 1000
- pool_values: bfloat16 [16384, 16, 1024], P(('req', 'seq')), may hold values from -6 to 6
- cache_lengths: int32 [32], replicated, may hold values from 2 to 8188, as said below
- owner: int32 [32], replicated, may hold values from 0 to 31, as said below
- page_table: int32 [32, 512], replicated, may hold values from 0 to 16383, as said below
Outputs:
- out_hidden: bfloat16 [32, 4, 2048], P('req')
- keys_out: bfloat16 [32, 8192, 1024], P('req', 'seq')
- values_out: bfloat16 [32, 8192, 1024], P('req', 'seq')
Inputs may be any that keep to these rules, and one draw needn't show every extreme that they name: A permutation: request r goes to owner slot owner[r], held by request group owner[r] // 8. page_table[r, j] is the pool page holding positions j * 16 to (j + 1) * 16 - 1 of request r; every pool page is named exactly once. Pool pages d * 128 to (d + 1) * 128 - 1 lie on device d of req+seq. The home of page j of request r is the device with req index owner[r] // 8 and seq index j // 16; every device's pool pages include exactly 1 pages of every home. `cache_lengths`: 8188 is reached in every draw.
All inputs are finite; a program needn't handle non-finite values.
Results may differ from a plain program's by a relative error of at most 0.015.
Values may be sent and summed in bfloat16 or wider, within the bound.
No kernel may reach another device: no remote copies, remote signals or barrier semaphores. Data moves between devices by JAX's collectives and lax.ppermute only.
A program may use at most 128 MiB of HBM per device.

v0:
```python
import math

import jax
import jax.numpy as jnp
from jax import lax
from jax.sharding import PartitionSpec as P

H = 16
KVH = 8
HD = 128


NORM_EPS = 1e-05
ROPE_BASE = 1000000.0
MASKED = -1e30


def rotate(values, places):
    half_dim = values.shape[-1] // 2
    steps_up = jnp.arange(half_dim, dtype=jnp.float32) * (2.0 / values.shape[-1])
    inverse = ROPE_BASE ** (-steps_up)
    angles = places.astype(jnp.float32)[..., None] * inverse
    cosine = jnp.cos(angles)[..., None, :]
    sine_part = jnp.sin(angles)[..., None, :]
    first_half = values[..., :half_dim]
    second_half = values[..., half_dim:]
    return jnp.concatenate(
        [
            first_half * cosine - second_half * sine_part,
            second_half * cosine + first_half * sine_part,
        ],
        axis=-1,
    )


def shards(
    new_tokens,
    norm_gain,
    w_query,
    w_key,
    w_value,
    w_out,
    pool_keys,
    pool_values,
    cache_lengths,
    owner,
    page_table,
):
    req_count = lax.axis_size("req")
    seq_count = lax.axis_size("seq")
    devices = req_count * seq_count
    req_index = lax.axis_index("req")
    seq_index = lax.axis_index("seq")
    device_index = req_index * seq_count + seq_index
    local_reqs, new_count, model_width = new_tokens.shape
    request_total = owner.shape[0]
    pages_dev, page_len, kv_width = pool_keys.shape
    pages_req = page_table.shape[1]
    pages_home = pages_req // seq_count
    positions = pages_home * page_len
    per_peer = pages_dev // devices
    groups = H // KVH
    query_cols = w_query.shape[1]
    key_cols = w_key.shape[1]
    all_requests = jnp.arange(request_total, dtype=jnp.int32)
    slot_request = jnp.zeros((request_total,), jnp.int32).at[owner].set(all_requests)
    slot_lengths = cache_lengths[slot_request]
    my_lengths = lax.dynamic_slice_in_dim(slot_lengths, req_index * local_reqs, local_reqs)
    owner_col = owner[:, None]
    logical = jnp.arange(pages_req, dtype=jnp.int32)[None, :]
    home_index = (
        (owner_col // local_reqs * seq_count + logical // pages_home) * pages_dev
        + owner_col % local_reqs * pages_home
        + logical % pages_home
    )
    pool_total = devices * pages_dev
    home_of_slot = (
        jnp.zeros((pool_total,), jnp.int32).at[page_table.reshape(-1)].set(home_index.reshape(-1))
    )
    slot_of_home = (
        jnp.zeros((pool_total,), jnp.int32).at[home_index.reshape(-1)].set(page_table.reshape(-1))
    )
    held_homes = lax.dynamic_slice_in_dim(home_of_slot, device_index * pages_dev, pages_dev)
    send_order = jnp.argsort(held_homes)
    arrival = (
        lax.dynamic_slice_in_dim(slot_of_home, device_index * pages_dev, pages_dev) // pages_dev
    )
    arrival_order = jnp.argsort(arrival * pages_dev + jnp.arange(pages_dev, dtype=jnp.int32))
    placement = jnp.argsort(arrival_order)
    outgoing = jnp.stack([pool_keys[send_order], pool_values[send_order]], axis=1)
    outgoing = outgoing.reshape(devices, per_peer, 2, page_len, kv_width)
    incoming = lax.all_to_all(outgoing, ("req", "seq"), split_axis=0, concat_axis=0, tiled=True)
    arrived = incoming.reshape(pages_dev, 2, page_len, kv_width)[placement]
    arrived = arrived.reshape(local_reqs, pages_home, 2, page_len, kv_width)
    cache_keys = arrived[:, :, 0].reshape(local_reqs, positions, kv_width)
    cache_values = arrived[:, :, 1].reshape(local_reqs, positions, kv_width)
    tokens_wide = new_tokens.astype(jnp.float32)
    square_mean = jnp.mean(tokens_wide * tokens_wide, axis=-1, keepdims=True)
    normed = (tokens_wide * lax.rsqrt(square_mean + NORM_EPS) * norm_gain).astype(jnp.bfloat16)
    new_index = jnp.arange(new_count, dtype=jnp.int32)
    row_block = lax.all_gather(normed, "req", axis=0, tiled=True)
    row_count = row_block.shape[0]
    flat_rows = row_block.reshape(row_count * new_count, model_width)
    places = slot_lengths[:, None] + new_index[None, :]
    queries_now = jnp.dot(flat_rows, w_query, preferred_element_type=jnp.float32).reshape(
        row_count, new_count, query_cols // HD, HD
    )
    keys_now = jnp.dot(flat_rows, w_key, preferred_element_type=jnp.float32).reshape(
        row_count, new_count, key_cols // HD, HD
    )
    values_now = jnp.dot(flat_rows, w_value, preferred_element_type=jnp.float32).reshape(
        row_count, new_count, key_cols
    )
    queries_now = rotate(queries_now, places).reshape(row_count, new_count, query_cols)
    keys_now = rotate(keys_now, places).reshape(row_count, new_count, key_cols)
    projected = jnp.concatenate([queries_now, keys_now, values_now], axis=-1).astype(jnp.bfloat16)
    owned_rows = lax.all_to_all(projected, "req", split_axis=0, concat_axis=2, tiled=True)
    owned_rows = owned_rows.reshape(local_reqs, new_count, req_count, query_cols + 2 * key_cols)
    queries = owned_rows[..., :query_cols].reshape(local_reqs, new_count, KVH, groups, HD)
    fresh_keys = owned_rows[..., query_cols : query_cols + key_cols].reshape(
        local_reqs, new_count, KVH, HD
    )
    fresh_values = owned_rows[..., query_cols + key_cols :].reshape(local_reqs, new_count, KVH, HD)
    score_scale = 1.0 / math.sqrt(HD)
    grid_keys = cache_keys.reshape(local_reqs, positions, KVH, HD)
    grid_values = cache_values.reshape(local_reqs, positions, KVH, HD)
    scores = (
        jnp.einsum("rtkgd,rpkd->rkgtp", queries, grid_keys, preferred_element_type=jnp.float32)
        * score_scale
    )
    key_spots = seq_index * positions + jnp.arange(positions, dtype=jnp.int32)
    live_mask = (key_spots[None, :] < my_lengths[:, None])[:, None, None, None, :]
    scores = jnp.where(live_mask, scores, MASKED)
    row_peak = jnp.max(scores, axis=-1)
    weights = jnp.where(live_mask, jnp.exp(scores - row_peak[..., None]), 0.0)
    row_mass = jnp.sum(weights, axis=-1)
    gathered_sum = jnp.einsum(
        "rkgtp,rpkd->rkgtd",
        weights.astype(jnp.bfloat16),
        grid_values,
        preferred_element_type=jnp.float32,
    )
    global_peak = lax.pmax(row_peak, "seq")
    rescale = jnp.exp(row_peak - global_peak)
    row_mass, gathered_sum = (
        lax.psum((row_mass * rescale).astype(jnp.bfloat16), "seq").astype(jnp.float32),
        lax.psum((gathered_sum * rescale[..., None]).astype(jnp.bfloat16), "seq").astype(
            jnp.float32
        ),
    )
    row_peak = global_peak
    own_scores = (
        jnp.einsum("rtkgd,rskd->rkgts", queries, fresh_keys, preferred_element_type=jnp.float32)
        * score_scale
    )
    causal = new_index[None, :] <= new_index[:, None]
    own_scores = jnp.where(causal, own_scores, MASKED)
    final_peak = jnp.maximum(row_peak, jnp.max(own_scores, axis=-1))
    carried = jnp.exp(row_peak - final_peak)
    own_weights = jnp.where(causal, jnp.exp(own_scores - final_peak[..., None]), 0.0)
    row_mass = row_mass * carried + jnp.sum(own_weights, axis=-1)
    gathered_sum = gathered_sum * carried[..., None] + jnp.einsum(
        "rkgts,rskd->rkgtd",
        own_weights.astype(jnp.bfloat16),
        fresh_values,
        preferred_element_type=jnp.float32,
    )
    attended = (
        jnp.transpose(gathered_sum / row_mass[..., None], (0, 3, 1, 2, 4))
        .reshape(local_reqs, new_count, KVH * groups * HD)
        .astype(jnp.bfloat16)
    )
    headed = lax.all_to_all(attended, "req", split_axis=2, concat_axis=0, tiled=True)
    row_count = lax.axis_size("req") * local_reqs
    projected_out = lax.psum_scatter(
        jnp.dot(
            headed.reshape(row_count * new_count, -1), w_out, preferred_element_type=jnp.float32
        )
        .reshape(row_count, new_count, model_width)
        .astype(jnp.bfloat16),
        "req",
        scatter_dimension=0,
        tiled=True,
    ).astype(jnp.float32)
    out_hidden = (tokens_wide + projected_out).astype(jnp.bfloat16)
    new_hits = key_spots[None, :, None] == my_lengths[:, None, None] + new_index[None, None, :]
    filler = new_hits.astype(jnp.bfloat16)
    placed_keys = jnp.einsum(
        "rpt,rtc->rpc",
        filler,
        fresh_keys.reshape(local_reqs, new_count, kv_width),
        preferred_element_type=jnp.float32,
    ).astype(jnp.bfloat16)
    placed_values = jnp.einsum(
        "rpt,rtc->rpc",
        filler,
        fresh_values.reshape(local_reqs, new_count, kv_width),
        preferred_element_type=jnp.float32,
    ).astype(jnp.bfloat16)
    touched = jnp.any(new_hits, axis=-1)[..., None]
    keys_out = jnp.where(touched, placed_keys, cache_keys)
    values_out = jnp.where(touched, placed_values, cache_values)
    return (out_hidden, keys_out, values_out)


def solution(mesh):
    return jax.shard_map(
        shards,
        mesh=mesh,
        in_specs=(
            P("req", None, None),
            P(),
            P(None, "req"),
            P(None, "req"),
            P(None, "req"),
            P("req", None),
            P(("req", "seq"), None, None),
            P(("req", "seq"), None, None),
            P(),
            P(),
            P(),
        ),
        out_specs=(P("req", None, None), P("req", "seq", None), P("req", "seq", None)),
        check_vma=False,
    )
```

profile of v0, /device:TPU:32, one launch (start us, length us, event | category | flops | bytes accessed | tf_op | source)
XLA Modules:
  0.0 664.4 jit_solution(227160449569236609)
XLA Ops:
  7.2 0.8 fusion.65
  8.0 0.7 scatter_custom_fusion
  8.7 1.4 gather_fusion
  10.1 1.1 fusion.29
  11.2 1.0 fusion.31
  12.3 13.1 %all_gather.3 = bf16[32,4,2048]{2,0,1:T(8,128)(2,1)S(1)} all-gather(bf16[8,4,2048]{2,0,1:T(8,128)(2,1)S(1)} %fusion.31), channel_id=1, replica_groups=mesh['req'=4,'seq'=32] {'req'}, dimensions={0}, use_global_device_ids=true | all-gather | bytes 655360 | tf_op jit(solution)/shard_map/all_gather | solution.py:101
  25.4 3.9 copy.178
  29.3 2.3 copy.179
  31.6 2.5 fusion.27
  34.1 1.7 fusion.25
  35.8 0.3 multiply_cosine_fusion
  36.2 0.2 subtract_convert_fusion
  36.3 0.1 subtract_convert_fusion.1
  36.4 0.3 convolution_convert_fusion.1
  36.8 0.1 copy_bitcast_fusion.1
  36.9 0.1 copy_bitcast_fusion.2
  37.0 0.9 copy.137
  37.9 4.3 all-to-all-start.1
  42.4 60.3 %scatter_custom_fusion.1 = s32[16384]{0:T(1024)S(1)} fusion(s32[16384]{0:T(1024)S(1)} %bitcast.147, s32[16384]{0:T(1024)S(1)} %bitcast.146, s32[]{:T(128)} %constant.90.clone.1), kind=kCustom, calls=%fused_computation.82 | custom fusion | bytes 65540 | tf_op jit(solution)/shard_map/scatter | solution.py:78
  102.9 2.5 sort.45
  105.4 5.0 gather_fusion.1
  110.4 5.0 gather_fusion.2
  115.5 7.5 %maximum_bitcast_fusion = bf16[128,1,2,16,1024]{4,3,2,1,0:T(8,128)(2,1)} fusion(bf16[128,1,16,1024]{3,2,1,0:T(8,128)(2,1)} %bitcast.129, bf16[128,1,16,1024]{3,2,1,0:T(8,128)(2,1)} %bitcast.128), kind=kLoop, calls=%fused_computation.7 | loop fusion | flops 4194304 | bytes 16777216 | tf_op jit(solution)/shard_map/reshape | solution.py:91
  122.9 11.2 %all-to-all-start = ((bf16[128,1,2,16,1024]{4,3,2,1,0:T(8,128)(2,1)}), bf16[128,1,2,16,1024]{4,3,2,1,0:T(8,128)(2,1)}, u32[]{:S(2)}, u32[]{:S(2)}) async-start(bf16[128,1,2,16,1024]{4,3,2,1,0:T(8,128)(2,1)} %maximum_bitcast_fusion), calls=%async_computation | async-start | bytes 16777216 | tf_op jit(solution)/shard_map/all_to_all | solution.py:92
  134.4 60.5 %scatter_custom_fusion.2 = s32[16384]{0:T(1024)S(1)} fusion(s32[16384]{0:T(1024)S(1)} %bitcast.148, s32[16384]{0:T(1024)S(1)} %bitcast.145, s32[]{:T(128)} %constant.90.clone.1), kind=kCustom, calls=%fused_computation.80 | custom fusion | bytes 65540 | tf_op jit(solution)/shard_map/scatter | solution.py:81
  195.1 2.5 sort.46
  197.6 2.5 sort.47
  200.6 0.3 fusion.40
  200.9 0.5 copy.151
  201.5 32.8 %all-to-all-done = bf16[128,1,2,16,1024]{4,3,2,1,0:T(8,128)(2,1)} async-done(((bf16[128,1,2,16,1024]{4,3,2,1,0:T(8,128)(2,1)}), bf16[128,1,2,16,1024]{4,3,2,1,0:T(8,128)(2,1)}, u32[]{:S(2)}, u32[]{:S(2)}) %all-to-all-start) | async-done | bytes 8388640 | tf_op jit(solution)/shard_map/all_to_all | solution.py:92
  234.3 9.9 %gather_fusion.3 = bf16[128,2,16,1024]{3,2,1,0:T(8,128)(2,1)} fusion(bf16[128,2,16,1024]{3,2,1,0:T(8,128)(2,1)} %bitcast.4, s32[1024]{0:T(1024)S(1)} %pad_clamp_fusion), kind=kCustom, calls=%fused_computation.3 | custom fusion | bytes 16777728 | tf_op jit(solution)/shard_map/gather | solution.py:93
  244.3 5.4 fusion.68
  249.7 1.1 copy.205
  250.9 0.9 copy-done.1
  251.8 0.3 bitcast_bitcast_fusion.1
  252.1 1.6 fusion.70
  253.6 0.3 copy.146
  253.9 0.8 fusion.38
  254.7 0.3 copy.158
  255.0 112.4 %pmax.7 = f32[8,8,2,4]{1,0,3,2:T(8,128)S(1)} all-reduce(f32[8,8,2,4]{1,0,3,2:T(8,128)S(1)} %copy.146), channel_id=1, replica_groups=mesh['req'=4,'seq'=32] {'seq'}, use_global_device_ids=true, to_apply=%region_8.9 | all-reduce | flops 512 | bytes 4096 | tf_op jit(solution)/shard_map/pmax | solution.py:143
  367.4 0.1 fusion.36
  367.5 123.8 %psum.15 = bf16[8,8,2,4]{1,0,3,2:T(8,128)(2,1)S(1)} all-reduce(bf16[8,8,2,4]{1,0,3,2:T(8,128)(2,1)S(1)} %get-tuple-element.29), channel_id=1, replica_groups=mesh['req'=4,'seq'=32] {'seq'}, use_global_device_ids=true, to_apply=%region_12.13 | all-reduce | flops 512 | bytes 2048 | tf_op jit(solution)/shard_map/psum | solution.py:146
  491.3 0.2 copy.147
  491.5 3.3 copy.206
  494.8 0.3 bitcast_bitcast_fusion
  495.1 1.3 fusion.14
  496.5 0.2 copy.154
  496.7 0.2 copy.161
  496.9 0.5 copy.156
  497.3 113.8 %all-reduce.2.cloned.1.call-done = bf16[8,8,2,4,128]{4,3,2,1,0:T(4,128)(2,1)} async-done(((bf16[8,8,2,4,128]{4,3,2,1,0:T(4,128)(2,1)}), bf16[8,8,2,4,128]{4,3,2,1,0:T(4,128)(2,1)}) %all-reduce.2.cloned.1.call-update) | async-done | bytes 131088 | tf_op jit(solution)/shard_map/psum | solution.py:147
  611.2 1.3 fusion.17
  612.4 2.4 copy.188
  614.9 3.4 reshape.418
  618.3 10.0 %all_to_all.35 = bf16[4,2,8192]{2,1,0:T(2,128)(2,1)S(1)} all-to-all(bf16[4,2,8192]{2,1,0:T(2,128)(2,1)S(1)} %reshape.418), channel_id=1, replica_groups=mesh['req'=4,'seq'=32] {'req'}, dimensions={0} | all-to-all | bytes 262144 | tf_op jit(solution)/shard_map/all_to_all | solution.py:173
  628.3 3.4 reshape.419
  631.8 2.8 copy.165
  634.6 0.5 fusion.4
  635.1 0.8 copy.200
  636.0 0.1 compare_reduce_fusion
  636.2 5.3 bitcast_select_fusion
  641.5 3.9 bitcast_select_fusion.1
  645.4 10.4 %reduce-scatter.4.cloned.1.call-done = bf16[8,8192]{1,0:T(8,128)(2,1)} async-done(((bf16[32,8192]{1,0:T(8,128)(2,1)}), bf16[8,8192]{1,0:T(8,128)(2,1)}) %reduce-scatter.4.cloned.1.call-update) | async-done | bytes 131088
  655.8 1.0 fusion.32
  656.8 0.8 copy.168
  (59 shorter events, 1.6 us)
Async XLA Ops:
  7.2 627.4 %copy-start = (bf16[512,2048]{1,0:T(8,128)(2,1)S(1)}, bf16[512,2048]{1,0:T(8,128)(2,1)}, u32[]{:S(2)}) copy-start(bf16[512,2048]{1,0:T(8,128)(2,1)} %param.16) | copy-start | bytes 6291460
  31.6 4.9 copy-start.4
  34.1 8.2 %copy-start.5 = (s32[32,512]{1,0:T(8,128)S(1)}, s32[32,512]{1,0:T(8,128)}, u32[]{:S(2)}) copy-start(s32[32,512]{1,0:T(8,128)} %param.21) | copy-start | bytes 196612
  37.9 85.0 %all-to-all-start.1 = ((bf16[32,4,1024]{2,1,0:T(4,128)(2,1)}), bf16[32,4,1024]{2,1,0:T(4,128)(2,1)S(1)}, u32[]{:S(2)}, u32[]{:S(2)}) async-start(bf16[32,4,1024]{2,1,0:T(4,128)(2,1)} %copy.137), calls=%async_computation.1 | async-start | bytes 524288 | tf_op jit(solution)/shard_map/all_to_all | solution.py:117
  122.9 111.4 %all-to-all-start = ((bf16[128,1,2,16,1024]{4,3,2,1,0:T(8,128)(2,1)}), bf16[128,1,2,16,1024]{4,3,2,1,0:T(8,128)(2,1)}, u32[]{:S(2)}, u32[]{:S(2)}) async-start(bf16[128,1,2,16,1024]{4,3,2,1,0:T(8,128)(2,1)} %maximum_bitcast_fusion), calls=%async_computation | async-start | bytes 16777216 | tf_op jit(solution)/shard_map/all_to_all | solution.py:92
  134.1 477.0 %all-reduce.2.cloned.1.call-start = ((), (), s32[]{:S(2)}) async-start(), calls=%async_computation.4 | async-start | bytes 262144 | tf_op jit(solution)/shard_map/psum | solution.py:147
  249.7 2.1 copy-start.1
  496.4 159.4 %reduce-scatter.4.cloned.1.call-start = ((), (), s32[]{:S(2)}) async-start(), calls=%async_computation.5 | async-start | bytes 655360
  636.2 5.3 copy-start.2
  641.5 14.3 %copy-start.3 = (bf16[8,4,2048]{2,1,0:T(4,128)(2,1)S(1)}, bf16[8,4,2048]{2,1,0:T(4,128)(2,1)}, u32[]{:S(2)}) copy-start(bf16[8,4,2048]{2,1,0:T(4,128)(2,1)} %param.11) | copy-start | bytes 393220
Sparse Core Ops, SparseCore 0:
  496.5 114.5 all-reduce.1
  636.1 19.6 reduce-scatter.3
where the time goes:
time: 666 us; the launch traced here: 664 us
  blocking collectives  259 us (39%)
  local copies, waits for them, and re-layouts  178 us (27%)
  waiting for transfers between devices  157 us (24%)
  other arithmetic  21.5 us (3%)
  matrix products  18.7 us (3%)
  starting transfers between devices  15.5 us (2%)
  between operations  14.4 us (2%)
    psum x1, blocking collectives, shards(): lax.psum((row_mass * rescale).astype(jnp.bfloat16), 'seq')  124 us
    psum x1, waiting for transfers between devices, shards(): lax.psum((gathered_sum * rescale[..., None]).astype(jnp.bfloat16), 'seq')  114 us
    pmax x1, blocking collectives, shards(): global_peak = lax.pmax(row_peak, 'seq')  112 us
    scatter x1, local copies, waits for them, and re-layouts, shards(): jnp.zeros((pool_total,), jnp.int32).at[home_index.reshape(-1)]  60.5 us
    scatter x1, local copies, waits for them, and re-layouts, shards(): jnp.zeros((pool_total,), jnp.int32).at[page_table.reshape(-1)]  60.3 us
    all_to_all x1, waiting for transfers between devices, shards(): lax.all_to_all(outgoing, ('req', 'seq'), split_axis=0, concat_axis=0, til...  32.8 us
    unnamed x22, local copies, waits for them, and re-layouts  14 us
  transfers between devices with their start and end apart: 4, of which 3 were waited for; matrix products, arithmetic and copies ran while one was open for 24% of the time, Pallas kernels for 0%

commit v1 on v0

--- a/solution.py
+++ b/solution.py
@@ -63,37 +63,28 @@
     query_cols = w_query.shape[1]
     key_cols = w_key.shape[1]
     all_requests = jnp.arange(request_total, dtype=jnp.int32)
-    slot_request = jnp.zeros((request_total,), jnp.int32).at[owner].set(all_requests)
-    slot_lengths = cache_lengths[slot_request]
+    hits = owner[None, :] == all_requests[:, None]
+    slot_request = jnp.sum(jnp.where(hits, all_requests[None, :], 0), axis=1)
+    slot_lengths = jnp.sum(jnp.where(hits, cache_lengths[None, :], 0), axis=1)
     my_lengths = lax.dynamic_slice_in_dim(slot_lengths, req_index * local_reqs, local_reqs)
-    owner_col = owner[:, None]
-    logical = jnp.arange(pages_req, dtype=jnp.int32)[None, :]
-    home_index = (
-        (owner_col // local_reqs * seq_count + logical // pages_home) * pages_dev
-        + owner_col % local_reqs * pages_home
-        + logical % pages_home
-    )
-    pool_total = devices * pages_dev
-    home_of_slot = (
-        jnp.zeros((pool_total,), jnp.int32).at[page_table.reshape(-1)].set(home_index.reshape(-1))
-    )
-    slot_of_home = (
-        jnp.zeros((pool_total,), jnp.int32).at[home_index.reshape(-1)].set(page_table.reshape(-1))
-    )
-    held_homes = lax.dynamic_slice_in_dim(home_of_slot, device_index * pages_dev, pages_dev)
-    send_order = jnp.argsort(held_homes)
-    arrival = (
-        lax.dynamic_slice_in_dim(slot_of_home, device_index * pages_dev, pages_dev) // pages_dev
-    )
-    arrival_order = jnp.argsort(arrival * pages_dev + jnp.arange(pages_dev, dtype=jnp.int32))
-    placement = jnp.argsort(arrival_order)
-    outgoing = jnp.stack([pool_keys[send_order], pool_values[send_order]], axis=1)
-    outgoing = outgoing.reshape(devices, per_peer, 2, page_len, kv_width)
-    incoming = lax.all_to_all(outgoing, ("req", "seq"), split_axis=0, concat_axis=0, tiled=True)
-    arrived = incoming.reshape(pages_dev, 2, page_len, kv_width)[placement]
-    arrived = arrived.reshape(local_reqs, pages_home, 2, page_len, kv_width)
-    cache_keys = arrived[:, :, 0].reshape(local_reqs, positions, kv_width)
-    cache_values = arrived[:, :, 1].reshape(local_reqs, positions, kv_width)
+    slot_pages = page_table[slot_request]
+    home_table = jnp.transpose(
+        slot_pages.reshape(req_count, local_reqs, seq_count, pages_home), (0, 2, 1, 3)
+    ).reshape(devices, local_reqs * pages_home)
+    my_home = lax.dynamic_slice_in_dim(home_table, device_index, 1, axis=0).reshape(-1)
+    arrival_src = my_home // pages_dev
+    held_here = (home_table // pages_dev) == device_index
+    send_pick = jnp.sum(jnp.where(held_here, home_table % pages_dev, 0), axis=1)
+    outgoing_k = pool_keys[send_pick].reshape(devices, per_peer, page_len, kv_width)
+    outgoing_v = pool_values[send_pick].reshape(devices, per_peer, page_len, kv_width)
+    incoming_k = lax.all_to_all(outgoing_k, ("req", "seq"), split_axis=0, concat_axis=0, tiled=True)
+    incoming_v = lax.all_to_all(outgoing_v, ("req", "seq"), split_axis=0, concat_axis=0, tiled=True)
+    cache_keys = incoming_k.reshape(pages_dev, page_len, kv_width)[arrival_src].reshape(
+        local_reqs, positions, kv_width
+    )
+    cache_values = incoming_v.reshape(pages_dev, page_len, kv_width)[arrival_src].reshape(
+        local_reqs, positions, kv_width
+    )
     tokens_wide = new_tokens.astype(jnp.float32)
     square_mean = jnp.mean(tokens_wide * tokens_wide, axis=-1, keepdims=True)
     normed = (tokens_wide * lax.rsqrt(square_mean + NORM_EPS) * norm_gain).astype(jnp.bfloat16)
@@ -140,15 +131,24 @@
         grid_values,
         preferred_element_type=jnp.float32,
     )
-    global_peak = lax.pmax(row_peak, "seq")
-    rescale = jnp.exp(row_peak - global_peak)
-    row_mass, gathered_sum = (
-        lax.psum((row_mass * rescale).astype(jnp.bfloat16), "seq").astype(jnp.float32),
-        lax.psum((gathered_sum * rescale[..., None]).astype(jnp.bfloat16), "seq").astype(
-            jnp.float32
-        ),
-    )
-    row_peak = global_peak
+    step = 1
+    while step < seq_count:
+        pairs = [(i, i ^ step) for i in range(seq_count)]
+        peer_peak, peer_mass, peer_sum = lax.ppermute((row_peak, row_mass, gathered_sum), "seq", pairs)
+        upper = (seq_index & step) != 0
+        peak_lo = jnp.where(upper, peer_peak, row_peak)
+        peak_hi = jnp.where(upper, row_peak, peer_peak)
+        mass_lo = jnp.where(upper, peer_mass, row_mass)
+        mass_hi = jnp.where(upper, row_mass, peer_mass)
+        sum_lo = jnp.where(upper, peer_sum, gathered_sum)
+        sum_hi = jnp.where(upper, gathered_sum, peer_sum)
+        merged_peak = jnp.maximum(peak_lo, peak_hi)
+        scale_lo = jnp.exp(peak_lo - merged_peak)
+        scale_hi = jnp.exp(peak_hi - merged_peak)
+        row_mass = mass_lo * scale_lo + mass_hi * scale_hi
+        gathered_sum = sum_lo * scale_lo[..., None] + sum_hi * scale_hi[..., None]
+        row_peak = merged_peak
+        step *= 2
     own_scores = (
         jnp.einsum("rtkgd,rskd->rkgts", queries, fresh_keys, preferred_element_type=jnp.float32)
         * score_scale

time: 666 us -> 278 us (0.42)
  blocking collectives: 259 us -> 13.1 us
  local copies, waits for them, and re-layouts: 178 us -> 58.3 us
  waiting for transfers between devices: 157 us -> 113 us
  starting transfers between devices: 15.5 us -> 42.7 us
    psum x1 -> x0, blocking collectives: 124 us -> none  [shards(): lax.psum((row_mass * rescale).astype(jnp.bfloat16), 'seq')]
    scatter x3 -> x0, local copies, waits for them, and re-layouts: 122 us -> none  [the longest x1 60.5 us: shards(): jnp.zeros((pool_total,), jnp.int32).at[home_index.reshape(-1)]]
    psum x1 -> x0, waiting for transfers between devices: 114 us -> none  [shards(): lax.psum((gathered_sum * rescale[..., None]).astype(jnp.bfloat16), 'seq')]
    pmax x1 -> x0, blocking collectives: 112 us -> none  [shards(): global_peak = lax.pmax(row_peak, 'seq')]
    all_to_all x1 -> x3, waiting for transfers between devices: 32.8 us -> 89.1 us  [the longest x1 47.1 us: shards(): lax.all_to_all(outgoing_k, ('req', 'seq'), split_axis=0, concat_axis=0, t...]
    ppermute x0 -> x15, starting transfers between devices: none -> 17.6 us  [shards(): lax.ppermute((row_peak, row_mass, gathered_sum), 'seq', pairs)]
    ppermute x0 -> x15, waiting for transfers between devices: none -> 11.9 us  [shards(): lax.ppermute((row_peak, row_mass, gathered_sum), 'seq', pairs)]
    all_to_all x1 -> x0, blocking collectives: 10 us -> none  [shards(): lax.all_to_all(attended, 'req', split_axis=2, concat_axis=0, tiled=True)]
  transfers between devices with their start and end apart: 4 -> 20, of which waited for: 3 -> 13; matrix products, arithmetic and copies ran while one was open for 24% -> 18% of each run, Pallas kernels for 0% -> 0%
where the time goes in v1:
time: 278 us; the launch traced here: 277 us
  waiting for transfers between devices  113 us (41%)
  local copies, waits for them, and re-layouts  58.3 us (21%)
  starting transfers between devices  42.7 us (15%)
  other arithmetic  19.5 us (7%)
  matrix products  15.4 us (6%)
  between operations  14.5 us (5%)
  blocking collectives  13.1 us (5%)
    all_to_all x1, waiting for transfers between devices, shards(): lax.all_to_all(outgoing_k, ('req', 'seq'), split_axis=0, concat_axis=0, t...  47.1 us
    all_to_all x1, waiting for transfers between devices, shards(): lax.all_to_all(outgoing_v, ('req', 'seq'), split_axis=0, concat_axis=0, t...  39.6 us
    ppermute x15, starting transfers between devices, shards(): lax.ppermute((row_peak, row_mass, gathered_sum), 'seq', pairs)  17.6 us
    unnamed x20, local copies, waits for them, and re-layouts  16.4 us
    all_gather x1, blocking collectives, shards(): row_block = lax.all_gather(normed, 'req', axis=0, tiled=True)  13.1 us
    ppermute x15, waiting for transfers between devices, shards(): lax.ppermute((row_peak, row_mass, gathered_sum), 'seq', pairs)  11.9 us
    unnamed x2, waiting for transfers between devices  11.9 us
    all_to_all x1, starting transfers between devices, shards(): lax.all_to_all(outgoing_k, ('req', 'seq'), split_axis=0, concat_axis=0, t...  11.1 us
  transfers between devices with their start and end apart: 20, of which 13 were waited for; matrix products, arithmetic and copies ran while one was open for 18% of the time, Pallas kernels for 0%

profile of v1, /device:TPU:32, one launch (start us, length us, event | category | flops | bytes accessed | tf_op | source)
XLA Modules:
  0.0 276.6 jit_solution(15925189236282462206)
XLA Ops:
  7.2 0.9 select_reduce_fusion
  8.1 1.1 fusion.25
  9.3 1.0 fusion.27
  10.3 13.1 %all_gather.3 = bf16[32,4,2048]{2,0,1:T(8,128)(2,1)S(1)} all-gather(bf16[8,4,2048]{2,0,1:T(8,128)(2,1)S(1)} %fusion.27), channel_id=1, replica_groups=mesh['req'=4,'seq'=32] {'req'}, dimensions={0}, use_global_device_ids=true | all-gather | bytes 655360 | tf_op jit(solution)/shard_map/all_gather | solution.py:92
  23.4 3.9 %copy.245 = bf16[512,2048]{1,0:T(8,128)(2,1)} copy(bf16[512,2048]{0,1:T(8,128)(2,1)} %bitcast.133) | data formatting | bytes 4194304 | tf_op jit(solution)/shard_map/dot_general | solution.py:96
  27.4 2.3 copy.246
  29.6 2.5 fusion.21
  32.1 1.7 fusion.19
  35.1 0.9 copy.193
  36.0 4.3 %all-to-all-start.1 = ((bf16[32,4,1024]{2,1,0:T(4,128)(2,1)}), bf16[32,4,1024]{2,1,0:T(4,128)(2,1)S(1)}, u32[]{:S(2)}, u32[]{:S(2)}) async-start(bf16[32,4,1024]{2,1,0:T(4,128)(2,1)} %copy.193), calls=%async_computation.1 | async-start | bytes 524288 | tf_op jit(solution)/shard_map/all_to_all | solution.py:108
  40.2 0.6 gather_fusion
  41.1 0.6 fusion.18
  41.8 5.0 %gather_fusion.1 = bf16[128,16,1024]{2,1,0:T(8,128)(2,1)} fusion(bf16[128,16,1024]{2,1,0:T(8,128)(2,1)} %param.17, s32[1024]{0:T(1024)S(1)} %pad_clamp_fusion.1), kind=kCustom, calls=%fused_computation.1 | custom fusion | bytes 8389120 | tf_op jit(solution)/shard_map/gather | solution.py:78
  46.9 11.1 %all-to-all-start = ((bf16[128,1,16,1024]{3,2,1,0:T(8,128)(2,1)}), bf16[128,1,16,1024]{3,2,1,0:T(8,128)(2,1)}, u32[]{:S(2)}, u32[]{:S(2)}) async-start(bf16[128,1,16,1024]{3,2,1,0:T(8,128)(2,1)} %bitcast.125), calls=%async_computation | async-start | bytes 8388608 | tf_op jit(solution)/shard_map/all_to_all | solution.py:80
  58.0 5.0 %gather_fusion.3 = bf16[128,16,1024]{2,1,0:T(8,128)(2,1)} fusion(bf16[128,16,1024]{2,1,0:T(8,128)(2,1)} %param.18, s32[1024]{0:T(1024)S(1)} %pad_clamp_fusion.1), kind=kCustom, calls=%fused_computation.3 | custom fusion | bytes 8389120 | tf_op jit(solution)/shard_map/gather | solution.py:79
  63.0 47.1 %all-to-all-done = bf16[128,1,16,1024]{3,2,1,0:T(8,128)(2,1)} async-done(((bf16[128,1,16,1024]{3,2,1,0:T(8,128)(2,1)}), bf16[128,1,16,1024]{3,2,1,0:T(8,128)(2,1)}, u32[]{:S(2)}, u32[]{:S(2)}) %all-to-all-start) | async-done | bytes 4194336 | tf_op jit(solution)/shard_map/all_to_all | solution.py:80
  110.1 6.4 %all-to-all-start.2 = ((bf16[128,1,16,1024]{3,2,1,0:T(8,128)(2,1)}), bf16[128,1,16,1024]{3,2,1,0:T(8,128)(2,1)}, u32[]{:S(2)}, u32[]{:S(2)}) async-start(bf16[128,1,16,1024]{3,2,1,0:T(8,128)(2,1)} %bitcast.124), calls=%async_computation.2 | async-start | bytes 8388608 | tf_op jit(solution)/shard_map/all_to_all | solution.py:81
  117.7 5.1 %gather_fusion.2 = bf16[128,16,1024]{2,1,0:T(8,128)(2,1)} fusion(bf16[128,16,1024]{2,1,0:T(8,128)(2,1)} %bitcast.5, s32[1024]{0:T(1024)S(1)} %pad_clamp_fusion), kind=kCustom, calls=%fused_computation.2 | custom fusion | bytes 8389120 | tf_op jit(solution)/shard_map/gather | solution.py:82
  122.8 3.3 %copy.266 = bf16[256,8,8,128]{3,2,1,0:T(8,128)(2,1)S(1)} copy(bf16[256,8,8,128]{3,1,2,0:T(8,128)(2,1)} %bitcast.120) | data formatting | bytes 8388608
  126.4 1.6 fusion.66
  128.2 0.8 fusion.37
  129.0 39.6 %all-to-all-done.2 = bf16[128,1,16,1024]{3,2,1,0:T(8,128)(2,1)} async-done(((bf16[128,1,16,1024]{3,2,1,0:T(8,128)(2,1)}), bf16[128,1,16,1024]{3,2,1,0:T(8,128)(2,1)}, u32[]{:S(2)}, u32[]{:S(2)}) %all-to-all-start.2) | async-done | bytes 4194336 | tf_op jit(solution)/shard_map/all_to_all | solution.py:81
  168.7 5.0 %gather_fusion.4 = bf16[128,16,1024]{2,1,0:T(8,128)(2,1)} fusion(bf16[128,16,1024]{2,1,0:T(8,128)(2,1)} %bitcast.22, s32[1024]{0:T(1024)S(1)} %pad_clamp_fusion), kind=kCustom, calls=%fused_computation.4 | custom fusion | bytes 8389120 | tf_op jit(solution)/shard_map/gather | solution.py:85
  173.7 3.3 %copy.267 = bf16[256,8,8,128]{3,2,1,0:T(8,128)(2,1)S(1)} copy(bf16[256,8,8,128]{3,1,2,0:T(8,128)(2,1)} %bitcast.122) | data formatting | bytes 8388608
  177.0 2.3 bitcast_bitcast_fusion
  180.1 2.8 %fusion = f32[8,8,2,4,128]{4,3,2,1,0:T(4,128)S(1)} fusion(bf16[8,256,8,128,1]{3,2,1,0,4:T(8,128)(2,1)} %bitcast_bitcast_fusion, bf16[8,8,2,4,256]{4,2,3,1,0:T(2,128)(2,1)S(1)} %get-tuple-element.46), kind=kOutput, calls=%fused_computation.9 | convolution fusion | flops 33554432 | bytes 4718592 | tf_op jit(solution)/shard_map/rkgtp,rpkd->rkgtd/dot_general | solution.py:128
  183.2 2.0 collective-permute-start.3
  185.5 1.7 collective-permute-done.11
  187.6 0.7 multiply_add_fusion.7
  188.2 0.7 collective-permute-start.12
  189.0 2.8 %collective-permute-start.5 = (f32[8,8,2,4]{1,0,3,2:T(8,128)}, f32[8,8,2,4]{1,0,3,2:T(8,128)}, u32[]{:S(2)}, u32[]{:S(2)}) collective-permute-start(f32[8,8,2,4]{1,0,3,2:T(8,128)} %get-tuple-element.41), channel_id=1, source_target_pairs={{0,4},{1,5},{2,6},{3,7},{4,0},{5,1},{6,2},{7,3},{8,12},{9,13},{10,... | collective-permute-start | bytes 6152 | tf_op jit(solution)/shard_map/ppermute | solution.py:137
  192.1 1.6 collective-permute-start.2
  194.2 0.8 collective-permute-done.5
  195.0 1.4 multiply_add_fusion.6
  196.5 2.1 collective-permute-start.13
  198.6 1.2 collective-permute-done.2
  200.1 1.6 collective-permute-start.4
  202.9 1.5 multiply_add_fusion.5
  204.3 1.8 collective-permute-start.9
  206.2 2.2 collective-permute-done.4
  208.8 1.5 collective-permute-start.6
  210.5 0.9 copy.209
  211.4 0.9 copy.210
  212.4 0.6 collective-permute-start.14
  212.9 0.8 fusion.57
  213.7 1.7 collective-permute-done.6
  215.7 2.0 collective-permute-start.8
  218.4 0.8 multiply_add_fusion.4
  220.4 3.3 %collective-permute-done.8 = f32[8,8,2,4,128]{4,3,2,1,0:T(4,128)S(1)} collective-permute-done((f32[8,8,2,4,128]{4,3,2,1,0:T(4,128)S(1)}, f32[8,8,2,4,128]{4,3,2,1,0:T(4,128)S(1)}, u32[]{:S(2)}, u32[]{:S(2)}) %collective-permute-start.8) | collective-permute-done | bytes 262176 | tf_op jit(solution)/shard_map/ppermute | solution.py:137
  223.7 0.7 fusion.32
  224.4 2.5 copy.255
  226.9 4.0 %reshape.368 = bf16[4,2,8192]{2,1,0:T(2,128)(2,1)} reshape(bf16[2048,4,8]{2,1,0:T(4,128)(2,1)} %bitcast.129) | data formatting | bytes 262144
  230.9 3.3 %all-to-all-start.3 = ((bf16[4,2,8192]{2,1,0:T(2,128)(2,1)}), bf16[4,2,8192]{2,1,0:T(2,128)(2,1)S(1)}, u32[]{:S(2)}, u32[]{:S(2)}) async-start(bf16[4,2,8192]{2,1,0:T(2,128)(2,1)} %reshape.368), calls=%async_computation.3 | async-start | bytes 262144 | tf_op jit(solution)/shard_map/all_to_all | solution.py:173
  234.3 3.5 %fusion.44 = bf16[8,256,1024]{2,1,0:T(8,128)(2,1)} fusion(bf16[8,4,1024]{2,1,0:T(4,128)(2,1)S(1)} %reshape_reshape.15, s32[8,4]{1,0:T(8,128)S(1)} %iota_add_fusion, s32[256]{0:T(256)S(1)} %iota_add_fusion.1), kind=kOutput, calls=%fused_computation.79 | convolution fusion | flops 16785408 | bytes 4260992 | tf_op jit(solution)/shard_map/rpt,rtc->rpc/dot_general | solution.py:194
  237.8 2.4 all-to-all-done.3
  240.2 3.5 %reshape.369 = bf16[2048,4,8]{2,1,0:T(4,128)(2,1)} reshape(bf16[4,2,8192]{2,1,0:T(2,128)(2,1)S(1)} %all-to-all-done.3) | data formatting | bytes 262144
  243.7 2.8 %copy.232 = bf16[4,8,4,512]{3,1,0,2:T(8,128)(2,1)S(1)} copy(bf16[4,8,4,512]{1,2,3,0:T(4,128)(2,1)} %bitcast.130) | data formatting | bytes 262144 | tf_op jit(solution)/shard_map/all_to_all | solution.py:173
  247.0 0.9 copy.265
  247.9 1.5 fusion.46
  249.4 0.7 copy-done.1
  250.1 6.1 %bitcast_select_fusion = (bf16[8,256,1024]{2,1,0:T(8,128)(2,1)}, bf16[8,256,1024]{2,1,0:T(8,128)(2,1)}) fusion(bf16[8,256,1024]{2,1,0:T(8,128)(2,1)} %fusion.44, pred[8,256]{1,0:T(8,128)(4,1)S(1)} %compare_reduce_fusion, bf16[8,256,1024]{2,1,0:T(8,128)(2,1)S(1)} %fusion.46, bf16[8,256,1024]{2,1,0:T(8,128)(2,1)} %bitcast.123, ...), kind=kLoop, calls=%fused_computation.7 | loop fusion | flops 4194304 | bytes 25167872 | tf_op jit(solution)/shard_map/jit(_where)/select_n | solution.py:202
  256.1 11.8 %reduce-scatter.4.cloned.1.call-done = bf16[8,8192]{1,0:T(8,128)(2,1)} async-done(((bf16[32,8192]{1,0:T(8,128)(2,1)}), bf16[8,8192]{1,0:T(8,128)(2,1)}) %reduce-scatter.4.cloned.1.call-update) | async-done | bytes 131088
  268.0 1.0 fusion.28
  269.0 0.8 copy.235
  (92 shorter events, 10.6 us)
Async XLA Ops:
  7.2 239.4 %copy-start = (bf16[512,2048]{1,0:T(8,128)(2,1)S(1)}, bf16[512,2048]{1,0:T(8,128)(2,1)}, u32[]{:S(2)}) copy-start(bf16[512,2048]{1,0:T(8,128)(2,1)} %param.16) | copy-start | bytes 6291460
  29.6 4.9 %copy-start.4 = (bf16[2048,256]{1,0:T(8,128)(2,1)S(1)}, bf16[2048,256]{1,0:T(8,128)(2,1)}, u32[]{:S(2)}) copy-start(bf16[2048,256]{1,0:T(8,128)(2,1)} %param.15) | copy-start | bytes 3145732
  32.1 8.1 %copy-start.2 = (s32[32,512]{1,0:T(8,128)S(1)}, s32[32,512]{1,0:T(8,128)}, u32[]{:S(2)}) copy-start(s32[32,512]{1,0:T(8,128)} %param.21) | copy-start | bytes 196612
  36.0 10.9 %all-to-all-start.1 = ((bf16[32,4,1024]{2,1,0:T(4,128)(2,1)}), bf16[32,4,1024]{2,1,0:T(4,128)(2,1)S(1)}, u32[]{:S(2)}, u32[]{:S(2)}) async-start(bf16[32,4,1024]{2,1,0:T(4,128)(2,1)} %copy.193), calls=%async_computation.1 | async-start | bytes 524288 | tf_op jit(solution)/shard_map/all_to_all | solution.py:108
  46.9 63.2 %all-to-all-start = ((bf16[128,1,16,1024]{3,2,1,0:T(8,128)(2,1)}), bf16[128,1,16,1024]{3,2,1,0:T(8,128)(2,1)}, u32[]{:S(2)}, u32[]{:S(2)}) async-start(bf16[128,1,16,1024]{3,2,1,0:T(8,128)(2,1)} %bitcast.125), calls=%async_computation | async-start | bytes 8388608 | tf_op jit(solution)/shard_map/all_to_all | solution.py:80
  110.1 58.5 %all-to-all-start.2 = ((bf16[128,1,16,1024]{3,2,1,0:T(8,128)(2,1)}), bf16[128,1,16,1024]{3,2,1,0:T(8,128)(2,1)}, u32[]{:S(2)}, u32[]{:S(2)}) async-start(bf16[128,1,16,1024]{3,2,1,0:T(8,128)(2,1)} %bitcast.124), calls=%async_computation.2 | async-start | bytes 8388608 | tf_op jit(solution)/shard_map/all_to_all | solution.py:81
  117.7 8.6 %copy-start.5 = (bf16[8,4,8,2,128]{4,3,2,1,0:T(2,128)(2,1)}, bf16[8,4,8,2,128]{4,3,2,1,0:T(2,128)(2,1)S(1)}, u32[]{:S(2)}) copy-start(bf16[8,4,8,2,128]{4,3,2,1,0:T(2,128)(2,1)S(1)} %reshape.309) | copy-start | bytes 393220
  179.2 22.5 %copy-start.6 = (bf16[8,4,8,2,128]{4,3,2,1,0:T(2,128)(2,1)S(1)}, bf16[8,4,8,2,128]{4,3,2,1,0:T(2,128)(2,1)}, u32[]{:S(2)}) copy-start(bf16[8,4,8,2,128]{4,3,2,1,0:T(2,128)(2,1)} %copy-done.5) | copy-start | bytes 393220
  179.5 3.6 %collective-permute-start.10 = (f32[8,8,2,4]{1,0,3,2:T(8,128)S(1)}, f32[8,8,2,4]{1,0,3,2:T(8,128)S(1)}, u32[]{:S(2)}, u32[]{:S(2)}) collective-permute-start(f32[8,8,2,4]{1,0,3,2:T(8,128)S(1)} %copy.223), channel_id=1, source_target_pairs={{0,1},{1,0},{2,3},{3,2},{4,5},{5,4},{6,7},{7,6},{8,9},{9,8},{10,11... | collective-permute-start | bytes 6152 | tf_op jit(solution)/shard_map/ppermute | solution.py:137
  179.6 3.5 %collective-permute-start.1 = (f32[8,8,2,4]{1,0,3,2:T(8,128)S(1)}, f32[8,8,2,4]{1,0,3,2:T(8,128)S(1)}, u32[]{:S(2)}, u32[]{:S(2)}) collective-permute-start(f32[8,8,2,4]{1,0,3,2:T(8,128)S(1)} %copy.200), channel_id=1, source_target_pairs={{0,1},{1,0},{2,3},{3,2},{4,5},{5,4},{6,7},{7,6},{8,9},{9,8},{10,11... | collective-permute-start | bytes 6152 | tf_op jit(solution)/shard_map/ppermute | solution.py:137
  182.9 8.9 %collective-permute-start = (f32[8,8,2,4,128]{4,3,2,1,0:T(4,128)S(1)}, f32[8,8,2,4,128]{4,3,2,1,0:T(4,128)S(1)}, u32[]{:S(2)}, u32[]{:S(2)}) collective-permute-start(f32[8,8,2,4,128]{4,3,2,1,0:T(4,128)S(1)} %fusion), channel_id=1, source_target_pairs={{0,1},{1,0},{2,3},{3,2},{4,5},{5,4},{6,7},{7,6},{8,9},{9,8},{10,11... | collective-permute-start | bytes 786440 | tf_op jit(solution)/shard_map/ppermute | solution.py:137
  183.1 4.1 %collective-permute-start.11 = (f32[8,8,2,4]{1,0,3,2:T(8,128)S(1)}, f32[8,8,2,4]{1,0,3,2:T(8,128)S(1)}, u32[]{:S(2)}, u32[]{:S(2)}) collective-permute-start(f32[8,8,2,4]{1,0,3,2:T(8,128)S(1)} %get-tuple-element.42), channel_id=1, source_target_pairs={{0,2},{1,3},{2,0},{3,1},{4,6},{5,7},{6,4},{7,5},{8,10},{9,11},{10,... | collective-permute-start | bytes 6152 | tf_op jit(solution)/shard_map/ppermute | solution.py:137
  183.2 4.4 %collective-permute-start.3 = (f32[8,8,2,4]{1,0,3,2:T(8,128)S(1)}, f32[8,8,2,4]{1,0,3,2:T(8,128)S(1)}, u32[]{:S(2)}, u32[]{:S(2)}) collective-permute-start(f32[8,8,2,4]{1,0,3,2:T(8,128)S(1)} %get-tuple-element.45), channel_id=1, source_target_pairs={{0,2},{1,3},{2,0},{3,1},{4,6},{5,7},{6,4},{7,5},{8,10},{9,11},{10,... | collective-permute-start | bytes 6152 | tf_op jit(solution)/shard_map/ppermute | solution.py:137
  188.2 6.0 %collective-permute-start.12 = (f32[8,8,2,4]{1,0,3,2:T(8,128)}, f32[8,8,2,4]{1,0,3,2:T(8,128)}, u32[]{:S(2)}, u32[]{:S(2)}) collective-permute-start(f32[8,8,2,4]{1,0,3,2:T(8,128)} %get-tuple-element.38), channel_id=1, source_target_pairs={{0,4},{1,5},{2,6},{3,7},{4,0},{5,1},{6,2},{7,3},{8,12},{9,13},{10,... | collective-permute-start | bytes 6152 | tf_op jit(solution)/shard_map/ppermute | solution.py:137
  189.0 6.1 %collective-permute-start.5 = (f32[8,8,2,4]{1,0,3,2:T(8,128)}, f32[8,8,2,4]{1,0,3,2:T(8,128)}, u32[]{:S(2)}, u32[]{:S(2)}) collective-permute-start(f32[8,8,2,4]{1,0,3,2:T(8,128)} %get-tuple-element.41), channel_id=1, source_target_pairs={{0,4},{1,5},{2,6},{3,7},{4,0},{5,1},{6,2},{7,3},{8,12},{9,13},{10,... | collective-permute-start | bytes 6152 | tf_op jit(solution)/shard_map/ppermute | solution.py:137
  192.1 7.6 %collective-permute-start.2 = (f32[8,8,2,4,128]{4,3,2,1,0:T(4,128)S(1)}, f32[8,8,2,4,128]{4,3,2,1,0:T(4,128)S(1)}, u32[]{:S(2)}, u32[]{:S(2)}) collective-permute-start(f32[8,8,2,4,128]{4,3,2,1,0:T(4,128)S(1)} %multiply_add_fusion.3), channel_id=1, source_target_pairs={{0,2},{1,3},{2,0},{3,1},{4,6},{5,7},{6,4},{7,5},{8,10},{9,11},{10,... | collective-permute-start | bytes 786440 | tf_op jit(solution)/shard_map/ppermute | solution.py:137
  196.5 6.4 %collective-permute-start.13 = (f32[8,8,2,4]{1,0,3,2:T(8,128)}, f32[8,8,2,4]{1,0,3,2:T(8,128)}, u32[]{:S(2)}, u32[]{:S(2)}) collective-permute-start(f32[8,8,2,4]{1,0,3,2:T(8,128)} %get-tuple-element.34), channel_id=1, source_target_pairs={{0,8},{1,9},{2,10},{3,11},{4,12},{5,13},{6,14},{7,15},{8,0},{9,1},... | collective-permute-start | bytes 6152 | tf_op jit(solution)/shard_map/ppermute | solution.py:137
  198.6 4.3 %collective-permute-start.7 = (f32[8,8,2,4]{1,0,3,2:T(8,128)}, f32[8,8,2,4]{1,0,3,2:T(8,128)}, u32[]{:S(2)}, u32[]{:S(2)}) collective-permute-start(f32[8,8,2,4]{1,0,3,2:T(8,128)} %get-tuple-element.37), channel_id=1, source_target_pairs={{0,8},{1,9},{2,10},{3,11},{4,12},{5,13},{6,14},{7,15},{8,0},{9,1},... | collective-permute-start | bytes 6152 | tf_op jit(solution)/shard_map/ppermute | solution.py:137
  200.1 8.3 %collective-permute-start.4 = (f32[8,8,2,4,128]{4,3,2,1,0:T(4,128)S(1)}, f32[8,8,2,4,128]{4,3,2,1,0:T(4,128)S(1)}, u32[]{:S(2)}, u32[]{:S(2)}) collective-permute-start(f32[8,8,2,4,128]{4,3,2,1,0:T(4,128)S(1)} %multiply_add_fusion.2), channel_id=1, source_target_pairs={{0,4},{1,5},{2,6},{3,7},{4,0},{5,1},{6,2},{7,3},{8,12},{9,13},{10,... | collective-permute-start | bytes 786440 | tf_op jit(solution)/shard_map/ppermute | solution.py:137
  204.3 8.6 %collective-permute-start.9 = (f32[8,8,2,4]{1,0,3,2:T(8,128)S(1)}, f32[8,8,2,4]{1,0,3,2:T(8,128)}, u32[]{:S(2)}, u32[]{:S(2)}) collective-permute-start(f32[8,8,2,4]{1,0,3,2:T(8,128)S(1)} %get-tuple-element.33), channel_id=1, source_target_pairs={{0,16},{1,17},{2,18},{3,19},{4,20},{5,21},{6,22},{7,23},{8,24},{9,... | collective-permute-start | bytes 6152 | tf_op jit(solution)/shard_map/ppermute | solution.py:137
  208.8 6.6 %collective-permute-start.6 = (f32[8,8,2,4,128]{4,3,2,1,0:T(4,128)S(1)}, f32[8,8,2,4,128]{4,3,2,1,0:T(4,128)S(1)}, u32[]{:S(2)}, u32[]{:S(2)}) collective-permute-start(f32[8,8,2,4,128]{4,3,2,1,0:T(4,128)S(1)} %multiply_add_fusion.1), channel_id=1, source_target_pairs={{0,8},{1,9},{2,10},{3,11},{4,12},{5,13},{6,14},{7,15},{8,0},{9,1},... | collective-permute-start | bytes 786440 | tf_op jit(solution)/shard_map/ppermute | solution.py:137
  212.4 6.0 %collective-permute-start.14 = (f32[8,8,2,4]{1,0,3,2:T(8,128)}, f32[8,8,2,4]{1,0,3,2:T(8,128)S(1)}, u32[]{:S(2)}, u32[]{:S(2)}) collective-permute-start(f32[8,8,2,4]{1,0,3,2:T(8,128)} %get-tuple-element.30), channel_id=1, source_target_pairs={{0,16},{1,17},{2,18},{3,19},{4,20},{5,21},{6,22},{7,23},{8,24},{9,... | collective-permute-start | bytes 6152 | tf_op jit(solution)/shard_map/ppermute | solution.py:137
  215.7 8.0 %collective-permute-start.8 = (f32[8,8,2,4,128]{4,3,2,1,0:T(4,128)S(1)}, f32[8,8,2,4,128]{4,3,2,1,0:T(4,128)S(1)}, u32[]{:S(2)}, u32[]{:S(2)}) collective-permute-start(f32[8,8,2,4,128]{4,3,2,1,0:T(4,128)S(1)} %multiply_add_fusion), channel_id=1, source_target_pairs={{0,16},{1,17},{2,18},{3,19},{4,20},{5,21},{6,22},{7,23},{8,24},{9,... | collective-permute-start | bytes 786440 | tf_op jit(solution)/shard_map/ppermute | solution.py:137
  230.9 9.3 %all-to-all-start.3 = ((bf16[4,2,8192]{2,1,0:T(2,128)(2,1)}), bf16[4,2,8192]{2,1,0:T(2,128)(2,1)S(1)}, u32[]{:S(2)}, u32[]{:S(2)}) async-start(bf16[4,2,8192]{2,1,0:T(2,128)(2,1)} %reshape.368), calls=%async_computation.3 | async-start | bytes 262144 | tf_op jit(solution)/shard_map/all_to_all | solution.py:173
  234.3 33.7 %reduce-scatter.4.cloned.1.call-start = ((), (), s32[]{:S(2)}) async-start(), calls=%async_computation.5 | async-start | bytes 655360
  247.9 2.2 copy-start.1
  250.1 17.9 %copy-start.3 = (bf16[8,4,2048]{2,1,0:T(4,128)(2,1)S(1)}, bf16[8,4,2048]{2,1,0:T(4,128)(2,1)}, u32[]{:S(2)}) copy-start(bf16[8,4,2048]{2,1,0:T(4,128)(2,1)} %param.11) | copy-start | bytes 393220
Sparse Core Ops, SparseCore 0:
  248.0 19.9 reduce-scatter.3

commit v2 on v1

--- a/solution.py
+++ b/solution.py
@@ -75,24 +75,29 @@
     arrival_src = my_home // pages_dev
     held_here = (home_table // pages_dev) == device_index
     send_pick = jnp.sum(jnp.where(held_here, home_table % pages_dev, 0), axis=1)
-    outgoing_k = pool_keys[send_pick].reshape(devices, per_peer, page_len, kv_width)
-    outgoing_v = pool_values[send_pick].reshape(devices, per_peer, page_len, kv_width)
-    incoming_k = lax.all_to_all(outgoing_k, ("req", "seq"), split_axis=0, concat_axis=0, tiled=True)
-    incoming_v = lax.all_to_all(outgoing_v, ("req", "seq"), split_axis=0, concat_axis=0, tiled=True)
-    cache_keys = incoming_k.reshape(pages_dev, page_len, kv_width)[arrival_src].reshape(
-        local_reqs, positions, kv_width
-    )
-    cache_values = incoming_v.reshape(pages_dev, page_len, kv_width)[arrival_src].reshape(
-        local_reqs, positions, kv_width
-    )
+    outgoing = jnp.stack([pool_keys[send_pick], pool_values[send_pick]], axis=1)
+    outgoing = outgoing.reshape(devices, per_peer, 2, page_len, kv_width)
+    incoming = lax.all_to_all(outgoing, ("req", "seq"), split_axis=0, concat_axis=0, tiled=True)
+    arrived = incoming.reshape(pages_dev, 2, page_len, kv_width)[arrival_src]
+    arrived = arrived.reshape(local_reqs, pages_home, 2, page_len, kv_width)
+    cache_keys = arrived[:, :, 0].reshape(local_reqs, positions, kv_width)
+    cache_values = arrived[:, :, 1].reshape(local_reqs, positions, kv_width)
     tokens_wide = new_tokens.astype(jnp.float32)
     square_mean = jnp.mean(tokens_wide * tokens_wide, axis=-1, keepdims=True)
     normed = (tokens_wide * lax.rsqrt(square_mean + NORM_EPS) * norm_gain).astype(jnp.bfloat16)
     new_index = jnp.arange(new_count, dtype=jnp.int32)
-    row_block = lax.all_gather(normed, "req", axis=0, tiled=True)
+    def shift(value, places):
+        if places % req_count == 0:
+            return value
+        pairs = [(i, (i + places) % req_count) for i in range(req_count)]
+        return lax.ppermute(value, "req", pairs)
+
+    row_block = jnp.concatenate([shift(normed, k) for k in range(req_count)], axis=0)
     row_count = row_block.shape[0]
     flat_rows = row_block.reshape(row_count * new_count, model_width)
-    places = slot_lengths[:, None] + new_index[None, :]
+    row_group = (req_index - jnp.arange(req_count, dtype=jnp.int32)) % req_count
+    row_lengths = jnp.take(slot_lengths.reshape(req_count, local_reqs), row_group, axis=0).reshape(-1)
+    places = row_lengths[:, None] + new_index[None, :]
     queries_now = jnp.dot(flat_rows, w_query, preferred_element_type=jnp.float32).reshape(
         row_count, new_count, query_cols // HD, HD
     )
@@ -105,8 +110,11 @@
     queries_now = rotate(queries_now, places).reshape(row_count, new_count, query_cols)
     keys_now = rotate(keys_now, places).reshape(row_count, new_count, key_cols)
     projected = jnp.concatenate([queries_now, keys_now, values_now], axis=-1).astype(jnp.bfloat16)
-    owned_rows = lax.all_to_all(projected, "req", split_axis=0, concat_axis=2, tiled=True)
-    owned_rows = owned_rows.reshape(local_reqs, new_count, req_count, query_cols + 2 * key_cols)
+    projected = projected.reshape(req_count, local_reqs, new_count, query_cols + 2 * key_cols)
+    by_shift = jnp.stack([shift(projected[k], -k) for k in range(req_count)], axis=0)
+    source_block = (jnp.arange(req_count, dtype=jnp.int32) - req_index) % req_count
+    owned_rows = jnp.take(by_shift, source_block, axis=0)
+    owned_rows = jnp.transpose(owned_rows, (1, 2, 0, 3))
     queries = owned_rows[..., :query_cols].reshape(local_reqs, new_count, KVH, groups, HD)
     fresh_keys = owned_rows[..., query_cols : query_cols + key_cols].reshape(
         local_reqs, new_count, KVH, HD
@@ -131,10 +139,22 @@
         grid_values,
         preferred_element_type=jnp.float32,
     )
+    stat_rows = row_peak.size // HD
     step = 1
     while step < seq_count:
         pairs = [(i, i ^ step) for i in range(seq_count)]
-        peer_peak, peer_mass, peer_sum = lax.ppermute((row_peak, row_mass, gathered_sum), "seq", pairs)
+        packed = jnp.concatenate(
+            [
+                gathered_sum.reshape(-1, HD),
+                row_peak.reshape(stat_rows, HD),
+                row_mass.reshape(stat_rows, HD),
+            ],
+            axis=0,
+        )
+        other = lax.ppermute(packed, "seq", pairs)
+        peer_sum = other[: gathered_sum.size // HD].reshape(gathered_sum.shape)
+        peer_peak = other[gathered_sum.size // HD : -stat_rows].reshape(row_peak.shape)
+        peer_mass = other[-stat_rows:].reshape(row_mass.shape)
         upper = (seq_index & step) != 0
         peak_lo = jnp.where(upper, peer_peak, row_peak)
         peak_hi = jnp.where(upper, row_peak, peer_peak)
@@ -170,18 +190,27 @@
         .reshape(local_reqs, new_count, KVH * groups * HD)
         .astype(jnp.bfloat16)
     )
-    headed = lax.all_to_all(attended, "req", split_axis=2, concat_axis=0, tiled=True)
-    row_count = lax.axis_size("req") * local_reqs
-    projected_out = lax.psum_scatter(
-        jnp.dot(
-            headed.reshape(row_count * new_count, -1), w_out, preferred_element_type=jnp.float32
-        )
-        .reshape(row_count, new_count, model_width)
-        .astype(jnp.bfloat16),
-        "req",
-        scatter_dimension=0,
-        tiled=True,
-    ).astype(jnp.float32)
+    head_cols = attended.shape[-1] // req_count
+    headed = jnp.concatenate(
+        [
+            shift(
+                lax.dynamic_slice_in_dim(
+                    attended, ((req_index + k) % req_count) * head_cols, head_cols, axis=2
+                ),
+                k,
+            )
+            for k in range(req_count)
+        ],
+        axis=0,
+    )
+    partial_out = (
+        jnp.dot(headed.reshape(row_count * new_count, -1), w_out, preferred_element_type=jnp.float32)
+        .reshape(req_count, local_reqs, new_count, model_width)
+        .astype(jnp.bfloat16)
+    )
+    projected_out = shift(partial_out[0], 0).astype(jnp.float32)
+    for k in range(1, req_count):
+        projected_out = projected_out + shift(partial_out[k], -k).astype(jnp.float32)
     out_hidden = (tokens_wide + projected_out).astype(jnp.bfloat16)
     new_hits = key_spots[None, :, None] == my_lengths[:, None, None] + new_index[None, None, :]
     filler = new_hits.astype(jnp.bfloat16)

time: 278 us -> 266 us (0.957)
  waiting for transfers between devices: 113 us -> 128 us
  starting transfers between devices: 42.7 us -> 29.4 us
  between operations: 14.5 us -> 1.38 us
  blocking collectives: 13.1 us -> 0 us
  matrix products: 15.4 us -> 22.9 us
  local copies, waits for them, and re-layouts: 58.3 us -> 61.9 us
    ppermute x15 -> x17, waiting for transfers between devices: 11.9 us -> 128 us  [the longest x12 104 us: shift(): return lax.ppermute(value, 'req', pairs)]
    all_to_all x4 -> x1, waiting for transfers between devices: 89.2 us -> 0.01 us  [shards(): lax.all_to_all(outgoing, ('req', 'seq'), split_axis=0, concat_axis=0, til...]
    all_to_all x4 -> x1, starting transfers between devices: 25.1 us -> 10.7 us  [shards(): lax.all_to_all(outgoing, ('req', 'seq'), split_axis=0, concat_axis=0, til...]
    all_gather x1 -> x0, blocking collectives: 13.1 us -> none  [shards(): row_block = lax.all_gather(normed, 'req', axis=0, tiled=True)]
    unnamed x2 -> x0, waiting for transfers between devices: 11.9 us -> none
    slice x0 -> x8, local copies, waits for them, and re-layouts: none -> 11.1 us  [the longest x1 5.43 us: shards(): cache_values = arrived[:, :, 1].reshape(local_reqs, positions, kv_width)]
    unnamed x20 -> x25, local copies, waits for them, and re-layouts: 16.4 us -> 6.86 us
    reshape x0 -> x1, other arithmetic: none -> 7.49 us  [shards(): outgoing = outgoing.reshape(devices, per_peer, 2, page_len, kv_width)]
  transfers between devices with their start and end apart: 20 -> 18, of which waited for: 13 -> 11; matrix products, arithmetic and copies ran while one was open for 18% -> 12% of each run, Pallas kernels for 0% -> 0%
where the time goes in v2:
time: 266 us; the launch traced here: 265 us
  waiting for transfers between devices  128 us (48%)
  local copies, waits for them, and re-layouts  61.9 us (23%)
  starting transfers between devices  29.4 us (11%)
  matrix products  22.9 us (9%)
  other arithmetic  20.7 us (8%)
    ppermute x12, waiting for transfers between devices, shift(): return lax.ppermute(value, 'req', pairs)  104 us
    ppermute x5, waiting for transfers between devices, shards(): other = lax.ppermute(packed, 'seq', pairs)  23.9 us
    ppermute x12, starting transfers between devices, shift(): return lax.ppermute(value, 'req', pairs)  15.5 us
    all_to_all x1, starting transfers between devices, shards(): lax.all_to_all(outgoing, ('req', 'seq'), split_axis=0, concat_axis=0, til...  10.7 us
    gather x2, local copies, waits for them, and re-layouts, shards(): outgoing = jnp.stack([pool_keys[send_pick], pool_values[send_pick]], axis=1)  10 us
    gather x1, local copies, waits for them, and re-layouts, shards(): arrived = incoming.reshape(pages_dev, 2, page_len, kv_width)[arrival_src]  10 us
    reshape x1, other arithmetic, shards(): outgoing = outgoing.reshape(devices, per_peer, 2, page_len, kv_width)  7.49 us
    unnamed x25, local copies, waits for them, and re-layouts  6.86 us
  transfers between devices with their start and end apart: 18, of which 11 were waited for; matrix products, arithmetic and copies ran while one was open for 12% of the time, Pallas kernels for 0%

profile of v2, /device:TPU:32, one launch (start us, length us, event | category | flops | bytes accessed | tf_op | source)
XLA Modules:
  0.0 264.6 jit_solution(5137333303807264241)
XLA Ops:
  0.7 0.9 select_reduce_fusion
  1.6 1.5 gather_fusion
  3.3 0.6 fusion.20
  4.0 5.0 %gather_fusion.1 = bf16[128,16,1024]{2,1,0:T(8,128)(2,1)} fusion(bf16[128,16,1024]{2,1,0:T(8,128)(2,1)} %param.17, s32[1024]{0:T(1024)S(1)} %pad_clamp_fusion.3), kind=kCustom, calls=%fused_computation.1 | custom fusion | bytes 8389120 | tf_op jit(solution)/shard_map/gather | solution.py:78
  9.0 5.0 %gather_fusion.2 = bf16[128,16,1024]{2,1,0:T(8,128)(2,1)} fusion(bf16[128,16,1024]{2,1,0:T(8,128)(2,1)} %param.18, s32[1024]{0:T(1024)S(1)} %pad_clamp_fusion.3), kind=kCustom, calls=%fused_computation.2 | custom fusion | bytes 8389120 | tf_op jit(solution)/shard_map/gather | solution.py:78
  14.0 7.5 %maximum_bitcast_fusion = bf16[128,1,2,16,1024]{4,3,2,1,0:T(8,128)(2,1)} fusion(bf16[128,1,16,1024]{3,2,1,0:T(8,128)(2,1)} %bitcast.154, bf16[128,1,16,1024]{3,2,1,0:T(8,128)(2,1)} %bitcast.153), kind=kLoop, calls=%fused_computation.6 | loop fusion | flops 4194304 | bytes 16777216 | tf_op jit(solution)/shard_map/reshape | solution.py:79
  21.5 10.7 %all-to-all-start = ((bf16[128,1,2,16,1024]{4,3,2,1,0:T(8,128)(2,1)}), bf16[128,1,2,16,1024]{4,3,2,1,0:T(8,128)(2,1)}, u32[]{:S(2)}, u32[]{:S(2)}) async-start(bf16[128,1,2,16,1024]{4,3,2,1,0:T(8,128)(2,1)} %maximum_bitcast_fusion), calls=%async_computation | async-start | bytes 16777216 | tf_op jit(solution)/shard_map/all_to_all | solution.py:80
  32.6 1.5 collective-permute-start
  34.1 2.7 %collective-permute-start.1 = (bf16[8,4,2048]{2,0,1:T(8,128)(2,1)S(1)}, bf16[8,4,2048]{2,0,1:T(8,128)(2,1)S(1)}, u32[]{:S(2)}, u32[]{:S(2)}) collective-permute-start(bf16[8,4,2048]{2,0,1:T(8,128)(2,1)S(1)} %fusion.29), channel_id=1, source_target_pairs={{0,64},{32,96},{64,0},{96,32},{1,65},{33,97},{65,1},{97,33},{2,66}... | collective-permute-start | bytes 393224 | tf_op jit(solution)/shard_map/ppermute | solution.py:93
  36.9 1.4 collective-permute-start.2
  40.2 3.9 %copy.328 = bf16[512,2048]{1,0:T(8,128)(2,1)} copy(bf16[512,2048]{0,1:T(8,128)(2,1)} %bitcast.160) | data formatting | bytes 4194304 | tf_op jit(solution)/shard_map/dot_general | solution.py:101
  44.2 2.3 copy.329
  46.4 85.3 %collective-permute-done = bf16[8,4,2048]{2,0,1:T(8,128)(2,1)S(1)} collective-permute-done((bf16[8,4,2048]{2,0,1:T(8,128)(2,1)S(1)}, bf16[8,4,2048]{2,0,1:T(8,128)(2,1)S(1)}, u32[]{:S(2)}, u32[]{:S(2)}) %collective-permute-start) | collective-permute-done | bytes 131104 | tf_op jit(solution)/shard_map/ppermute | solution.py:93
  131.8 11.8 %collective-permute-done.1 = bf16[8,4,2048]{2,0,1:T(8,128)(2,1)S(1)} collective-permute-done((bf16[8,4,2048]{2,0,1:T(8,128)(2,1)S(1)}, bf16[8,4,2048]{2,0,1:T(8,128)(2,1)S(1)}, u32[]{:S(2)}, u32[]{:S(2)}) %collective-permute-start.1) | collective-permute-done | bytes 131104 | tf_op jit(solution)/shard_map/ppermute | solution.py:93
  143.6 1.9 fusion.21
  145.7 2.5 fusion.23
  148.5 1.2 convolution_convert_fusion.1
  149.9 1.9 collective-permute-start.5
  151.8 2.2 collective-permute-done.3
  154.1 1.7 collective-permute-done.4
  155.8 0.9 collective-permute-done.5
  157.7 10.0 %gather_fusion.3 = bf16[128,2,16,1024]{3,2,1,0:T(8,128)(2,1)} fusion(bf16[128,2,16,1024]{3,2,1,0:T(8,128)(2,1)} %bitcast.7, s32[1024]{0:T(1024)S(1)} %pad_clamp_fusion.2), kind=kCustom, calls=%fused_computation.3 | custom fusion | bytes 16777728 | tf_op jit(solution)/shard_map/gather | solution.py:81
  167.7 5.4 %fusion.71 = (bf16[8,16,1,16,1024]{4,3,2,1,0:T(8,128)(2,1)}, bf16[8,16,1,16,1024]{4,3,2,1,0:T(8,128)(2,1)S(1)}) fusion(bf16[8,16,2,16,1024]{4,3,2,1,0:T(8,128)(2,1)} %bitcast.150), kind=kLoop, calls=%fused_computation.200 | loop fusion | bytes 16777216 | tf_op jit(solution)/shard_map/slice | solution.py:84
  173.1 1.1 copy.344
  174.3 0.9 copy-done.1
  175.5 2.3 fusion.74
  178.3 1.8 fusion.39
  180.1 3.3 %copy.345 = bf16[256,8,8,128]{3,2,1,0:T(8,128)(2,1)S(1)} copy(bf16[256,8,8,128]{3,1,2,0:T(8,128)(2,1)} %bitcast.149) | data formatting | bytes 8388608
  183.4 2.3 bitcast_bitcast_fusion
  186.4 2.8 %fusion = f32[8,8,2,4,128]{4,3,2,1,0:T(4,128)S(1)} fusion(bf16[8,256,8,128,1]{3,2,1,0,4:T(8,128)(2,1)} %bitcast_bitcast_fusion, bf16[8,8,2,4,256]{4,2,3,1,0:T(2,128)(2,1)S(1)} %get-tuple-element.44), kind=kOutput, calls=%fused_computation.11 | convolution fusion | flops 33554432 | bytes 4718592 | tf_op jit(solution)/shard_map/rkgtp,rpkd->rkgtd/dot_general | solution.py:136
  189.7 1.4 collective-permute-done.6
  191.1 1.3 multiply_add_fusion.8
  193.1 1.0 slice.158
  194.4 0.7 pad_maximum_fusion.2
  195.2 8.7 %collective-permute-done.7 = f32[520,128]{1,0:T(8,128)} collective-permute-done((f32[520,128]{1,0:T(8,128)}, f32[520,128]{1,0:T(8,128)}, u32[]{:S(2)}, u32[]{:S(2)}) %collective-permute-start.7) | collective-permute-done | bytes 266272 | tf_op jit(solution)/shard_map/ppermute | solution.py:154
  203.9 1.3 multiply_add_fusion.7
  206.0 1.0 slice.161
  207.3 3.2 %collective-permute-start.8 = (f32[520,128]{1,0:T(8,128)S(1)}, f32[520,128]{1,0:T(8,128)S(1)}, u32[]{:S(2)}, u32[]{:S(2)}) collective-permute-start(f32[520,128]{1,0:T(8,128)S(1)} %pad_maximum_fusion.3), channel_id=1, source_target_pairs={{0,4},{1,5},{2,6},{3,7},{4,0},{5,1},{6,2},{7,3},{8,12},{9,13},{10,... | collective-permute-start | bytes 798728 | tf_op jit(solution)/shard_map/ppermute | solution.py:154
  210.7 5.8 %collective-permute-done.8 = f32[520,128]{1,0:T(8,128)S(1)} collective-permute-done((f32[520,128]{1,0:T(8,128)S(1)}, f32[520,128]{1,0:T(8,128)S(1)}, u32[]{:S(2)}, u32[]{:S(2)}) %collective-permute-start.8) | collective-permute-done | bytes 266272 | tf_op jit(solution)/shard_map/ppermute | solution.py:154
  216.5 0.7 copy-done.4
  217.2 0.6 multiply_add_fusion.6
  218.5 1.0 slice.164
  219.8 0.7 pad_maximum_fusion.4
  220.8 0.7 reshape.894
  221.5 6.0 %collective-permute-done.9 = f32[520,128]{1,0:T(8,128)} collective-permute-done((f32[520,128]{1,0:T(8,128)}, f32[520,128]{1,0:T(8,128)}, u32[]{:S(2)}, u32[]{:S(2)}) %collective-permute-start.9) | collective-permute-done | bytes 266272 | tf_op jit(solution)/shard_map/ppermute | solution.py:154
  227.6 0.8 fusion.58
  229.1 1.0 slice.167
  230.4 0.7 pad_maximum_fusion.5
  231.1 1.9 fusion.40
  233.1 1.4 copy.291
  234.9 0.8 reshape.900
  235.9 0.8 reshape.899
  237.5 1.8 collective-permute-done.10
  239.4 0.8 fusion.72
  242.2 1.0 slice.170
  243.2 0.8 fusion.10
  244.1 0.9 collective-permute-start.11
  245.1 2.6 collective-permute-start.12
  248.0 5.2 %bitcast_select_fusion = bf16[8,256,1024]{2,1,0:T(8,128)(2,1)} fusion(bf16[8,16,1,16,1024]{4,3,2,1,0:T(8,128)(2,1)} %get-tuple-element.42, pred[8,256]{1,0:T(8,128)(4,1)S(1)} %compare_reduce_fusion, bf16[8,4,1024]{2,1,0:T(4,128)(2,1)S(1)} %reshape_reshape.7, s32[8,4]{1,0:T(8,128)S(1)} %iota_add_fusion, s32[256]{0:T(256)S(1)} %copy-done.7), kind=kOutput, calls=%fused_computation.9 | convolution fusion | flops 20979712 | bytes 8457344 | tf_op jit(solution)/shard_map/rpt,rtc->rpc/dot_general | solution.py:223
  253.6 1.3 collective-permute-start.14
  254.9 2.6 collective-permute-start.15
  257.6 3.9 %bitcast_select_fusion.1 = bf16[8,256,1024]{2,1,0:T(8,128)(2,1)} fusion(bf16[8,16,1,16,1024]{4,3,2,1,0:T(8,128)(2,1)S(1)} %copy-done.2, pred[8,256]{1,0:T(8,128)(4,1)S(1)} %compare_reduce_fusion, bf16[8,4,1024]{2,1,0:T(4,128)(2,1)S(1)} %reshape_reshape.6, s32[8,4]{1,0:T(8,128)S(1)} %iota_add_fusion, s32[256]{0:T(256)S(1)} %copy-done.7), kind=kOutput, calls=%fused_computation.10 | convolution fusion | flops 20979712 | bytes 8457344 | tf_op jit(solution)/shard_map/rpt,rtc->rpc/dot_general | solution.py:217
  261.5 2.3 collective-permute-done.16
  263.9 0.8 copy.317
  (145 shorter events, 15.1 us)
Async XLA Ops:
  0.6 252.5 %copy-start = (bf16[512,2048]{1,0:T(8,128)(2,1)S(1)}, bf16[512,2048]{1,0:T(8,128)(2,1)}, u32[]{:S(2)}) copy-start(bf16[512,2048]{1,0:T(8,128)(2,1)} %param.16) | copy-start | bytes 6291460
  21.5 10.7 %copy-start.3 = (bf16[8,4,2048]{2,1,0:T(4,128)(2,1)S(1)}, bf16[8,4,2048]{2,1,0:T(4,128)(2,1)}, u32[]{:S(2)}) copy-start(bf16[8,4,2048]{2,1,0:T(4,128)(2,1)} %param.11) | copy-start | bytes 393220
  21.5 10.9 %copy-start.8 = (f32[2048]{0:T(1024)S(1)}, f32[2048]{0:T(1024)}, u32[]{:S(2)}) copy-start(f32[2048]{0:T(1024)} %param.12) | copy-start | bytes 24580
  21.5 136.1 %all-to-all-start = ((bf16[128,1,2,16,1024]{4,3,2,1,0:T(8,128)(2,1)}), bf16[128,1,2,16,1024]{4,3,2,1,0:T(8,128)(2,1)}, u32[]{:S(2)}, u32[]{:S(2)}) async-start(bf16[128,1,2,16,1024]{4,3,2,1,0:T(8,128)(2,1)} %maximum_bitcast_fusion), calls=%async_computation | async-start | bytes 16777216 | tf_op jit(solution)/shard_map/all_to_all | solution.py:80
  32.6 99.2 %collective-permute-start = (bf16[8,4,2048]{2,0,1:T(8,128)(2,1)S(1)}, bf16[8,4,2048]{2,0,1:T(8,128)(2,1)S(1)}, u32[]{:S(2)}, u32[]{:S(2)}) collective-permute-start(bf16[8,4,2048]{2,0,1:T(8,128)(2,1)S(1)} %fusion.29), channel_id=1, source_target_pairs={{0,32},{32,64},{64,96},{96,0},{1,33},{33,65},{65,97},{97,1},{2,34}... | collective-permute-start | bytes 393224 | tf_op jit(solution)/shard_map/ppermute | solution.py:93
  34.1 109.4 %collective-permute-start.1 = (bf16[8,4,2048]{2,0,1:T(8,128)(2,1)S(1)}, bf16[8,4,2048]{2,0,1:T(8,128)(2,1)S(1)}, u32[]{:S(2)}, u32[]{:S(2)}) collective-permute-start(bf16[8,4,2048]{2,0,1:T(8,128)(2,1)S(1)} %fusion.29), channel_id=1, source_target_pairs={{0,64},{32,96},{64,0},{96,32},{1,65},{33,97},{65,1},{97,33},{2,66}... | collective-permute-start | bytes 393224 | tf_op jit(solution)/shard_map/ppermute | solution.py:93
  36.9 106.7 %collective-permute-start.2 = (bf16[8,4,2048]{2,0,1:T(8,128)(2,1)S(1)}, bf16[8,4,2048]{2,0,1:T(8,128)(2,1)}, u32[]{:S(2)}, u32[]{:S(2)}) collective-permute-start(bf16[8,4,2048]{2,0,1:T(8,128)(2,1)S(1)} %fusion.29), channel_id=1, source_target_pairs={{0,96},{32,0},{64,32},{96,64},{1,97},{33,1},{65,33},{97,65},{2,98}... | collective-permute-start | bytes 393224 | tf_op jit(solution)/shard_map/ppermute | solution.py:93
  39.8 170.8 %copy-start.6 = (s32[256]{0:T(256)}, s32[256]{0:T(256)S(1)}, u32[]{:S(2)}) copy-start(s32[256]{0:T(256)S(1)} %iota_add_fusion.1) | copy-start | bytes 3076
  143.6 4.9 %copy-start.10 = (bf16[2048,256]{1,0:T(8,128)(2,1)S(1)}, bf16[2048,256]{1,0:T(8,128)(2,1)}, u32[]{:S(2)}) copy-start(bf16[2048,256]{1,0:T(8,128)(2,1)} %param.15) | copy-start | bytes 3145732
  149.7 4.3 %collective-permute-start.3 = (bf16[8,4,1024]{2,0,1:T(8,128)(2,1)S(1)}, bf16[8,4,1024]{2,0,1:T(8,128)(2,1)S(1)}, u32[]{:S(2)}, u32[]{:S(2)}) collective-permute-start(bf16[8,4,1024]{2,0,1:T(8,128)(2,1)S(1)} %get-tuple-element.68), channel_id=1, source_target_pairs={{0,96},{32,0},{64,32},{96,64},{1,97},{33,1},{65,33},{97,65},{2,98}... | collective-permute-start | bytes 196616 | tf_op jit(solution)/shard_map/ppermute | solution.py:93
  149.8 6.0 %collective-permute-start.4 = (bf16[8,4,1024]{2,0,1:T(8,128)(2,1)S(1)}, bf16[8,4,1024]{2,0,1:T(8,128)(2,1)S(1)}, u32[]{:S(2)}, u32[]{:S(2)}) collective-permute-start(bf16[8,4,1024]{2,0,1:T(8,128)(2,1)S(1)} %get-tuple-element.67), channel_id=1, source_target_pairs={{0,64},{32,96},{64,0},{96,32},{1,65},{33,97},{65,1},{97,33},{2,66}... | collective-permute-start | bytes 196616 | tf_op jit(solution)/shard_map/ppermute | solution.py:93
  149.9 6.8 %collective-permute-start.5 = (bf16[8,4,1024]{2,0,1:T(8,128)(2,1)S(1)}, bf16[8,4,1024]{2,0,1:T(8,128)(2,1)S(1)}, u32[]{:S(2)}, u32[]{:S(2)}) collective-permute-start(bf16[8,4,1024]{2,0,1:T(8,128)(2,1)S(1)} %get-tuple-element.66), channel_id=1, source_target_pairs={{0,32},{32,64},{64,96},{96,0},{1,33},{33,65},{65,97},{97,1},{2,34}... | collective-permute-start | bytes 196616 | tf_op jit(solution)/shard_map/ppermute | solution.py:93
  157.6 17.8 %copy-start.5 = (bf16[8,4,8,2,128]{4,3,2,1,0:T(2,128)(2,1)}, bf16[8,4,8,2,128]{4,3,2,1,0:T(2,128)(2,1)S(1)}, u32[]{:S(2)}) copy-start(bf16[8,4,8,2,128]{4,3,2,1,0:T(2,128)(2,1)S(1)} %reshape.876) | copy-start | bytes 393220
  173.1 2.1 copy-start.1
  189.3 1.8 collective-permute-start.6
  195.2 8.8 %collective-permute-start.7 = (f32[520,128]{1,0:T(8,128)}, f32[520,128]{1,0:T(8,128)}, u32[]{:S(2)}, u32[]{:S(2)}) collective-permute-start(f32[520,128]{1,0:T(8,128)} %pad_maximum_fusion.2), channel_id=1, source_target_pairs={{0,2},{1,3},{2,0},{3,1},{4,6},{5,7},{6,4},{7,5},{8,10},{9,11},{10,... | collective-permute-start | bytes 798728 | tf_op jit(solution)/shard_map/ppermute | solution.py:154
  207.3 9.2 %collective-permute-start.8 = (f32[520,128]{1,0:T(8,128)S(1)}, f32[520,128]{1,0:T(8,128)S(1)}, u32[]{:S(2)}, u32[]{:S(2)}) collective-permute-start(f32[520,128]{1,0:T(8,128)S(1)} %pad_maximum_fusion.3), channel_id=1, source_target_pairs={{0,4},{1,5},{2,6},{3,7},{4,0},{5,1},{6,2},{7,3},{8,12},{9,13},{10,... | collective-permute-start | bytes 798728 | tf_op jit(solution)/shard_map/ppermute | solution.py:154
  216.5 0.7 copy-start.4
  219.8 17.1 %copy-start.9 = (f32[4,128]{1,0:T(4,128)S(1)}, f32[4,128]{1,0:T(4,128)}, u32[]{:S(2)}) copy-start(f32[4,128]{1,0:T(4,128)} %get-tuple-element.55) | copy-start | bytes 6148
  220.5 7.0 %collective-permute-start.9 = (f32[520,128]{1,0:T(8,128)}, f32[520,128]{1,0:T(8,128)}, u32[]{:S(2)}, u32[]{:S(2)}) collective-permute-start(f32[520,128]{1,0:T(8,128)} %pad_maximum_fusion.4), channel_id=1, source_target_pairs={{0,8},{1,9},{2,10},{3,11},{4,12},{5,13},{6,14},{7,15},{8,0},{9,1},... | collective-permute-start | bytes 798728 | tf_op jit(solution)/shard_map/ppermute | solution.py:154
  231.1 8.2 %collective-permute-start.10 = (f32[520,128]{1,0:T(8,128)}, f32[520,128]{1,0:T(8,128)}, u32[]{:S(2)}, u32[]{:S(2)}) collective-permute-start(f32[520,128]{1,0:T(8,128)} %pad_maximum_fusion.5), channel_id=1, source_target_pairs={{0,16},{1,17},{2,18},{3,19},{4,20},{5,21},{6,22},{7,23},{8,24},{9,... | collective-permute-start | bytes 798728 | tf_op jit(solution)/shard_map/ppermute | solution.py:154
  243.1 4.8 %copy-start.7 = (s32[256]{0:T(256)S(1)}, s32[256]{0:T(256)}, u32[]{:S(2)}) copy-start(s32[256]{0:T(256)} %copy-done.6) | copy-start | bytes 3076
  244.1 9.0 %collective-permute-start.11 = (bf16[8,4,512]{2,0,1:T(8,128)(2,1)S(1)}, bf16[8,4,512]{2,0,1:T(8,128)(2,1)S(1)}, u32[]{:S(2)}, u32[]{:S(2)}) collective-permute-start(bf16[8,4,512]{2,0,1:T(8,128)(2,1)S(1)} %get-tuple-element.76), channel_id=1, source_target_pairs={{0,32},{32,64},{64,96},{96,0},{1,33},{33,65},{65,97},{97,1},{2,34}... | collective-permute-start | bytes 98312 | tf_op jit(solution)/shard_map/ppermute | solution.py:93
  245.1 8.1 %collective-permute-start.12 = (bf16[8,4,512]{2,0,1:T(8,128)(2,1)S(1)}, bf16[8,4,512]{2,0,1:T(8,128)(2,1)S(1)}, u32[]{:S(2)}, u32[]{:S(2)}) collective-permute-start(bf16[8,4,512]{2,0,1:T(8,128)(2,1)S(1)} %get-tuple-element.75), channel_id=1, source_target_pairs={{0,64},{32,96},{64,0},{96,32},{1,65},{33,97},{65,1},{97,33},{2,66}... | collective-permute-start | bytes 98312 | tf_op jit(solution)/shard_map/ppermute | solution.py:93
  247.7 5.5 %collective-permute-start.13 = (bf16[8,4,512]{2,0,1:T(8,128)(2,1)S(1)}, bf16[8,4,512]{2,0,1:T(8,128)(2,1)S(1)}, u32[]{:S(2)}, u32[]{:S(2)}) collective-permute-start(bf16[8,4,512]{2,0,1:T(8,128)(2,1)S(1)} %get-tuple-element.74), channel_id=1, source_target_pairs={{0,96},{32,0},{64,32},{96,64},{1,97},{33,1},{65,33},{97,65},{2,98}... | collective-permute-start | bytes 98312 | tf_op jit(solution)/shard_map/ppermute | solution.py:93
  253.1 4.4 %copy-start.2 = (bf16[8,16,1,16,1024]{4,3,2,1,0:T(8,128)(2,1)S(1)}, bf16[8,16,1,16,1024]{4,3,2,1,0:T(8,128)(2,1)}, u32[]{:S(2)}) copy-start(bf16[8,16,1,16,1024]{4,3,2,1,0:T(8,128)(2,1)} %copy-done.1) | copy-start | bytes 12582916
  253.6 7.8 %collective-permute-start.14 = (bf16[8,4,2048]{2,0,1:T(8,128)(2,1)S(1)}, bf16[8,4,2048]{2,0,1:T(8,128)(2,1)S(1)}, u32[]{:S(2)}, u32[]{:S(2)}) collective-permute-start(bf16[8,4,2048]{2,0,1:T(8,128)(2,1)S(1)} %get-tuple-element.46), channel_id=1, source_target_pairs={{0,96},{32,0},{64,32},{96,64},{1,97},{33,1},{65,33},{97,65},{2,98}... | collective-permute-start | bytes 393224 | tf_op jit(solution)/shard_map/ppermute | solution.py:93
  254.9 6.5 %collective-permute-start.15 = (bf16[8,4,2048]{2,0,1:T(8,128)(2,1)S(1)}, bf16[8,4,2048]{2,0,1:T(8,128)(2,1)S(1)}, u32[]{:S(2)}, u32[]{:S(2)}) collective-permute-start(bf16[8,4,2048]{2,0,1:T(8,128)(2,1)S(1)} %get-tuple-element.48), channel_id=1, source_target_pairs={{0,64},{32,96},{64,0},{96,32},{1,65},{33,97},{65,1},{97,33},{2,66}... | collective-permute-start | bytes 393224 | tf_op jit(solution)/shard_map/ppermute | solution.py:93
  257.5 6.2 %collective-permute-start.16 = (bf16[8,4,2048]{2,0,1:T(8,128)(2,1)S(1)}, bf16[8,4,2048]{2,0,1:T(8,128)(2,1)S(1)}, u32[]{:S(2)}, u32[]{:S(2)}) collective-permute-start(bf16[8,4,2048]{2,0,1:T(8,128)(2,1)S(1)} %get-tuple-element.47), channel_id=1, source_target_pairs={{0,32},{32,64},{64,96},{96,0},{1,33},{33,65},{65,97},{97,1},{2,34}... | collective-permute-start | bytes 393224 | tf_op jit(solution)/shard_map/ppermute | solution.py:93

commit v3 on v2

--- a/solution.py
+++ b/solution.py
@@ -75,13 +75,6 @@
     arrival_src = my_home // pages_dev
     held_here = (home_table // pages_dev) == device_index
     send_pick = jnp.sum(jnp.where(held_here, home_table % pages_dev, 0), axis=1)
-    outgoing = jnp.stack([pool_keys[send_pick], pool_values[send_pick]], axis=1)
-    outgoing = outgoing.reshape(devices, per_peer, 2, page_len, kv_width)
-    incoming = lax.all_to_all(outgoing, ("req", "seq"), split_axis=0, concat_axis=0, tiled=True)
-    arrived = incoming.reshape(pages_dev, 2, page_len, kv_width)[arrival_src]
-    arrived = arrived.reshape(local_reqs, pages_home, 2, page_len, kv_width)
-    cache_keys = arrived[:, :, 0].reshape(local_reqs, positions, kv_width)
-    cache_values = arrived[:, :, 1].reshape(local_reqs, positions, kv_width)
     tokens_wide = new_tokens.astype(jnp.float32)
     square_mean = jnp.mean(tokens_wide * tokens_wide, axis=-1, keepdims=True)
     normed = (tokens_wide * lax.rsqrt(square_mean + NORM_EPS) * norm_gain).astype(jnp.bfloat16)
@@ -112,6 +105,14 @@
     projected = jnp.concatenate([queries_now, keys_now, values_now], axis=-1).astype(jnp.bfloat16)
     projected = projected.reshape(req_count, local_reqs, new_count, query_cols + 2 * key_cols)
     by_shift = jnp.stack([shift(projected[k], -k) for k in range(req_count)], axis=0)
+    outgoing = jnp.stack([pool_keys[send_pick], pool_values[send_pick]], axis=1)
+    outgoing = outgoing.reshape(devices, per_peer, 2, page_len, kv_width)
+    outgoing, by_shift = lax.optimization_barrier((outgoing, by_shift))
+    incoming = lax.all_to_all(outgoing, ("req", "seq"), split_axis=0, concat_axis=0, tiled=True)
+    arrived = incoming.reshape(pages_dev, 2, page_len, kv_width)[arrival_src]
+    arrived = arrived.reshape(local_reqs, pages_home, 2, page_len, kv_width)
+    cache_keys = arrived[:, :, 0].reshape(local_reqs, positions, kv_width)
+    cache_values = arrived[:, :, 1].reshape(local_reqs, positions, kv_width)
     source_block = (jnp.arange(req_count, dtype=jnp.int32) - req_index) % req_count
     owned_rows = jnp.take(by_shift, source_block, axis=0)
     owned_rows = jnp.transpose(owned_rows, (1, 2, 0, 3))

time: 266 us -> 273 us (1.026)
  starting transfers between devices: 29.4 us -> 40.6 us
  waiting for transfers between devices: 128 us -> 119 us
  other arithmetic: 20.7 us -> 24.5 us
    ppermute x12, waiting for transfers between devices: 104 us -> 1.78 us  [shift(): return lax.ppermute(value, 'req', pairs)]
    all_to_all x1, waiting for transfers between devices: 0.01 us -> 99.6 us  [shards(): lax.all_to_all(outgoing, ('req', 'seq'), split_axis=0, concat_axis=0, til...]
    ppermute x5, starting transfers between devices: 3.25 us -> 13.3 us  [shards(): other = lax.ppermute(packed, 'seq', pairs)]
    ppermute x5, waiting for transfers between devices: 23.9 us -> 17.6 us  [shards(): other = lax.ppermute(packed, 'seq', pairs)]
    unnamed x25 -> x43, local copies, waits for them, and re-layouts: 6.86 us -> 6.22 us
  transfers between devices with their start and end apart: 18 -> 18, of which waited for: 11 -> 6; matrix products, arithmetic and copies ran while one was open for 12% -> 17% of each run, Pallas kernels for 0% -> 0%
where the time goes in v3:
time: 273 us; the launch traced here: 271 us
  waiting for transfers between devices  119 us (44%)
  local copies, waits for them, and re-layouts  61.2 us (22%)
  starting transfers between devices  40.6 us (15%)
  other arithmetic  24.5 us (9%)
  matrix products  23.8 us (9%)
    all_to_all x1, waiting for transfers between devices, shards(): lax.all_to_all(outgoing, ('req', 'seq'), split_axis=0, concat_axis=0, til...  99.6 us
    ppermute x5, waiting for transfers between devices, shards(): other = lax.ppermute(packed, 'seq', pairs)  17.6 us
    ppermute x12, starting transfers between devices, shift(): return lax.ppermute(value, 'req', pairs)  16.2 us
    ppermute x5, starting transfers between devices, shards(): other = lax.ppermute(packed, 'seq', pairs)  13.3 us
    all_to_all x1, starting transfers between devices, shards(): lax.all_to_all(outgoing, ('req', 'seq'), split_axis=0, concat_axis=0, til...  11.2 us
    gather x2, local copies, waits for them, and re-layouts, shards(): outgoing = jnp.stack([pool_keys[send_pick], pool_values[send_pick]], axis=1)  10 us
    gather x1, local copies, waits for them, and re-layouts, shards(): arrived = incoming.reshape(pages_dev, 2, page_len, kv_width)[arrival_src]  9.97 us
    reshape x1, other arithmetic, shards(): outgoing = outgoing.reshape(devices, per_peer, 2, page_len, kv_width)  6.3 us
  transfers between devices with their start and end apart: 18, of which 6 were waited for; matrix products, arithmetic and copies ran while one was open for 17% of the time, Pallas kernels for 0%

profile of v3, /device:TPU:32, one launch (start us, length us, event | category | flops | bytes accessed | tf_op | source)
XLA Modules:
  0.0 270.6 jit_solution(8976534864896484127)
XLA Ops:
  0.7 1.3 fusion.27
  2.0 1.0 fusion.29
  3.0 1.6 collective-permute-start
  4.6 2.7 %collective-permute-start.1 = (bf16[8,4,2048]{2,0,1:T(8,128)(2,1)S(1)}, bf16[8,4,2048]{2,0,1:T(8,128)(2,1)}, u32[]{:S(2)}, u32[]{:S(2)}) collective-permute-start(bf16[8,4,2048]{2,0,1:T(8,128)(2,1)S(1)} %fusion.29), channel_id=1, source_target_pairs={{0,64},{32,96},{64,0},{96,32},{1,65},{33,97},{65,1},{97,33},{2,66}... | collective-permute-start | bytes 393224 | tf_op jit(solution)/shard_map/ppermute | solution.py:86
  7.3 1.4 collective-permute-start.2
  9.3 4.0 %copy.326 = bf16[512,2048]{1,0:T(8,128)(2,1)} copy(bf16[512,2048]{0,1:T(8,128)(2,1)} %bitcast.160) | data formatting | bytes 4194304 | tf_op jit(solution)/shard_map/dot_general | solution.py:94
  14.2 1.4 copy.327
  17.2 5.0 %gather_fusion.1 = bf16[128,16,1024]{2,1,0:T(8,128)(2,1)} fusion(bf16[128,16,1024]{2,1,0:T(8,128)(2,1)} %param.17, s32[1024]{0:T(1024)S(1)} %pad_clamp_fusion.3), kind=kCustom, calls=%fused_computation.1 | custom fusion | bytes 8389120 | tf_op jit(solution)/shard_map/gather | solution.py:108
  22.2 5.0 %gather_fusion.2 = bf16[128,16,1024]{2,1,0:T(8,128)(2,1)} fusion(bf16[128,16,1024]{2,1,0:T(8,128)(2,1)} %param.18, s32[1024]{0:T(1024)S(1)} %pad_clamp_fusion.3), kind=kCustom, calls=%fused_computation.2 | custom fusion | bytes 8389120 | tf_op jit(solution)/shard_map/gather | solution.py:108
  27.6 2.6 fusion.23
  30.4 1.6 fusion.21
  32.4 1.3 convolution_convert_fusion.1
  33.8 2.6 collective-permute-start.4
  36.5 6.3 %maximum_bitcast_fusion = bf16[128,1,2,16,1024]{4,3,2,1,0:T(8,128)(2,1)} fusion(bf16[128,1,16,1024]{3,2,1,0:T(8,128)(2,1)} %bitcast.154, bf16[128,1,16,1024]{3,2,1,0:T(8,128)(2,1)S(1)} %bitcast.153), kind=kLoop, calls=%fused_computation.6 | loop fusion | flops 4194304 | bytes 16777216 | tf_op jit(solution)/shard_map/reshape | solution.py:109
  42.8 0.9 pad_maximum_fusion.7
  43.7 11.2 %all-to-all-start = ((bf16[128,1,2,16,1024]{4,3,2,1,0:T(8,128)(2,1)}), bf16[128,1,2,16,1024]{4,3,2,1,0:T(8,128)(2,1)}, u32[]{:S(2)}, u32[]{:S(2)}) async-start(bf16[128,1,2,16,1024]{4,3,2,1,0:T(8,128)(2,1)} %maximum_bitcast_fusion), calls=%async_computation | async-start | bytes 16777216 | tf_op jit(solution)/shard_map/all_to_all | solution.py:111
  56.5 99.6 %all-to-all-done = bf16[128,1,2,16,1024]{4,3,2,1,0:T(8,128)(2,1)} async-done(((bf16[128,1,2,16,1024]{4,3,2,1,0:T(8,128)(2,1)}), bf16[128,1,2,16,1024]{4,3,2,1,0:T(8,128)(2,1)}, u32[]{:S(2)}, u32[]{:S(2)}) %all-to-all-start) | async-done | bytes 8388640 | tf_op jit(solution)/shard_map/all_to_all | solution.py:111
  156.2 10.0 %gather_fusion.4 = bf16[128,2,16,1024]{3,2,1,0:T(8,128)(2,1)} fusion(bf16[128,2,16,1024]{3,2,1,0:T(8,128)(2,1)} %bitcast.22, s32[1024]{0:T(1024)S(1)} %pad_clamp_fusion.1), kind=kCustom, calls=%fused_computation.4 | custom fusion | bytes 16777728 | tf_op jit(solution)/shard_map/gather | solution.py:112
  166.2 5.4 %fusion.71 = (bf16[8,16,1,16,1024]{4,3,2,1,0:T(8,128)(2,1)}, bf16[8,16,1,16,1024]{4,3,2,1,0:T(8,128)(2,1)S(1)}) fusion(bf16[8,16,2,16,1024]{4,3,2,1,0:T(8,128)(2,1)} %bitcast.150), kind=kLoop, calls=%fused_computation.200 | loop fusion | bytes 16777216 | tf_op jit(solution)/shard_map/slice | solution.py:115
  171.6 1.1 copy.344
  172.7 0.9 copy-done.1
  174.0 2.3 fusion.74
  176.8 1.8 fusion.39
  178.6 3.3 %copy.345 = bf16[256,8,8,128]{3,2,1,0:T(8,128)(2,1)S(1)} copy(bf16[256,8,8,128]{3,1,2,0:T(8,128)(2,1)} %bitcast.149) | data formatting | bytes 8388608
  181.9 2.3 bitcast_bitcast_fusion
  184.9 2.8 %fusion = f32[8,8,2,4,128]{4,3,2,1,0:T(4,128)S(1)} fusion(bf16[8,256,8,128,1]{3,2,1,0,4:T(8,128)(2,1)} %bitcast_bitcast_fusion, bf16[8,8,2,4,256]{4,2,3,1,0:T(2,128)(2,1)S(1)} %get-tuple-element.48), kind=kOutput, calls=%fused_computation.11 | convolution fusion | flops 33554432 | bytes 4718592 | tf_op jit(solution)/shard_map/rkgtp,rpkd->rkgtd/dot_general | solution.py:137
  188.2 1.4 collective-permute-done.6
  189.6 1.4 multiply_add_fusion.8
  191.6 1.0 slice.158
  193.0 1.9 collective-permute-start.7
  194.9 7.0 %collective-permute-done.7 = f32[520,128]{1,0:T(8,128)} collective-permute-done((f32[520,128]{1,0:T(8,128)S(1)}, f32[520,128]{1,0:T(8,128)}, u32[]{:S(2)}, u32[]{:S(2)}) %collective-permute-start.7) | collective-permute-done | bytes 266272 | tf_op jit(solution)/shard_map/ppermute | solution.py:155
  201.9 1.3 multiply_add_fusion.7
  204.0 1.0 slice.161
  205.4 3.2 %collective-permute-start.8 = (f32[520,128]{1,0:T(8,128)S(1)}, f32[520,128]{1,0:T(8,128)S(1)}, u32[]{:S(2)}, u32[]{:S(2)}) collective-permute-start(f32[520,128]{1,0:T(8,128)S(1)} %pad_maximum_fusion.3), channel_id=1, source_target_pairs={{0,4},{1,5},{2,6},{3,7},{4,0},{5,1},{6,2},{7,3},{8,12},{9,13},{10,... | collective-permute-start | bytes 798728 | tf_op jit(solution)/shard_map/ppermute | solution.py:155
  208.8 6.2 %collective-permute-done.8 = f32[520,128]{1,0:T(8,128)S(1)} collective-permute-done((f32[520,128]{1,0:T(8,128)S(1)}, f32[520,128]{1,0:T(8,128)S(1)}, u32[]{:S(2)}, u32[]{:S(2)}) %collective-permute-start.8) | collective-permute-done | bytes 266272 | tf_op jit(solution)/shard_map/ppermute | solution.py:155
  215.0 1.3 multiply_add_fusion.6
  216.6 0.8 copy.278
  217.4 0.8 copy.279
  218.2 1.2 multiply_add_fusion.1
  219.4 0.7 pad_maximum_fusion.4
  220.1 5.3 %collective-permute-start.9 = (f32[520,128]{1,0:T(8,128)S(1)}, f32[520,128]{1,0:T(8,128)}, u32[]{:S(2)}, u32[]{:S(2)}) collective-permute-start(f32[520,128]{1,0:T(8,128)S(1)} %pad_maximum_fusion.4), channel_id=1, source_target_pairs={{0,8},{1,9},{2,10},{3,11},{4,12},{5,13},{6,14},{7,15},{8,0},{9,1},... | collective-permute-start | bytes 798728 | tf_op jit(solution)/shard_map/ppermute | solution.py:155
  226.0 0.7 reshape.895
  227.4 3.0 %collective-permute-done.9 = f32[520,128]{1,0:T(8,128)} collective-permute-done((f32[520,128]{1,0:T(8,128)S(1)}, f32[520,128]{1,0:T(8,128)}, u32[]{:S(2)}, u32[]{:S(2)}) %collective-permute-start.9) | collective-permute-done | bytes 266272 | tf_op jit(solution)/shard_map/ppermute | solution.py:155
  230.5 1.3 fusion.58
  232.5 1.0 slice.167
  233.9 2.8 %collective-permute-start.10 = (f32[520,128]{1,0:T(8,128)S(1)}, f32[520,128]{1,0:T(8,128)}, u32[]{:S(2)}, u32[]{:S(2)}) collective-permute-start(f32[520,128]{1,0:T(8,128)S(1)} %pad_maximum_fusion.5), channel_id=1, source_target_pairs={{0,16},{1,17},{2,18},{3,19},{4,20},{5,21},{6,22},{7,23},{8,24},{9,... | collective-permute-start | bytes 798728 | tf_op jit(solution)/shard_map/ppermute | solution.py:155
  236.7 1.9 fusion.40
  238.6 1.4 copy.291
  240.0 0.7 fusion.35
  241.0 0.8 reshape.900
  242.0 0.8 reshape.899
  243.3 0.8 reshape.897
  244.3 0.8 fusion.72
  245.5 0.7 fusion.36
  247.8 1.0 slice.170
  248.8 1.7 fusion.10
  250.6 0.8 collective-permute-start.11
  251.5 2.2 collective-permute-start.12
  254.3 5.2 %bitcast_select_fusion = bf16[8,256,1024]{2,1,0:T(8,128)(2,1)} fusion(bf16[8,16,1,16,1024]{4,3,2,1,0:T(8,128)(2,1)} %get-tuple-element.46, pred[8,256]{1,0:T(8,128)(4,1)S(1)} %compare_reduce_fusion, bf16[8,4,1024]{2,1,0:T(4,128)(2,1)S(1)} %reshape_reshape.7, s32[8,4]{1,0:T(8,128)S(1)} %iota_add_fusion, s32[256]{0:T(256)S(1)} %copy-done.14), kind=kOutput, calls=%fused_computation.9 | convolution fusion | flops 20979712 | bytes 8457344 | tf_op jit(solution)/shard_map/rpt,rtc->rpc/dot_general | solution.py:224
  259.9 1.4 collective-permute-start.14
  261.3 2.2 collective-permute-start.15
  264.1 3.9 %bitcast_select_fusion.1 = bf16[8,256,1024]{2,1,0:T(8,128)(2,1)} fusion(bf16[8,16,1,16,1024]{4,3,2,1,0:T(8,128)(2,1)S(1)} %copy-done.2, pred[8,256]{1,0:T(8,128)(4,1)S(1)} %compare_reduce_fusion, bf16[8,4,1024]{2,1,0:T(4,128)(2,1)S(1)} %reshape_reshape.6, s32[8,4]{1,0:T(8,128)S(1)} %iota_add_fusion, s32[256]{0:T(256)S(1)} %copy-done.14), kind=kOutput, calls=%fused_computation.10 | convolution fusion | flops 20979712 | bytes 8457344 | tf_op jit(solution)/shard_map/rpt,rtc->rpc/dot_general | solution.py:218
  268.0 1.7 collective-permute-done.16
  269.8 0.8 copy.317
  (162 shorter events, 17.5 us)
Async XLA Ops:
  0.6 258.8 %copy-start = (bf16[512,2048]{1,0:T(8,128)(2,1)S(1)}, bf16[512,2048]{1,0:T(8,128)(2,1)}, u32[]{:S(2)}) copy-start(bf16[512,2048]{1,0:T(8,128)(2,1)} %param.16) | copy-start | bytes 6291460
  0.6 12.6 %copy-start.17 = (s32[32]{0:T(128)S(1)}, s32[32]{0:T(128)}, u32[]{:S(2)}) copy-start(s32[32]{0:T(128)} %param.19) | copy-start | bytes 388
  0.7 12.6 %copy-start.18 = (s32[32]{0:T(128)S(1)}, s32[32]{0:T(128)}, u32[]{:S(2)}) copy-start(s32[32]{0:T(128)} %param.20) | copy-start | bytes 388
  0.7 13.6 %copy-start.8 = (bf16[2048,256]{1,0:T(8,128)(2,1)S(1)}, bf16[2048,256]{1,0:T(8,128)(2,1)}, u32[]{:S(2)}) copy-start(bf16[2048,256]{1,0:T(8,128)(2,1)} %param.14) | copy-start | bytes 3145732
  0.7 15.0 %copy-start.6 = (s32[32,512]{1,0:T(8,128)S(1)}, s32[32,512]{1,0:T(8,128)}, u32[]{:S(2)}) copy-start(s32[32,512]{1,0:T(8,128)} %param.21) | copy-start | bytes 196612
  3.0 24.6 %collective-permute-start = (bf16[8,4,2048]{2,0,1:T(8,128)(2,1)S(1)}, bf16[8,4,2048]{2,0,1:T(8,128)(2,1)S(1)}, u32[]{:S(2)}, u32[]{:S(2)}) collective-permute-start(bf16[8,4,2048]{2,0,1:T(8,128)(2,1)S(1)} %fusion.29), channel_id=1, source_target_pairs={{0,32},{32,64},{64,96},{96,0},{1,33},{33,65},{65,97},{97,1},{2,34}... | collective-permute-start | bytes 393224 | tf_op jit(solution)/shard_map/ppermute | solution.py:86
  4.6 23.0 %collective-permute-start.1 = (bf16[8,4,2048]{2,0,1:T(8,128)(2,1)S(1)}, bf16[8,4,2048]{2,0,1:T(8,128)(2,1)}, u32[]{:S(2)}, u32[]{:S(2)}) collective-permute-start(bf16[8,4,2048]{2,0,1:T(8,128)(2,1)S(1)} %fusion.29), channel_id=1, source_target_pairs={{0,64},{32,96},{64,0},{96,32},{1,65},{33,97},{65,1},{97,33},{2,66}... | collective-permute-start | bytes 393224 | tf_op jit(solution)/shard_map/ppermute | solution.py:86
  7.3 20.3 %collective-permute-start.2 = (bf16[8,4,2048]{2,0,1:T(8,128)(2,1)S(1)}, bf16[8,4,2048]{2,0,1:T(8,128)(2,1)}, u32[]{:S(2)}, u32[]{:S(2)}) collective-permute-start(bf16[8,4,2048]{2,0,1:T(8,128)(2,1)S(1)} %fusion.29), channel_id=1, source_target_pairs={{0,96},{32,0},{64,32},{96,64},{1,97},{33,1},{65,33},{97,65},{2,98}... | collective-permute-start | bytes 393224 | tf_op jit(solution)/shard_map/ppermute | solution.py:86
  16.5 5.8 %copy-start.4 = (s32[4,8,32,16]{3,2,1,0:T(8,128)}, s32[4,8,32,16]{3,2,1,0:T(8,128)S(1)}, u32[]{:S(2)}) copy-start(s32[4,8,32,16]{3,2,1,0:T(8,128)S(1)} %reshape.867) | copy-start | bytes 196612
  27.2 3.2 %copy-start.9 = (bf16[256,2048]{1,0:T(8,128)(2,1)S(1)}, bf16[256,2048]{1,0:T(8,128)(2,1)}, u32[]{:S(2)}) copy-start(bf16[256,2048]{1,0:T(8,128)(2,1)} %copy.327) | copy-start | bytes 3145732
  27.6 4.8 %copy-start.19 = (bf16[2048,256]{1,0:T(8,128)(2,1)S(1)}, bf16[2048,256]{1,0:T(8,128)(2,1)}, u32[]{:S(2)}) copy-start(bf16[2048,256]{1,0:T(8,128)(2,1)} %param.15) | copy-start | bytes 3145732
  30.3 6.2 %copy-start.3 = (bf16[128,16,1024]{2,1,0:T(8,128)(2,1)S(1)}, bf16[128,16,1024]{2,1,0:T(8,128)(2,1)}, u32[]{:S(2)}) copy-start(bf16[128,16,1024]{2,1,0:T(8,128)(2,1)} %gather_fusion.1) | copy-start | bytes 12582916
  33.7 9.0 %collective-permute-start.3 = (bf16[8,4,1024]{2,0,1:T(8,128)(2,1)S(1)}, bf16[8,4,1024]{2,0,1:T(8,128)(2,1)S(1)}, u32[]{:S(2)}, u32[]{:S(2)}) collective-permute-start(bf16[8,4,1024]{2,0,1:T(8,128)(2,1)S(1)} %get-tuple-element.72), channel_id=1, source_target_pairs={{0,96},{32,0},{64,32},{96,64},{1,97},{33,1},{65,33},{97,65},{2,98}... | collective-permute-start | bytes 196616 | tf_op jit(solution)/shard_map/ppermute | solution.py:86
  33.8 9.0 %collective-permute-start.4 = (bf16[8,4,1024]{2,0,1:T(8,128)(2,1)S(1)}, bf16[8,4,1024]{2,0,1:T(8,128)(2,1)S(1)}, u32[]{:S(2)}, u32[]{:S(2)}) collective-permute-start(bf16[8,4,1024]{2,0,1:T(8,128)(2,1)S(1)} %get-tuple-element.71), channel_id=1, source_target_pairs={{0,64},{32,96},{64,0},{96,32},{1,65},{33,97},{65,1},{97,33},{2,66}... | collective-permute-start | bytes 196616 | tf_op jit(solution)/shard_map/ppermute | solution.py:86
  36.5 6.3 %collective-permute-start.5 = (bf16[8,4,1024]{2,0,1:T(8,128)(2,1)S(1)}, bf16[8,4,1024]{2,0,1:T(8,128)(2,1)}, u32[]{:S(2)}, u32[]{:S(2)}) collective-permute-start(bf16[8,4,1024]{2,0,1:T(8,128)(2,1)S(1)} %get-tuple-element.70), channel_id=1, source_target_pairs={{0,32},{32,64},{64,96},{96,0},{1,33},{33,65},{65,97},{97,1},{2,34}... | collective-permute-start | bytes 196616 | tf_op jit(solution)/shard_map/ppermute | solution.py:86
  43.7 11.2 %copy-start.5 = (s32[4,8,32,16]{3,2,1,0:T(8,128)S(1)}, s32[4,8,32,16]{3,2,1,0:T(8,128)}, u32[]{:S(2)}) copy-start(s32[4,8,32,16]{3,2,1,0:T(8,128)} %copy-done.4) | copy-start | bytes 196612
  43.7 11.9 %copy-start.16 = (s32[4]{0:T(128)S(1)}, s32[4]{0:T(128)}, u32[]{:S(2)}) copy-start(s32[4]{0:T(128)} %get-tuple-element.92) | copy-start | bytes 52
  43.7 112.5 %all-to-all-start = ((bf16[128,1,2,16,1024]{4,3,2,1,0:T(8,128)(2,1)}), bf16[128,1,2,16,1024]{4,3,2,1,0:T(8,128)(2,1)}, u32[]{:S(2)}, u32[]{:S(2)}) async-start(bf16[128,1,2,16,1024]{4,3,2,1,0:T(8,128)(2,1)} %maximum_bitcast_fusion), calls=%async_computation | async-start | bytes 16777216 | tf_op jit(solution)/shard_map/all_to_all | solution.py:111
  55.5 153.1 %copy-start.13 = (s32[256]{0:T(256)}, s32[256]{0:T(256)S(1)}, u32[]{:S(2)}) copy-start(s32[256]{0:T(256)S(1)} %iota_add_fusion.1) | copy-start | bytes 3076
  56.5 117.4 %copy-start.10 = (bf16[8,4,8,2,128]{4,3,2,1,0:T(2,128)(2,1)}, bf16[8,4,8,2,128]{4,3,2,1,0:T(2,128)(2,1)S(1)}, u32[]{:S(2)}) copy-start(bf16[8,4,8,2,128]{4,3,2,1,0:T(2,128)(2,1)S(1)} %reshape.876) | copy-start | bytes 393220
  171.6 2.1 copy-start.1
  187.8 1.8 collective-permute-start.6
  193.0 8.9 %collective-permute-start.7 = (f32[520,128]{1,0:T(8,128)S(1)}, f32[520,128]{1,0:T(8,128)}, u32[]{:S(2)}, u32[]{:S(2)}) collective-permute-start(f32[520,128]{1,0:T(8,128)S(1)} %pad_maximum_fusion.2), channel_id=1, source_target_pairs={{0,2},{1,3},{2,0},{3,1},{4,6},{5,7},{6,4},{7,5},{8,10},{9,11},{10,... | collective-permute-start | bytes 798728 | tf_op jit(solution)/shard_map/ppermute | solution.py:155
  203.2 2.1 copy-start.11
  203.3 2.1 copy-start.12
  205.4 9.6 %collective-permute-start.8 = (f32[520,128]{1,0:T(8,128)S(1)}, f32[520,128]{1,0:T(8,128)S(1)}, u32[]{:S(2)}, u32[]{:S(2)}) collective-permute-start(f32[520,128]{1,0:T(8,128)S(1)} %pad_maximum_fusion.3), channel_id=1, source_target_pairs={{0,4},{1,5},{2,6},{3,7},{4,0},{5,1},{6,2},{7,3},{8,12},{9,13},{10,... | collective-permute-start | bytes 798728 | tf_op jit(solution)/shard_map/ppermute | solution.py:155
  220.1 10.4 %collective-permute-start.9 = (f32[520,128]{1,0:T(8,128)S(1)}, f32[520,128]{1,0:T(8,128)}, u32[]{:S(2)}, u32[]{:S(2)}) collective-permute-start(f32[520,128]{1,0:T(8,128)S(1)} %pad_maximum_fusion.4), channel_id=1, source_target_pairs={{0,8},{1,9},{2,10},{3,11},{4,12},{5,13},{6,14},{7,15},{8,0},{9,1},... | collective-permute-start | bytes 798728 | tf_op jit(solution)/shard_map/ppermute | solution.py:155
  231.8 11.2 %copy-start.15 = (f32[4,128]{1,0:T(4,128)S(1)}, f32[4,128]{1,0:T(4,128)}, u32[]{:S(2)}) copy-start(f32[4,128]{1,0:T(4,128)} %get-tuple-element.59) | copy-start | bytes 6148
  233.9 10.5 %collective-permute-start.10 = (f32[520,128]{1,0:T(8,128)S(1)}, f32[520,128]{1,0:T(8,128)}, u32[]{:S(2)}, u32[]{:S(2)}) collective-permute-start(f32[520,128]{1,0:T(8,128)S(1)} %pad_maximum_fusion.5), channel_id=1, source_target_pairs={{0,16},{1,17},{2,18},{3,19},{4,20},{5,21},{6,22},{7,23},{8,24},{9,... | collective-permute-start | bytes 798728 | tf_op jit(solution)/shard_map/ppermute | solution.py:155
  248.7 5.5 %copy-start.14 = (s32[256]{0:T(256)S(1)}, s32[256]{0:T(256)}, u32[]{:S(2)}) copy-start(s32[256]{0:T(256)} %copy-done.13) | copy-start | bytes 3076
  250.6 8.8 %collective-permute-start.11 = (bf16[8,4,512]{2,0,1:T(8,128)(2,1)S(1)}, bf16[8,4,512]{2,0,1:T(8,128)(2,1)S(1)}, u32[]{:S(2)}, u32[]{:S(2)}) collective-permute-start(bf16[8,4,512]{2,0,1:T(8,128)(2,1)S(1)} %get-tuple-element.80), channel_id=1, source_target_pairs={{0,32},{32,64},{64,96},{96,0},{1,33},{33,65},{65,97},{97,1},{2,34}... | collective-permute-start | bytes 98312 | tf_op jit(solution)/shard_map/ppermute | solution.py:86
  251.5 7.9 %collective-permute-start.12 = (bf16[8,4,512]{2,0,1:T(8,128)(2,1)S(1)}, bf16[8,4,512]{2,0,1:T(8,128)(2,1)S(1)}, u32[]{:S(2)}, u32[]{:S(2)}) collective-permute-start(bf16[8,4,512]{2,0,1:T(8,128)(2,1)S(1)} %get-tuple-element.79), channel_id=1, source_target_pairs={{0,64},{32,96},{64,0},{96,32},{1,65},{33,97},{65,1},{97,33},{2,66}... | collective-permute-start | bytes 98312 | tf_op jit(solution)/shard_map/ppermute | solution.py:86
  253.7 5.8 %collective-permute-start.13 = (bf16[8,4,512]{2,0,1:T(8,128)(2,1)S(1)}, bf16[8,4,512]{2,0,1:T(8,128)(2,1)S(1)}, u32[]{:S(2)}, u32[]{:S(2)}) collective-permute-start(bf16[8,4,512]{2,0,1:T(8,128)(2,1)S(1)} %get-tuple-element.78), channel_id=1, source_target_pairs={{0,96},{32,0},{64,32},{96,64},{1,97},{33,1},{65,33},{97,65},{2,98}... | collective-permute-start | bytes 98312 | tf_op jit(solution)/shard_map/ppermute | solution.py:86
  259.4 4.6 %copy-start.2 = (bf16[8,16,1,16,1024]{4,3,2,1,0:T(8,128)(2,1)S(1)}, bf16[8,16,1,16,1024]{4,3,2,1,0:T(8,128)(2,1)}, u32[]{:S(2)}) copy-start(bf16[8,16,1,16,1024]{4,3,2,1,0:T(8,128)(2,1)} %copy-done.1) | copy-start | bytes 12582916
  259.9 8.0 %collective-permute-start.14 = (bf16[8,4,2048]{2,0,1:T(8,128)(2,1)S(1)}, bf16[8,4,2048]{2,0,1:T(8,128)(2,1)S(1)}, u32[]{:S(2)}, u32[]{:S(2)}) collective-permute-start(bf16[8,4,2048]{2,0,1:T(8,128)(2,1)S(1)} %get-tuple-element.50), channel_id=1, source_target_pairs={{0,96},{32,0},{64,32},{96,64},{1,97},{33,1},{65,33},{97,65},{2,98}... | collective-permute-start | bytes 393224 | tf_op jit(solution)/shard_map/ppermute | solution.py:86
  261.3 6.6 %collective-permute-start.15 = (bf16[8,4,2048]{2,0,1:T(8,128)(2,1)S(1)}, bf16[8,4,2048]{2,0,1:T(8,128)(2,1)S(1)}, u32[]{:S(2)}, u32[]{:S(2)}) collective-permute-start(bf16[8,4,2048]{2,0,1:T(8,128)(2,1)S(1)} %get-tuple-element.52), channel_id=1, source_target_pairs={{0,64},{32,96},{64,0},{96,32},{1,65},{33,97},{65,1},{97,33},{2,66}... | collective-permute-start | bytes 393224 | tf_op jit(solution)/shard_map/ppermute | solution.py:86
  263.5 6.2 %copy-start.7 = (bf16[8,4,2048]{2,1,0:T(4,128)(2,1)S(1)}, bf16[8,4,2048]{2,1,0:T(4,128)(2,1)}, u32[]{:S(2)}) copy-start(bf16[8,4,2048]{2,1,0:T(4,128)(2,1)} %param.11) | copy-start | bytes 393220
  263.5 6.2 %collective-permute-start.16 = (bf16[8,4,2048]{2,0,1:T(8,128)(2,1)S(1)}, bf16[8,4,2048]{2,0,1:T(8,128)(2,1)S(1)}, u32[]{:S(2)}, u32[]{:S(2)}) collective-permute-start(bf16[8,4,2048]{2,0,1:T(8,128)(2,1)S(1)} %get-tuple-element.51), channel_id=1, source_target_pairs={{0,32},{32,64},{64,96},{96,0},{1,33},{33,65},{65,97},{97,1},{2,34}... | collective-permute-start | bytes 393224 | tf_op jit(solution)/shard_map/ppermute | solution.py:86

commit v4 on v3

--- a/solution.py
+++ b/solution.py
@@ -1,8 +1,11 @@
+import functools
 import math
 
 import jax
 import jax.numpy as jnp
 from jax import lax
+from jax.experimental import pallas as pl
+from jax.experimental.pallas import tpu as pltpu
 from jax.sharding import PartitionSpec as P
 
 H = 16
@@ -31,6 +34,113 @@
         ],
         axis=-1,
     )
+
+
+def _arrive_kernel(
+    arrival_ref, lengths_ref, base_ref, incoming_ref, q_ref, fk_ref, fv_ref,
+    keys_out_ref, values_out_ref, acc_ref, peak_ref, mass_ref, in_sem, *, scale
+):
+    r = pl.program_id(0)
+    positions = keys_out_ref.shape[1]
+    page_len = incoming_ref.shape[2]
+    pages = positions // page_len
+    heads = q_ref.shape[1]
+    head_dim = q_ref.shape[3]
+    new_count = fk_ref.shape[1]
+    copies = []
+    for pp in range(pages):
+        src = arrival_ref[r * pages + pp]
+        rows = pl.ds(pp * page_len, page_len)
+        for half, dst in ((0, keys_out_ref), (1, values_out_ref)):
+            copy = pltpu.make_async_copy(
+                incoming_ref.at[src, half], dst.at[0, rows], in_sem.at[half, pp]
+            )
+            copy.start()
+            copies.append(copy)
+    for copy in copies:
+        copy.wait()
+    length = lengths_ref[r]
+    base = base_ref[0]
+    spots = base + lax.broadcasted_iota(jnp.int32, (1, positions), 1)
+    live = spots < length
+    for kh in range(heads):
+        cols = pl.ds(kh * head_dim, head_dim)
+        keys_h = keys_out_ref[0, :, cols]
+        query_h = q_ref[0, kh]
+        scores = lax.dot_general(
+            query_h, keys_h, (((1,), (1,)), ((), ())), preferred_element_type=jnp.float32
+        ) * scale
+        scores = jnp.where(live, scores, MASKED)
+        peak = jnp.max(scores, axis=1, keepdims=True)
+        weights = jnp.where(live, jnp.exp(scores - peak), 0.0)
+        peak_ref[0, kh] = peak
+        mass_ref[0, kh] = jnp.sum(weights, axis=1, keepdims=True)
+        acc_ref[0, kh] = jnp.dot(
+            weights.astype(jnp.bfloat16), values_out_ref[0, :, cols],
+            preferred_element_type=jnp.float32,
+        )
+    first = length - base
+    tile0 = (first // page_len) * page_len
+    row_ids = lax.broadcasted_iota(jnp.int32, (page_len, 1), 0)
+    fresh_k = fk_ref[0]
+    fresh_v = fv_ref[0]
+    for tile in (tile0, tile0 + page_len):
+        @pl.when(jnp.logical_and(tile >= 0, tile < positions))
+        def _():
+            start = pl.multiple_of(tile, page_len)
+            rows = pl.ds(start, page_len)
+            block_k = keys_out_ref[0, rows, :]
+            block_v = values_out_ref[0, rows, :]
+            for t in range(new_count):
+                hit = row_ids == first + t - tile
+                block_k = jnp.where(hit, fresh_k[t : t + 1, :], block_k)
+                block_v = jnp.where(hit, fresh_v[t : t + 1, :], block_v)
+            keys_out_ref[0, rows, :] = block_k
+            values_out_ref[0, rows, :] = block_v
+
+
+def arrive_and_attend(arrival_src, lengths, base, incoming, queries, fresh_k, fresh_v, scale):
+    local_reqs, new_count, kv_width = fresh_k.shape
+    _, heads, rows, head_dim = queries.shape
+    positions = arrival_src.shape[0] // local_reqs * incoming.shape[2]
+    pages = positions // incoming.shape[2]
+    grid_spec = pltpu.PrefetchScalarGridSpec(
+        num_scalar_prefetch=3,
+        grid=(local_reqs,),
+        in_specs=[
+            pl.BlockSpec(memory_space=pl.ANY),
+            pl.BlockSpec((1, heads, rows, head_dim), lambda r, *_: (r, 0, 0, 0)),
+            pl.BlockSpec((1, new_count, kv_width), lambda r, *_: (r, 0, 0)),
+            pl.BlockSpec((1, new_count, kv_width), lambda r, *_: (r, 0, 0)),
+        ],
+        out_specs=[
+            pl.BlockSpec((1, positions, kv_width), lambda r, *_: (r, 0, 0)),
+            pl.BlockSpec((1, positions, kv_width), lambda r, *_: (r, 0, 0)),
+            pl.BlockSpec((1, heads, rows, head_dim), lambda r, *_: (r, 0, 0, 0)),
+            pl.BlockSpec((1, heads, rows, 1), lambda r, *_: (r, 0, 0, 0)),
+            pl.BlockSpec((1, heads, rows, 1), lambda r, *_: (r, 0, 0, 0)),
+        ],
+        scratch_shapes=[pltpu.SemaphoreType.DMA((2, pages))],
+    )
+    cache_bytes = 2 * local_reqs * positions * kv_width * 2
+    return pl.pallas_call(
+        functools.partial(_arrive_kernel, scale=scale),
+        out_shape=[
+            jax.ShapeDtypeStruct((local_reqs, positions, kv_width), jnp.bfloat16),
+            jax.ShapeDtypeStruct((local_reqs, positions, kv_width), jnp.bfloat16),
+            jax.ShapeDtypeStruct((local_reqs, heads, rows, head_dim), jnp.float32),
+            jax.ShapeDtypeStruct((local_reqs, heads, rows, 1), jnp.float32),
+            jax.ShapeDtypeStruct((local_reqs, heads, rows, 1), jnp.float32),
+        ],
+        grid_spec=grid_spec,
+        compiler_params=pltpu.CompilerParams(dimension_semantics=("arbitrary",)),
+        cost_estimate=pl.CostEstimate(
+            flops=4 * local_reqs * heads * rows * positions * head_dim,
+            transcendentals=local_reqs * heads * rows * positions,
+            bytes_accessed=2 * cache_bytes,
+        ),
+        name="arrive_and_attend",
+    )(arrival_src, lengths, base, incoming, queries, fresh_k, fresh_v)
 
 
 def shards(
@@ -109,10 +219,6 @@
     outgoing = outgoing.reshape(devices, per_peer, 2, page_len, kv_width)
     outgoing, by_shift = lax.optimization_barrier((outgoing, by_shift))
     incoming = lax.all_to_all(outgoing, ("req", "seq"), split_axis=0, concat_axis=0, tiled=True)
-    arrived = incoming.reshape(pages_dev, 2, page_len, kv_width)[arrival_src]
-    arrived = arrived.reshape(local_reqs, pages_home, 2, page_len, kv_width)
-    cache_keys = arrived[:, :, 0].reshape(local_reqs, positions, kv_width)
-    cache_values = arrived[:, :, 1].reshape(local_reqs, positions, kv_width)
     source_block = (jnp.arange(req_count, dtype=jnp.int32) - req_index) % req_count
     owned_rows = jnp.take(by_shift, source_block, axis=0)
     owned_rows = jnp.transpose(owned_rows, (1, 2, 0, 3))
@@ -122,24 +228,22 @@
     )
     fresh_values = owned_rows[..., query_cols + key_cols :].reshape(local_reqs, new_count, KVH, HD)
     score_scale = 1.0 / math.sqrt(HD)
-    grid_keys = cache_keys.reshape(local_reqs, positions, KVH, HD)
-    grid_values = cache_values.reshape(local_reqs, positions, KVH, HD)
-    scores = (
-        jnp.einsum("rtkgd,rpkd->rkgtp", queries, grid_keys, preferred_element_type=jnp.float32)
-        * score_scale
-    )
-    key_spots = seq_index * positions + jnp.arange(positions, dtype=jnp.int32)
-    live_mask = (key_spots[None, :] < my_lengths[:, None])[:, None, None, None, :]
-    scores = jnp.where(live_mask, scores, MASKED)
-    row_peak = jnp.max(scores, axis=-1)
-    weights = jnp.where(live_mask, jnp.exp(scores - row_peak[..., None]), 0.0)
-    row_mass = jnp.sum(weights, axis=-1)
-    gathered_sum = jnp.einsum(
-        "rkgtp,rpkd->rkgtd",
-        weights.astype(jnp.bfloat16),
-        grid_values,
-        preferred_element_type=jnp.float32,
-    )
+    kernel_queries = jnp.transpose(queries, (0, 2, 3, 1, 4)).reshape(
+        local_reqs, KVH, groups * new_count, HD
+    )
+    keys_out, values_out, gathered_sum, row_peak, row_mass = arrive_and_attend(
+        arrival_src,
+        my_lengths,
+        (seq_index * positions).reshape(1).astype(jnp.int32),
+        incoming.reshape(pages_dev, 2, page_len, kv_width),
+        kernel_queries,
+        fresh_keys.reshape(local_reqs, new_count, kv_width),
+        fresh_values.reshape(local_reqs, new_count, kv_width),
+        score_scale,
+    )
+    gathered_sum = gathered_sum.reshape(local_reqs, KVH, groups, new_count, HD)
+    row_peak = row_peak.reshape(local_reqs, KVH, groups, new_count)
+    row_mass = row_mass.reshape(local_reqs, KVH, groups, new_count)
     stat_rows = row_peak.size // HD
     step = 1
     while step < seq_count:
@@ -213,23 +317,6 @@
     for k in range(1, req_count):
         projected_out = projected_out + shift(partial_out[k], -k).astype(jnp.float32)
     out_hidden = (tokens_wide + projected_out).astype(jnp.bfloat16)
-    new_hits = key_spots[None, :, None] == my_lengths[:, None, None] + new_index[None, None, :]
-    filler = new_hits.astype(jnp.bfloat16)
-    placed_keys = jnp.einsum(
-        "rpt,rtc->rpc",
-        filler,
-        fresh_keys.reshape(local_reqs, new_count, kv_width),
-        preferred_element_type=jnp.float32,
-    ).astype(jnp.bfloat16)
-    placed_values = jnp.einsum(
-        "rpt,rtc->rpc",
-        filler,
-        fresh_values.reshape(local_reqs, new_count, kv_width),
-        preferred_element_type=jnp.float32,
-    ).astype(jnp.bfloat16)
-    touched = jnp.any(new_hits, axis=-1)[..., None]
-    keys_out = jnp.where(touched, placed_keys, cache_keys)
-    values_out = jnp.where(touched, placed_values, cache_values)
     return (out_hidden, keys_out, values_out)
 
 

time: 273 us -> 281 us (1.029)
  Pallas kernels: 0 us -> 31.1 us
  local copies, waits for them, and re-layouts: 61.2 us -> 37.2 us
  matrix products: 23.8 us -> 10 us
  other arithmetic: 24.5 us -> 32.8 us
  waiting for transfers between devices: 119 us -> 124 us
    pallas_call x0 -> x1, Pallas kernels: none -> 31.1 us  [arrive_and_attend(): pl.pallas_call(functools.partial(_arrive_kernel, scale=scale), out_shape=...]
    dot_general x4 -> x0, matrix products: 14.2 us -> none  [the longest x1 5.17 us: shards(): jnp.einsum('rpt,rtc->rpc', filler, fresh_values.reshape(local_reqs, new_c...]
    gather x1 -> x0, local copies, waits for them, and re-layouts: 9.97 us -> none  [shards(): arrived = incoming.reshape(pages_dev, 2, page_len, kv_width)[arrival_src]]
    slice x0 -> x4, other arithmetic: none -> 7.31 us  [shards(): peer_sum = other[:gathered_sum.size // HD].reshape(gathered_sum.shape)]
    ppermute x12, waiting for transfers between devices: 1.78 us -> 8.62 us  [shift(): return lax.ppermute(value, 'req', pairs)]
    slice x1 -> x0, local copies, waits for them, and re-layouts: 5.43 us -> none  [shards(): cache_values = arrived[:, :, 1].reshape(local_reqs, positions, kv_width)]
    unnamed x43 -> x23, local copies, waits for them, and re-layouts: 6.22 us -> 1.49 us
    all_to_all x1, waiting for transfers between devices: 99.6 us -> 95.4 us  [shards(): lax.all_to_all(outgoing, ('req', 'seq'), split_axis=0, concat_axis=0, til...]
  transfers between devices with their start and end apart: 18 -> 18, of which waited for: 6 -> 10; matrix products, arithmetic and copies ran while one was open for 17% -> 14% of each run, Pallas kernels for 0% -> 0%
where the time goes in v4:
time: 281 us; the launch traced here: 276 us
  waiting for transfers between devices  124 us (44%)
  starting transfers between devices  40 us (14%)
  local copies, waits for them, and re-layouts  37.2 us (13%)
  other arithmetic  32.8 us (12%)
  Pallas kernels  31.1 us (11%)
  matrix products  10 us (4%)
    all_to_all x1, waiting for transfers between devices, shards(): lax.all_to_all(outgoing, ('req', 'seq'), split_axis=0, concat_axis=0, til...  95.4 us
    pallas_call x1, Pallas kernels, arrive_and_attend(): pl.pallas_call(functools.partial(_arrive_kernel, scale=scale), out_shape=...  31.1 us
    ppermute x5, waiting for transfers between devices, shards(): other = lax.ppermute(packed, 'seq', pairs)  20.1 us
    ppermute x12, starting transfers between devices, shift(): return lax.ppermute(value, 'req', pairs)  17 us
    ppermute x5, starting transfers between devices, shards(): other = lax.ppermute(packed, 'seq', pairs)  13.7 us
    gather x2, local copies, waits for them, and re-layouts, shards(): outgoing = jnp.stack([pool_keys[send_pick], pool_values[send_pick]], axis=1)  10 us
    all_to_all x1, starting transfers between devices, shards(): lax.all_to_all(outgoing, ('req', 'seq'), split_axis=0, concat_axis=0, til...  9.25 us
    ppermute x12, waiting for transfers between devices, shift(): return lax.ppermute(value, 'req', pairs)  8.62 us
  transfers between devices with their start and end apart: 18, of which 10 were waited for; matrix products, arithmetic and copies ran while one was open for 14% of the time, Pallas kernels for 0%

profile of v4, /device:TPU:32, one launch (start us, length us, event | category | flops | bytes accessed | tf_op | source)
XLA Modules:
  0.0 276.3 jit_solution(8581239769232284598)
XLA Ops:
  0.6 1.3 fusion.14
  1.9 1.0 fusion.16
  3.0 2.8 %collective-permute-start.2 = (bf16[8,4,2048]{2,0,1:T(8,128)(2,1)S(1)}, bf16[8,4,2048]{2,0,1:T(8,128)(2,1)S(1)}, u32[]{:S(2)}, u32[]{:S(2)}) collective-permute-start(bf16[8,4,2048]{2,0,1:T(8,128)(2,1)S(1)} %fusion.16), channel_id=1, source_target_pairs={{0,96},{32,0},{64,32},{96,64},{1,97},{33,1},{65,33},{97,65},{2,98}... | collective-permute-start | bytes 393224 | tf_op jit(solution)/shard_map/ppermute | solution.py:196
  5.8 0.8 collective-permute-start.1
  6.6 0.9 collective-permute-start
  7.5 0.8 select_reduce_fusion
  8.3 1.5 gather_fusion
  10.8 5.0 %gather_fusion.2 = bf16[128,16,1024]{2,1,0:T(8,128)(2,1)} fusion(bf16[128,16,1024]{2,1,0:T(8,128)(2,1)} %param.18, s32[1024]{0:T(1024)S(1)} %pad_clamp_fusion.2), kind=kCustom, calls=%fused_computation.2 | custom fusion | bytes 8389120 | tf_op jit(solution)/shard_map/gather | solution.py:218
  15.8 5.0 %gather_fusion.1 = bf16[128,16,1024]{2,1,0:T(8,128)(2,1)} fusion(bf16[128,16,1024]{2,1,0:T(8,128)(2,1)} %param.17, s32[1024]{0:T(1024)S(1)} %pad_clamp_fusion.2), kind=kCustom, calls=%fused_computation.1 | custom fusion | bytes 8389120 | tf_op jit(solution)/shard_map/gather | solution.py:218
  20.8 1.5 copy.208
  23.1 4.0 %copy.207 = bf16[512,2048]{1,0:T(8,128)(2,1)} copy(bf16[512,2048]{0,1:T(8,128)(2,1)} %bitcast.159) | data formatting | bytes 4194304 | tf_op jit(solution)/shard_map/dot_general | solution.py:204
  27.4 1.5 fusion.8
  29.1 2.7 fusion.10
  32.2 1.3 convolution_convert_fusion.1
  33.5 1.9 collective-permute-start.5
  35.4 2.0 collective-permute-start.4
  37.4 0.8 collective-permute-start.3
  38.2 6.3 %maximum_bitcast_fusion = bf16[128,1,2,16,1024]{4,3,2,1,0:T(8,128)(2,1)} fusion(bf16[128,1,16,1024]{3,2,1,0:T(8,128)(2,1)S(1)} %bitcast.156, bf16[128,1,16,1024]{3,2,1,0:T(8,128)(2,1)} %bitcast.157), kind=kLoop, calls=%fused_computation.5 | loop fusion | flops 4194304 | bytes 16777216 | tf_op jit(solution)/shard_map/reshape | solution.py:219
  44.5 0.9 pad_maximum_fusion.7
  45.4 9.3 %all-to-all-start = ((bf16[128,1,2,16,1024]{4,3,2,1,0:T(8,128)(2,1)}), bf16[128,1,2,16,1024]{4,3,2,1,0:T(8,128)(2,1)}, u32[]{:S(2)}, u32[]{:S(2)}) async-start(bf16[128,1,2,16,1024]{4,3,2,1,0:T(8,128)(2,1)} %maximum_bitcast_fusion), calls=%async_computation | async-start | bytes 16777216 | tf_op jit(solution)/shard_map/all_to_all | solution.py:221
  57.4 0.7 copy.154
  59.4 95.4 %all-to-all-done = bf16[128,1,2,16,1024]{4,3,2,1,0:T(8,128)(2,1)} async-done(((bf16[128,1,2,16,1024]{4,3,2,1,0:T(8,128)(2,1)}), bf16[128,1,2,16,1024]{4,3,2,1,0:T(8,128)(2,1)}, u32[]{:S(2)}, u32[]{:S(2)}) %all-to-all-start) | async-done | bytes 8388640 | tf_op jit(solution)/shard_map/all_to_all | solution.py:221
  154.8 31.1 %arrive_and_attend.1 = (bf16[8,256,1024]{2,1,0:T(8,128)(2,1)}, bf16[8,256,1024]{2,1,0:T(8,128)(2,1)}, f32[8,8,8,128]{3,2,1,0:T(8,128)}, f32[8,8,8,1]{3,2,1,0:T(8,128)}, f32[8,8,8,1]{3,2,1,0:T(8,128)}) custom-call(s32[128]{0:T(128)} %and_select_fusion.4.arrival_ref, s32[8]{0:T(128)} %dynamic_slice.19.lengths_ref, s32[1]{0:T(128)} %bitcast.3.base_ref, ...), custom_call_target="tpu_custom_call" | custom-call | flops 67108864 | bytes 16777216 | tf_op jit(solution)/shard_map/arrive_and_attend/pallas_call | solution.py:126
  185.9 1.1 reduce.3
  187.1 1.1 reduce.2
  188.3 1.0 pad_maximum_fusion.1
  189.5 1.4 collective-permute-done.6
  191.6 1.9 fusion.52
  193.5 0.7 pad_maximum_fusion.2
  194.3 2.9 %collective-permute-start.7 = (f32[520,128]{1,0:T(8,128)}, f32[520,128]{1,0:T(8,128)}, u32[]{:S(2)}, u32[]{:S(2)}) collective-permute-start(f32[520,128]{1,0:T(8,128)} %pad_maximum_fusion.2), channel_id=1, source_target_pairs={{0,2},{1,3},{2,0},{3,1},{4,6},{5,7},{6,4},{7,5},{8,10},{9,11},{10,... | collective-permute-start | bytes 798728 | tf_op jit(solution)/shard_map/ppermute | solution.py:259
  197.2 7.2 %collective-permute-done.7 = f32[520,128]{1,0:T(8,128)} collective-permute-done((f32[520,128]{1,0:T(8,128)}, f32[520,128]{1,0:T(8,128)}, u32[]{:S(2)}, u32[]{:S(2)}) %collective-permute-start.7) | collective-permute-done | bytes 266272 | tf_op jit(solution)/shard_map/ppermute | solution.py:259
  205.1 0.8 multiply_add_fusion.7
  205.9 1.8 fusion.53
  207.7 0.7 pad_maximum_fusion.3
  208.4 3.1 %collective-permute-start.8 = (f32[520,128]{1,0:T(8,128)}, f32[520,128]{1,0:T(8,128)}, u32[]{:S(2)}, u32[]{:S(2)}) collective-permute-start(f32[520,128]{1,0:T(8,128)} %pad_maximum_fusion.3), channel_id=1, source_target_pairs={{0,4},{1,5},{2,6},{3,7},{4,0},{5,1},{6,2},{7,3},{8,12},{9,13},{10,... | collective-permute-start | bytes 798728 | tf_op jit(solution)/shard_map/ppermute | solution.py:259
  211.5 6.8 %collective-permute-done.8 = f32[520,128]{1,0:T(8,128)} collective-permute-done((f32[520,128]{1,0:T(8,128)}, f32[520,128]{1,0:T(8,128)}, u32[]{:S(2)}, u32[]{:S(2)}) %collective-permute-start.8) | collective-permute-done | bytes 266272 | tf_op jit(solution)/shard_map/ppermute | solution.py:259
  218.3 0.8 multiply_add_fusion.6
  219.8 1.8 fusion.54
  221.5 0.7 pad_maximum_fusion.4
  222.3 5.0 %collective-permute-start.9 = (f32[520,128]{1,0:T(8,128)}, f32[520,128]{1,0:T(8,128)}, u32[]{:S(2)}, u32[]{:S(2)}) collective-permute-start(f32[520,128]{1,0:T(8,128)} %pad_maximum_fusion.4), channel_id=1, source_target_pairs={{0,8},{1,9},{2,10},{3,11},{4,12},{5,13},{6,14},{7,15},{8,0},{9,1},... | collective-permute-start | bytes 798728 | tf_op jit(solution)/shard_map/ppermute | solution.py:259
  227.9 4.6 %collective-permute-done.9 = f32[520,128]{1,0:T(8,128)} collective-permute-done((f32[520,128]{1,0:T(8,128)}, f32[520,128]{1,0:T(8,128)}, u32[]{:S(2)}, u32[]{:S(2)}) %collective-permute-start.9) | collective-permute-done | bytes 266272 | tf_op jit(solution)/shard_map/ppermute | solution.py:259
  233.2 0.8 fusion.37
  234.0 1.8 fusion.55
  235.8 0.7 pad_maximum_fusion.5
  236.6 2.6 collective-permute-start.10
  239.2 1.0 fusion.21
  240.2 1.4 copy.181
  245.4 0.8 fusion.51
  246.5 0.7 fusion.24
  247.2 1.1 copy.184
  248.6 1.5 multiply_add_fusion.4
  250.1 0.9 copy.197
  252.4 0.8 copy.164
  253.4 0.8 copy.160
  254.2 1.0 slice.160
  255.2 3.0 %fusion.3 = bf16[8,4,8,2,128]{4,1,3,2,0:T(4,128)(2,1)S(1)} fusion(bf16[8,8,2,4,4]{4,3,2,1,0:T(4,128)(2,1)} %copy.184, f32[8,8,2,4,128]{4,3,2,1,0:T(4,128)S(1)} %bitcast.169, f32[8,8,2,4,128]{4,3,2,1,0:T(4,128)S(1)} %bitcast.173, f32[8,8,2,4,128]{4,3,2,1,0:T(4,128)} %bitcast.172, f32[8,8,2,4,128]{4,3,2,1,0:T(4,128)} %bitcast.171, ...), kind=kOutput, calls=%fused_computation.11 | convolution fusion | flops 2424832 | bytes 1798149 | tf_op jit(solution)/shard_map/rkgts,rskd->rkgtd/dot_general | solution.py:287
  258.5 2.2 collective-permute-start.13
  261.6 0.8 collective-permute-done.13
  262.4 3.8 %collective-permute-done.12 = bf16[8,4,512]{2,0,1:T(8,128)(2,1)S(1)} collective-permute-done((bf16[8,4,512]{2,0,1:T(8,128)(2,1)S(1)}, bf16[8,4,512]{2,0,1:T(8,128)(2,1)S(1)}, u32[]{:S(2)}, u32[]{:S(2)}) %collective-permute-start.12) | collective-permute-done | bytes 32800 | tf_op jit(solution)/shard_map/ppermute | solution.py:196
  267.0 2.5 collective-permute-start.15
  269.5 2.2 collective-permute-start.14
  271.7 2.9 %collective-permute-done.16 = bf16[8,4,2048]{2,0,1:T(8,128)(2,1)S(1)} collective-permute-done((bf16[8,4,2048]{2,0,1:T(8,128)(2,1)S(1)}, bf16[8,4,2048]{2,0,1:T(8,128)(2,1)S(1)}, u32[]{:S(2)}, u32[]{:S(2)}) %collective-permute-start.16) | collective-permute-done | bytes 131104 | tf_op jit(solution)/shard_map/ppermute | solution.py:196
  274.6 0.9 collective-permute-done.14
  275.6 0.8 copy.200
  (127 shorter events, 18.4 us)
Async XLA Ops:
  0.6 265.8 %copy-start = (bf16[512,2048]{1,0:T(8,128)(2,1)S(1)}, bf16[512,2048]{1,0:T(8,128)(2,1)}, u32[]{:S(2)}) copy-start(bf16[512,2048]{1,0:T(8,128)(2,1)} %param.16) | copy-start | bytes 6291460
  3.0 24.4 %collective-permute-start.2 = (bf16[8,4,2048]{2,0,1:T(8,128)(2,1)S(1)}, bf16[8,4,2048]{2,0,1:T(8,128)(2,1)S(1)}, u32[]{:S(2)}, u32[]{:S(2)}) collective-permute-start(bf16[8,4,2048]{2,0,1:T(8,128)(2,1)S(1)} %fusion.16), channel_id=1, source_target_pairs={{0,96},{32,0},{64,32},{96,64},{1,97},{33,1},{65,33},{97,65},{2,98}... | collective-permute-start | bytes 393224 | tf_op jit(solution)/shard_map/ppermute | solution.py:196
  5.8 21.6 %collective-permute-start.1 = (bf16[8,4,2048]{2,0,1:T(8,128)(2,1)S(1)}, bf16[8,4,2048]{2,0,1:T(8,128)(2,1)}, u32[]{:S(2)}, u32[]{:S(2)}) collective-permute-start(bf16[8,4,2048]{2,0,1:T(8,128)(2,1)S(1)} %fusion.16), channel_id=1, source_target_pairs={{0,64},{32,96},{64,0},{96,32},{1,65},{33,97},{65,1},{97,33},{2,66}... | collective-permute-start | bytes 393224 | tf_op jit(solution)/shard_map/ppermute | solution.py:196
  6.6 20.8 %collective-permute-start = (bf16[8,4,2048]{2,0,1:T(8,128)(2,1)S(1)}, bf16[8,4,2048]{2,0,1:T(8,128)(2,1)}, u32[]{:S(2)}, u32[]{:S(2)}) collective-permute-start(bf16[8,4,2048]{2,0,1:T(8,128)(2,1)S(1)} %fusion.16), channel_id=1, source_target_pairs={{0,32},{32,64},{64,96},{96,0},{1,33},{33,65},{65,97},{97,1},{2,34}... | collective-permute-start | bytes 393224 | tf_op jit(solution)/shard_map/ppermute | solution.py:196
  10.0 5.8 %copy-start.2 = (s32[4,8,32,16]{3,2,1,0:T(8,128)}, s32[4,8,32,16]{3,2,1,0:T(8,128)S(1)}, u32[]{:S(2)}) copy-start(s32[4,8,32,16]{3,2,1,0:T(8,128)S(1)} %reshape.885) | copy-start | bytes 196612
  27.4 4.8 %copy-start.10 = (bf16[2048,256]{1,0:T(8,128)(2,1)S(1)}, bf16[2048,256]{1,0:T(8,128)(2,1)}, u32[]{:S(2)}) copy-start(bf16[2048,256]{1,0:T(8,128)(2,1)} %param.15) | copy-start | bytes 3145732
  29.1 9.1 %copy-start.1 = (bf16[128,16,1024]{2,1,0:T(8,128)(2,1)S(1)}, bf16[128,16,1024]{2,1,0:T(8,128)(2,1)}, u32[]{:S(2)}) copy-start(bf16[128,16,1024]{2,1,0:T(8,128)(2,1)} %gather_fusion.2) | copy-start | bytes 12582916
  33.5 10.9 %collective-permute-start.5 = (bf16[8,4,1024]{2,0,1:T(8,128)(2,1)S(1)}, bf16[8,4,1024]{2,0,1:T(8,128)(2,1)S(1)}, u32[]{:S(2)}, u32[]{:S(2)}) collective-permute-start(bf16[8,4,1024]{2,0,1:T(8,128)(2,1)S(1)} %get-tuple-element.103), channel_id=1, source_target_pairs={{0,32},{32,64},{64,96},{96,0},{1,33},{33,65},{65,97},{97,1},{2,34}... | collective-permute-start | bytes 196616 | tf_op jit(solution)/shard_map/ppermute | solution.py:196
  35.4 9.1 %collective-permute-start.4 = (bf16[8,4,1024]{2,0,1:T(8,128)(2,1)S(1)}, bf16[8,4,1024]{2,0,1:T(8,128)(2,1)S(1)}, u32[]{:S(2)}, u32[]{:S(2)}) collective-permute-start(bf16[8,4,1024]{2,0,1:T(8,128)(2,1)S(1)} %get-tuple-element.104), channel_id=1, source_target_pairs={{0,64},{32,96},{64,0},{96,32},{1,65},{33,97},{65,1},{97,33},{2,66}... | collective-permute-start | bytes 196616 | tf_op jit(solution)/shard_map/ppermute | solution.py:196
  37.4 7.1 %collective-permute-start.3 = (bf16[8,4,1024]{2,0,1:T(8,128)(2,1)S(1)}, bf16[8,4,1024]{2,0,1:T(8,128)(2,1)}, u32[]{:S(2)}, u32[]{:S(2)}) collective-permute-start(bf16[8,4,1024]{2,0,1:T(8,128)(2,1)S(1)} %get-tuple-element.105), channel_id=1, source_target_pairs={{0,96},{32,0},{64,32},{96,64},{1,97},{33,1},{65,33},{97,65},{2,98}... | collective-permute-start | bytes 196616 | tf_op jit(solution)/shard_map/ppermute | solution.py:196
  45.3 9.3 %copy-start.3 = (s32[4,8,32,16]{3,2,1,0:T(8,128)S(1)}, s32[4,8,32,16]{3,2,1,0:T(8,128)}, u32[]{:S(2)}) copy-start(s32[4,8,32,16]{3,2,1,0:T(8,128)} %copy-done.2) | copy-start | bytes 196612
  45.4 109.4 %all-to-all-start = ((bf16[128,1,2,16,1024]{4,3,2,1,0:T(8,128)(2,1)}), bf16[128,1,2,16,1024]{4,3,2,1,0:T(8,128)(2,1)}, u32[]{:S(2)}, u32[]{:S(2)}) async-start(bf16[128,1,2,16,1024]{4,3,2,1,0:T(8,128)(2,1)} %maximum_bitcast_fusion), calls=%async_computation | async-start | bytes 16777216 | tf_op jit(solution)/shard_map/all_to_all | solution.py:221
  189.3 52.5 %copy-start.6 = (f32[8,8,8,1]{3,2,1,0:T(8,128)S(1)}, f32[8,8,8,1]{3,2,1,0:T(8,128)}, u32[]{:S(2)}) copy-start(f32[8,8,8,1]{3,2,1,0:T(8,128)} %get-tuple-element.13) | copy-start | bytes 6148
  189.3 1.6 collective-permute-start.6
  190.9 0.7 copy-start.8
  191.6 50.6 %copy-start.5 = (f32[8,8,8,1]{3,2,1,0:T(8,128)S(1)}, f32[8,8,8,1]{3,2,1,0:T(8,128)}, u32[]{:S(2)}) copy-start(f32[8,8,8,1]{3,2,1,0:T(8,128)} %get-tuple-element.14) | copy-start | bytes 6148
  194.3 10.2 %collective-permute-start.7 = (f32[520,128]{1,0:T(8,128)}, f32[520,128]{1,0:T(8,128)}, u32[]{:S(2)}, u32[]{:S(2)}) collective-permute-start(f32[520,128]{1,0:T(8,128)} %pad_maximum_fusion.2), channel_id=1, source_target_pairs={{0,2},{1,3},{2,0},{3,1},{4,6},{5,7},{6,4},{7,5},{8,10},{9,11},{10,... | collective-permute-start | bytes 798728 | tf_op jit(solution)/shard_map/ppermute | solution.py:259
  208.4 9.9 %collective-permute-start.8 = (f32[520,128]{1,0:T(8,128)}, f32[520,128]{1,0:T(8,128)}, u32[]{:S(2)}, u32[]{:S(2)}) collective-permute-start(f32[520,128]{1,0:T(8,128)} %pad_maximum_fusion.3), channel_id=1, source_target_pairs={{0,4},{1,5},{2,6},{3,7},{4,0},{5,1},{6,2},{7,3},{8,12},{9,13},{10,... | collective-permute-start | bytes 798728 | tf_op jit(solution)/shard_map/ppermute | solution.py:259
  222.3 10.3 %collective-permute-start.9 = (f32[520,128]{1,0:T(8,128)}, f32[520,128]{1,0:T(8,128)}, u32[]{:S(2)}, u32[]{:S(2)}) collective-permute-start(f32[520,128]{1,0:T(8,128)} %pad_maximum_fusion.4), channel_id=1, source_target_pairs={{0,8},{1,9},{2,10},{3,11},{4,12},{5,13},{6,14},{7,15},{8,0},{9,1},... | collective-permute-start | bytes 798728 | tf_op jit(solution)/shard_map/ppermute | solution.py:259
  234.0 21.1 %copy-start.7 = (f32[8,8,8,128]{3,2,1,0:T(8,128)S(1)}, f32[8,8,8,128]{3,2,1,0:T(8,128)}, u32[]{:S(2)}) copy-start(f32[8,8,8,128]{3,2,1,0:T(8,128)} %get-tuple-element.12) | copy-start | bytes 786436
  236.6 8.8 %collective-permute-start.10 = (f32[520,128]{1,0:T(8,128)}, f32[520,128]{1,0:T(8,128)}, u32[]{:S(2)}, u32[]{:S(2)}) collective-permute-start(f32[520,128]{1,0:T(8,128)} %pad_maximum_fusion.5), channel_id=1, source_target_pairs={{0,16},{1,17},{2,18},{3,19},{4,20},{5,21},{6,22},{7,23},{8,24},{9,... | collective-permute-start | bytes 798728 | tf_op jit(solution)/shard_map/ppermute | solution.py:259
  240.2 15.0 %copy-start.9 = (f32[512,128]{1,0:T(8,128)S(1)}, f32[512,128]{1,0:T(8,128)}, u32[]{:S(2)}) copy-start(f32[512,128]{1,0:T(8,128)} %get-tuple-element.94) | copy-start | bytes 786436
  258.2 17.2 %copy-start.4 = (bf16[8,4,2048]{2,1,0:T(4,128)(2,1)S(1)}, bf16[8,4,2048]{2,1,0:T(4,128)(2,1)}, u32[]{:S(2)}) copy-start(bf16[8,4,2048]{2,1,0:T(4,128)(2,1)} %param.11) | copy-start | bytes 393220
  258.5 4.0 %collective-permute-start.13 = (bf16[8,4,512]{2,0,1:T(8,128)(2,1)S(1)}, bf16[8,4,512]{2,0,1:T(8,128)(2,1)S(1)}, u32[]{:S(2)}, u32[]{:S(2)}) collective-permute-start(bf16[8,4,512]{2,0,1:T(8,128)(2,1)S(1)} %get-tuple-element.111), channel_id=1, source_target_pairs={{0,96},{32,0},{64,32},{96,64},{1,97},{33,1},{65,33},{97,65},{2,98}... | collective-permute-start | bytes 98312 | tf_op jit(solution)/shard_map/ppermute | solution.py:196
  260.7 5.5 %collective-permute-start.12 = (bf16[8,4,512]{2,0,1:T(8,128)(2,1)S(1)}, bf16[8,4,512]{2,0,1:T(8,128)(2,1)S(1)}, u32[]{:S(2)}, u32[]{:S(2)}) collective-permute-start(bf16[8,4,512]{2,0,1:T(8,128)(2,1)S(1)} %get-tuple-element.112), channel_id=1, source_target_pairs={{0,64},{32,96},{64,0},{96,32},{1,65},{33,97},{65,1},{97,33},{2,66}... | collective-permute-start | bytes 98312 | tf_op jit(solution)/shard_map/ppermute | solution.py:196
  261.1 5.4 %collective-permute-start.11 = (bf16[8,4,512]{2,0,1:T(8,128)(2,1)S(1)}, bf16[8,4,512]{2,0,1:T(8,128)(2,1)S(1)}, u32[]{:S(2)}, u32[]{:S(2)}) collective-permute-start(bf16[8,4,512]{2,0,1:T(8,128)(2,1)S(1)} %get-tuple-element.113), channel_id=1, source_target_pairs={{0,32},{32,64},{64,96},{96,0},{1,33},{33,65},{65,97},{97,1},{2,34}... | collective-permute-start | bytes 98312 | tf_op jit(solution)/shard_map/ppermute | solution.py:196
  266.9 7.7 %collective-permute-start.16 = (bf16[8,4,2048]{2,0,1:T(8,128)(2,1)S(1)}, bf16[8,4,2048]{2,0,1:T(8,128)(2,1)S(1)}, u32[]{:S(2)}, u32[]{:S(2)}) collective-permute-start(bf16[8,4,2048]{2,0,1:T(8,128)(2,1)S(1)} %get-tuple-element.72), channel_id=1, source_target_pairs={{0,32},{32,64},{64,96},{96,0},{1,33},{33,65},{65,97},{97,1},{2,34}... | collective-permute-start | bytes 393224 | tf_op jit(solution)/shard_map/ppermute | solution.py:196
  267.0 7.6 %collective-permute-start.15 = (bf16[8,4,2048]{2,0,1:T(8,128)(2,1)S(1)}, bf16[8,4,2048]{2,0,1:T(8,128)(2,1)S(1)}, u32[]{:S(2)}, u32[]{:S(2)}) collective-permute-start(bf16[8,4,2048]{2,0,1:T(8,128)(2,1)S(1)} %get-tuple-element.73), channel_id=1, source_target_pairs={{0,64},{32,96},{64,0},{96,32},{1,65},{33,97},{65,1},{97,33},{2,66}... | collective-permute-start | bytes 393224 | tf_op jit(solution)/shard_map/ppermute | solution.py:196
  269.5 5.9 %collective-permute-start.14 = (bf16[8,4,2048]{2,0,1:T(8,128)(2,1)S(1)}, bf16[8,4,2048]{2,0,1:T(8,128)(2,1)S(1)}, u32[]{:S(2)}, u32[]{:S(2)}) collective-permute-start(bf16[8,4,2048]{2,0,1:T(8,128)(2,1)S(1)} %get-tuple-element.71), channel_id=1, source_target_pairs={{0,96},{32,0},{64,32},{96,64},{1,97},{33,1},{65,33},{97,65},{2,98}... | collective-permute-start | bytes 393224 | tf_op jit(solution)/shard_map/ppermute | solution.py:196

commit v5 on v4

--- a/solution.py
+++ b/solution.py
@@ -38,34 +38,64 @@
 
 def _arrive_kernel(
     arrival_ref, lengths_ref, base_ref, incoming_ref, q_ref, fk_ref, fv_ref,
-    keys_out_ref, values_out_ref, acc_ref, peak_ref, mass_ref, in_sem, *, scale
+    keys_out_ref, values_out_ref, acc_ref, peak_ref, mass_ref,
+    kbuf, vbuf, in_sem, out_sem, *, scale
 ):
     r = pl.program_id(0)
-    positions = keys_out_ref.shape[1]
+    n = pl.num_programs(0)
+    slot = r % 2
+    positions = kbuf.shape[1]
     page_len = incoming_ref.shape[2]
     pages = positions // page_len
     heads = q_ref.shape[1]
     head_dim = q_ref.shape[3]
     new_count = fk_ref.shape[1]
-    copies = []
-    for pp in range(pages):
-        src = arrival_ref[r * pages + pp]
-        rows = pl.ds(pp * page_len, page_len)
-        for half, dst in ((0, keys_out_ref), (1, values_out_ref)):
-            copy = pltpu.make_async_copy(
-                incoming_ref.at[src, half], dst.at[0, rows], in_sem.at[half, pp]
-            )
-            copy.start()
-            copies.append(copy)
-    for copy in copies:
-        copy.wait()
+    bufs = (kbuf, vbuf)
+    outs = (keys_out_ref, values_out_ref)
+
+    def page_copy(req, s, half, pp, src):
+        return pltpu.make_async_copy(
+            incoming_ref.at[src, half],
+            bufs[half].at[s, pl.ds(pp * page_len, page_len)],
+            in_sem.at[half, s, pp],
+        )
+
+    def fetch(req, s):
+        for pp in range(pages):
+            src = arrival_ref[req * pages + pp]
+            for half in range(2):
+                page_copy(req, s, half, pp, src).start()
+
+    def wait_fetch(s):
+        for pp in range(pages):
+            for half in range(2):
+                page_copy(0, s, half, pp, 0).wait()
+
+    def out_copy(req, s, half):
+        return pltpu.make_async_copy(bufs[half].at[s], outs[half].at[req], out_sem.at[half, s])
+
+    @pl.when(r == 0)
+    def _():
+        fetch(0, 0)
+
+    wait_fetch(slot)
+
+    @pl.when(r + 1 < n)
+    def _():
+        @pl.when(r >= 1)
+        def _():
+            for half in range(2):
+                out_copy(r - 1, 1 - slot, half).wait()
+
+        fetch(r + 1, 1 - slot)
+
     length = lengths_ref[r]
     base = base_ref[0]
     spots = base + lax.broadcasted_iota(jnp.int32, (1, positions), 1)
     live = spots < length
     for kh in range(heads):
         cols = pl.ds(kh * head_dim, head_dim)
-        keys_h = keys_out_ref[0, :, cols]
+        keys_h = kbuf[slot, :, cols]
         query_h = q_ref[0, kh]
         scores = lax.dot_general(
             query_h, keys_h, (((1,), (1,)), ((), ())), preferred_element_type=jnp.float32
@@ -76,7 +106,7 @@
         peak_ref[0, kh] = peak
         mass_ref[0, kh] = jnp.sum(weights, axis=1, keepdims=True)
         acc_ref[0, kh] = jnp.dot(
-            weights.astype(jnp.bfloat16), values_out_ref[0, :, cols],
+            weights.astype(jnp.bfloat16), vbuf[slot, :, cols],
             preferred_element_type=jnp.float32,
         )
     first = length - base
@@ -89,14 +119,27 @@
         def _():
             start = pl.multiple_of(tile, page_len)
             rows = pl.ds(start, page_len)
-            block_k = keys_out_ref[0, rows, :]
-            block_v = values_out_ref[0, rows, :]
+            block_k = kbuf[slot, rows, :]
+            block_v = vbuf[slot, rows, :]
             for t in range(new_count):
                 hit = row_ids == first + t - tile
                 block_k = jnp.where(hit, fresh_k[t : t + 1, :], block_k)
                 block_v = jnp.where(hit, fresh_v[t : t + 1, :], block_v)
-            keys_out_ref[0, rows, :] = block_k
-            values_out_ref[0, rows, :] = block_v
+            kbuf[slot, rows, :] = block_k
+            vbuf[slot, rows, :] = block_v
+
+    for half in range(2):
+        out_copy(r, slot, half).start()
+
+    @pl.when(r == n - 1)
+    def _():
+        @pl.when(r >= 1)
+        def _():
+            for half in range(2):
+                out_copy(r - 1, 1 - slot, half).wait()
+
+        for half in range(2):
+            out_copy(r, slot, half).wait()
 
 
 def arrive_and_attend(arrival_src, lengths, base, incoming, queries, fresh_k, fresh_v, scale):
@@ -114,13 +157,18 @@
             pl.BlockSpec((1, new_count, kv_width), lambda r, *_: (r, 0, 0)),
         ],
         out_specs=[
-            pl.BlockSpec((1, positions, kv_width), lambda r, *_: (r, 0, 0)),
-            pl.BlockSpec((1, positions, kv_width), lambda r, *_: (r, 0, 0)),
+            pl.BlockSpec(memory_space=pl.ANY),
+            pl.BlockSpec(memory_space=pl.ANY),
             pl.BlockSpec((1, heads, rows, head_dim), lambda r, *_: (r, 0, 0, 0)),
             pl.BlockSpec((1, heads, rows, 1), lambda r, *_: (r, 0, 0, 0)),
             pl.BlockSpec((1, heads, rows, 1), lambda r, *_: (r, 0, 0, 0)),
         ],
-        scratch_shapes=[pltpu.SemaphoreType.DMA((2, pages))],
+        scratch_shapes=[
+            pltpu.VMEM((2, positions, kv_width), jnp.bfloat16),
+            pltpu.VMEM((2, positions, kv_width), jnp.bfloat16),
+            pltpu.SemaphoreType.DMA((2, 2, pages)),
+            pltpu.SemaphoreType.DMA((2, 2)),
+        ],
     )
     cache_bytes = 2 * local_reqs * positions * kv_width * 2
     return pl.pallas_call(

time: 281 us -> 275 us (0.979)
  Pallas kernels: 31.1 us -> 26.8 us
    pallas_call x1, Pallas kernels: 31.1 us -> 26.8 us  [arrive_and_attend(): pl.pallas_call(functools.partial(_arrive_kernel, scale=scale), out_shape=...]
where the time goes in v5:
time: 275 us; the launch traced here: 272 us
  waiting for transfers between devices  124 us (45%)
  starting transfers between devices  40.1 us (15%)
  local copies, waits for them, and re-layouts  37.2 us (14%)
  other arithmetic  32.8 us (12%)
  Pallas kernels  26.8 us (10%)
  matrix products  10 us (4%)
    all_to_all x1, waiting for transfers between devices, shards(): lax.all_to_all(outgoing, ('req', 'seq'), split_axis=0, concat_axis=0, til...  95.4 us
    pallas_call x1, Pallas kernels, arrive_and_attend(): pl.pallas_call(functools.partial(_arrive_kernel, scale=scale), out_shape=...  26.8 us
    ppermute x5, waiting for transfers between devices, shards(): other = lax.ppermute(packed, 'seq', pairs)  20 us
    ppermute x12, starting transfers between devices, shift(): return lax.ppermute(value, 'req', pairs)  17 us
    ppermute x5, starting transfers between devices, shards(): other = lax.ppermute(packed, 'seq', pairs)  13.8 us
    gather x2, local copies, waits for them, and re-layouts, shards(): outgoing = jnp.stack([pool_keys[send_pick], pool_values[send_pick]], axis=1)  10 us
    all_to_all x1, starting transfers between devices, shards(): lax.all_to_all(outgoing, ('req', 'seq'), split_axis=0, concat_axis=0, til...  9.25 us
    ppermute x12, waiting for transfers between devices, shift(): return lax.ppermute(value, 'req', pairs)  8.62 us
  transfers between devices with their start and end apart: 18, of which 10 were waited for; matrix products, arithmetic and copies ran while one was open for 14% of the time, Pallas kernels for 0%

profile of v5, /device:TPU:32, one launch (start us, length us, event | category | flops | bytes accessed | tf_op | source)
XLA Modules:
  0.0 272.1 jit_solution(13056953136144240643)
XLA Ops:
  0.6 1.3 fusion.14
  1.9 1.0 fusion.16
  3.0 2.8 %collective-permute-start.2 = (bf16[8,4,2048]{2,0,1:T(8,128)(2,1)S(1)}, bf16[8,4,2048]{2,0,1:T(8,128)(2,1)S(1)}, u32[]{:S(2)}, u32[]{:S(2)}) collective-permute-start(bf16[8,4,2048]{2,0,1:T(8,128)(2,1)S(1)} %fusion.16), channel_id=1, source_target_pairs={{0,96},{32,0},{64,32},{96,64},{1,97},{33,1},{65,33},{97,65},{2,98}... | collective-permute-start | bytes 393224 | tf_op jit(solution)/shard_map/ppermute | solution.py:244
  5.8 0.8 collective-permute-start.1
  6.6 0.9 collective-permute-start
  7.5 0.8 select_reduce_fusion
  8.3 1.5 gather_fusion
  10.8 5.0 %gather_fusion.2 = bf16[128,16,1024]{2,1,0:T(8,128)(2,1)} fusion(bf16[128,16,1024]{2,1,0:T(8,128)(2,1)} %param.18, s32[1024]{0:T(1024)S(1)} %pad_clamp_fusion.2), kind=kCustom, calls=%fused_computation.2 | custom fusion | bytes 8389120 | tf_op jit(solution)/shard_map/gather | solution.py:266
  15.8 5.0 %gather_fusion.1 = bf16[128,16,1024]{2,1,0:T(8,128)(2,1)} fusion(bf16[128,16,1024]{2,1,0:T(8,128)(2,1)} %param.17, s32[1024]{0:T(1024)S(1)} %pad_clamp_fusion.2), kind=kCustom, calls=%fused_computation.1 | custom fusion | bytes 8389120 | tf_op jit(solution)/shard_map/gather | solution.py:266
  20.8 1.5 copy.208
  23.1 4.0 %copy.207 = bf16[512,2048]{1,0:T(8,128)(2,1)} copy(bf16[512,2048]{0,1:T(8,128)(2,1)} %bitcast.159) | data formatting | bytes 4194304 | tf_op jit(solution)/shard_map/dot_general | solution.py:252
  27.4 1.5 fusion.8
  29.1 2.7 fusion.10
  32.2 1.3 convolution_convert_fusion.1
  33.5 1.9 collective-permute-start.5
  35.4 2.0 collective-permute-start.4
  37.4 0.8 collective-permute-start.3
  38.2 6.3 %maximum_bitcast_fusion = bf16[128,1,2,16,1024]{4,3,2,1,0:T(8,128)(2,1)} fusion(bf16[128,1,16,1024]{3,2,1,0:T(8,128)(2,1)S(1)} %bitcast.156, bf16[128,1,16,1024]{3,2,1,0:T(8,128)(2,1)} %bitcast.157), kind=kLoop, calls=%fused_computation.5 | loop fusion | flops 4194304 | bytes 16777216 | tf_op jit(solution)/shard_map/reshape | solution.py:267
  44.5 0.9 pad_maximum_fusion.7
  45.4 9.3 %all-to-all-start = ((bf16[128,1,2,16,1024]{4,3,2,1,0:T(8,128)(2,1)}), bf16[128,1,2,16,1024]{4,3,2,1,0:T(8,128)(2,1)}, u32[]{:S(2)}, u32[]{:S(2)}) async-start(bf16[128,1,2,16,1024]{4,3,2,1,0:T(8,128)(2,1)} %maximum_bitcast_fusion), calls=%async_computation | async-start | bytes 16777216 | tf_op jit(solution)/shard_map/all_to_all | solution.py:269
  57.4 0.7 copy.154
  59.4 95.4 %all-to-all-done = bf16[128,1,2,16,1024]{4,3,2,1,0:T(8,128)(2,1)} async-done(((bf16[128,1,2,16,1024]{4,3,2,1,0:T(8,128)(2,1)}), bf16[128,1,2,16,1024]{4,3,2,1,0:T(8,128)(2,1)}, u32[]{:S(2)}, u32[]{:S(2)}) %all-to-all-start) | async-done | bytes 8388640 | tf_op jit(solution)/shard_map/all_to_all | solution.py:269
  154.8 26.8 %arrive_and_attend.1 = (bf16[8,256,1024]{2,1,0:T(8,128)(2,1)}, bf16[8,256,1024]{2,1,0:T(8,128)(2,1)}, f32[8,8,8,128]{3,2,1,0:T(8,128)}, f32[8,8,8,1]{3,2,1,0:T(8,128)}, f32[8,8,8,1]{3,2,1,0:T(8,128)}) custom-call(s32[128]{0:T(128)} %and_select_fusion.4.arrival_ref, s32[8]{0:T(128)} %dynamic_slice.19.lengths_ref, s32[1]{0:T(128)} %bitcast.3.base_ref, ...), custom_call_target="tpu_custom_call" | custom-call | flops 67108864 | bytes 16777216 | tf_op jit(solution)/shard_map/arrive_and_attend/pallas_call | solution.py:174
  181.6 1.1 reduce.3
  182.8 1.1 reduce.2
  184.0 1.0 pad_maximum_fusion.1
  185.2 1.4 collective-permute-done.6
  187.3 1.9 fusion.52
  189.3 0.7 pad_maximum_fusion.2
  190.0 2.9 %collective-permute-start.7 = (f32[520,128]{1,0:T(8,128)}, f32[520,128]{1,0:T(8,128)}, u32[]{:S(2)}, u32[]{:S(2)}) collective-permute-start(f32[520,128]{1,0:T(8,128)} %pad_maximum_fusion.2), channel_id=1, source_target_pairs={{0,2},{1,3},{2,0},{3,1},{4,6},{5,7},{6,4},{7,5},{8,10},{9,11},{10,... | collective-permute-start | bytes 798728 | tf_op jit(solution)/shard_map/ppermute | solution.py:307
  192.9 7.2 %collective-permute-done.7 = f32[520,128]{1,0:T(8,128)} collective-permute-done((f32[520,128]{1,0:T(8,128)}, f32[520,128]{1,0:T(8,128)}, u32[]{:S(2)}, u32[]{:S(2)}) %collective-permute-start.7) | collective-permute-done | bytes 266272 | tf_op jit(solution)/shard_map/ppermute | solution.py:307
  200.8 0.8 multiply_add_fusion.7
  201.6 1.8 fusion.53
  203.4 0.7 pad_maximum_fusion.3
  204.1 3.2 %collective-permute-start.8 = (f32[520,128]{1,0:T(8,128)}, f32[520,128]{1,0:T(8,128)}, u32[]{:S(2)}, u32[]{:S(2)}) collective-permute-start(f32[520,128]{1,0:T(8,128)} %pad_maximum_fusion.3), channel_id=1, source_target_pairs={{0,4},{1,5},{2,6},{3,7},{4,0},{5,1},{6,2},{7,3},{8,12},{9,13},{10,... | collective-permute-start | bytes 798728 | tf_op jit(solution)/shard_map/ppermute | solution.py:307
  207.3 6.7 %collective-permute-done.8 = f32[520,128]{1,0:T(8,128)} collective-permute-done((f32[520,128]{1,0:T(8,128)}, f32[520,128]{1,0:T(8,128)}, u32[]{:S(2)}, u32[]{:S(2)}) %collective-permute-start.8) | collective-permute-done | bytes 266272 | tf_op jit(solution)/shard_map/ppermute | solution.py:307
  214.0 0.8 multiply_add_fusion.6
  215.5 1.8 fusion.54
  217.3 0.7 pad_maximum_fusion.4
  218.0 4.9 %collective-permute-start.9 = (f32[520,128]{1,0:T(8,128)}, f32[520,128]{1,0:T(8,128)}, u32[]{:S(2)}, u32[]{:S(2)}) collective-permute-start(f32[520,128]{1,0:T(8,128)} %pad_maximum_fusion.4), channel_id=1, source_target_pairs={{0,8},{1,9},{2,10},{3,11},{4,12},{5,13},{6,14},{7,15},{8,0},{9,1},... | collective-permute-start | bytes 798728 | tf_op jit(solution)/shard_map/ppermute | solution.py:307
  223.6 4.6 %collective-permute-done.9 = f32[520,128]{1,0:T(8,128)} collective-permute-done((f32[520,128]{1,0:T(8,128)}, f32[520,128]{1,0:T(8,128)}, u32[]{:S(2)}, u32[]{:S(2)}) %collective-permute-start.9) | collective-permute-done | bytes 266272 | tf_op jit(solution)/shard_map/ppermute | solution.py:307
  228.9 0.8 fusion.37
  229.7 1.8 fusion.55
  231.5 0.7 pad_maximum_fusion.5
  232.2 2.7 %collective-permute-start.10 = (f32[520,128]{1,0:T(8,128)}, f32[520,128]{1,0:T(8,128)}, u32[]{:S(2)}, u32[]{:S(2)}) collective-permute-start(f32[520,128]{1,0:T(8,128)} %pad_maximum_fusion.5), channel_id=1, source_target_pairs={{0,16},{1,17},{2,18},{3,19},{4,20},{5,21},{6,22},{7,23},{8,24},{9,... | collective-permute-start | bytes 798728 | tf_op jit(solution)/shard_map/ppermute | solution.py:307
  235.0 1.0 fusion.21
  236.0 1.4 copy.181
  241.1 0.8 fusion.51
  242.3 0.7 fusion.24
  243.0 1.1 copy.184
  244.4 1.5 multiply_add_fusion.4
  245.9 0.9 copy.197
  248.2 0.8 copy.164
  249.2 0.8 copy.160
  250.0 1.0 slice.160
  251.0 3.0 %fusion.3 = bf16[8,4,8,2,128]{4,1,3,2,0:T(4,128)(2,1)S(1)} fusion(bf16[8,8,2,4,4]{4,3,2,1,0:T(4,128)(2,1)} %copy.184, f32[8,8,2,4,128]{4,3,2,1,0:T(4,128)S(1)} %bitcast.169, f32[8,8,2,4,128]{4,3,2,1,0:T(4,128)S(1)} %bitcast.173, f32[8,8,2,4,128]{4,3,2,1,0:T(4,128)} %bitcast.172, f32[8,8,2,4,128]{4,3,2,1,0:T(4,128)} %bitcast.171, ...), kind=kOutput, calls=%fused_computation.11 | convolution fusion | flops 2424832 | bytes 1798149 | tf_op jit(solution)/shard_map/rkgts,rskd->rkgtd/dot_general | solution.py:335
  254.2 2.2 collective-permute-start.13
  257.4 0.8 collective-permute-done.13
  258.2 3.8 %collective-permute-done.12 = bf16[8,4,512]{2,0,1:T(8,128)(2,1)S(1)} collective-permute-done((bf16[8,4,512]{2,0,1:T(8,128)(2,1)S(1)}, bf16[8,4,512]{2,0,1:T(8,128)(2,1)S(1)}, u32[]{:S(2)}, u32[]{:S(2)}) %collective-permute-start.12) | collective-permute-done | bytes 32800 | tf_op jit(solution)/shard_map/ppermute | solution.py:244
  262.8 2.5 collective-permute-start.15
  265.3 2.1 collective-permute-start.14
  267.4 2.9 %collective-permute-done.16 = bf16[8,4,2048]{2,0,1:T(8,128)(2,1)S(1)} collective-permute-done((bf16[8,4,2048]{2,0,1:T(8,128)(2,1)S(1)}, bf16[8,4,2048]{2,0,1:T(8,128)(2,1)S(1)}, u32[]{:S(2)}, u32[]{:S(2)}) %collective-permute-start.16) | collective-permute-done | bytes 131104 | tf_op jit(solution)/shard_map/ppermute | solution.py:244
  270.4 0.9 collective-permute-done.14
  271.3 0.8 copy.200
  (127 shorter events, 18.4 us)
Async XLA Ops:
  0.6 261.6 %copy-start = (bf16[512,2048]{1,0:T(8,128)(2,1)S(1)}, bf16[512,2048]{1,0:T(8,128)(2,1)}, u32[]{:S(2)}) copy-start(bf16[512,2048]{1,0:T(8,128)(2,1)} %param.16) | copy-start | bytes 6291460
  3.0 24.4 %collective-permute-start.2 = (bf16[8,4,2048]{2,0,1:T(8,128)(2,1)S(1)}, bf16[8,4,2048]{2,0,1:T(8,128)(2,1)S(1)}, u32[]{:S(2)}, u32[]{:S(2)}) collective-permute-start(bf16[8,4,2048]{2,0,1:T(8,128)(2,1)S(1)} %fusion.16), channel_id=1, source_target_pairs={{0,96},{32,0},{64,32},{96,64},{1,97},{33,1},{65,33},{97,65},{2,98}... | collective-permute-start | bytes 393224 | tf_op jit(solution)/shard_map/ppermute | solution.py:244
  5.8 21.6 %collective-permute-start.1 = (bf16[8,4,2048]{2,0,1:T(8,128)(2,1)S(1)}, bf16[8,4,2048]{2,0,1:T(8,128)(2,1)}, u32[]{:S(2)}, u32[]{:S(2)}) collective-permute-start(bf16[8,4,2048]{2,0,1:T(8,128)(2,1)S(1)} %fusion.16), channel_id=1, source_target_pairs={{0,64},{32,96},{64,0},{96,32},{1,65},{33,97},{65,1},{97,33},{2,66}... | collective-permute-start | bytes 393224 | tf_op jit(solution)/shard_map/ppermute | solution.py:244
  6.6 20.8 %collective-permute-start = (bf16[8,4,2048]{2,0,1:T(8,128)(2,1)S(1)}, bf16[8,4,2048]{2,0,1:T(8,128)(2,1)}, u32[]{:S(2)}, u32[]{:S(2)}) collective-permute-start(bf16[8,4,2048]{2,0,1:T(8,128)(2,1)S(1)} %fusion.16), channel_id=1, source_target_pairs={{0,32},{32,64},{64,96},{96,0},{1,33},{33,65},{65,97},{97,1},{2,34}... | collective-permute-start | bytes 393224 | tf_op jit(solution)/shard_map/ppermute | solution.py:244
  10.0 5.8 %copy-start.2 = (s32[4,8,32,16]{3,2,1,0:T(8,128)}, s32[4,8,32,16]{3,2,1,0:T(8,128)S(1)}, u32[]{:S(2)}) copy-start(s32[4,8,32,16]{3,2,1,0:T(8,128)S(1)} %reshape.885) | copy-start | bytes 196612
  27.4 4.8 %copy-start.10 = (bf16[2048,256]{1,0:T(8,128)(2,1)S(1)}, bf16[2048,256]{1,0:T(8,128)(2,1)}, u32[]{:S(2)}) copy-start(bf16[2048,256]{1,0:T(8,128)(2,1)} %param.15) | copy-start | bytes 3145732
  29.1 9.1 %copy-start.1 = (bf16[128,16,1024]{2,1,0:T(8,128)(2,1)S(1)}, bf16[128,16,1024]{2,1,0:T(8,128)(2,1)}, u32[]{:S(2)}) copy-start(bf16[128,16,1024]{2,1,0:T(8,128)(2,1)} %gather_fusion.2) | copy-start | bytes 12582916
  33.5 10.9 %collective-permute-start.5 = (bf16[8,4,1024]{2,0,1:T(8,128)(2,1)S(1)}, bf16[8,4,1024]{2,0,1:T(8,128)(2,1)S(1)}, u32[]{:S(2)}, u32[]{:S(2)}) collective-permute-start(bf16[8,4,1024]{2,0,1:T(8,128)(2,1)S(1)} %get-tuple-element.103), channel_id=1, source_target_pairs={{0,32},{32,64},{64,96},{96,0},{1,33},{33,65},{65,97},{97,1},{2,34}... | collective-permute-start | bytes 196616 | tf_op jit(solution)/shard_map/ppermute | solution.py:244
  35.4 9.1 %collective-permute-start.4 = (bf16[8,4,1024]{2,0,1:T(8,128)(2,1)S(1)}, bf16[8,4,1024]{2,0,1:T(8,128)(2,1)S(1)}, u32[]{:S(2)}, u32[]{:S(2)}) collective-permute-start(bf16[8,4,1024]{2,0,1:T(8,128)(2,1)S(1)} %get-tuple-element.104), channel_id=1, source_target_pairs={{0,64},{32,96},{64,0},{96,32},{1,65},{33,97},{65,1},{97,33},{2,66}... | collective-permute-start | bytes 196616 | tf_op jit(solution)/shard_map/ppermute | solution.py:244
  37.4 7.1 %collective-permute-start.3 = (bf16[8,4,1024]{2,0,1:T(8,128)(2,1)S(1)}, bf16[8,4,1024]{2,0,1:T(8,128)(2,1)}, u32[]{:S(2)}, u32[]{:S(2)}) collective-permute-start(bf16[8,4,1024]{2,0,1:T(8,128)(2,1)S(1)} %get-tuple-element.105), channel_id=1, source_target_pairs={{0,96},{32,0},{64,32},{96,64},{1,97},{33,1},{65,33},{97,65},{2,98}... | collective-permute-start | bytes 196616 | tf_op jit(solution)/shard_map/ppermute | solution.py:244
  45.3 9.3 %copy-start.3 = (s32[4,8,32,16]{3,2,1,0:T(8,128)S(1)}, s32[4,8,32,16]{3,2,1,0:T(8,128)}, u32[]{:S(2)}) copy-start(s32[4,8,32,16]{3,2,1,0:T(8,128)} %copy-done.2) | copy-start | bytes 196612
  45.4 109.4 %all-to-all-start = ((bf16[128,1,2,16,1024]{4,3,2,1,0:T(8,128)(2,1)}), bf16[128,1,2,16,1024]{4,3,2,1,0:T(8,128)(2,1)}, u32[]{:S(2)}, u32[]{:S(2)}) async-start(bf16[128,1,2,16,1024]{4,3,2,1,0:T(8,128)(2,1)} %maximum_bitcast_fusion), calls=%async_computation | async-start | bytes 16777216 | tf_op jit(solution)/shard_map/all_to_all | solution.py:269
  185.0 52.5 %copy-start.6 = (f32[8,8,8,1]{3,2,1,0:T(8,128)S(1)}, f32[8,8,8,1]{3,2,1,0:T(8,128)}, u32[]{:S(2)}) copy-start(f32[8,8,8,1]{3,2,1,0:T(8,128)} %get-tuple-element.13) | copy-start | bytes 6148
  185.0 1.6 collective-permute-start.6
  186.6 0.7 copy-start.8
  187.3 50.7 %copy-start.5 = (f32[8,8,8,1]{3,2,1,0:T(8,128)S(1)}, f32[8,8,8,1]{3,2,1,0:T(8,128)}, u32[]{:S(2)}) copy-start(f32[8,8,8,1]{3,2,1,0:T(8,128)} %get-tuple-element.14) | copy-start | bytes 6148
  190.0 10.2 %collective-permute-start.7 = (f32[520,128]{1,0:T(8,128)}, f32[520,128]{1,0:T(8,128)}, u32[]{:S(2)}, u32[]{:S(2)}) collective-permute-start(f32[520,128]{1,0:T(8,128)} %pad_maximum_fusion.2), channel_id=1, source_target_pairs={{0,2},{1,3},{2,0},{3,1},{4,6},{5,7},{6,4},{7,5},{8,10},{9,11},{10,... | collective-permute-start | bytes 798728 | tf_op jit(solution)/shard_map/ppermute | solution.py:307
  204.1 9.9 %collective-permute-start.8 = (f32[520,128]{1,0:T(8,128)}, f32[520,128]{1,0:T(8,128)}, u32[]{:S(2)}, u32[]{:S(2)}) collective-permute-start(f32[520,128]{1,0:T(8,128)} %pad_maximum_fusion.3), channel_id=1, source_target_pairs={{0,4},{1,5},{2,6},{3,7},{4,0},{5,1},{6,2},{7,3},{8,12},{9,13},{10,... | collective-permute-start | bytes 798728 | tf_op jit(solution)/shard_map/ppermute | solution.py:307
  218.0 10.2 %collective-permute-start.9 = (f32[520,128]{1,0:T(8,128)}, f32[520,128]{1,0:T(8,128)}, u32[]{:S(2)}, u32[]{:S(2)}) collective-permute-start(f32[520,128]{1,0:T(8,128)} %pad_maximum_fusion.4), channel_id=1, source_target_pairs={{0,8},{1,9},{2,10},{3,11},{4,12},{5,13},{6,14},{7,15},{8,0},{9,1},... | collective-permute-start | bytes 798728 | tf_op jit(solution)/shard_map/ppermute | solution.py:307
  229.7 21.3 %copy-start.7 = (f32[8,8,8,128]{3,2,1,0:T(8,128)S(1)}, f32[8,8,8,128]{3,2,1,0:T(8,128)}, u32[]{:S(2)}) copy-start(f32[8,8,8,128]{3,2,1,0:T(8,128)} %get-tuple-element.12) | copy-start | bytes 786436
  232.2 8.9 %collective-permute-start.10 = (f32[520,128]{1,0:T(8,128)}, f32[520,128]{1,0:T(8,128)}, u32[]{:S(2)}, u32[]{:S(2)}) collective-permute-start(f32[520,128]{1,0:T(8,128)} %pad_maximum_fusion.5), channel_id=1, source_target_pairs={{0,16},{1,17},{2,18},{3,19},{4,20},{5,21},{6,22},{7,23},{8,24},{9,... | collective-permute-start | bytes 798728 | tf_op jit(solution)/shard_map/ppermute | solution.py:307
  236.0 15.0 %copy-start.9 = (f32[512,128]{1,0:T(8,128)S(1)}, f32[512,128]{1,0:T(8,128)}, u32[]{:S(2)}) copy-start(f32[512,128]{1,0:T(8,128)} %get-tuple-element.94) | copy-start | bytes 786436
  254.0 17.2 %copy-start.4 = (bf16[8,4,2048]{2,1,0:T(4,128)(2,1)S(1)}, bf16[8,4,2048]{2,1,0:T(4,128)(2,1)}, u32[]{:S(2)}) copy-start(bf16[8,4,2048]{2,1,0:T(4,128)(2,1)} %param.11) | copy-start | bytes 393220
  254.2 4.0 %collective-permute-start.13 = (bf16[8,4,512]{2,0,1:T(8,128)(2,1)S(1)}, bf16[8,4,512]{2,0,1:T(8,128)(2,1)S(1)}, u32[]{:S(2)}, u32[]{:S(2)}) collective-permute-start(bf16[8,4,512]{2,0,1:T(8,128)(2,1)S(1)} %get-tuple-element.111), channel_id=1, source_target_pairs={{0,96},{32,0},{64,32},{96,64},{1,97},{33,1},{65,33},{97,65},{2,98}... | collective-permute-start | bytes 98312 | tf_op jit(solution)/shard_map/ppermute | solution.py:244
  256.4 5.6 %collective-permute-start.12 = (bf16[8,4,512]{2,0,1:T(8,128)(2,1)S(1)}, bf16[8,4,512]{2,0,1:T(8,128)(2,1)S(1)}, u32[]{:S(2)}, u32[]{:S(2)}) collective-permute-start(bf16[8,4,512]{2,0,1:T(8,128)(2,1)S(1)} %get-tuple-element.112), channel_id=1, source_target_pairs={{0,64},{32,96},{64,0},{96,32},{1,65},{33,97},{65,1},{97,33},{2,66}... | collective-permute-start | bytes 98312 | tf_op jit(solution)/shard_map/ppermute | solution.py:244
  256.8 5.4 %collective-permute-start.11 = (bf16[8,4,512]{2,0,1:T(8,128)(2,1)S(1)}, bf16[8,4,512]{2,0,1:T(8,128)(2,1)S(1)}, u32[]{:S(2)}, u32[]{:S(2)}) collective-permute-start(bf16[8,4,512]{2,0,1:T(8,128)(2,1)S(1)} %get-tuple-element.113), channel_id=1, source_target_pairs={{0,32},{32,64},{64,96},{96,0},{1,33},{33,65},{65,97},{97,1},{2,34}... | collective-permute-start | bytes 98312 | tf_op jit(solution)/shard_map/ppermute | solution.py:244
  262.7 7.7 %collective-permute-start.16 = (bf16[8,4,2048]{2,0,1:T(8,128)(2,1)S(1)}, bf16[8,4,2048]{2,0,1:T(8,128)(2,1)S(1)}, u32[]{:S(2)}, u32[]{:S(2)}) collective-permute-start(bf16[8,4,2048]{2,0,1:T(8,128)(2,1)S(1)} %get-tuple-element.72), channel_id=1, source_target_pairs={{0,32},{32,64},{64,96},{96,0},{1,33},{33,65},{65,97},{97,1},{2,34}... | collective-permute-start | bytes 393224 | tf_op jit(solution)/shard_map/ppermute | solution.py:244
  262.8 7.6 %collective-permute-start.15 = (bf16[8,4,2048]{2,0,1:T(8,128)(2,1)S(1)}, bf16[8,4,2048]{2,0,1:T(8,128)(2,1)S(1)}, u32[]{:S(2)}, u32[]{:S(2)}) collective-permute-start(bf16[8,4,2048]{2,0,1:T(8,128)(2,1)S(1)} %get-tuple-element.73), channel_id=1, source_target_pairs={{0,64},{32,96},{64,0},{96,32},{1,65},{33,97},{65,1},{97,33},{2,66}... | collective-permute-start | bytes 393224 | tf_op jit(solution)/shard_map/ppermute | solution.py:244
  265.3 5.9 %collective-permute-start.14 = (bf16[8,4,2048]{2,0,1:T(8,128)(2,1)S(1)}, bf16[8,4,2048]{2,0,1:T(8,128)(2,1)S(1)}, u32[]{:S(2)}, u32[]{:S(2)}) collective-permute-start(bf16[8,4,2048]{2,0,1:T(8,128)(2,1)S(1)} %get-tuple-element.71), channel_id=1, source_target_pairs={{0,96},{32,0},{64,32},{96,64},{1,97},{33,1},{65,33},{97,65},{2,98}... | collective-permute-start | bytes 393224 | tf_op jit(solution)/shard_map/ppermute | solution.py:244

commit v6 on v5

--- a/solution.py
+++ b/solution.py
@@ -244,6 +244,10 @@
         return lax.ppermute(value, "req", pairs)
 
     row_block = jnp.concatenate([shift(normed, k) for k in range(req_count)], axis=0)
+    outgoing = jnp.stack([pool_keys[send_pick], pool_values[send_pick]], axis=1)
+    outgoing = outgoing.reshape(devices, per_peer, 2, page_len, kv_width)
+    outgoing, row_block = lax.optimization_barrier((outgoing, row_block))
+    incoming = lax.all_to_all(outgoing, ("req", "seq"), split_axis=0, concat_axis=0, tiled=True)
     row_count = row_block.shape[0]
     flat_rows = row_block.reshape(row_count * new_count, model_width)
     row_group = (req_index - jnp.arange(req_count, dtype=jnp.int32)) % req_count
@@ -263,10 +267,6 @@
     projected = jnp.concatenate([queries_now, keys_now, values_now], axis=-1).astype(jnp.bfloat16)
     projected = projected.reshape(req_count, local_reqs, new_count, query_cols + 2 * key_cols)
     by_shift = jnp.stack([shift(projected[k], -k) for k in range(req_count)], axis=0)
-    outgoing = jnp.stack([pool_keys[send_pick], pool_values[send_pick]], axis=1)
-    outgoing = outgoing.reshape(devices, per_peer, 2, page_len, kv_width)
-    outgoing, by_shift = lax.optimization_barrier((outgoing, by_shift))
-    incoming = lax.all_to_all(outgoing, ("req", "seq"), split_axis=0, concat_axis=0, tiled=True)
     source_block = (jnp.arange(req_count, dtype=jnp.int32) - req_index) % req_count
     owned_rows = jnp.take(by_shift, source_block, axis=0)
     owned_rows = jnp.transpose(owned_rows, (1, 2, 0, 3))

time: 275 us -> 263 us (0.956)
  starting transfers between devices: 40.1 us -> 29.2 us
    all_to_all x1, waiting for transfers between devices: 95.4 us -> 0.01 us  [shards(): lax.all_to_all(outgoing, ('req', 'seq'), split_axis=0, concat_axis=0, til...]
    ppermute x12, waiting for transfers between devices: 8.62 us -> 98.4 us  [shift(): return lax.ppermute(value, 'req', pairs)]
    ppermute x5, starting transfers between devices: 13.8 us -> 3.17 us  [shards(): other = lax.ppermute(packed, 'seq', pairs)]
    ppermute x5, waiting for transfers between devices: 20 us -> 24.9 us  [shards(): other = lax.ppermute(packed, 'seq', pairs)]
  transfers between devices with their start and end apart: 18 -> 18, of which waited for: 10 -> 13; matrix products, arithmetic and copies ran while one was open for 14% -> 17% of each run, Pallas kernels for 0% -> 0%
where the time goes in v6:
time: 263 us; the launch traced here: 261 us
  waiting for transfers between devices  123 us (47%)
  local copies, waits for them, and re-layouts  37.9 us (14%)
  other arithmetic  34.1 us (13%)
  starting transfers between devices  29.2 us (11%)
  Pallas kernels  26.8 us (10%)
  matrix products  8.94 us (3%)
    ppermute x12, waiting for transfers between devices, shift(): return lax.ppermute(value, 'req', pairs)  98.4 us
    pallas_call x1, Pallas kernels, arrive_and_attend(): pl.pallas_call(functools.partial(_arrive_kernel, scale=scale), out_shape=...  26.8 us
    ppermute x5, waiting for transfers between devices, shards(): other = lax.ppermute(packed, 'seq', pairs)  24.9 us
    ppermute x12, starting transfers between devices, shift(): return lax.ppermute(value, 'req', pairs)  16 us
    gather x2, local copies, waits for them, and re-layouts, shards(): outgoing = jnp.stack([pool_keys[send_pick], pool_values[send_pick]], axis=1)  10 us
    all_to_all x1, starting transfers between devices, shards(): lax.all_to_all(outgoing, ('req', 'seq'), split_axis=0, concat_axis=0, til...  10 us
    reshape x1, other arithmetic, shards(): outgoing = outgoing.reshape(devices, per_peer, 2, page_len, kv_width)  7.49 us
    slice x4, other arithmetic, shards(): peer_sum = other[:gathered_sum.size // HD].reshape(gathered_sum.shape)  7.32 us
  transfers between devices with their start and end apart: 18, of which 13 were waited for; matrix products, arithmetic and copies ran while one was open for 17% of the time, Pallas kernels for 0%

profile of v6, /device:TPU:32, one launch (start us, length us, event | category | flops | bytes accessed | tf_op | source)
XLA Modules:
  0.0 261.4 jit_solution(18005861615365111003)
XLA Ops:
  0.6 1.3 fusion.14
  1.9 1.0 fusion.16
  3.0 2.8 %collective-permute-start.2 = (bf16[8,4,2048]{2,0,1:T(8,128)(2,1)S(1)}, bf16[8,4,2048]{2,0,1:T(8,128)(2,1)S(1)}, u32[]{:S(2)}, u32[]{:S(2)}) collective-permute-start(bf16[8,4,2048]{2,0,1:T(8,128)(2,1)S(1)} %fusion.16), channel_id=1, source_target_pairs={{0,96},{32,0},{64,32},{96,64},{1,97},{33,1},{65,33},{97,65},{2,98}... | collective-permute-start | bytes 393224 | tf_op jit(solution)/shard_map/ppermute | solution.py:244
  5.8 0.8 collective-permute-start.1
  6.6 0.9 collective-permute-start
  7.5 0.8 select_reduce_fusion
  8.3 1.5 gather_fusion
  10.7 5.0 %gather_fusion.2 = bf16[128,16,1024]{2,1,0:T(8,128)(2,1)} fusion(bf16[128,16,1024]{2,1,0:T(8,128)(2,1)} %param.18, s32[1024]{0:T(1024)S(1)} %pad_clamp_fusion.2), kind=kCustom, calls=%fused_computation.2 | custom fusion | bytes 8389120 | tf_op jit(solution)/shard_map/gather | solution.py:247
  15.7 5.0 %gather_fusion.1 = bf16[128,16,1024]{2,1,0:T(8,128)(2,1)} fusion(bf16[128,16,1024]{2,1,0:T(8,128)(2,1)} %param.17, s32[1024]{0:T(1024)S(1)} %pad_clamp_fusion.2), kind=kCustom, calls=%fused_computation.1 | custom fusion | bytes 8389120 | tf_op jit(solution)/shard_map/gather | solution.py:247
  20.7 7.5 %maximum_bitcast_fusion = bf16[128,1,2,16,1024]{4,3,2,1,0:T(8,128)(2,1)} fusion(bf16[128,1,16,1024]{3,2,1,0:T(8,128)(2,1)} %bitcast.157, bf16[128,1,16,1024]{3,2,1,0:T(8,128)(2,1)} %bitcast.158), kind=kLoop, calls=%fused_computation.5 | loop fusion | flops 4194304 | bytes 16777216 | tf_op jit(solution)/shard_map/reshape | solution.py:248
  28.2 0.9 pad_maximum_fusion
  29.2 10.0 %all-to-all-start = ((bf16[128,1,2,16,1024]{4,3,2,1,0:T(8,128)(2,1)}), bf16[128,1,2,16,1024]{4,3,2,1,0:T(8,128)(2,1)}, u32[]{:S(2)}, u32[]{:S(2)}) async-start(bf16[128,1,2,16,1024]{4,3,2,1,0:T(8,128)(2,1)} %maximum_bitcast_fusion), calls=%async_computation | async-start | bytes 16777216 | tf_op jit(solution)/shard_map/all_to_all | solution.py:250
  39.2 2.3 copy.208
  42.3 3.9 %copy.207 = bf16[512,2048]{1,0:T(8,128)(2,1)} copy(bf16[512,2048]{0,1:T(8,128)(2,1)} %bitcast.162) | data formatting | bytes 4194304 | tf_op jit(solution)/shard_map/dot_general | solution.py:256
  48.4 1.7 fusion.8
  50.3 2.4 fusion.10
  53.4 1.5 collective-permute-start.5
  55.0 2.7 %collective-permute-start.4 = (bf16[8,4,1024]{2,0,1:T(8,128)(2,1)S(1)}, bf16[8,4,1024]{2,0,1:T(8,128)(2,1)S(1)}, u32[]{:S(2)}, u32[]{:S(2)}) collective-permute-start(bf16[8,4,1024]{2,0,1:T(8,128)(2,1)S(1)} %get-tuple-element.104), channel_id=1, source_target_pairs={{0,64},{32,96},{64,0},{96,32},{1,65},{33,97},{65,1},{97,33},{2,66}... | collective-permute-start | bytes 196616 | tf_op jit(solution)/shard_map/ppermute | solution.py:244
  57.7 1.4 collective-permute-start.3
  59.1 78.2 %collective-permute-done.5 = bf16[8,4,1024]{2,0,1:T(8,128)(2,1)S(1)} collective-permute-done((bf16[8,4,1024]{2,0,1:T(8,128)(2,1)S(1)}, bf16[8,4,1024]{2,0,1:T(8,128)(2,1)S(1)}, u32[]{:S(2)}, u32[]{:S(2)}) %collective-permute-start.5) | collective-permute-done | bytes 65568 | tf_op jit(solution)/shard_map/ppermute | solution.py:244
  137.4 10.4 %collective-permute-done.4 = bf16[8,4,1024]{2,0,1:T(8,128)(2,1)S(1)} collective-permute-done((bf16[8,4,1024]{2,0,1:T(8,128)(2,1)S(1)}, bf16[8,4,1024]{2,0,1:T(8,128)(2,1)S(1)}, u32[]{:S(2)}, u32[]{:S(2)}) %collective-permute-start.4) | collective-permute-done | bytes 65568 | tf_op jit(solution)/shard_map/ppermute | solution.py:244
  148.7 0.7 copy.154
  150.8 26.8 %arrive_and_attend.1 = (bf16[8,256,1024]{2,1,0:T(8,128)(2,1)}, bf16[8,256,1024]{2,1,0:T(8,128)(2,1)}, f32[8,8,8,128]{3,2,1,0:T(8,128)}, f32[8,8,8,1]{3,2,1,0:T(8,128)}, f32[8,8,8,1]{3,2,1,0:T(8,128)}) custom-call(s32[128]{0:T(128)} %and_select_fusion.4.arrival_ref, s32[8]{0:T(128)} %dynamic_slice.19.lengths_ref, s32[1]{0:T(128)} %bitcast.3.base_ref, ...), custom_call_target="tpu_custom_call" | custom-call | flops 67108864 | bytes 16777216 | tf_op jit(solution)/shard_map/arrive_and_attend/pallas_call | solution.py:174
  177.6 1.1 reduce.3
  178.8 1.1 reduce.2
  180.0 1.0 pad_maximum_fusion.1
  181.2 1.4 collective-permute-done.6
  183.3 1.9 fusion.52
  185.3 0.7 pad_maximum_fusion.2
  186.0 8.7 %collective-permute-done.7 = f32[520,128]{1,0:T(8,128)} collective-permute-done((f32[520,128]{1,0:T(8,128)}, f32[520,128]{1,0:T(8,128)}, u32[]{:S(2)}, u32[]{:S(2)}) %collective-permute-start.7) | collective-permute-done | bytes 266272 | tf_op jit(solution)/shard_map/ppermute | solution.py:307
  195.4 0.8 multiply_add_fusion.7
  196.2 1.8 fusion.53
  198.0 0.7 pad_maximum_fusion.3
  198.7 3.1 %collective-permute-start.8 = (f32[520,128]{1,0:T(8,128)}, f32[520,128]{1,0:T(8,128)}, u32[]{:S(2)}, u32[]{:S(2)}) collective-permute-start(f32[520,128]{1,0:T(8,128)} %pad_maximum_fusion.3), channel_id=1, source_target_pairs={{0,4},{1,5},{2,6},{3,7},{4,0},{5,1},{6,2},{7,3},{8,12},{9,13},{10,... | collective-permute-start | bytes 798728 | tf_op jit(solution)/shard_map/ppermute | solution.py:307
  201.8 6.3 %collective-permute-done.8 = f32[520,128]{1,0:T(8,128)} collective-permute-done((f32[520,128]{1,0:T(8,128)}, f32[520,128]{1,0:T(8,128)}, u32[]{:S(2)}, u32[]{:S(2)}) %collective-permute-start.8) | collective-permute-done | bytes 266272 | tf_op jit(solution)/shard_map/ppermute | solution.py:307
  208.1 0.8 multiply_add_fusion.6
  209.6 1.8 fusion.54
  211.4 0.7 pad_maximum_fusion.4
  212.8 6.3 %collective-permute-done.9 = f32[520,128]{1,0:T(8,128)} collective-permute-done((f32[520,128]{1,0:T(8,128)}, f32[520,128]{1,0:T(8,128)}, u32[]{:S(2)}, u32[]{:S(2)}) %collective-permute-start.9) | collective-permute-done | bytes 266272 | tf_op jit(solution)/shard_map/ppermute | solution.py:307
  219.8 0.8 fusion.37
  220.6 1.8 fusion.55
  222.5 0.7 pad_maximum_fusion.5
  223.2 1.0 fusion.21
  224.2 1.4 copy.181
  229.3 2.1 collective-permute-done.10
  231.4 0.8 fusion.51
  232.5 0.7 fusion.24
  233.3 1.1 copy.184
  234.7 1.5 multiply_add_fusion.4
  236.2 0.9 copy.197
  238.5 0.8 copy.164
  239.4 0.8 copy.160
  240.2 1.0 slice.160
  241.2 3.0 %fusion.3 = bf16[8,4,8,2,128]{4,1,3,2,0:T(4,128)(2,1)S(1)} fusion(bf16[8,8,2,4,4]{4,3,2,1,0:T(4,128)(2,1)} %copy.184, f32[8,8,2,4,128]{4,3,2,1,0:T(4,128)S(1)} %bitcast.170, f32[8,8,2,4,128]{4,3,2,1,0:T(4,128)S(1)} %bitcast.174, f32[8,8,2,4,128]{4,3,2,1,0:T(4,128)} %bitcast.173, f32[8,8,2,4,128]{4,3,2,1,0:T(4,128)} %bitcast.172, ...), kind=kOutput, calls=%fused_computation.11 | convolution fusion | flops 2424832 | bytes 1798149 | tf_op jit(solution)/shard_map/rkgts,rskd->rkgtd/dot_general | solution.py:335
  244.6 0.9 collective-permute-start.12
  245.5 1.2 collective-permute-start.11
  246.6 1.9 collective-permute-done.13
  248.5 1.6 collective-permute-done.12
  250.1 1.4 collective-permute-done.11
  252.0 0.8 collective-permute-start.16
  252.8 2.7 %collective-permute-start.15 = (bf16[8,4,2048]{2,0,1:T(8,128)(2,1)S(1)}, bf16[8,4,2048]{2,0,1:T(8,128)(2,1)S(1)}, u32[]{:S(2)}, u32[]{:S(2)}) collective-permute-start(bf16[8,4,2048]{2,0,1:T(8,128)(2,1)S(1)} %get-tuple-element.73), channel_id=1, source_target_pairs={{0,64},{32,96},{64,0},{96,32},{1,65},{33,97},{65,1},{97,33},{2,66}... | collective-permute-start | bytes 393224 | tf_op jit(solution)/shard_map/ppermute | solution.py:244
  255.7 2.5 collective-permute-done.16
  258.3 1.6 collective-permute-done.15
  260.7 0.8 copy.200
  (123 shorter events, 18.4 us)
Async XLA Ops:
  0.6 250.9 %copy-start = (bf16[512,2048]{1,0:T(8,128)(2,1)S(1)}, bf16[512,2048]{1,0:T(8,128)(2,1)}, u32[]{:S(2)}) copy-start(bf16[512,2048]{1,0:T(8,128)(2,1)} %param.16) | copy-start | bytes 6291460
  3.0 25.3 %collective-permute-start.2 = (bf16[8,4,2048]{2,0,1:T(8,128)(2,1)S(1)}, bf16[8,4,2048]{2,0,1:T(8,128)(2,1)S(1)}, u32[]{:S(2)}, u32[]{:S(2)}) collective-permute-start(bf16[8,4,2048]{2,0,1:T(8,128)(2,1)S(1)} %fusion.16), channel_id=1, source_target_pairs={{0,96},{32,0},{64,32},{96,64},{1,97},{33,1},{65,33},{97,65},{2,98}... | collective-permute-start | bytes 393224 | tf_op jit(solution)/shard_map/ppermute | solution.py:244
  5.8 22.4 %collective-permute-start.1 = (bf16[8,4,2048]{2,0,1:T(8,128)(2,1)S(1)}, bf16[8,4,2048]{2,0,1:T(8,128)(2,1)S(1)}, u32[]{:S(2)}, u32[]{:S(2)}) collective-permute-start(bf16[8,4,2048]{2,0,1:T(8,128)(2,1)S(1)} %fusion.16), channel_id=1, source_target_pairs={{0,64},{32,96},{64,0},{96,32},{1,65},{33,97},{65,1},{97,33},{2,66}... | collective-permute-start | bytes 393224 | tf_op jit(solution)/shard_map/ppermute | solution.py:244
  6.6 21.6 %collective-permute-start = (bf16[8,4,2048]{2,0,1:T(8,128)(2,1)S(1)}, bf16[8,4,2048]{2,0,1:T(8,128)(2,1)}, u32[]{:S(2)}, u32[]{:S(2)}) collective-permute-start(bf16[8,4,2048]{2,0,1:T(8,128)(2,1)S(1)} %fusion.16), channel_id=1, source_target_pairs={{0,32},{32,64},{64,96},{96,0},{1,33},{33,65},{65,97},{97,1},{2,34}... | collective-permute-start | bytes 393224 | tf_op jit(solution)/shard_map/ppermute | solution.py:244
  29.2 121.6 %all-to-all-start = ((bf16[128,1,2,16,1024]{4,3,2,1,0:T(8,128)(2,1)}), bf16[128,1,2,16,1024]{4,3,2,1,0:T(8,128)(2,1)}, u32[]{:S(2)}, u32[]{:S(2)}) async-start(bf16[128,1,2,16,1024]{4,3,2,1,0:T(8,128)(2,1)} %maximum_bitcast_fusion), calls=%async_computation | async-start | bytes 16777216 | tf_op jit(solution)/shard_map/all_to_all | solution.py:250
  47.3 5.8 %copy-start.4 = (bf16[2048,256]{1,0:T(8,128)(2,1)S(1)}, bf16[2048,256]{1,0:T(8,128)(2,1)}, u32[]{:S(2)}) copy-start(bf16[2048,256]{1,0:T(8,128)(2,1)} %param.15) | copy-start | bytes 3145732
  53.4 83.9 %collective-permute-start.5 = (bf16[8,4,1024]{2,0,1:T(8,128)(2,1)S(1)}, bf16[8,4,1024]{2,0,1:T(8,128)(2,1)S(1)}, u32[]{:S(2)}, u32[]{:S(2)}) collective-permute-start(bf16[8,4,1024]{2,0,1:T(8,128)(2,1)S(1)} %get-tuple-element.103), channel_id=1, source_target_pairs={{0,32},{32,64},{64,96},{96,0},{1,33},{33,65},{65,97},{97,1},{2,34}... | collective-permute-start | bytes 196616 | tf_op jit(solution)/shard_map/ppermute | solution.py:244
  55.0 92.8 %collective-permute-start.4 = (bf16[8,4,1024]{2,0,1:T(8,128)(2,1)S(1)}, bf16[8,4,1024]{2,0,1:T(8,128)(2,1)S(1)}, u32[]{:S(2)}, u32[]{:S(2)}) collective-permute-start(bf16[8,4,1024]{2,0,1:T(8,128)(2,1)S(1)} %get-tuple-element.104), channel_id=1, source_target_pairs={{0,64},{32,96},{64,0},{96,32},{1,65},{33,97},{65,1},{97,33},{2,66}... | collective-permute-start | bytes 196616 | tf_op jit(solution)/shard_map/ppermute | solution.py:244
  57.7 90.1 %collective-permute-start.3 = (bf16[8,4,1024]{2,0,1:T(8,128)(2,1)S(1)}, bf16[8,4,1024]{2,0,1:T(8,128)(2,1)S(1)}, u32[]{:S(2)}, u32[]{:S(2)}) collective-permute-start(bf16[8,4,1024]{2,0,1:T(8,128)(2,1)S(1)} %get-tuple-element.105), channel_id=1, source_target_pairs={{0,96},{32,0},{64,32},{96,64},{1,97},{33,1},{65,33},{97,65},{2,98}... | collective-permute-start | bytes 196616 | tf_op jit(solution)/shard_map/ppermute | solution.py:244
  181.0 44.7 %copy-start.3 = (f32[8,8,8,1]{3,2,1,0:T(8,128)S(1)}, f32[8,8,8,1]{3,2,1,0:T(8,128)}, u32[]{:S(2)}) copy-start(f32[8,8,8,1]{3,2,1,0:T(8,128)} %get-tuple-element.13) | copy-start | bytes 6148
  181.0 1.6 collective-permute-start.6
  182.6 0.7 copy-start.6
  183.3 42.9 %copy-start.2 = (f32[8,8,8,1]{3,2,1,0:T(8,128)S(1)}, f32[8,8,8,1]{3,2,1,0:T(8,128)}, u32[]{:S(2)}) copy-start(f32[8,8,8,1]{3,2,1,0:T(8,128)} %get-tuple-element.14) | copy-start | bytes 6148
  186.0 8.8 %collective-permute-start.7 = (f32[520,128]{1,0:T(8,128)}, f32[520,128]{1,0:T(8,128)}, u32[]{:S(2)}, u32[]{:S(2)}) collective-permute-start(f32[520,128]{1,0:T(8,128)} %pad_maximum_fusion.2), channel_id=1, source_target_pairs={{0,2},{1,3},{2,0},{3,1},{4,6},{5,7},{6,4},{7,5},{8,10},{9,11},{10,... | collective-permute-start | bytes 798728 | tf_op jit(solution)/shard_map/ppermute | solution.py:307
  198.7 9.4 %collective-permute-start.8 = (f32[520,128]{1,0:T(8,128)}, f32[520,128]{1,0:T(8,128)}, u32[]{:S(2)}, u32[]{:S(2)}) collective-permute-start(f32[520,128]{1,0:T(8,128)} %pad_maximum_fusion.3), channel_id=1, source_target_pairs={{0,4},{1,5},{2,6},{3,7},{4,0},{5,1},{6,2},{7,3},{8,12},{9,13},{10,... | collective-permute-start | bytes 798728 | tf_op jit(solution)/shard_map/ppermute | solution.py:307
  212.1 7.0 %collective-permute-start.9 = (f32[520,128]{1,0:T(8,128)}, f32[520,128]{1,0:T(8,128)}, u32[]{:S(2)}, u32[]{:S(2)}) collective-permute-start(f32[520,128]{1,0:T(8,128)} %pad_maximum_fusion.4), channel_id=1, source_target_pairs={{0,8},{1,9},{2,10},{3,11},{4,12},{5,13},{6,14},{7,15},{8,0},{9,1},... | collective-permute-start | bytes 798728 | tf_op jit(solution)/shard_map/ppermute | solution.py:307
  220.6 20.6 %copy-start.5 = (f32[8,8,8,128]{3,2,1,0:T(8,128)S(1)}, f32[8,8,8,128]{3,2,1,0:T(8,128)}, u32[]{:S(2)}) copy-start(f32[8,8,8,128]{3,2,1,0:T(8,128)} %get-tuple-element.12) | copy-start | bytes 786436
  223.2 8.2 %collective-permute-start.10 = (f32[520,128]{1,0:T(8,128)}, f32[520,128]{1,0:T(8,128)}, u32[]{:S(2)}, u32[]{:S(2)}) collective-permute-start(f32[520,128]{1,0:T(8,128)} %pad_maximum_fusion.5), channel_id=1, source_target_pairs={{0,16},{1,17},{2,18},{3,19},{4,20},{5,21},{6,22},{7,23},{8,24},{9,... | collective-permute-start | bytes 798728 | tf_op jit(solution)/shard_map/ppermute | solution.py:307
  224.2 17.0 %copy-start.7 = (f32[512,128]{1,0:T(8,128)S(1)}, f32[512,128]{1,0:T(8,128)}, u32[]{:S(2)}) copy-start(f32[512,128]{1,0:T(8,128)} %get-tuple-element.94) | copy-start | bytes 786436
  244.3 16.3 %copy-start.1 = (bf16[8,4,2048]{2,1,0:T(4,128)(2,1)S(1)}, bf16[8,4,2048]{2,1,0:T(4,128)(2,1)}, u32[]{:S(2)}) copy-start(bf16[8,4,2048]{2,1,0:T(4,128)(2,1)} %param.11) | copy-start | bytes 393220
  244.5 4.0 %collective-permute-start.13 = (bf16[8,4,512]{2,0,1:T(8,128)(2,1)S(1)}, bf16[8,4,512]{2,0,1:T(8,128)(2,1)S(1)}, u32[]{:S(2)}, u32[]{:S(2)}) collective-permute-start(bf16[8,4,512]{2,0,1:T(8,128)(2,1)S(1)} %get-tuple-element.111), channel_id=1, source_target_pairs={{0,96},{32,0},{64,32},{96,64},{1,97},{33,1},{65,33},{97,65},{2,98}... | collective-permute-start | bytes 98312 | tf_op jit(solution)/shard_map/ppermute | solution.py:244
  244.6 5.5 %collective-permute-start.12 = (bf16[8,4,512]{2,0,1:T(8,128)(2,1)S(1)}, bf16[8,4,512]{2,0,1:T(8,128)(2,1)S(1)}, u32[]{:S(2)}, u32[]{:S(2)}) collective-permute-start(bf16[8,4,512]{2,0,1:T(8,128)(2,1)S(1)} %get-tuple-element.112), channel_id=1, source_target_pairs={{0,64},{32,96},{64,0},{96,32},{1,65},{33,97},{65,1},{97,33},{2,66}... | collective-permute-start | bytes 98312 | tf_op jit(solution)/shard_map/ppermute | solution.py:244
  245.5 6.1 %collective-permute-start.11 = (bf16[8,4,512]{2,0,1:T(8,128)(2,1)S(1)}, bf16[8,4,512]{2,0,1:T(8,128)(2,1)S(1)}, u32[]{:S(2)}, u32[]{:S(2)}) collective-permute-start(bf16[8,4,512]{2,0,1:T(8,128)(2,1)S(1)} %get-tuple-element.113), channel_id=1, source_target_pairs={{0,32},{32,64},{64,96},{96,0},{1,33},{33,65},{65,97},{97,1},{2,34}... | collective-permute-start | bytes 98312 | tf_op jit(solution)/shard_map/ppermute | solution.py:244
  252.0 6.2 %collective-permute-start.16 = (bf16[8,4,2048]{2,0,1:T(8,128)(2,1)S(1)}, bf16[8,4,2048]{2,0,1:T(8,128)(2,1)S(1)}, u32[]{:S(2)}, u32[]{:S(2)}) collective-permute-start(bf16[8,4,2048]{2,0,1:T(8,128)(2,1)S(1)} %get-tuple-element.72), channel_id=1, source_target_pairs={{0,32},{32,64},{64,96},{96,0},{1,33},{33,65},{65,97},{97,1},{2,34}... | collective-permute-start | bytes 393224 | tf_op jit(solution)/shard_map/ppermute | solution.py:244
  252.8 7.1 %collective-permute-start.15 = (bf16[8,4,2048]{2,0,1:T(8,128)(2,1)S(1)}, bf16[8,4,2048]{2,0,1:T(8,128)(2,1)S(1)}, u32[]{:S(2)}, u32[]{:S(2)}) collective-permute-start(bf16[8,4,2048]{2,0,1:T(8,128)(2,1)S(1)} %get-tuple-element.73), channel_id=1, source_target_pairs={{0,64},{32,96},{64,0},{96,32},{1,65},{33,97},{65,1},{97,33},{2,66}... | collective-permute-start | bytes 393224 | tf_op jit(solution)/shard_map/ppermute | solution.py:244
  255.6 5.0 %collective-permute-start.14 = (bf16[8,4,2048]{2,0,1:T(8,128)(2,1)S(1)}, bf16[8,4,2048]{2,0,1:T(8,128)(2,1)S(1)}, u32[]{:S(2)}, u32[]{:S(2)}) collective-permute-start(bf16[8,4,2048]{2,0,1:T(8,128)(2,1)S(1)} %get-tuple-element.71), channel_id=1, source_target_pairs={{0,96},{32,0},{64,32},{96,64},{1,97},{33,1},{65,33},{97,65},{2,98}... | collective-permute-start | bytes 393224 | tf_op jit(solution)/shard_map/ppermute | solution.py:244

commit v7 on v6

--- a/solution.py
+++ b/solution.py
@@ -292,36 +292,58 @@
     gathered_sum = gathered_sum.reshape(local_reqs, KVH, groups, new_count, HD)
     row_peak = row_peak.reshape(local_reqs, KVH, groups, new_count)
     row_mass = row_mass.reshape(local_reqs, KVH, groups, new_count)
-    stat_rows = row_peak.size // HD
-    step = 1
-    while step < seq_count:
+    def pack(total, peak, mass):
+        stat_rows = peak.size // HD
+        return jnp.concatenate(
+            [total.reshape(-1, HD), peak.reshape(stat_rows, HD), mass.reshape(stat_rows, HD)], axis=0
+        )
+
+    def unpack(packed, total, peak, mass):
+        stat_rows = peak.size // HD
+        return (
+            packed[: total.size // HD].reshape(total.shape),
+            packed[total.size // HD : -stat_rows].reshape(peak.shape),
+            packed[-stat_rows:].reshape(mass.shape),
+        )
+
+    def merge(step, total, peak, mass):
         pairs = [(i, i ^ step) for i in range(seq_count)]
-        packed = jnp.concatenate(
-            [
-                gathered_sum.reshape(-1, HD),
-                row_peak.reshape(stat_rows, HD),
-                row_mass.reshape(stat_rows, HD),
-            ],
-            axis=0,
-        )
-        other = lax.ppermute(packed, "seq", pairs)
-        peer_sum = other[: gathered_sum.size // HD].reshape(gathered_sum.shape)
-        peer_peak = other[gathered_sum.size // HD : -stat_rows].reshape(row_peak.shape)
-        peer_mass = other[-stat_rows:].reshape(row_mass.shape)
+        other = lax.ppermute(pack(total, peak, mass), "seq", pairs)
+        peer_sum, peer_peak, peer_mass = unpack(other, total, peak, mass)
         upper = (seq_index & step) != 0
-        peak_lo = jnp.where(upper, peer_peak, row_peak)
-        peak_hi = jnp.where(upper, row_peak, peer_peak)
-        mass_lo = jnp.where(upper, peer_mass, row_mass)
-        mass_hi = jnp.where(upper, row_mass, peer_mass)
-        sum_lo = jnp.where(upper, peer_sum, gathered_sum)
-        sum_hi = jnp.where(upper, gathered_sum, peer_sum)
+        peak_lo = jnp.where(upper, peer_peak, peak)
+        peak_hi = jnp.where(upper, peak, peer_peak)
+        mass_lo = jnp.where(upper, peer_mass, mass)
+        mass_hi = jnp.where(upper, mass, peer_mass)
+        sum_lo = jnp.where(upper, peer_sum, total)
+        sum_hi = jnp.where(upper, total, peer_sum)
         merged_peak = jnp.maximum(peak_lo, peak_hi)
         scale_lo = jnp.exp(peak_lo - merged_peak)
         scale_hi = jnp.exp(peak_hi - merged_peak)
-        row_mass = mass_lo * scale_lo + mass_hi * scale_hi
-        gathered_sum = sum_lo * scale_lo[..., None] + sum_hi * scale_hi[..., None]
-        row_peak = merged_peak
+        return (
+            sum_lo * scale_lo[..., None] + sum_hi * scale_hi[..., None],
+            merged_peak,
+            mass_lo * scale_lo + mass_hi * scale_hi,
+        )
+
+    gathered_sum, row_peak, row_mass = merge(1, gathered_sum, row_peak, row_mass)
+    half = local_reqs // 2
+    core = seq_index % 2
+    mine = tuple(
+        lax.dynamic_slice_in_dim(x, core * half, half, axis=0)
+        for x in (gathered_sum, row_peak, row_mass)
+    )
+    step = 2
+    while step < seq_count:
+        mine = merge(step, *mine)
         step *= 2
+    mine_packed = pack(*mine)
+    other_packed = lax.ppermute(mine_packed, "seq", [(i, i ^ 1) for i in range(seq_count)])
+    first_half = unpack(jnp.where(core == 0, mine_packed, other_packed), *mine)
+    second_half = unpack(jnp.where(core == 0, other_packed, mine_packed), *mine)
+    gathered_sum, row_peak, row_mass = (
+        jnp.concatenate([p, q], axis=0) for p, q in zip(first_half, second_half)
+    )
     own_scores = (
         jnp.einsum("rtkgd,rskd->rkgts", queries, fresh_keys, preferred_element_type=jnp.float32)
         * score_scale

time: 263 us -> 236 us (0.90)
  other arithmetic: 34.1 us -> 19.6 us
  local copies, waits for them, and re-layouts: 37.9 us -> 31.8 us
  matrix products: 8.94 us -> 5.53 us
  waiting for transfers between devices: 123 us -> 120 us
    slice x4 -> x0, other arithmetic: 7.32 us -> none  [shards(): peer_sum = other[:gathered_sum.size // HD].reshape(gathered_sum.shape)]
    ppermute x5 -> x6, waiting for transfers between devices: 24.9 us -> 21.7 us  [the longest x5 21.3 us: merge(): other = lax.ppermute(pack(total, peak, mass), 'seq', pairs)]
    exp x10 -> x0, local copies, waits for them, and re-layouts: 2.96 us -> none  [the longest x5 2.1 us: shards(): scale_lo = jnp.exp(peak_lo - merged_peak)]
    concatenate x5 -> x6, other arithmetic: 3.87 us -> 1.03 us  [pack(): jnp.concatenate([total.reshape(-1, HD), peak.reshape(stat_rows, HD), mass...]
    dot_general x1, matrix products: 3.04 us -> 0.36 us  [shards(): jnp.einsum('rkgts,rskd->rkgtd', own_weights.astype(jnp.bfloat16), fresh_v...]
  transfers between devices with their start and end apart: 18 -> 19, of which waited for: 13 -> 12; matrix products, arithmetic and copies ran while one was open for 17% -> 18% of each run, Pallas kernels for 0% -> 0%
where the time goes in v7:
time: 236 us
  waiting for transfers between devices  120 us (51%)
  local copies, waits for them, and re-layouts  31.8 us (13%)
  starting transfers between devices  30 us (13%)
  Pallas kernels  26.8 us (11%)
  other arithmetic  19.6 us (8%)
  matrix products  5.53 us (2%)
    ppermute x12, waiting for transfers between devices, shift(): return lax.ppermute(value, 'req', pairs)  98.6 us
    pallas_call x1, Pallas kernels, arrive_and_attend(): pl.pallas_call(functools.partial(_arrive_kernel, scale=scale), out_shape=...  26.8 us
    ppermute x5, waiting for transfers between devices, merge(): other = lax.ppermute(pack(total, peak, mass), 'seq', pairs)  21.3 us
    ppermute x12, starting transfers between devices, shift(): return lax.ppermute(value, 'req', pairs)  16.2 us
    gather x2, local copies, waits for them, and re-layouts, shards(): outgoing = jnp.stack([pool_keys[send_pick], pool_values[send_pick]], axis=1)  10 us
    all_to_all x1, starting transfers between devices, shards(): lax.all_to_all(outgoing, ('req', 'seq'), split_axis=0, concat_axis=0, til...  10 us
    reshape x1, other arithmetic, shards(): outgoing = outgoing.reshape(devices, per_peer, 2, page_len, kv_width)  7.5 us
  transfers between devices with their start and end apart: 19, of which 12 were waited for; matrix products, arithmetic and copies ran while one was open for 18% of the time, Pallas kernels for 0%

profile of v7, /device:TPU:32, one launch (start us, length us, event | category | flops | bytes accessed | tf_op | source)
XLA Modules:
  0.0 235.6 jit_solution(5626434915881038222)
XLA Ops:
  0.6 1.3 fusion.14
  1.9 1.0 fusion.16
  3.0 2.8 %collective-permute-start.2 = (bf16[8,4,2048]{2,0,1:T(8,128)(2,1)S(1)}, bf16[8,4,2048]{2,0,1:T(8,128)(2,1)S(1)}, u32[]{:S(2)}, u32[]{:S(2)}) collective-permute-start(bf16[8,4,2048]{2,0,1:T(8,128)(2,1)S(1)} %fusion.16), channel_id=1, source_target_pairs={{0,96},{32,0},{64,32},{96,64},{1,97},{33,1},{65,33},{97,65},{2,98}... | collective-permute-start | bytes 393224 | tf_op jit(solution)/shard_map/ppermute | solution.py:244
  5.8 0.8 collective-permute-start.1
  6.6 0.9 collective-permute-start
  7.5 0.8 select_reduce_fusion
  8.3 1.5 gather_fusion
  10.0 0.6 fusion.7
  10.7 5.0 %gather_fusion.2 = bf16[128,16,1024]{2,1,0:T(8,128)(2,1)} fusion(bf16[128,16,1024]{2,1,0:T(8,128)(2,1)} %param.18, s32[1024]{0:T(1024)S(1)} %pad_clamp_fusion.2), kind=kCustom, calls=%fused_computation.2 | custom fusion | bytes 8389120 | tf_op jit(solution)/shard_map/gather | solution.py:247
  15.7 5.0 %gather_fusion.1 = bf16[128,16,1024]{2,1,0:T(8,128)(2,1)} fusion(bf16[128,16,1024]{2,1,0:T(8,128)(2,1)} %param.17, s32[1024]{0:T(1024)S(1)} %pad_clamp_fusion.2), kind=kCustom, calls=%fused_computation.1 | custom fusion | bytes 8389120 | tf_op jit(solution)/shard_map/gather | solution.py:247
  20.7 7.5 %maximum_bitcast_fusion = bf16[128,1,2,16,1024]{4,3,2,1,0:T(8,128)(2,1)} fusion(bf16[128,1,16,1024]{3,2,1,0:T(8,128)(2,1)} %bitcast.142, bf16[128,1,16,1024]{3,2,1,0:T(8,128)(2,1)} %bitcast.143), kind=kLoop, calls=%fused_computation.5 | loop fusion | flops 4194304 | bytes 16777216 | tf_op jit(solution)/shard_map/reshape | solution.py:248
  28.2 0.9 pad_maximum_fusion
  29.2 10.0 %all-to-all-start = ((bf16[128,1,2,16,1024]{4,3,2,1,0:T(8,128)(2,1)}), bf16[128,1,2,16,1024]{4,3,2,1,0:T(8,128)(2,1)}, u32[]{:S(2)}, u32[]{:S(2)}) async-start(bf16[128,1,2,16,1024]{4,3,2,1,0:T(8,128)(2,1)} %maximum_bitcast_fusion), calls=%async_computation | async-start | bytes 16777216 | tf_op jit(solution)/shard_map/all_to_all | solution.py:250
  39.2 2.3 copy.186
  41.6 0.6 gather_fusion.3
  42.3 3.9 %copy.185 = bf16[512,2048]{1,0:T(8,128)(2,1)} copy(bf16[512,2048]{0,1:T(8,128)(2,1)} %bitcast.147) | data formatting | bytes 4194304 | tf_op jit(solution)/shard_map/dot_general | solution.py:256
  46.2 0.2 copy.148
  46.6 0.6 dynamic_slice.28.lengths_ref
  47.4 0.5 and_select_fusion.4.arrival_ref
  48.0 0.3 multiply_cosine_fusion
  48.3 1.7 fusion.8
  50.2 2.4 %fusion.10 = f32[32,4,4,128]{3,0,2,1:T(8,128)S(1)} fusion(bf16[4,128,2048,1]{2,1,0,3:T(8,128)(2,1)} %bitcast.144, bf16[32,4,2048]{2,0,1:T(8,128)(2,1)S(1)} %pad_maximum_fusion), kind=kOutput, calls=%fused_computation.25 | convolution fusion | flops 268435456 | bytes 2883584 | tf_op jit(solution)/shard_map/dot_general | solution.py:256
  52.9 0.3 convolution_convert_fusion.1
  53.3 1.5 collective-permute-start.5
  54.8 2.7 %collective-permute-start.4 = (bf16[8,4,1024]{2,0,1:T(8,128)(2,1)S(1)}, bf16[8,4,1024]{2,0,1:T(8,128)(2,1)S(1)}, u32[]{:S(2)}, u32[]{:S(2)}) collective-permute-start(bf16[8,4,1024]{2,0,1:T(8,128)(2,1)S(1)} %get-tuple-element.70), channel_id=1, source_target_pairs={{0,64},{32,96},{64,0},{96,32},{1,65},{33,97},{65,1},{97,33},{2,66}... | collective-permute-start | bytes 196616 | tf_op jit(solution)/shard_map/ppermute | solution.py:244
  57.6 1.4 collective-permute-start.3
  59.0 78.3 %collective-permute-done.5 = bf16[8,4,1024]{2,0,1:T(8,128)(2,1)S(1)} collective-permute-done((bf16[8,4,1024]{2,0,1:T(8,128)(2,1)S(1)}, bf16[8,4,1024]{2,0,1:T(8,128)(2,1)S(1)}, u32[]{:S(2)}, u32[]{:S(2)}) %collective-permute-start.5) | collective-permute-done | bytes 65568 | tf_op jit(solution)/shard_map/ppermute | solution.py:244
  137.4 10.4 %collective-permute-done.4 = bf16[8,4,1024]{2,0,1:T(8,128)(2,1)S(1)} collective-permute-done((bf16[8,4,1024]{2,0,1:T(8,128)(2,1)S(1)}, bf16[8,4,1024]{2,0,1:T(8,128)(2,1)S(1)}, u32[]{:S(2)}, u32[]{:S(2)}) %collective-permute-start.4) | collective-permute-done | bytes 65568 | tf_op jit(solution)/shard_map/ppermute | solution.py:244
  147.8 0.6 gather_fusion.4
  148.7 0.7 copy.154
  149.4 0.7 reshape_reshape.15.fk_ref
  150.1 0.7 reshape_reshape.16.fv_ref
  150.8 26.8 %arrive_and_attend.1 = (bf16[8,256,1024]{2,1,0:T(8,128)(2,1)}, bf16[8,256,1024]{2,1,0:T(8,128)(2,1)}, f32[8,8,8,128]{3,2,1,0:T(8,128)}, f32[8,8,8,1]{3,2,1,0:T(8,128)}, f32[8,8,8,1]{3,2,1,0:T(8,128)}) custom-call(s32[128]{0:T(128)} %and_select_fusion.4.arrival_ref, s32[8]{0:T(128)} %dynamic_slice.28.lengths_ref, s32[1]{0:T(128)} %bitcast.3.base_ref, ...), custom_call_target="tpu_custom_call" | custom-call | flops 67108864 | bytes 16777216 | tf_op jit(solution)/shard_map/arrive_and_attend/pallas_call | solution.py:174
  177.7 1.1 reduce.3
  178.8 1.1 reduce.2
  180.0 1.0 pad_maximum_fusion.1
  181.1 1.4 copy.157
  182.5 1.4 copy.160
  184.9 1.1 multiply_add_fusion.4
  186.1 0.3 collective-permute-start.7
  186.3 5.9 %collective-permute-done.7 = f32[260,128]{1,0:T(8,128)S(1)} collective-permute-done((f32[260,128]{1,0:T(8,128)S(1)}, f32[260,128]{1,0:T(8,128)S(1)}, u32[]{:S(2)}, u32[]{:S(2)}) %collective-permute-start.7) | collective-permute-done | bytes 133152 | tf_op jit(solution)/shard_map/ppermute | solution.py:311
  192.9 0.2 multiply_add_fusion.3
  193.1 3.2 %collective-permute-start.8 = (f32[260,128]{1,0:T(8,128)S(1)}, f32[260,128]{1,0:T(8,128)S(1)}, u32[]{:S(2)}, u32[]{:S(2)}) collective-permute-start(f32[260,128]{1,0:T(8,128)S(1)} %pad_maximum_fusion.5), channel_id=1, source_target_pairs={{0,4},{1,5},{2,6},{3,7},{4,0},{5,1},{6,2},{7,3},{8,12},{9,13},{10,... | collective-permute-start | bytes 399368 | tf_op jit(solution)/shard_map/ppermute | solution.py:311
  196.3 3.5 %collective-permute-done.8 = f32[260,128]{1,0:T(8,128)S(1)} collective-permute-done((f32[260,128]{1,0:T(8,128)S(1)}, f32[260,128]{1,0:T(8,128)S(1)}, u32[]{:S(2)}, u32[]{:S(2)}) %collective-permute-start.8) | collective-permute-done | bytes 133152 | tf_op jit(solution)/shard_map/ppermute | solution.py:311
  200.3 0.2 multiply_add_fusion.2
  200.7 5.4 %collective-permute-done.9 = f32[260,128]{1,0:T(8,128)S(1)} collective-permute-done((f32[260,128]{1,0:T(8,128)S(1)}, f32[260,128]{1,0:T(8,128)S(1)}, u32[]{:S(2)}, u32[]{:S(2)}) %collective-permute-start.9) | collective-permute-done | bytes 133152 | tf_op jit(solution)/shard_map/ppermute | solution.py:311
  207.0 6.4 %collective-permute-done.10 = f32[260,128]{1,0:T(8,128)S(1)} collective-permute-done((f32[260,128]{1,0:T(8,128)S(1)}, f32[260,128]{1,0:T(8,128)S(1)}, u32[]{:S(2)}, u32[]{:S(2)}) %collective-permute-start.10) | collective-permute-done | bytes 133152 | tf_op jit(solution)/shard_map/ppermute | solution.py:311
  214.3 0.3 fusion.21
  214.6 0.5 copy.168
  215.2 0.4 collective-permute-done.11
  216.4 0.5 copy.171
  217.7 0.4 fusion.3
  218.4 0.3 collective-permute-start.13
  218.7 1.7 collective-permute-start.12
  220.4 1.9 collective-permute-done.14
  222.3 1.7 collective-permute-done.13
  224.0 1.0 collective-permute-done.12
  225.0 0.4 convolution_convert_fusion
  225.5 0.9 collective-permute-start.17
  226.4 2.6 %collective-permute-start.16 = (bf16[8,4,2048]{2,0,1:T(8,128)(2,1)S(1)}, bf16[8,4,2048]{2,0,1:T(8,128)(2,1)S(1)}, u32[]{:S(2)}, u32[]{:S(2)}) collective-permute-start(bf16[8,4,2048]{2,0,1:T(8,128)(2,1)S(1)} %get-tuple-element.59), channel_id=1, source_target_pairs={{0,64},{32,96},{64,0},{96,32},{1,65},{33,97},{65,1},{97,33},{2,66}... | collective-permute-start | bytes 393224 | tf_op jit(solution)/shard_map/ppermute | solution.py:244
  229.1 0.3 collective-permute-start.15
  229.4 4.7 %collective-permute-done.17 = bf16[8,4,2048]{2,0,1:T(8,128)(2,1)S(1)} collective-permute-done((bf16[8,4,2048]{2,0,1:T(8,128)(2,1)S(1)}, bf16[8,4,2048]{2,0,1:T(8,128)(2,1)S(1)}, u32[]{:S(2)}, u32[]{:S(2)}) %collective-permute-start.17) | collective-permute-done | bytes 131104 | tf_op jit(solution)/shard_map/ppermute | solution.py:244
  234.1 0.6 collective-permute-done.15
  234.8 0.8 copy.178
  (127 shorter events, 8.1 us)
Async XLA Ops:
  0.6 224.4 %copy-start = (bf16[512,2048]{1,0:T(8,128)(2,1)S(1)}, bf16[512,2048]{1,0:T(8,128)(2,1)}, u32[]{:S(2)}) copy-start(bf16[512,2048]{1,0:T(8,128)(2,1)} %param.16) | copy-start | bytes 6291460
  3.0 25.3 %collective-permute-start.2 = (bf16[8,4,2048]{2,0,1:T(8,128)(2,1)S(1)}, bf16[8,4,2048]{2,0,1:T(8,128)(2,1)S(1)}, u32[]{:S(2)}, u32[]{:S(2)}) collective-permute-start(bf16[8,4,2048]{2,0,1:T(8,128)(2,1)S(1)} %fusion.16), channel_id=1, source_target_pairs={{0,96},{32,0},{64,32},{96,64},{1,97},{33,1},{65,33},{97,65},{2,98}... | collective-permute-start | bytes 393224 | tf_op jit(solution)/shard_map/ppermute | solution.py:244
  5.8 22.4 %collective-permute-start.1 = (bf16[8,4,2048]{2,0,1:T(8,128)(2,1)S(1)}, bf16[8,4,2048]{2,0,1:T(8,128)(2,1)S(1)}, u32[]{:S(2)}, u32[]{:S(2)}) collective-permute-start(bf16[8,4,2048]{2,0,1:T(8,128)(2,1)S(1)} %fusion.16), channel_id=1, source_target_pairs={{0,64},{32,96},{64,0},{96,32},{1,65},{33,97},{65,1},{97,33},{2,66}... | collective-permute-start | bytes 393224 | tf_op jit(solution)/shard_map/ppermute | solution.py:244
  6.6 21.6 %collective-permute-start = (bf16[8,4,2048]{2,0,1:T(8,128)(2,1)S(1)}, bf16[8,4,2048]{2,0,1:T(8,128)(2,1)}, u32[]{:S(2)}, u32[]{:S(2)}) collective-permute-start(bf16[8,4,2048]{2,0,1:T(8,128)(2,1)S(1)} %fusion.16), channel_id=1, source_target_pairs={{0,32},{32,64},{64,96},{96,0},{1,33},{33,65},{65,97},{97,1},{2,34}... | collective-permute-start | bytes 393224 | tf_op jit(solution)/shard_map/ppermute | solution.py:244
  29.2 121.6 %all-to-all-start = ((bf16[128,1,2,16,1024]{4,3,2,1,0:T(8,128)(2,1)}), bf16[128,1,2,16,1024]{4,3,2,1,0:T(8,128)(2,1)}, u32[]{:S(2)}, u32[]{:S(2)}) async-start(bf16[128,1,2,16,1024]{4,3,2,1,0:T(8,128)(2,1)} %maximum_bitcast_fusion), calls=%async_computation | async-start | bytes 16777216 | tf_op jit(solution)/shard_map/all_to_all | solution.py:250
  47.2 5.7 %copy-start.2 = (bf16[2048,256]{1,0:T(8,128)(2,1)S(1)}, bf16[2048,256]{1,0:T(8,128)(2,1)}, u32[]{:S(2)}) copy-start(bf16[2048,256]{1,0:T(8,128)(2,1)} %param.15) | copy-start | bytes 3145732
  53.3 84.1 %collective-permute-start.5 = (bf16[8,4,1024]{2,0,1:T(8,128)(2,1)S(1)}, bf16[8,4,1024]{2,0,1:T(8,128)(2,1)S(1)}, u32[]{:S(2)}, u32[]{:S(2)}) collective-permute-start(bf16[8,4,1024]{2,0,1:T(8,128)(2,1)S(1)} %get-tuple-element.69), channel_id=1, source_target_pairs={{0,32},{32,64},{64,96},{96,0},{1,33},{33,65},{65,97},{97,1},{2,34}... | collective-permute-start | bytes 196616 | tf_op jit(solution)/shard_map/ppermute | solution.py:244
  54.8 92.9 %collective-permute-start.4 = (bf16[8,4,1024]{2,0,1:T(8,128)(2,1)S(1)}, bf16[8,4,1024]{2,0,1:T(8,128)(2,1)S(1)}, u32[]{:S(2)}, u32[]{:S(2)}) collective-permute-start(bf16[8,4,1024]{2,0,1:T(8,128)(2,1)S(1)} %get-tuple-element.70), channel_id=1, source_target_pairs={{0,64},{32,96},{64,0},{96,32},{1,65},{33,97},{65,1},{97,33},{2,66}... | collective-permute-start | bytes 196616 | tf_op jit(solution)/shard_map/ppermute | solution.py:244
  57.6 90.2 %collective-permute-start.3 = (bf16[8,4,1024]{2,0,1:T(8,128)(2,1)S(1)}, bf16[8,4,1024]{2,0,1:T(8,128)(2,1)S(1)}, u32[]{:S(2)}, u32[]{:S(2)}) collective-permute-start(bf16[8,4,1024]{2,0,1:T(8,128)(2,1)S(1)} %get-tuple-element.71), channel_id=1, source_target_pairs={{0,96},{32,0},{64,32},{96,64},{1,97},{33,1},{65,33},{97,65},{2,98}... | collective-permute-start | bytes 196616 | tf_op jit(solution)/shard_map/ppermute | solution.py:244
  181.0 3.2 %collective-permute-start.6 = (f32[520,128]{1,0:T(8,128)S(1)}, f32[520,128]{1,0:T(8,128)S(1)}, u32[]{:S(2)}, u32[]{:S(2)}) collective-permute-start(f32[520,128]{1,0:T(8,128)S(1)} %pad_maximum_fusion.1), channel_id=1, source_target_pairs={{0,1},{1,0},{2,3},{3,2},{4,5},{5,4},{6,7},{7,6},{8,9},{9,8},{10,11... | collective-permute-start | bytes 798728 | tf_op jit(solution)/shard_map/ppermute | solution.py:311
  186.1 6.2 %collective-permute-start.7 = (f32[260,128]{1,0:T(8,128)S(1)}, f32[260,128]{1,0:T(8,128)S(1)}, u32[]{:S(2)}, u32[]{:S(2)}) collective-permute-start(f32[260,128]{1,0:T(8,128)S(1)} %pad_maximum_fusion.4), channel_id=1, source_target_pairs={{0,2},{1,3},{2,0},{3,1},{4,6},{5,7},{6,4},{7,5},{8,10},{9,11},{10,... | collective-permute-start | bytes 399368 | tf_op jit(solution)/shard_map/ppermute | solution.py:311
  193.1 6.7 %collective-permute-start.8 = (f32[260,128]{1,0:T(8,128)S(1)}, f32[260,128]{1,0:T(8,128)S(1)}, u32[]{:S(2)}, u32[]{:S(2)}) collective-permute-start(f32[260,128]{1,0:T(8,128)S(1)} %pad_maximum_fusion.5), channel_id=1, source_target_pairs={{0,4},{1,5},{2,6},{3,7},{4,0},{5,1},{6,2},{7,3},{8,12},{9,13},{10,... | collective-permute-start | bytes 399368 | tf_op jit(solution)/shard_map/ppermute | solution.py:311
  200.6 5.5 %collective-permute-start.9 = (f32[260,128]{1,0:T(8,128)S(1)}, f32[260,128]{1,0:T(8,128)S(1)}, u32[]{:S(2)}, u32[]{:S(2)}) collective-permute-start(f32[260,128]{1,0:T(8,128)S(1)} %pad_maximum_fusion.6), channel_id=1, source_target_pairs={{0,8},{1,9},{2,10},{3,11},{4,12},{5,13},{6,14},{7,15},{8,0},{9,1},... | collective-permute-start | bytes 399368 | tf_op jit(solution)/shard_map/ppermute | solution.py:311
  206.8 6.6 %collective-permute-start.10 = (f32[260,128]{1,0:T(8,128)S(1)}, f32[260,128]{1,0:T(8,128)S(1)}, u32[]{:S(2)}, u32[]{:S(2)}) collective-permute-start(f32[260,128]{1,0:T(8,128)S(1)} %pad_maximum_fusion.7), channel_id=1, source_target_pairs={{0,16},{1,17},{2,18},{3,19},{4,20},{5,21},{6,22},{7,23},{8,24},{9,... | collective-permute-start | bytes 399368 | tf_op jit(solution)/shard_map/ppermute | solution.py:311
  214.2 1.4 collective-permute-start.11
  218.1 16.6 %copy-start.1 = (bf16[8,4,2048]{2,1,0:T(4,128)(2,1)S(1)}, bf16[8,4,2048]{2,1,0:T(4,128)(2,1)}, u32[]{:S(2)}) copy-start(bf16[8,4,2048]{2,1,0:T(4,128)(2,1)} %param.11) | copy-start | bytes 393220
  218.3 4.0 %collective-permute-start.14 = (bf16[8,4,512]{2,0,1:T(8,128)(2,1)S(1)}, bf16[8,4,512]{2,0,1:T(8,128)(2,1)S(1)}, u32[]{:S(2)}, u32[]{:S(2)}) collective-permute-start(bf16[8,4,512]{2,0,1:T(8,128)(2,1)S(1)} %get-tuple-element.89), channel_id=1, source_target_pairs={{0,96},{32,0},{64,32},{96,64},{1,97},{33,1},{65,33},{97,65},{2,98}... | collective-permute-start | bytes 98312 | tf_op jit(solution)/shard_map/ppermute | solution.py:244
  218.4 5.6 %collective-permute-start.13 = (bf16[8,4,512]{2,0,1:T(8,128)(2,1)S(1)}, bf16[8,4,512]{2,0,1:T(8,128)(2,1)S(1)}, u32[]{:S(2)}, u32[]{:S(2)}) collective-permute-start(bf16[8,4,512]{2,0,1:T(8,128)(2,1)S(1)} %get-tuple-element.90), channel_id=1, source_target_pairs={{0,64},{32,96},{64,0},{96,32},{1,65},{33,97},{65,1},{97,33},{2,66}... | collective-permute-start | bytes 98312 | tf_op jit(solution)/shard_map/ppermute | solution.py:244
  218.7 6.3 %collective-permute-start.12 = (bf16[8,4,512]{2,0,1:T(8,128)(2,1)S(1)}, bf16[8,4,512]{2,0,1:T(8,128)(2,1)S(1)}, u32[]{:S(2)}, u32[]{:S(2)}) collective-permute-start(bf16[8,4,512]{2,0,1:T(8,128)(2,1)S(1)} %get-tuple-element.91), channel_id=1, source_target_pairs={{0,32},{32,64},{64,96},{96,0},{1,33},{33,65},{65,97},{97,1},{2,34}... | collective-permute-start | bytes 98312 | tf_op jit(solution)/shard_map/ppermute | solution.py:244
  225.5 8.6 %collective-permute-start.17 = (bf16[8,4,2048]{2,0,1:T(8,128)(2,1)S(1)}, bf16[8,4,2048]{2,0,1:T(8,128)(2,1)S(1)}, u32[]{:S(2)}, u32[]{:S(2)}) collective-permute-start(bf16[8,4,2048]{2,0,1:T(8,128)(2,1)S(1)} %get-tuple-element.58), channel_id=1, source_target_pairs={{0,32},{32,64},{64,96},{96,0},{1,33},{33,65},{65,97},{97,1},{2,34}... | collective-permute-start | bytes 393224 | tf_op jit(solution)/shard_map/ppermute | solution.py:244
  226.4 7.6 %collective-permute-start.16 = (bf16[8,4,2048]{2,0,1:T(8,128)(2,1)S(1)}, bf16[8,4,2048]{2,0,1:T(8,128)(2,1)S(1)}, u32[]{:S(2)}, u32[]{:S(2)}) collective-permute-start(bf16[8,4,2048]{2,0,1:T(8,128)(2,1)S(1)} %get-tuple-element.59), channel_id=1, source_target_pairs={{0,64},{32,96},{64,0},{96,32},{1,65},{33,97},{65,1},{97,33},{2,66}... | collective-permute-start | bytes 393224 | tf_op jit(solution)/shard_map/ppermute | solution.py:244
  229.1 5.6 %collective-permute-start.15 = (bf16[8,4,2048]{2,0,1:T(8,128)(2,1)S(1)}, bf16[8,4,2048]{2,0,1:T(8,128)(2,1)S(1)}, u32[]{:S(2)}, u32[]{:S(2)}) collective-permute-start(bf16[8,4,2048]{2,0,1:T(8,128)(2,1)S(1)} %get-tuple-element.57), channel_id=1, source_target_pairs={{0,96},{32,0},{64,32},{96,64},{1,97},{33,1},{65,33},{97,65},{2,98}... | collective-permute-start | bytes 393224 | tf_op jit(solution)/shard_map/ppermute | solution.py:244

commit v8 on v7

--- a/solution.py
+++ b/solution.py
@@ -39,40 +39,32 @@
 def _arrive_kernel(
     arrival_ref, lengths_ref, base_ref, incoming_ref, q_ref, fk_ref, fv_ref,
     keys_out_ref, values_out_ref, acc_ref, peak_ref, mass_ref,
-    kbuf, vbuf, in_sem, out_sem, *, scale
+    buf, in_sem, out_sem, *, scale
 ):
     r = pl.program_id(0)
     n = pl.num_programs(0)
     slot = r % 2
-    positions = kbuf.shape[1]
-    page_len = incoming_ref.shape[2]
-    pages = positions // page_len
+    pages = buf.shape[1]
+    page_len = buf.shape[3]
+    positions = pages * page_len
     heads = q_ref.shape[1]
     head_dim = q_ref.shape[3]
     new_count = fk_ref.shape[1]
-    bufs = (kbuf, vbuf)
     outs = (keys_out_ref, values_out_ref)
 
-    def page_copy(req, s, half, pp, src):
-        return pltpu.make_async_copy(
-            incoming_ref.at[src, half],
-            bufs[half].at[s, pl.ds(pp * page_len, page_len)],
-            in_sem.at[half, s, pp],
-        )
+    def page_copy(s, pp, src):
+        return pltpu.make_async_copy(incoming_ref.at[src], buf.at[s, pp], in_sem.at[s, pp])
 
     def fetch(req, s):
         for pp in range(pages):
-            src = arrival_ref[req * pages + pp]
-            for half in range(2):
-                page_copy(req, s, half, pp, src).start()
+            page_copy(s, pp, arrival_ref[req * pages + pp]).start()
 
     def wait_fetch(s):
         for pp in range(pages):
-            for half in range(2):
-                page_copy(0, s, half, pp, 0).wait()
+            page_copy(s, pp, 0).wait()
 
     def out_copy(req, s, half):
-        return pltpu.make_async_copy(bufs[half].at[s], outs[half].at[req], out_sem.at[half, s])
+        return pltpu.make_async_copy(buf.at[s, :, half], outs[half].at[req], out_sem.at[half, s])
 
     @pl.when(r == 0)
     def _():
@@ -95,7 +87,8 @@
     live = spots < length
     for kh in range(heads):
         cols = pl.ds(kh * head_dim, head_dim)
-        keys_h = kbuf[slot, :, cols]
+        keys_h = buf[slot, :, 0, :, cols].reshape(positions, head_dim)
+        values_h = buf[slot, :, 1, :, cols].reshape(positions, head_dim)
         query_h = q_ref[0, kh]
         scores = lax.dot_general(
             query_h, keys_h, (((1,), (1,)), ((), ())), preferred_element_type=jnp.float32
@@ -106,27 +99,21 @@
         peak_ref[0, kh] = peak
         mass_ref[0, kh] = jnp.sum(weights, axis=1, keepdims=True)
         acc_ref[0, kh] = jnp.dot(
-            weights.astype(jnp.bfloat16), vbuf[slot, :, cols],
-            preferred_element_type=jnp.float32,
+            weights.astype(jnp.bfloat16), values_h, preferred_element_type=jnp.float32
         )
     first = length - base
-    tile0 = (first // page_len) * page_len
+    page0 = first // page_len
     row_ids = lax.broadcasted_iota(jnp.int32, (page_len, 1), 0)
-    fresh_k = fk_ref[0]
-    fresh_v = fv_ref[0]
-    for tile in (tile0, tile0 + page_len):
-        @pl.when(jnp.logical_and(tile >= 0, tile < positions))
+    fresh = (fk_ref[0], fv_ref[0])
+    for page in (page0, page0 + 1):
+        @pl.when(jnp.logical_and(page >= 0, page < pages))
         def _():
-            start = pl.multiple_of(tile, page_len)
-            rows = pl.ds(start, page_len)
-            block_k = kbuf[slot, rows, :]
-            block_v = vbuf[slot, rows, :]
-            for t in range(new_count):
-                hit = row_ids == first + t - tile
-                block_k = jnp.where(hit, fresh_k[t : t + 1, :], block_k)
-                block_v = jnp.where(hit, fresh_v[t : t + 1, :], block_v)
-            kbuf[slot, rows, :] = block_k
-            vbuf[slot, rows, :] = block_v
+            for half in range(2):
+                block = buf[slot, page, half]
+                for t in range(new_count):
+                    hit = row_ids == first + t - page * page_len
+                    block = jnp.where(hit, fresh[half][t : t + 1, :], block)
+                buf[slot, page, half] = block
 
     for half in range(2):
         out_copy(r, slot, half).start()
@@ -145,8 +132,9 @@
 def arrive_and_attend(arrival_src, lengths, base, incoming, queries, fresh_k, fresh_v, scale):
     local_reqs, new_count, kv_width = fresh_k.shape
     _, heads, rows, head_dim = queries.shape
-    positions = arrival_src.shape[0] // local_reqs * incoming.shape[2]
-    pages = positions // incoming.shape[2]
+    page_len = incoming.shape[2]
+    pages = arrival_src.shape[0] // local_reqs
+    positions = pages * page_len
     grid_spec = pltpu.PrefetchScalarGridSpec(
         num_scalar_prefetch=3,
         grid=(local_reqs,),
@@ -164,18 +152,17 @@
             pl.BlockSpec((1, heads, rows, 1), lambda r, *_: (r, 0, 0, 0)),
         ],
         scratch_shapes=[
-            pltpu.VMEM((2, positions, kv_width), jnp.bfloat16),
-            pltpu.VMEM((2, positions, kv_width), jnp.bfloat16),
-            pltpu.SemaphoreType.DMA((2, 2, pages)),
+            pltpu.VMEM((2, pages, 2, page_len, kv_width), jnp.bfloat16),
+            pltpu.SemaphoreType.DMA((2, pages)),
             pltpu.SemaphoreType.DMA((2, 2)),
         ],
     )
     cache_bytes = 2 * local_reqs * positions * kv_width * 2
-    return pl.pallas_call(
+    keys_out, values_out, acc, peak, mass = pl.pallas_call(
         functools.partial(_arrive_kernel, scale=scale),
         out_shape=[
-            jax.ShapeDtypeStruct((local_reqs, positions, kv_width), jnp.bfloat16),
-            jax.ShapeDtypeStruct((local_reqs, positions, kv_width), jnp.bfloat16),
+            jax.ShapeDtypeStruct((local_reqs, pages, page_len, kv_width), jnp.bfloat16),
+            jax.ShapeDtypeStruct((local_reqs, pages, page_len, kv_width), jnp.bfloat16),
             jax.ShapeDtypeStruct((local_reqs, heads, rows, head_dim), jnp.float32),
             jax.ShapeDtypeStruct((local_reqs, heads, rows, 1), jnp.float32),
             jax.ShapeDtypeStruct((local_reqs, heads, rows, 1), jnp.float32),
@@ -189,6 +176,9 @@
         ),
         name="arrive_and_attend",
     )(arrival_src, lengths, base, incoming, queries, fresh_k, fresh_v)
+    keys_out = keys_out.reshape(local_reqs, positions, kv_width)
+    values_out = values_out.reshape(local_reqs, positions, kv_width)
+    return keys_out, values_out, acc, peak, mass
 
 
 def shards(

time: 236 us -> 236 us (level)
  no operation moved by 1% of the time
where the time goes in v8:
time: 236 us; the launch traced here: 235 us
  waiting for transfers between devices  120 us (51%)
  local copies, waits for them, and re-layouts  31.8 us (13%)
  starting transfers between devices  29.8 us (13%)
  Pallas kernels  26.6 us (11%)
  other arithmetic  19.6 us (8%)
  matrix products  5.53 us (2%)
    ppermute x12, waiting for transfers between devices, shift(): return lax.ppermute(value, 'req', pairs)  98.6 us
    pallas_call x1, Pallas kernels, arrive_and_attend(): pl.pallas_call(functools.partial(_arrive_kernel, scale=scale), out_shape=...  26.6 us
    ppermute x5, waiting for transfers between devices, merge(): other = lax.ppermute(pack(total, peak, mass), 'seq', pairs)  21.4 us
    ppermute x12, starting transfers between devices, shift(): return lax.ppermute(value, 'req', pairs)  16.2 us
    gather x2, local copies, waits for them, and re-layouts, shards(): outgoing = jnp.stack([pool_keys[send_pick], pool_values[send_pick]], axis=1)  10 us
    all_to_all x1, starting transfers between devices, shards(): lax.all_to_all(outgoing, ('req', 'seq'), split_axis=0, concat_axis=0, til...  10 us
    reshape x1, other arithmetic, shards(): outgoing = outgoing.reshape(devices, per_peer, 2, page_len, kv_width)  7.5 us
  transfers between devices with their start and end apart: 19, of which 12 were waited for; matrix products, arithmetic and copies ran while one was open for 18% of the time, Pallas kernels for 0%

profile of v8, /device:TPU:32, one launch (start us, length us, event | category | flops | bytes accessed | tf_op | source)
XLA Modules:
  0.0 235.3 jit_solution(12381732091266564449)
XLA Ops:
  0.6 1.3 fusion.14
  1.9 1.0 fusion.16
  3.0 2.8 %collective-permute-start.2 = (bf16[8,4,2048]{2,0,1:T(8,128)(2,1)S(1)}, bf16[8,4,2048]{2,0,1:T(8,128)(2,1)S(1)}, u32[]{:S(2)}, u32[]{:S(2)}) collective-permute-start(bf16[8,4,2048]{2,0,1:T(8,128)(2,1)S(1)} %fusion.16), channel_id=1, source_target_pairs={{0,96},{32,0},{64,32},{96,64},{1,97},{33,1},{65,33},{97,65},{2,98}... | collective-permute-start | bytes 393224 | tf_op jit(solution)/shard_map/ppermute | solution.py:234
  5.8 0.8 collective-permute-start.1
  6.6 0.9 collective-permute-start
  7.5 0.8 select_reduce_fusion
  8.3 1.5 gather_fusion
  10.0 0.6 fusion.7
  10.7 5.0 %gather_fusion.2 = bf16[128,16,1024]{2,1,0:T(8,128)(2,1)} fusion(bf16[128,16,1024]{2,1,0:T(8,128)(2,1)} %param.18, s32[1024]{0:T(1024)S(1)} %pad_clamp_fusion.2), kind=kCustom, calls=%fused_computation.2 | custom fusion | bytes 8389120 | tf_op jit(solution)/shard_map/gather | solution.py:237
  15.7 5.0 %gather_fusion.1 = bf16[128,16,1024]{2,1,0:T(8,128)(2,1)} fusion(bf16[128,16,1024]{2,1,0:T(8,128)(2,1)} %param.17, s32[1024]{0:T(1024)S(1)} %pad_clamp_fusion.2), kind=kCustom, calls=%fused_computation.1 | custom fusion | bytes 8389120 | tf_op jit(solution)/shard_map/gather | solution.py:237
  20.7 7.5 %maximum_bitcast_fusion = bf16[128,1,2,16,1024]{4,3,2,1,0:T(8,128)(2,1)} fusion(bf16[128,1,16,1024]{3,2,1,0:T(8,128)(2,1)} %bitcast.144, bf16[128,1,16,1024]{3,2,1,0:T(8,128)(2,1)} %bitcast.145), kind=kLoop, calls=%fused_computation.5 | loop fusion | flops 4194304 | bytes 16777216 | tf_op jit(solution)/shard_map/reshape | solution.py:238
  28.2 0.9 pad_maximum_fusion
  29.2 10.0 %all-to-all-start = ((bf16[128,1,2,16,1024]{4,3,2,1,0:T(8,128)(2,1)}), bf16[128,1,2,16,1024]{4,3,2,1,0:T(8,128)(2,1)}, u32[]{:S(2)}, u32[]{:S(2)}) async-start(bf16[128,1,2,16,1024]{4,3,2,1,0:T(8,128)(2,1)} %maximum_bitcast_fusion), calls=%async_computation | async-start | bytes 16777216 | tf_op jit(solution)/shard_map/all_to_all | solution.py:240
  39.2 2.3 copy.186
  41.6 0.6 gather_fusion.3
  42.3 3.9 %copy.185 = bf16[512,2048]{1,0:T(8,128)(2,1)} copy(bf16[512,2048]{0,1:T(8,128)(2,1)} %bitcast.149) | data formatting | bytes 4194304 | tf_op jit(solution)/shard_map/dot_general | solution.py:246
  46.2 0.2 copy.148
  46.6 0.6 dynamic_slice.28.lengths_ref
  47.4 0.5 and_select_fusion.4.arrival_ref
  48.0 0.3 multiply_cosine_fusion
  48.3 1.7 fusion.8
  50.2 2.4 %fusion.10 = f32[32,4,4,128]{3,0,2,1:T(8,128)S(1)} fusion(bf16[4,128,2048,1]{2,1,0,3:T(8,128)(2,1)} %bitcast.146, bf16[32,4,2048]{2,0,1:T(8,128)(2,1)S(1)} %pad_maximum_fusion), kind=kOutput, calls=%fused_computation.25 | convolution fusion | flops 268435456 | bytes 2883584 | tf_op jit(solution)/shard_map/dot_general | solution.py:246
  52.9 0.3 convolution_convert_fusion.1
  53.3 1.5 collective-permute-start.5
  54.8 2.7 %collective-permute-start.4 = (bf16[8,4,1024]{2,0,1:T(8,128)(2,1)S(1)}, bf16[8,4,1024]{2,0,1:T(8,128)(2,1)S(1)}, u32[]{:S(2)}, u32[]{:S(2)}) collective-permute-start(bf16[8,4,1024]{2,0,1:T(8,128)(2,1)S(1)} %get-tuple-element.70), channel_id=1, source_target_pairs={{0,64},{32,96},{64,0},{96,32},{1,65},{33,97},{65,1},{97,33},{2,66}... | collective-permute-start | bytes 196616 | tf_op jit(solution)/shard_map/ppermute | solution.py:234
  57.6 1.4 collective-permute-start.3
  59.0 78.3 %collective-permute-done.5 = bf16[8,4,1024]{2,0,1:T(8,128)(2,1)S(1)} collective-permute-done((bf16[8,4,1024]{2,0,1:T(8,128)(2,1)S(1)}, bf16[8,4,1024]{2,0,1:T(8,128)(2,1)S(1)}, u32[]{:S(2)}, u32[]{:S(2)}) %collective-permute-start.5) | collective-permute-done | bytes 65568 | tf_op jit(solution)/shard_map/ppermute | solution.py:234
  137.4 10.4 %collective-permute-done.4 = bf16[8,4,1024]{2,0,1:T(8,128)(2,1)S(1)} collective-permute-done((bf16[8,4,1024]{2,0,1:T(8,128)(2,1)S(1)}, bf16[8,4,1024]{2,0,1:T(8,128)(2,1)S(1)}, u32[]{:S(2)}, u32[]{:S(2)}) %collective-permute-start.4) | collective-permute-done | bytes 65568 | tf_op jit(solution)/shard_map/ppermute | solution.py:234
  147.8 0.6 gather_fusion.4
  148.7 0.7 copy.154
  149.4 0.7 reshape_reshape.15.fk_ref
  150.1 0.7 reshape_reshape.16.fv_ref
  150.8 26.6 %arrive_and_attend.1 = (bf16[8,16,16,1024]{3,2,1,0:T(8,128)(2,1)}, bf16[8,16,16,1024]{3,2,1,0:T(8,128)(2,1)}, f32[8,8,8,128]{3,2,1,0:T(8,128)}, f32[8,8,8,1]{3,2,1,0:T(8,128)}, f32[8,8,8,1]{3,2,1,0:T(8,128)}) custom-call(s32[128]{0:T(128)} %and_select_fusion.4.arrival_ref, s32[8]{0:T(128)} %dynamic_slice.28.lengths_ref, s32[1]{0:T(128)} %bitcast.3.base_ref, ...), custom_call_target="tpu_custom_call" | custom-call | flops 67108864 | bytes 16777216 | tf_op jit(solution)/shard_map/arrive_and_attend/pallas_call | solution.py:161
  177.4 1.1 reduce.3
  178.6 1.1 reduce.2
  179.8 1.0 pad_maximum_fusion.1
  180.9 1.4 copy.157
  182.3 1.4 copy.160
  184.7 1.1 multiply_add_fusion.4
  185.8 0.3 collective-permute-start.7
  186.1 5.9 %collective-permute-done.7 = f32[260,128]{1,0:T(8,128)S(1)} collective-permute-done((f32[260,128]{1,0:T(8,128)S(1)}, f32[260,128]{1,0:T(8,128)S(1)}, u32[]{:S(2)}, u32[]{:S(2)}) %collective-permute-start.7) | collective-permute-done | bytes 133152 | tf_op jit(solution)/shard_map/ppermute | solution.py:301
  192.6 0.2 multiply_add_fusion.3
  192.9 3.0 %collective-permute-start.8 = (f32[260,128]{1,0:T(8,128)S(1)}, f32[260,128]{1,0:T(8,128)S(1)}, u32[]{:S(2)}, u32[]{:S(2)}) collective-permute-start(f32[260,128]{1,0:T(8,128)S(1)} %pad_maximum_fusion.5), channel_id=1, source_target_pairs={{0,4},{1,5},{2,6},{3,7},{4,0},{5,1},{6,2},{7,3},{8,12},{9,13},{10,... | collective-permute-start | bytes 399368 | tf_op jit(solution)/shard_map/ppermute | solution.py:301
  195.9 3.7 %collective-permute-done.8 = f32[260,128]{1,0:T(8,128)S(1)} collective-permute-done((f32[260,128]{1,0:T(8,128)S(1)}, f32[260,128]{1,0:T(8,128)S(1)}, u32[]{:S(2)}, u32[]{:S(2)}) %collective-permute-start.8) | collective-permute-done | bytes 133152 | tf_op jit(solution)/shard_map/ppermute | solution.py:301
  200.1 0.2 multiply_add_fusion.2
  200.4 5.4 %collective-permute-done.9 = f32[260,128]{1,0:T(8,128)S(1)} collective-permute-done((f32[260,128]{1,0:T(8,128)S(1)}, f32[260,128]{1,0:T(8,128)S(1)}, u32[]{:S(2)}, u32[]{:S(2)}) %collective-permute-start.9) | collective-permute-done | bytes 133152 | tf_op jit(solution)/shard_map/ppermute | solution.py:301
  206.4 0.2 multiply_add_fusion.1
  206.8 6.4 %collective-permute-done.10 = f32[260,128]{1,0:T(8,128)S(1)} collective-permute-done((f32[260,128]{1,0:T(8,128)S(1)}, f32[260,128]{1,0:T(8,128)S(1)}, u32[]{:S(2)}, u32[]{:S(2)}) %collective-permute-start.10) | collective-permute-done | bytes 133152 | tf_op jit(solution)/shard_map/ppermute | solution.py:301
  214.0 0.3 fusion.21
  214.4 0.5 copy.168
  214.9 0.4 collective-permute-done.11
  216.1 0.5 copy.171
  217.5 0.4 fusion.3
  218.4 1.8 collective-permute-start.12
  220.2 1.9 collective-permute-done.14
  222.1 1.7 collective-permute-done.13
  223.8 1.0 collective-permute-done.12
  224.8 0.4 convolution_convert_fusion
  225.2 0.9 collective-permute-start.17
  226.2 2.6 %collective-permute-start.16 = (bf16[8,4,2048]{2,0,1:T(8,128)(2,1)S(1)}, bf16[8,4,2048]{2,0,1:T(8,128)(2,1)S(1)}, u32[]{:S(2)}, u32[]{:S(2)}) collective-permute-start(bf16[8,4,2048]{2,0,1:T(8,128)(2,1)S(1)} %get-tuple-element.59), channel_id=1, source_target_pairs={{0,64},{32,96},{64,0},{96,32},{1,65},{33,97},{65,1},{97,33},{2,66}... | collective-permute-start | bytes 393224 | tf_op jit(solution)/shard_map/ppermute | solution.py:234
  228.8 0.3 collective-permute-start.15
  229.1 4.7 %collective-permute-done.17 = bf16[8,4,2048]{2,0,1:T(8,128)(2,1)S(1)} collective-permute-done((bf16[8,4,2048]{2,0,1:T(8,128)(2,1)S(1)}, bf16[8,4,2048]{2,0,1:T(8,128)(2,1)S(1)}, u32[]{:S(2)}, u32[]{:S(2)}) %collective-permute-start.17) | collective-permute-done | bytes 131104 | tf_op jit(solution)/shard_map/ppermute | solution.py:234
  233.8 0.6 collective-permute-done.15
  234.6 0.8 copy.178
  (127 shorter events, 8.1 us)
Async XLA Ops:
  0.6 224.1 %copy-start = (bf16[512,2048]{1,0:T(8,128)(2,1)S(1)}, bf16[512,2048]{1,0:T(8,128)(2,1)}, u32[]{:S(2)}) copy-start(bf16[512,2048]{1,0:T(8,128)(2,1)} %param.16) | copy-start | bytes 6291460
  3.0 25.3 %collective-permute-start.2 = (bf16[8,4,2048]{2,0,1:T(8,128)(2,1)S(1)}, bf16[8,4,2048]{2,0,1:T(8,128)(2,1)S(1)}, u32[]{:S(2)}, u32[]{:S(2)}) collective-permute-start(bf16[8,4,2048]{2,0,1:T(8,128)(2,1)S(1)} %fusion.16), channel_id=1, source_target_pairs={{0,96},{32,0},{64,32},{96,64},{1,97},{33,1},{65,33},{97,65},{2,98}... | collective-permute-start | bytes 393224 | tf_op jit(solution)/shard_map/ppermute | solution.py:234
  5.8 22.4 %collective-permute-start.1 = (bf16[8,4,2048]{2,0,1:T(8,128)(2,1)S(1)}, bf16[8,4,2048]{2,0,1:T(8,128)(2,1)S(1)}, u32[]{:S(2)}, u32[]{:S(2)}) collective-permute-start(bf16[8,4,2048]{2,0,1:T(8,128)(2,1)S(1)} %fusion.16), channel_id=1, source_target_pairs={{0,64},{32,96},{64,0},{96,32},{1,65},{33,97},{65,1},{97,33},{2,66}... | collective-permute-start | bytes 393224 | tf_op jit(solution)/shard_map/ppermute | solution.py:234
  6.6 21.6 %collective-permute-start = (bf16[8,4,2048]{2,0,1:T(8,128)(2,1)S(1)}, bf16[8,4,2048]{2,0,1:T(8,128)(2,1)}, u32[]{:S(2)}, u32[]{:S(2)}) collective-permute-start(bf16[8,4,2048]{2,0,1:T(8,128)(2,1)S(1)} %fusion.16), channel_id=1, source_target_pairs={{0,32},{32,64},{64,96},{96,0},{1,33},{33,65},{65,97},{97,1},{2,34}... | collective-permute-start | bytes 393224 | tf_op jit(solution)/shard_map/ppermute | solution.py:234
  29.2 121.6 %all-to-all-start = ((bf16[128,1,2,16,1024]{4,3,2,1,0:T(8,128)(2,1)}), bf16[128,1,2,16,1024]{4,3,2,1,0:T(8,128)(2,1)}, u32[]{:S(2)}, u32[]{:S(2)}) async-start(bf16[128,1,2,16,1024]{4,3,2,1,0:T(8,128)(2,1)} %maximum_bitcast_fusion), calls=%async_computation | async-start | bytes 16777216 | tf_op jit(solution)/shard_map/all_to_all | solution.py:240
  47.2 5.7 %copy-start.2 = (bf16[2048,256]{1,0:T(8,128)(2,1)S(1)}, bf16[2048,256]{1,0:T(8,128)(2,1)}, u32[]{:S(2)}) copy-start(bf16[2048,256]{1,0:T(8,128)(2,1)} %param.15) | copy-start | bytes 3145732
  53.3 84.1 %collective-permute-start.5 = (bf16[8,4,1024]{2,0,1:T(8,128)(2,1)S(1)}, bf16[8,4,1024]{2,0,1:T(8,128)(2,1)S(1)}, u32[]{:S(2)}, u32[]{:S(2)}) collective-permute-start(bf16[8,4,1024]{2,0,1:T(8,128)(2,1)S(1)} %get-tuple-element.69), channel_id=1, source_target_pairs={{0,32},{32,64},{64,96},{96,0},{1,33},{33,65},{65,97},{97,1},{2,34}... | collective-permute-start | bytes 196616 | tf_op jit(solution)/shard_map/ppermute | solution.py:234
  54.8 92.9 %collective-permute-start.4 = (bf16[8,4,1024]{2,0,1:T(8,128)(2,1)S(1)}, bf16[8,4,1024]{2,0,1:T(8,128)(2,1)S(1)}, u32[]{:S(2)}, u32[]{:S(2)}) collective-permute-start(bf16[8,4,1024]{2,0,1:T(8,128)(2,1)S(1)} %get-tuple-element.70), channel_id=1, source_target_pairs={{0,64},{32,96},{64,0},{96,32},{1,65},{33,97},{65,1},{97,33},{2,66}... | collective-permute-start | bytes 196616 | tf_op jit(solution)/shard_map/ppermute | solution.py:234
  57.6 90.2 %collective-permute-start.3 = (bf16[8,4,1024]{2,0,1:T(8,128)(2,1)S(1)}, bf16[8,4,1024]{2,0,1:T(8,128)(2,1)S(1)}, u32[]{:S(2)}, u32[]{:S(2)}) collective-permute-start(bf16[8,4,1024]{2,0,1:T(8,128)(2,1)S(1)} %get-tuple-element.71), channel_id=1, source_target_pairs={{0,96},{32,0},{64,32},{96,64},{1,97},{33,1},{65,33},{97,65},{2,98}... | collective-permute-start | bytes 196616 | tf_op jit(solution)/shard_map/ppermute | solution.py:234
  180.8 3.2 %collective-permute-start.6 = (f32[520,128]{1,0:T(8,128)S(1)}, f32[520,128]{1,0:T(8,128)S(1)}, u32[]{:S(2)}, u32[]{:S(2)}) collective-permute-start(f32[520,128]{1,0:T(8,128)S(1)} %pad_maximum_fusion.1), channel_id=1, source_target_pairs={{0,1},{1,0},{2,3},{3,2},{4,5},{5,4},{6,7},{7,6},{8,9},{9,8},{10,11... | collective-permute-start | bytes 798728 | tf_op jit(solution)/shard_map/ppermute | solution.py:301
  185.8 6.2 %collective-permute-start.7 = (f32[260,128]{1,0:T(8,128)S(1)}, f32[260,128]{1,0:T(8,128)S(1)}, u32[]{:S(2)}, u32[]{:S(2)}) collective-permute-start(f32[260,128]{1,0:T(8,128)S(1)} %pad_maximum_fusion.4), channel_id=1, source_target_pairs={{0,2},{1,3},{2,0},{3,1},{4,6},{5,7},{6,4},{7,5},{8,10},{9,11},{10,... | collective-permute-start | bytes 399368 | tf_op jit(solution)/shard_map/ppermute | solution.py:301
  192.9 6.7 %collective-permute-start.8 = (f32[260,128]{1,0:T(8,128)S(1)}, f32[260,128]{1,0:T(8,128)S(1)}, u32[]{:S(2)}, u32[]{:S(2)}) collective-permute-start(f32[260,128]{1,0:T(8,128)S(1)} %pad_maximum_fusion.5), channel_id=1, source_target_pairs={{0,4},{1,5},{2,6},{3,7},{4,0},{5,1},{6,2},{7,3},{8,12},{9,13},{10,... | collective-permute-start | bytes 399368 | tf_op jit(solution)/shard_map/ppermute | solution.py:301
  200.3 5.5 %collective-permute-start.9 = (f32[260,128]{1,0:T(8,128)S(1)}, f32[260,128]{1,0:T(8,128)S(1)}, u32[]{:S(2)}, u32[]{:S(2)}) collective-permute-start(f32[260,128]{1,0:T(8,128)S(1)} %pad_maximum_fusion.6), channel_id=1, source_target_pairs={{0,8},{1,9},{2,10},{3,11},{4,12},{5,13},{6,14},{7,15},{8,0},{9,1},... | collective-permute-start | bytes 399368 | tf_op jit(solution)/shard_map/ppermute | solution.py:301
  206.6 6.6 %collective-permute-start.10 = (f32[260,128]{1,0:T(8,128)S(1)}, f32[260,128]{1,0:T(8,128)S(1)}, u32[]{:S(2)}, u32[]{:S(2)}) collective-permute-start(f32[260,128]{1,0:T(8,128)S(1)} %pad_maximum_fusion.7), channel_id=1, source_target_pairs={{0,16},{1,17},{2,18},{3,19},{4,20},{5,21},{6,22},{7,23},{8,24},{9,... | collective-permute-start | bytes 399368 | tf_op jit(solution)/shard_map/ppermute | solution.py:301
  213.9 1.4 collective-permute-start.11
  217.9 16.6 %copy-start.1 = (bf16[8,4,2048]{2,1,0:T(4,128)(2,1)S(1)}, bf16[8,4,2048]{2,1,0:T(4,128)(2,1)}, u32[]{:S(2)}) copy-start(bf16[8,4,2048]{2,1,0:T(4,128)(2,1)} %param.11) | copy-start | bytes 393220
  218.1 4.0 %collective-permute-start.14 = (bf16[8,4,512]{2,0,1:T(8,128)(2,1)S(1)}, bf16[8,4,512]{2,0,1:T(8,128)(2,1)S(1)}, u32[]{:S(2)}, u32[]{:S(2)}) collective-permute-start(bf16[8,4,512]{2,0,1:T(8,128)(2,1)S(1)} %get-tuple-element.89), channel_id=1, source_target_pairs={{0,96},{32,0},{64,32},{96,64},{1,97},{33,1},{65,33},{97,65},{2,98}... | collective-permute-start | bytes 98312 | tf_op jit(solution)/shard_map/ppermute | solution.py:234
  218.2 5.6 %collective-permute-start.13 = (bf16[8,4,512]{2,0,1:T(8,128)(2,1)S(1)}, bf16[8,4,512]{2,0,1:T(8,128)(2,1)S(1)}, u32[]{:S(2)}, u32[]{:S(2)}) collective-permute-start(bf16[8,4,512]{2,0,1:T(8,128)(2,1)S(1)} %get-tuple-element.90), channel_id=1, source_target_pairs={{0,64},{32,96},{64,0},{96,32},{1,65},{33,97},{65,1},{97,33},{2,66}... | collective-permute-start | bytes 98312 | tf_op jit(solution)/shard_map/ppermute | solution.py:234
  218.4 6.4 %collective-permute-start.12 = (bf16[8,4,512]{2,0,1:T(8,128)(2,1)S(1)}, bf16[8,4,512]{2,0,1:T(8,128)(2,1)S(1)}, u32[]{:S(2)}, u32[]{:S(2)}) collective-permute-start(bf16[8,4,512]{2,0,1:T(8,128)(2,1)S(1)} %get-tuple-element.91), channel_id=1, source_target_pairs={{0,32},{32,64},{64,96},{96,0},{1,33},{33,65},{65,97},{97,1},{2,34}... | collective-permute-start | bytes 98312 | tf_op jit(solution)/shard_map/ppermute | solution.py:234
  225.2 8.6 %collective-permute-start.17 = (bf16[8,4,2048]{2,0,1:T(8,128)(2,1)S(1)}, bf16[8,4,2048]{2,0,1:T(8,128)(2,1)S(1)}, u32[]{:S(2)}, u32[]{:S(2)}) collective-permute-start(bf16[8,4,2048]{2,0,1:T(8,128)(2,1)S(1)} %get-tuple-element.58), channel_id=1, source_target_pairs={{0,32},{32,64},{64,96},{96,0},{1,33},{33,65},{65,97},{97,1},{2,34}... | collective-permute-start | bytes 393224 | tf_op jit(solution)/shard_map/ppermute | solution.py:234
  226.2 7.6 %collective-permute-start.16 = (bf16[8,4,2048]{2,0,1:T(8,128)(2,1)S(1)}, bf16[8,4,2048]{2,0,1:T(8,128)(2,1)S(1)}, u32[]{:S(2)}, u32[]{:S(2)}) collective-permute-start(bf16[8,4,2048]{2,0,1:T(8,128)(2,1)S(1)} %get-tuple-element.59), channel_id=1, source_target_pairs={{0,64},{32,96},{64,0},{96,32},{1,65},{33,97},{65,1},{97,33},{2,66}... | collective-permute-start | bytes 393224 | tf_op jit(solution)/shard_map/ppermute | solution.py:234
  228.8 5.6 %collective-permute-start.15 = (bf16[8,4,2048]{2,0,1:T(8,128)(2,1)S(1)}, bf16[8,4,2048]{2,0,1:T(8,128)(2,1)S(1)}, u32[]{:S(2)}, u32[]{:S(2)}) collective-permute-start(bf16[8,4,2048]{2,0,1:T(8,128)(2,1)S(1)} %get-tuple-element.57), channel_id=1, source_target_pairs={{0,96},{32,0},{64,32},{96,64},{1,97},{33,1},{65,33},{97,65},{2,98}... | collective-permute-start | bytes 393224 | tf_op jit(solution)/shard_map/ppermute | solution.py:234

commit v9 on v8

--- a/solution.py
+++ b/solution.py
@@ -48,7 +48,7 @@
     page_len = buf.shape[3]
     positions = pages * page_len
     heads = q_ref.shape[1]
-    head_dim = q_ref.shape[3]
+    head_dim = q_ref.shape[2]
     new_count = fk_ref.shape[1]
     outs = (keys_out_ref, values_out_ref)
 
@@ -83,23 +83,22 @@
 
     length = lengths_ref[r]
     base = base_ref[0]
-    spots = base + lax.broadcasted_iota(jnp.int32, (1, positions), 1)
+    spots = base + lax.broadcasted_iota(jnp.int32, (positions, 1), 0)
     live = spots < length
     for kh in range(heads):
         cols = pl.ds(kh * head_dim, head_dim)
         keys_h = buf[slot, :, 0, :, cols].reshape(positions, head_dim)
         values_h = buf[slot, :, 1, :, cols].reshape(positions, head_dim)
-        query_h = q_ref[0, kh]
-        scores = lax.dot_general(
-            query_h, keys_h, (((1,), (1,)), ((), ())), preferred_element_type=jnp.float32
-        ) * scale
+        query_t = q_ref[0, kh]
+        scores = jnp.dot(keys_h, query_t, preferred_element_type=jnp.float32) * scale
         scores = jnp.where(live, scores, MASKED)
-        peak = jnp.max(scores, axis=1, keepdims=True)
+        peak = jnp.max(scores, axis=0, keepdims=True)
         weights = jnp.where(live, jnp.exp(scores - peak), 0.0)
         peak_ref[0, kh] = peak
-        mass_ref[0, kh] = jnp.sum(weights, axis=1, keepdims=True)
-        acc_ref[0, kh] = jnp.dot(
-            weights.astype(jnp.bfloat16), values_h, preferred_element_type=jnp.float32
+        mass_ref[0, kh] = jnp.sum(weights, axis=0, keepdims=True)
+        acc_ref[0, kh] = lax.dot_general(
+            weights.astype(jnp.bfloat16), values_h, (((0,), (0,)), ((), ())),
+            preferred_element_type=jnp.float32,
         )
     first = length - base
     page0 = first // page_len
@@ -131,7 +130,7 @@
 
 def arrive_and_attend(arrival_src, lengths, base, incoming, queries, fresh_k, fresh_v, scale):
     local_reqs, new_count, kv_width = fresh_k.shape
-    _, heads, rows, head_dim = queries.shape
+    _, heads, head_dim, rows = queries.shape
     page_len = incoming.shape[2]
     pages = arrival_src.shape[0] // local_reqs
     positions = pages * page_len
@@ -140,7 +139,7 @@
         grid=(local_reqs,),
         in_specs=[
             pl.BlockSpec(memory_space=pl.ANY),
-            pl.BlockSpec((1, heads, rows, head_dim), lambda r, *_: (r, 0, 0, 0)),
+            pl.BlockSpec((1, heads, head_dim, rows), lambda r, *_: (r, 0, 0, 0)),
             pl.BlockSpec((1, new_count, kv_width), lambda r, *_: (r, 0, 0)),
             pl.BlockSpec((1, new_count, kv_width), lambda r, *_: (r, 0, 0)),
         ],
@@ -148,8 +147,8 @@
             pl.BlockSpec(memory_space=pl.ANY),
             pl.BlockSpec(memory_space=pl.ANY),
             pl.BlockSpec((1, heads, rows, head_dim), lambda r, *_: (r, 0, 0, 0)),
-            pl.BlockSpec((1, heads, rows, 1), lambda r, *_: (r, 0, 0, 0)),
-            pl.BlockSpec((1, heads, rows, 1), lambda r, *_: (r, 0, 0, 0)),
+            pl.BlockSpec((1, heads, 1, rows), lambda r, *_: (r, 0, 0, 0)),
+            pl.BlockSpec((1, heads, 1, rows), lambda r, *_: (r, 0, 0, 0)),
         ],
         scratch_shapes=[
             pltpu.VMEM((2, pages, 2, page_len, kv_width), jnp.bfloat16),
@@ -164,8 +163,8 @@
             jax.ShapeDtypeStruct((local_reqs, pages, page_len, kv_width), jnp.bfloat16),
             jax.ShapeDtypeStruct((local_reqs, pages, page_len, kv_width), jnp.bfloat16),
             jax.ShapeDtypeStruct((local_reqs, heads, rows, head_dim), jnp.float32),
-            jax.ShapeDtypeStruct((local_reqs, heads, rows, 1), jnp.float32),
-            jax.ShapeDtypeStruct((local_reqs, heads, rows, 1), jnp.float32),
+            jax.ShapeDtypeStruct((local_reqs, heads, 1, rows), jnp.float32),
+            jax.ShapeDtypeStruct((local_reqs, heads, 1, rows), jnp.float32),
         ],
         grid_spec=grid_spec,
         compiler_params=pltpu.CompilerParams(dimension_semantics=("arbitrary",)),
@@ -266,8 +265,8 @@
     )
     fresh_values = owned_rows[..., query_cols + key_cols :].reshape(local_reqs, new_count, KVH, HD)
     score_scale = 1.0 / math.sqrt(HD)
-    kernel_queries = jnp.transpose(queries, (0, 2, 3, 1, 4)).reshape(
-        local_reqs, KVH, groups * new_count, HD
+    kernel_queries = jnp.transpose(queries, (0, 2, 4, 3, 1)).reshape(
+        local_reqs, KVH, HD, groups * new_count
     )
     keys_out, values_out, gathered_sum, row_peak, row_mass = arrive_and_attend(
         arrival_src,

time: 236 us -> 238 us (level)
  no operation moved by 1% of the time
where the time goes in v9:
time: 238 us
  waiting for transfers between devices  120 us (50%)
  local copies, waits for them, and re-layouts  32.3 us (14%)
  starting transfers between devices  29.9 us (13%)
  Pallas kernels  27.6 us (12%)
  other arithmetic  20.4 us (9%)
  matrix products  5.53 us (2%)
    ppermute x12, waiting for transfers between devices, shift(): return lax.ppermute(value, 'req', pairs)  98.6 us
    pallas_call x1, Pallas kernels, arrive_and_attend(): pl.pallas_call(functools.partial(_arrive_kernel, scale=scale), out_shape=...  27.6 us
    ppermute x5, waiting for transfers between devices, merge(): other = lax.ppermute(pack(total, peak, mass), 'seq', pairs)  21.3 us
    ppermute x12, starting transfers between devices, shift(): return lax.ppermute(value, 'req', pairs)  16.2 us
    gather x2, local copies, waits for them, and re-layouts, shards(): outgoing = jnp.stack([pool_keys[send_pick], pool_values[send_pick]], axis=1)  10 us
    all_to_all x1, starting transfers between devices, shards(): lax.all_to_all(outgoing, ('req', 'seq'), split_axis=0, concat_axis=0, til...  10 us
    reshape x1, other arithmetic, shards(): outgoing = outgoing.reshape(devices, per_peer, 2, page_len, kv_width)  7.5 us
  transfers between devices with their start and end apart: 19, of which 12 were waited for; matrix products, arithmetic and copies ran while one was open for 18% of the time, Pallas kernels for 0%

profile of v9, /device:TPU:32, one launch (start us, length us, event | category | flops | bytes accessed | tf_op | source)
XLA Modules:
  0.0 237.5 jit_solution(994193737115162459)
XLA Ops:
  0.6 1.3 fusion.14
  1.9 1.0 fusion.16
  3.0 2.8 %collective-permute-start.2 = (bf16[8,4,2048]{2,0,1:T(8,128)(2,1)S(1)}, bf16[8,4,2048]{2,0,1:T(8,128)(2,1)S(1)}, u32[]{:S(2)}, u32[]{:S(2)}) collective-permute-start(bf16[8,4,2048]{2,0,1:T(8,128)(2,1)S(1)} %fusion.16), channel_id=1, source_target_pairs={{0,96},{32,0},{64,32},{96,64},{1,97},{33,1},{65,33},{97,65},{2,98}... | collective-permute-start | bytes 393224 | tf_op jit(solution)/shard_map/ppermute | solution.py:233
  5.8 0.8 collective-permute-start.1
  6.6 0.9 collective-permute-start
  7.5 0.8 select_reduce_fusion
  8.3 1.5 gather_fusion
  10.0 0.6 fusion.7
  10.7 5.0 %gather_fusion.2 = bf16[128,16,1024]{2,1,0:T(8,128)(2,1)} fusion(bf16[128,16,1024]{2,1,0:T(8,128)(2,1)} %param.18, s32[1024]{0:T(1024)S(1)} %pad_clamp_fusion.2), kind=kCustom, calls=%fused_computation.2 | custom fusion | bytes 8389120 | tf_op jit(solution)/shard_map/gather | solution.py:236
  15.7 5.0 %gather_fusion.1 = bf16[128,16,1024]{2,1,0:T(8,128)(2,1)} fusion(bf16[128,16,1024]{2,1,0:T(8,128)(2,1)} %param.17, s32[1024]{0:T(1024)S(1)} %pad_clamp_fusion.2), kind=kCustom, calls=%fused_computation.1 | custom fusion | bytes 8389120 | tf_op jit(solution)/shard_map/gather | solution.py:236
  20.7 7.5 %maximum_bitcast_fusion = bf16[128,1,2,16,1024]{4,3,2,1,0:T(8,128)(2,1)} fusion(bf16[128,1,16,1024]{3,2,1,0:T(8,128)(2,1)} %bitcast.144, bf16[128,1,16,1024]{3,2,1,0:T(8,128)(2,1)} %bitcast.145), kind=kLoop, calls=%fused_computation.5 | loop fusion | flops 4194304 | bytes 16777216 | tf_op jit(solution)/shard_map/reshape | solution.py:237
  28.2 0.9 pad_maximum_fusion
  29.2 10.0 %all-to-all-start = ((bf16[128,1,2,16,1024]{4,3,2,1,0:T(8,128)(2,1)}), bf16[128,1,2,16,1024]{4,3,2,1,0:T(8,128)(2,1)}, u32[]{:S(2)}, u32[]{:S(2)}) async-start(bf16[128,1,2,16,1024]{4,3,2,1,0:T(8,128)(2,1)} %maximum_bitcast_fusion), calls=%async_computation | async-start | bytes 16777216 | tf_op jit(solution)/shard_map/all_to_all | solution.py:239
  39.2 2.3 copy.193
  41.6 0.6 gather_fusion.3
  42.3 3.9 %copy.192 = bf16[512,2048]{1,0:T(8,128)(2,1)} copy(bf16[512,2048]{0,1:T(8,128)(2,1)} %bitcast.149) | data formatting | bytes 4194304 | tf_op jit(solution)/shard_map/dot_general | solution.py:245
  46.6 0.6 dynamic_slice.28.lengths_ref
  47.4 0.5 and_select_fusion.4.arrival_ref
  48.0 0.3 multiply_cosine_fusion
  48.3 1.7 fusion.8
  50.2 2.4 %fusion.10 = f32[32,4,4,128]{3,0,2,1:T(8,128)S(1)} fusion(bf16[4,128,2048,1]{2,1,0,3:T(8,128)(2,1)} %bitcast.146, bf16[32,4,2048]{2,0,1:T(8,128)(2,1)S(1)} %pad_maximum_fusion), kind=kOutput, calls=%fused_computation.25 | convolution fusion | flops 268435456 | bytes 2883584 | tf_op jit(solution)/shard_map/dot_general | solution.py:245
  52.9 0.3 convolution_convert_fusion.1
  53.3 1.5 collective-permute-start.5
  54.9 2.7 %collective-permute-start.4 = (bf16[8,4,1024]{2,0,1:T(8,128)(2,1)S(1)}, bf16[8,4,1024]{2,0,1:T(8,128)(2,1)S(1)}, u32[]{:S(2)}, u32[]{:S(2)}) collective-permute-start(bf16[8,4,1024]{2,0,1:T(8,128)(2,1)S(1)} %get-tuple-element.70), channel_id=1, source_target_pairs={{0,64},{32,96},{64,0},{96,32},{1,65},{33,97},{65,1},{97,33},{2,66}... | collective-permute-start | bytes 196616 | tf_op jit(solution)/shard_map/ppermute | solution.py:233
  57.6 1.4 collective-permute-start.3
  59.0 78.3 %collective-permute-done.5 = bf16[8,4,1024]{2,0,1:T(8,128)(2,1)S(1)} collective-permute-done((bf16[8,4,1024]{2,0,1:T(8,128)(2,1)S(1)}, bf16[8,4,1024]{2,0,1:T(8,128)(2,1)S(1)}, u32[]{:S(2)}, u32[]{:S(2)}) %collective-permute-start.5) | collective-permute-done | bytes 65568 | tf_op jit(solution)/shard_map/ppermute | solution.py:233
  137.4 10.4 %collective-permute-done.4 = bf16[8,4,1024]{2,0,1:T(8,128)(2,1)S(1)} collective-permute-done((bf16[8,4,1024]{2,0,1:T(8,128)(2,1)S(1)}, bf16[8,4,1024]{2,0,1:T(8,128)(2,1)S(1)}, u32[]{:S(2)}, u32[]{:S(2)}) %collective-permute-start.4) | collective-permute-done | bytes 65568 | tf_op jit(solution)/shard_map/ppermute | solution.py:233
  147.8 0.6 gather_fusion.4
  148.8 1.7 copy.163.q_ref
  150.5 0.7 reshape_reshape.15.fk_ref
  151.2 0.7 reshape_reshape.16.fv_ref
  151.8 27.6 %arrive_and_attend.1 = (bf16[8,16,16,1024]{3,2,1,0:T(8,128)(2,1)}, bf16[8,16,16,1024]{3,2,1,0:T(8,128)(2,1)}, f32[8,8,8,128]{3,2,1,0:T(8,128)}, f32[8,8,1,8]{3,2,1,0:T(1,128)}, f32[8,8,1,8]{3,2,1,0:T(1,128)}) custom-call(s32[128]{0:T(128)} %and_select_fusion.4.arrival_ref, s32[8]{0:T(128)} %dynamic_slice.28.lengths_ref, s32[1]{0:T(128)} %bitcast.3.base_ref, ...), custom_call_target="tpu_custom_call" | custom-call | flops 67108864 | bytes 16777216 | tf_op jit(solution)/shard_map/arrive_and_attend/pallas_call | solution.py:160
  179.4 0.5 broadcast.386
  179.9 1.5 reduce.9
  181.5 1.5 reduce.10
  183.1 1.0 pad_maximum_fusion.1
  184.2 0.8 copy.164
  185.0 0.8 copy.167
  186.9 1.1 multiply_add_fusion.4
  188.0 0.3 collective-permute-start.7
  188.3 5.9 %collective-permute-done.7 = f32[260,128]{1,0:T(8,128)S(1)} collective-permute-done((f32[260,128]{1,0:T(8,128)S(1)}, f32[260,128]{1,0:T(8,128)S(1)}, u32[]{:S(2)}, u32[]{:S(2)}) %collective-permute-start.7) | collective-permute-done | bytes 133152 | tf_op jit(solution)/shard_map/ppermute | solution.py:300
  194.8 0.2 multiply_add_fusion.3
  195.1 3.1 %collective-permute-start.8 = (f32[260,128]{1,0:T(8,128)S(1)}, f32[260,128]{1,0:T(8,128)S(1)}, u32[]{:S(2)}, u32[]{:S(2)}) collective-permute-start(f32[260,128]{1,0:T(8,128)S(1)} %pad_maximum_fusion.5), channel_id=1, source_target_pairs={{0,4},{1,5},{2,6},{3,7},{4,0},{5,1},{6,2},{7,3},{8,12},{9,13},{10,... | collective-permute-start | bytes 399368 | tf_op jit(solution)/shard_map/ppermute | solution.py:300
  198.2 3.6 %collective-permute-done.8 = f32[260,128]{1,0:T(8,128)S(1)} collective-permute-done((f32[260,128]{1,0:T(8,128)S(1)}, f32[260,128]{1,0:T(8,128)S(1)}, u32[]{:S(2)}, u32[]{:S(2)}) %collective-permute-start.8) | collective-permute-done | bytes 133152 | tf_op jit(solution)/shard_map/ppermute | solution.py:300
  202.3 0.2 multiply_add_fusion.2
  202.6 5.4 %collective-permute-done.9 = f32[260,128]{1,0:T(8,128)S(1)} collective-permute-done((f32[260,128]{1,0:T(8,128)S(1)}, f32[260,128]{1,0:T(8,128)S(1)}, u32[]{:S(2)}, u32[]{:S(2)}) %collective-permute-start.9) | collective-permute-done | bytes 133152 | tf_op jit(solution)/shard_map/ppermute | solution.py:300
  209.0 6.4 %collective-permute-done.10 = f32[260,128]{1,0:T(8,128)S(1)} collective-permute-done((f32[260,128]{1,0:T(8,128)S(1)}, f32[260,128]{1,0:T(8,128)S(1)}, u32[]{:S(2)}, u32[]{:S(2)}) %collective-permute-start.10) | collective-permute-done | bytes 133152 | tf_op jit(solution)/shard_map/ppermute | solution.py:300
  216.2 0.3 fusion.21
  216.6 0.5 copy.175
  217.1 0.4 collective-permute-done.11
  218.3 0.5 copy.178
  219.7 0.4 fusion.3
  220.4 0.2 collective-permute-start.13
  220.6 1.8 collective-permute-start.12
  222.4 1.9 collective-permute-done.14
  224.3 1.7 collective-permute-done.13
  226.0 1.0 collective-permute-done.12
  227.0 0.4 convolution_convert_fusion
  227.4 0.9 collective-permute-start.17
  228.4 2.6 %collective-permute-start.16 = (bf16[8,4,2048]{2,0,1:T(8,128)(2,1)S(1)}, bf16[8,4,2048]{2,0,1:T(8,128)(2,1)S(1)}, u32[]{:S(2)}, u32[]{:S(2)}) collective-permute-start(bf16[8,4,2048]{2,0,1:T(8,128)(2,1)S(1)} %get-tuple-element.59), channel_id=1, source_target_pairs={{0,64},{32,96},{64,0},{96,32},{1,65},{33,97},{65,1},{97,33},{2,66}... | collective-permute-start | bytes 393224 | tf_op jit(solution)/shard_map/ppermute | solution.py:233
  231.0 0.3 collective-permute-start.15
  231.3 4.7 %collective-permute-done.17 = bf16[8,4,2048]{2,0,1:T(8,128)(2,1)S(1)} collective-permute-done((bf16[8,4,2048]{2,0,1:T(8,128)(2,1)S(1)}, bf16[8,4,2048]{2,0,1:T(8,128)(2,1)S(1)}, u32[]{:S(2)}, u32[]{:S(2)}) %collective-permute-start.17) | collective-permute-done | bytes 131104 | tf_op jit(solution)/shard_map/ppermute | solution.py:233
  236.0 0.6 collective-permute-done.15
  236.8 0.8 copy.185
  (129 shorter events, 8.3 us)
Async XLA Ops:
  0.6 226.3 %copy-start = (bf16[512,2048]{1,0:T(8,128)(2,1)S(1)}, bf16[512,2048]{1,0:T(8,128)(2,1)}, u32[]{:S(2)}) copy-start(bf16[512,2048]{1,0:T(8,128)(2,1)} %param.16) | copy-start | bytes 6291460
  3.0 25.3 %collective-permute-start.2 = (bf16[8,4,2048]{2,0,1:T(8,128)(2,1)S(1)}, bf16[8,4,2048]{2,0,1:T(8,128)(2,1)S(1)}, u32[]{:S(2)}, u32[]{:S(2)}) collective-permute-start(bf16[8,4,2048]{2,0,1:T(8,128)(2,1)S(1)} %fusion.16), channel_id=1, source_target_pairs={{0,96},{32,0},{64,32},{96,64},{1,97},{33,1},{65,33},{97,65},{2,98}... | collective-permute-start | bytes 393224 | tf_op jit(solution)/shard_map/ppermute | solution.py:233
  5.8 22.4 %collective-permute-start.1 = (bf16[8,4,2048]{2,0,1:T(8,128)(2,1)S(1)}, bf16[8,4,2048]{2,0,1:T(8,128)(2,1)S(1)}, u32[]{:S(2)}, u32[]{:S(2)}) collective-permute-start(bf16[8,4,2048]{2,0,1:T(8,128)(2,1)S(1)} %fusion.16), channel_id=1, source_target_pairs={{0,64},{32,96},{64,0},{96,32},{1,65},{33,97},{65,1},{97,33},{2,66}... | collective-permute-start | bytes 393224 | tf_op jit(solution)/shard_map/ppermute | solution.py:233
  6.6 21.6 %collective-permute-start = (bf16[8,4,2048]{2,0,1:T(8,128)(2,1)S(1)}, bf16[8,4,2048]{2,0,1:T(8,128)(2,1)}, u32[]{:S(2)}, u32[]{:S(2)}) collective-permute-start(bf16[8,4,2048]{2,0,1:T(8,128)(2,1)S(1)} %fusion.16), channel_id=1, source_target_pairs={{0,32},{32,64},{64,96},{96,0},{1,33},{33,65},{65,97},{97,1},{2,34}... | collective-permute-start | bytes 393224 | tf_op jit(solution)/shard_map/ppermute | solution.py:233
  29.2 122.7 %all-to-all-start = ((bf16[128,1,2,16,1024]{4,3,2,1,0:T(8,128)(2,1)}), bf16[128,1,2,16,1024]{4,3,2,1,0:T(8,128)(2,1)}, u32[]{:S(2)}, u32[]{:S(2)}) async-start(bf16[128,1,2,16,1024]{4,3,2,1,0:T(8,128)(2,1)} %maximum_bitcast_fusion), calls=%async_computation | async-start | bytes 16777216 | tf_op jit(solution)/shard_map/all_to_all | solution.py:239
  47.2 5.7 %copy-start.2 = (bf16[2048,256]{1,0:T(8,128)(2,1)S(1)}, bf16[2048,256]{1,0:T(8,128)(2,1)}, u32[]{:S(2)}) copy-start(bf16[2048,256]{1,0:T(8,128)(2,1)} %param.15) | copy-start | bytes 3145732
  53.3 84.0 %collective-permute-start.5 = (bf16[8,4,1024]{2,0,1:T(8,128)(2,1)S(1)}, bf16[8,4,1024]{2,0,1:T(8,128)(2,1)S(1)}, u32[]{:S(2)}, u32[]{:S(2)}) collective-permute-start(bf16[8,4,1024]{2,0,1:T(8,128)(2,1)S(1)} %get-tuple-element.69), channel_id=1, source_target_pairs={{0,32},{32,64},{64,96},{96,0},{1,33},{33,65},{65,97},{97,1},{2,34}... | collective-permute-start | bytes 196616 | tf_op jit(solution)/shard_map/ppermute | solution.py:233
  54.9 92.9 %collective-permute-start.4 = (bf16[8,4,1024]{2,0,1:T(8,128)(2,1)S(1)}, bf16[8,4,1024]{2,0,1:T(8,128)(2,1)S(1)}, u32[]{:S(2)}, u32[]{:S(2)}) collective-permute-start(bf16[8,4,1024]{2,0,1:T(8,128)(2,1)S(1)} %get-tuple-element.70), channel_id=1, source_target_pairs={{0,64},{32,96},{64,0},{96,32},{1,65},{33,97},{65,1},{97,33},{2,66}... | collective-permute-start | bytes 196616 | tf_op jit(solution)/shard_map/ppermute | solution.py:233
  57.6 90.2 %collective-permute-start.3 = (bf16[8,4,1024]{2,0,1:T(8,128)(2,1)S(1)}, bf16[8,4,1024]{2,0,1:T(8,128)(2,1)S(1)}, u32[]{:S(2)}, u32[]{:S(2)}) collective-permute-start(bf16[8,4,1024]{2,0,1:T(8,128)(2,1)S(1)} %get-tuple-element.71), channel_id=1, source_target_pairs={{0,96},{32,0},{64,32},{96,64},{1,97},{33,1},{65,33},{97,65},{2,98}... | collective-permute-start | bytes 196616 | tf_op jit(solution)/shard_map/ppermute | solution.py:233
  184.1 2.1 collective-permute-start.6
  188.0 6.2 %collective-permute-start.7 = (f32[260,128]{1,0:T(8,128)S(1)}, f32[260,128]{1,0:T(8,128)S(1)}, u32[]{:S(2)}, u32[]{:S(2)}) collective-permute-start(f32[260,128]{1,0:T(8,128)S(1)} %pad_maximum_fusion.4), channel_id=1, source_target_pairs={{0,2},{1,3},{2,0},{3,1},{4,6},{5,7},{6,4},{7,5},{8,10},{9,11},{10,... | collective-permute-start | bytes 399368 | tf_op jit(solution)/shard_map/ppermute | solution.py:300
  195.1 6.7 %collective-permute-start.8 = (f32[260,128]{1,0:T(8,128)S(1)}, f32[260,128]{1,0:T(8,128)S(1)}, u32[]{:S(2)}, u32[]{:S(2)}) collective-permute-start(f32[260,128]{1,0:T(8,128)S(1)} %pad_maximum_fusion.5), channel_id=1, source_target_pairs={{0,4},{1,5},{2,6},{3,7},{4,0},{5,1},{6,2},{7,3},{8,12},{9,13},{10,... | collective-permute-start | bytes 399368 | tf_op jit(solution)/shard_map/ppermute | solution.py:300
  202.5 5.5 %collective-permute-start.9 = (f32[260,128]{1,0:T(8,128)S(1)}, f32[260,128]{1,0:T(8,128)S(1)}, u32[]{:S(2)}, u32[]{:S(2)}) collective-permute-start(f32[260,128]{1,0:T(8,128)S(1)} %pad_maximum_fusion.6), channel_id=1, source_target_pairs={{0,8},{1,9},{2,10},{3,11},{4,12},{5,13},{6,14},{7,15},{8,0},{9,1},... | collective-permute-start | bytes 399368 | tf_op jit(solution)/shard_map/ppermute | solution.py:300
  208.8 6.6 %collective-permute-start.10 = (f32[260,128]{1,0:T(8,128)S(1)}, f32[260,128]{1,0:T(8,128)S(1)}, u32[]{:S(2)}, u32[]{:S(2)}) collective-permute-start(f32[260,128]{1,0:T(8,128)S(1)} %pad_maximum_fusion.7), channel_id=1, source_target_pairs={{0,16},{1,17},{2,18},{3,19},{4,20},{5,21},{6,22},{7,23},{8,24},{9,... | collective-permute-start | bytes 399368 | tf_op jit(solution)/shard_map/ppermute | solution.py:300
  216.1 1.4 collective-permute-start.11
  220.1 16.6 %copy-start.1 = (bf16[8,4,2048]{2,1,0:T(4,128)(2,1)S(1)}, bf16[8,4,2048]{2,1,0:T(4,128)(2,1)}, u32[]{:S(2)}) copy-start(bf16[8,4,2048]{2,1,0:T(4,128)(2,1)} %param.11) | copy-start | bytes 393220
  220.3 4.0 %collective-permute-start.14 = (bf16[8,4,512]{2,0,1:T(8,128)(2,1)S(1)}, bf16[8,4,512]{2,0,1:T(8,128)(2,1)S(1)}, u32[]{:S(2)}, u32[]{:S(2)}) collective-permute-start(bf16[8,4,512]{2,0,1:T(8,128)(2,1)S(1)} %get-tuple-element.89), channel_id=1, source_target_pairs={{0,96},{32,0},{64,32},{96,64},{1,97},{33,1},{65,33},{97,65},{2,98}... | collective-permute-start | bytes 98312 | tf_op jit(solution)/shard_map/ppermute | solution.py:233
  220.4 5.6 %collective-permute-start.13 = (bf16[8,4,512]{2,0,1:T(8,128)(2,1)S(1)}, bf16[8,4,512]{2,0,1:T(8,128)(2,1)S(1)}, u32[]{:S(2)}, u32[]{:S(2)}) collective-permute-start(bf16[8,4,512]{2,0,1:T(8,128)(2,1)S(1)} %get-tuple-element.90), channel_id=1, source_target_pairs={{0,64},{32,96},{64,0},{96,32},{1,65},{33,97},{65,1},{97,33},{2,66}... | collective-permute-start | bytes 98312 | tf_op jit(solution)/shard_map/ppermute | solution.py:233
  220.6 6.3 %collective-permute-start.12 = (bf16[8,4,512]{2,0,1:T(8,128)(2,1)S(1)}, bf16[8,4,512]{2,0,1:T(8,128)(2,1)S(1)}, u32[]{:S(2)}, u32[]{:S(2)}) collective-permute-start(bf16[8,4,512]{2,0,1:T(8,128)(2,1)S(1)} %get-tuple-element.91), channel_id=1, source_target_pairs={{0,32},{32,64},{64,96},{96,0},{1,33},{33,65},{65,97},{97,1},{2,34}... | collective-permute-start | bytes 98312 | tf_op jit(solution)/shard_map/ppermute | solution.py:233
  227.4 8.6 %collective-permute-start.17 = (bf16[8,4,2048]{2,0,1:T(8,128)(2,1)S(1)}, bf16[8,4,2048]{2,0,1:T(8,128)(2,1)S(1)}, u32[]{:S(2)}, u32[]{:S(2)}) collective-permute-start(bf16[8,4,2048]{2,0,1:T(8,128)(2,1)S(1)} %get-tuple-element.58), channel_id=1, source_target_pairs={{0,32},{32,64},{64,96},{96,0},{1,33},{33,65},{65,97},{97,1},{2,34}... | collective-permute-start | bytes 393224 | tf_op jit(solution)/shard_map/ppermute | solution.py:233
  228.4 7.6 %collective-permute-start.16 = (bf16[8,4,2048]{2,0,1:T(8,128)(2,1)S(1)}, bf16[8,4,2048]{2,0,1:T(8,128)(2,1)S(1)}, u32[]{:S(2)}, u32[]{:S(2)}) collective-permute-start(bf16[8,4,2048]{2,0,1:T(8,128)(2,1)S(1)} %get-tuple-element.59), channel_id=1, source_target_pairs={{0,64},{32,96},{64,0},{96,32},{1,65},{33,97},{65,1},{97,33},{2,66}... | collective-permute-start | bytes 393224 | tf_op jit(solution)/shard_map/ppermute | solution.py:233
  231.0 5.6 %collective-permute-start.15 = (bf16[8,4,2048]{2,0,1:T(8,128)(2,1)S(1)}, bf16[8,4,2048]{2,0,1:T(8,128)(2,1)S(1)}, u32[]{:S(2)}, u32[]{:S(2)}) collective-permute-start(bf16[8,4,2048]{2,0,1:T(8,128)(2,1)S(1)} %get-tuple-element.57), channel_id=1, source_target_pairs={{0,96},{32,0},{64,32},{96,64},{1,97},{33,1},{65,33},{97,65},{2,98}... | collective-permute-start | bytes 393224 | tf_op jit(solution)/shard_map/ppermute | solution.py:233

commit v10 on v8

--- a/solution.py
+++ b/solution.py
@@ -37,58 +37,27 @@
 
 
 def _arrive_kernel(
-    arrival_ref, lengths_ref, base_ref, incoming_ref, q_ref, fk_ref, fv_ref,
-    keys_out_ref, values_out_ref, acc_ref, peak_ref, mass_ref,
-    buf, in_sem, out_sem, *, scale
+    lengths_ref, base_ref, arrived_ref, q_ref, fk_ref, fv_ref,
+    keys_out_ref, values_out_ref, acc_ref, peak_ref, mass_ref, *, scale
 ):
     r = pl.program_id(0)
-    n = pl.num_programs(0)
-    slot = r % 2
-    pages = buf.shape[1]
-    page_len = buf.shape[3]
+    pages = arrived_ref.shape[1]
+    page_len = arrived_ref.shape[3]
     positions = pages * page_len
     heads = q_ref.shape[1]
     head_dim = q_ref.shape[3]
     new_count = fk_ref.shape[1]
     outs = (keys_out_ref, values_out_ref)
-
-    def page_copy(s, pp, src):
-        return pltpu.make_async_copy(incoming_ref.at[src], buf.at[s, pp], in_sem.at[s, pp])
-
-    def fetch(req, s):
-        for pp in range(pages):
-            page_copy(s, pp, arrival_ref[req * pages + pp]).start()
-
-    def wait_fetch(s):
-        for pp in range(pages):
-            page_copy(s, pp, 0).wait()
-
-    def out_copy(req, s, half):
-        return pltpu.make_async_copy(buf.at[s, :, half], outs[half].at[req], out_sem.at[half, s])
-
-    @pl.when(r == 0)
-    def _():
-        fetch(0, 0)
-
-    wait_fetch(slot)
-
-    @pl.when(r + 1 < n)
-    def _():
-        @pl.when(r >= 1)
-        def _():
-            for half in range(2):
-                out_copy(r - 1, 1 - slot, half).wait()
-
-        fetch(r + 1, 1 - slot)
-
+    keys_out_ref[0] = arrived_ref[0, :, 0]
+    values_out_ref[0] = arrived_ref[0, :, 1]
     length = lengths_ref[r]
     base = base_ref[0]
     spots = base + lax.broadcasted_iota(jnp.int32, (1, positions), 1)
     live = spots < length
     for kh in range(heads):
         cols = pl.ds(kh * head_dim, head_dim)
-        keys_h = buf[slot, :, 0, :, cols].reshape(positions, head_dim)
-        values_h = buf[slot, :, 1, :, cols].reshape(positions, head_dim)
+        keys_h = arrived_ref[0, :, 0, :, cols].reshape(positions, head_dim)
+        values_h = arrived_ref[0, :, 1, :, cols].reshape(positions, head_dim)
         query_h = q_ref[0, kh]
         scores = lax.dot_general(
             query_h, keys_h, (((1,), (1,)), ((), ())), preferred_element_type=jnp.float32
@@ -109,24 +78,11 @@
         @pl.when(jnp.logical_and(page >= 0, page < pages))
         def _():
             for half in range(2):
-                block = buf[slot, page, half]
+                block = outs[half][0, page]
                 for t in range(new_count):
                     hit = row_ids == first + t - page * page_len
                     block = jnp.where(hit, fresh[half][t : t + 1, :], block)
-                buf[slot, page, half] = block
-
-    for half in range(2):
-        out_copy(r, slot, half).start()
-
-    @pl.when(r == n - 1)
-    def _():
-        @pl.when(r >= 1)
-        def _():
-            for half in range(2):
-                out_copy(r - 1, 1 - slot, half).wait()
-
-        for half in range(2):
-            out_copy(r, slot, half).wait()
+                outs[half][0, page] = block
 
 
 def arrive_and_attend(arrival_src, lengths, base, incoming, queries, fresh_k, fresh_v, scale):
@@ -135,26 +91,22 @@
     page_len = incoming.shape[2]
     pages = arrival_src.shape[0] // local_reqs
     positions = pages * page_len
+    arrived = incoming[arrival_src].reshape(local_reqs, pages, 2, page_len, kv_width)
     grid_spec = pltpu.PrefetchScalarGridSpec(
-        num_scalar_prefetch=3,
+        num_scalar_prefetch=2,
         grid=(local_reqs,),
         in_specs=[
-            pl.BlockSpec(memory_space=pl.ANY),
+            pl.BlockSpec((1, pages, 2, page_len, kv_width), lambda r, *_: (r, 0, 0, 0, 0)),
             pl.BlockSpec((1, heads, rows, head_dim), lambda r, *_: (r, 0, 0, 0)),
             pl.BlockSpec((1, new_count, kv_width), lambda r, *_: (r, 0, 0)),
             pl.BlockSpec((1, new_count, kv_width), lambda r, *_: (r, 0, 0)),
         ],
         out_specs=[
-            pl.BlockSpec(memory_space=pl.ANY),
-            pl.BlockSpec(memory_space=pl.ANY),
+            pl.BlockSpec((1, pages, page_len, kv_width), lambda r, *_: (r, 0, 0, 0)),
+            pl.BlockSpec((1, pages, page_len, kv_width), lambda r, *_: (r, 0, 0, 0)),
             pl.BlockSpec((1, heads, rows, head_dim), lambda r, *_: (r, 0, 0, 0)),
             pl.BlockSpec((1, heads, rows, 1), lambda r, *_: (r, 0, 0, 0)),
             pl.BlockSpec((1, heads, rows, 1), lambda r, *_: (r, 0, 0, 0)),
-        ],
-        scratch_shapes=[
-            pltpu.VMEM((2, pages, 2, page_len, kv_width), jnp.bfloat16),
-            pltpu.SemaphoreType.DMA((2, pages)),
-            pltpu.SemaphoreType.DMA((2, 2)),
         ],
     )
     cache_bytes = 2 * local_reqs * positions * kv_width * 2
@@ -168,14 +120,16 @@
             jax.ShapeDtypeStruct((local_reqs, heads, rows, 1), jnp.float32),
         ],
         grid_spec=grid_spec,
-        compiler_params=pltpu.CompilerParams(dimension_semantics=("arbitrary",)),
+        compiler_params=pltpu.CompilerParams(
+            dimension_semantics=("arbitrary",), vmem_limit_bytes=48 * 1024 * 1024
+        ),
         cost_estimate=pl.CostEstimate(
             flops=4 * local_reqs * heads * rows * positions * head_dim,
             transcendentals=local_reqs * heads * rows * positions,
             bytes_accessed=2 * cache_bytes,
         ),
         name="arrive_and_attend",
-    )(arrival_src, lengths, base, incoming, queries, fresh_k, fresh_v)
+    )(lengths, base, arrived, queries, fresh_k, fresh_v)
     keys_out = keys_out.reshape(local_reqs, positions, kv_width)
     values_out = values_out.reshape(local_reqs, positions, kv_width)
     return keys_out, values_out, acc, peak, mass

time: 236 us -> 234 us (level)
  local copies, waits for them, and re-layouts: 31.8 us -> 39.2 us
  Pallas kernels: 26.6 us -> 19.3 us
  other arithmetic: 19.6 us -> 16 us
    gather x0 -> x1, local copies, waits for them, and re-layouts: none -> 9.96 us  [arrive_and_attend(): incoming[arrival_src].reshape(local_reqs, pages, 2, page_len, kv_width)]
    pallas_call x1, Pallas kernels: 26.6 us -> 19.3 us  [arrive_and_attend(): pl.pallas_call(functools.partial(_arrive_kernel, scale=scale), out_shape=...]
  transfers between devices with their start and end apart: 19 -> 19, of which waited for: 12 -> 13; matrix products, arithmetic and copies ran while one was open for 18% -> 16% of each run, Pallas kernels for 0% -> 0%
where the time goes in v10:
time: 234 us; the launch traced here: 233 us
  waiting for transfers between devices  122 us (52%)
  local copies, waits for them, and re-layouts  39.2 us (17%)
  starting transfers between devices  29.8 us (13%)
  Pallas kernels  19.3 us (8%)
  other arithmetic  16 us (7%)
  matrix products  5.57 us (2%)
    ppermute x12, waiting for transfers between devices, shift(): return lax.ppermute(value, 'req', pairs)  99.6 us
    ppermute x5, waiting for transfers between devices, merge(): other = lax.ppermute(pack(total, peak, mass), 'seq', pairs)  22 us
    pallas_call x1, Pallas kernels, arrive_and_attend(): pl.pallas_call(functools.partial(_arrive_kernel, scale=scale), out_shape=...  19.3 us
    ppermute x12, starting transfers between devices, shift(): return lax.ppermute(value, 'req', pairs)  16.2 us
    gather x2, local copies, waits for them, and re-layouts, shards(): outgoing = jnp.stack([pool_keys[send_pick], pool_values[send_pick]], axis=1)  10 us
    all_to_all x1, starting transfers between devices, shards(): lax.all_to_all(outgoing, ('req', 'seq'), split_axis=0, concat_axis=0, til...  10 us
    gather x1, local copies, waits for them, and re-layouts, arrive_and_attend(): incoming[arrival_src].reshape(local_reqs, pages, 2, page_len, kv_width)  9.96 us
    reshape x1, other arithmetic, shards(): outgoing = outgoing.reshape(devices, per_peer, 2, page_len, kv_width)  7.5 us
  transfers between devices with their start and end apart: 19, of which 13 were waited for; matrix products, arithmetic and copies ran while one was open for 16% of the time, Pallas kernels for 0%

profile of v10, /device:TPU:32, one launch (start us, length us, event | category | flops | bytes accessed | tf_op | source)
XLA Modules:
  0.0 233.4 jit_solution(1915687134699361894)
XLA Ops:
  0.6 1.3 fusion.14
  1.9 1.0 fusion.16
  3.0 2.8 %collective-permute-start.2 = (bf16[8,4,2048]{2,0,1:T(8,128)(2,1)S(1)}, bf16[8,4,2048]{2,0,1:T(8,128)(2,1)S(1)}, u32[]{:S(2)}, u32[]{:S(2)}) collective-permute-start(bf16[8,4,2048]{2,0,1:T(8,128)(2,1)S(1)} %fusion.16), channel_id=1, source_target_pairs={{0,96},{32,0},{64,32},{96,64},{1,97},{33,1},{65,33},{97,65},{2,98}... | collective-permute-start | bytes 393224 | tf_op jit(solution)/shard_map/ppermute | solution.py:188
  5.8 0.8 collective-permute-start.1
  6.6 0.9 collective-permute-start
  7.5 0.8 select_reduce_fusion.1
  8.3 1.5 gather_fusion
  9.8 0.2 reshape.606
  10.0 0.6 fusion.7
  10.7 5.0 %gather_fusion.2 = bf16[128,16,1024]{2,1,0:T(8,128)(2,1)} fusion(bf16[128,16,1024]{2,1,0:T(8,128)(2,1)} %param.18, s32[1024]{0:T(1024)S(1)} %pad_clamp_fusion.3), kind=kCustom, calls=%fused_computation.2 | custom fusion | bytes 8389120 | tf_op jit(solution)/shard_map/gather | solution.py:191
  15.7 5.0 %gather_fusion.1 = bf16[128,16,1024]{2,1,0:T(8,128)(2,1)} fusion(bf16[128,16,1024]{2,1,0:T(8,128)(2,1)} %param.17, s32[1024]{0:T(1024)S(1)} %pad_clamp_fusion.3), kind=kCustom, calls=%fused_computation.1 | custom fusion | bytes 8389120 | tf_op jit(solution)/shard_map/gather | solution.py:191
  20.7 7.5 %maximum_bitcast_fusion = bf16[128,1,2,16,1024]{4,3,2,1,0:T(8,128)(2,1)} fusion(bf16[128,1,16,1024]{3,2,1,0:T(8,128)(2,1)} %bitcast.161, bf16[128,1,16,1024]{3,2,1,0:T(8,128)(2,1)} %bitcast.162), kind=kLoop, calls=%fused_computation.6 | loop fusion | flops 4194304 | bytes 16777216 | tf_op jit(solution)/shard_map/reshape | solution.py:192
  28.2 0.9 pad_maximum_fusion
  29.2 10.0 %all-to-all-start = ((bf16[128,1,2,16,1024]{4,3,2,1,0:T(8,128)(2,1)}), bf16[128,1,2,16,1024]{4,3,2,1,0:T(8,128)(2,1)}, u32[]{:S(2)}, u32[]{:S(2)}) async-start(bf16[128,1,2,16,1024]{4,3,2,1,0:T(8,128)(2,1)} %maximum_bitcast_fusion), calls=%async_computation | async-start | bytes 16777216 | tf_op jit(solution)/shard_map/all_to_all | solution.py:194
  39.2 2.3 copy.186
  41.6 0.6 gather_fusion.4
  42.3 3.9 %copy.185 = bf16[512,2048]{1,0:T(8,128)(2,1)} copy(bf16[512,2048]{0,1:T(8,128)(2,1)} %bitcast.166) | data formatting | bytes 4194304 | tf_op jit(solution)/shard_map/dot_general | solution.py:200
  46.3 0.2 copy.148
  46.7 0.2 dynamic-slice_reduce_fusion
  47.0 0.3 multiply_cosine_fusion
  47.3 1.7 fusion.8
  49.2 2.4 %fusion.10 = f32[32,4,4,128]{3,0,2,1:T(8,128)S(1)} fusion(bf16[4,128,2048,1]{2,1,0,3:T(8,128)(2,1)} %bitcast.163, bf16[32,4,2048]{2,0,1:T(8,128)(2,1)S(1)} %pad_maximum_fusion), kind=kOutput, calls=%fused_computation.26 | convolution fusion | flops 268435456 | bytes 2883584 | tf_op jit(solution)/shard_map/dot_general | solution.py:200
  52.0 0.3 convolution_convert_fusion.1
  52.3 1.5 collective-permute-start.5
  53.9 2.7 %collective-permute-start.4 = (bf16[8,4,1024]{2,0,1:T(8,128)(2,1)S(1)}, bf16[8,4,1024]{2,0,1:T(8,128)(2,1)S(1)}, u32[]{:S(2)}, u32[]{:S(2)}) collective-permute-start(bf16[8,4,1024]{2,0,1:T(8,128)(2,1)S(1)} %get-tuple-element.70), channel_id=1, source_target_pairs={{0,64},{32,96},{64,0},{96,32},{1,65},{33,97},{65,1},{97,33},{2,66}... | collective-permute-start | bytes 196616 | tf_op jit(solution)/shard_map/ppermute | solution.py:188
  56.6 1.4 collective-permute-start.3
  58.0 79.3 %collective-permute-done.5 = bf16[8,4,1024]{2,0,1:T(8,128)(2,1)S(1)} collective-permute-done((bf16[8,4,1024]{2,0,1:T(8,128)(2,1)S(1)}, bf16[8,4,1024]{2,0,1:T(8,128)(2,1)S(1)}, u32[]{:S(2)}, u32[]{:S(2)}) %collective-permute-start.5) | collective-permute-done | bytes 65568 | tf_op jit(solution)/shard_map/ppermute | solution.py:188
  137.4 10.4 %collective-permute-done.4 = bf16[8,4,1024]{2,0,1:T(8,128)(2,1)S(1)} collective-permute-done((bf16[8,4,1024]{2,0,1:T(8,128)(2,1)S(1)}, bf16[8,4,1024]{2,0,1:T(8,128)(2,1)S(1)}, u32[]{:S(2)}, u32[]{:S(2)}) %collective-permute-start.4) | collective-permute-done | bytes 65568 | tf_op jit(solution)/shard_map/ppermute | solution.py:188
  147.8 0.6 gather_fusion.5
  148.9 10.0 %gather_fusion.3 = bf16[128,2,16,1024]{3,2,1,0:T(8,128)(2,1)} fusion(bf16[128,2,16,1024]{3,2,1,0:T(8,128)(2,1)} %bitcast.8, s32[1024]{0:T(1024)S(1)} %pad_clamp_fusion.2), kind=kCustom, calls=%fused_computation.3 | custom fusion | bytes 16777728 | tf_op jit(solution)/shard_map/gather | solution.py:94
  158.9 19.3 %arrive_and_attend.1 = (bf16[8,16,16,1024]{3,2,1,0:T(8,128)(2,1)}, bf16[8,16,16,1024]{3,2,1,0:T(8,128)(2,1)}, f32[8,8,8,128]{3,2,1,0:T(8,128)S(1)}, f32[8,8,8,1]{3,2,1,0:T(8,128)S(1)}, f32[8,8,8,1]{3,2,1,0:T(8,128)S(1)}) custom-call(s32[8]{0:T(128)S(1)} %dynamic_slice.27.lengths_ref, s32[1]{0:T(128)} %bitcast.base_ref, ...), custom_call_target="tpu_custom_call" | custom-call | flops 67108864 | bytes 16777216 | tf_op jit(solution)/shard_map/arrive_and_attend/pallas_call | solution.py:113
  178.7 0.7 pad_maximum_fusion.1
  179.4 0.5 copy.157
  179.8 0.5 copy.160
  180.6 0.7 collective-permute-done.6
  181.3 0.7 fusion.47
  182.7 1.0 slice.174
  183.6 0.2 multiply_add_fusion.4
  184.0 5.6 %collective-permute-done.7 = f32[260,128]{1,0:T(8,128)S(1)} collective-permute-done((f32[260,128]{1,0:T(8,128)S(1)}, f32[260,128]{1,0:T(8,128)S(1)}, u32[]{:S(2)}, u32[]{:S(2)}) %collective-permute-start.7) | collective-permute-done | bytes 133152 | tf_op jit(solution)/shard_map/ppermute | solution.py:255
  190.2 0.2 multiply_add_fusion.3
  190.4 3.2 %collective-permute-start.8 = (f32[260,128]{1,0:T(8,128)S(1)}, f32[260,128]{1,0:T(8,128)S(1)}, u32[]{:S(2)}, u32[]{:S(2)}) collective-permute-start(f32[260,128]{1,0:T(8,128)S(1)} %pad_maximum_fusion.5), channel_id=1, source_target_pairs={{0,4},{1,5},{2,6},{3,7},{4,0},{5,1},{6,2},{7,3},{8,12},{9,13},{10,... | collective-permute-start | bytes 399368 | tf_op jit(solution)/shard_map/ppermute | solution.py:255
  193.6 3.4 %collective-permute-done.8 = f32[260,128]{1,0:T(8,128)S(1)} collective-permute-done((f32[260,128]{1,0:T(8,128)S(1)}, f32[260,128]{1,0:T(8,128)S(1)}, u32[]{:S(2)}, u32[]{:S(2)}) %collective-permute-start.8) | collective-permute-done | bytes 133152 | tf_op jit(solution)/shard_map/ppermute | solution.py:255
  197.5 0.2 multiply_add_fusion.2
  197.9 6.0 %collective-permute-done.9 = f32[260,128]{1,0:T(8,128)S(1)} collective-permute-done((f32[260,128]{1,0:T(8,128)S(1)}, f32[260,128]{1,0:T(8,128)S(1)}, u32[]{:S(2)}, u32[]{:S(2)}) %collective-permute-start.9) | collective-permute-done | bytes 133152 | tf_op jit(solution)/shard_map/ppermute | solution.py:255
  204.4 0.2 multiply_add_fusion.1
  204.9 6.4 %collective-permute-done.10 = f32[260,128]{1,0:T(8,128)S(1)} collective-permute-done((f32[260,128]{1,0:T(8,128)S(1)}, f32[260,128]{1,0:T(8,128)S(1)}, u32[]{:S(2)}, u32[]{:S(2)}) %collective-permute-start.10) | collective-permute-done | bytes 133152 | tf_op jit(solution)/shard_map/ppermute | solution.py:255
  211.8 0.2 multiply_add_fusion
  212.1 0.3 fusion.21
  212.4 0.5 copy.168
  213.0 0.4 collective-permute-done.11
  214.2 0.5 copy.171
  215.2 0.2 copy.175
  215.6 0.4 fusion.3
  216.3 1.9 collective-permute-start.12
  218.3 1.9 collective-permute-done.14
  220.2 1.7 collective-permute-done.13
  221.9 1.0 collective-permute-done.12
  222.8 0.4 convolution_convert_fusion
  223.3 0.9 collective-permute-start.17
  224.2 2.6 %collective-permute-start.16 = (bf16[8,4,2048]{2,0,1:T(8,128)(2,1)S(1)}, bf16[8,4,2048]{2,0,1:T(8,128)(2,1)S(1)}, u32[]{:S(2)}, u32[]{:S(2)}) collective-permute-start(bf16[8,4,2048]{2,0,1:T(8,128)(2,1)S(1)} %get-tuple-element.59), channel_id=1, source_target_pairs={{0,64},{32,96},{64,0},{96,32},{1,65},{33,97},{65,1},{97,33},{2,66}... | collective-permute-start | bytes 393224 | tf_op jit(solution)/shard_map/ppermute | solution.py:188
  226.9 0.3 collective-permute-start.15
  227.2 4.7 %collective-permute-done.17 = bf16[8,4,2048]{2,0,1:T(8,128)(2,1)S(1)} collective-permute-done((bf16[8,4,2048]{2,0,1:T(8,128)(2,1)S(1)}, bf16[8,4,2048]{2,0,1:T(8,128)(2,1)S(1)}, u32[]{:S(2)}, u32[]{:S(2)}) %collective-permute-start.17) | collective-permute-done | bytes 131104 | tf_op jit(solution)/shard_map/ppermute | solution.py:188
  231.9 0.6 collective-permute-done.15
  232.7 0.8 copy.178
  (129 shorter events, 7.7 us)
Async XLA Ops:
  0.6 222.2 %copy-start = (bf16[512,2048]{1,0:T(8,128)(2,1)S(1)}, bf16[512,2048]{1,0:T(8,128)(2,1)}, u32[]{:S(2)}) copy-start(bf16[512,2048]{1,0:T(8,128)(2,1)} %param.16) | copy-start | bytes 6291460
  3.0 25.3 %collective-permute-start.2 = (bf16[8,4,2048]{2,0,1:T(8,128)(2,1)S(1)}, bf16[8,4,2048]{2,0,1:T(8,128)(2,1)S(1)}, u32[]{:S(2)}, u32[]{:S(2)}) collective-permute-start(bf16[8,4,2048]{2,0,1:T(8,128)(2,1)S(1)} %fusion.16), channel_id=1, source_target_pairs={{0,96},{32,0},{64,32},{96,64},{1,97},{33,1},{65,33},{97,65},{2,98}... | collective-permute-start | bytes 393224 | tf_op jit(solution)/shard_map/ppermute | solution.py:188
  5.8 22.4 %collective-permute-start.1 = (bf16[8,4,2048]{2,0,1:T(8,128)(2,1)S(1)}, bf16[8,4,2048]{2,0,1:T(8,128)(2,1)S(1)}, u32[]{:S(2)}, u32[]{:S(2)}) collective-permute-start(bf16[8,4,2048]{2,0,1:T(8,128)(2,1)S(1)} %fusion.16), channel_id=1, source_target_pairs={{0,64},{32,96},{64,0},{96,32},{1,65},{33,97},{65,1},{97,33},{2,66}... | collective-permute-start | bytes 393224 | tf_op jit(solution)/shard_map/ppermute | solution.py:188
  6.6 21.6 %collective-permute-start = (bf16[8,4,2048]{2,0,1:T(8,128)(2,1)S(1)}, bf16[8,4,2048]{2,0,1:T(8,128)(2,1)}, u32[]{:S(2)}, u32[]{:S(2)}) collective-permute-start(bf16[8,4,2048]{2,0,1:T(8,128)(2,1)S(1)} %fusion.16), channel_id=1, source_target_pairs={{0,32},{32,64},{64,96},{96,0},{1,33},{33,65},{65,97},{97,1},{2,34}... | collective-permute-start | bytes 393224 | tf_op jit(solution)/shard_map/ppermute | solution.py:188
  29.2 119.7 %all-to-all-start = ((bf16[128,1,2,16,1024]{4,3,2,1,0:T(8,128)(2,1)}), bf16[128,1,2,16,1024]{4,3,2,1,0:T(8,128)(2,1)}, u32[]{:S(2)}, u32[]{:S(2)}) async-start(bf16[128,1,2,16,1024]{4,3,2,1,0:T(8,128)(2,1)} %maximum_bitcast_fusion), calls=%async_computation | async-start | bytes 16777216 | tf_op jit(solution)/shard_map/all_to_all | solution.py:194
  46.7 5.3 %copy-start.2 = (bf16[2048,256]{1,0:T(8,128)(2,1)S(1)}, bf16[2048,256]{1,0:T(8,128)(2,1)}, u32[]{:S(2)}) copy-start(bf16[2048,256]{1,0:T(8,128)(2,1)} %param.15) | copy-start | bytes 3145732
  52.3 85.0 %collective-permute-start.5 = (bf16[8,4,1024]{2,0,1:T(8,128)(2,1)S(1)}, bf16[8,4,1024]{2,0,1:T(8,128)(2,1)S(1)}, u32[]{:S(2)}, u32[]{:S(2)}) collective-permute-start(bf16[8,4,1024]{2,0,1:T(8,128)(2,1)S(1)} %get-tuple-element.69), channel_id=1, source_target_pairs={{0,32},{32,64},{64,96},{96,0},{1,33},{33,65},{65,97},{97,1},{2,34}... | collective-permute-start | bytes 196616 | tf_op jit(solution)/shard_map/ppermute | solution.py:188
  53.9 93.9 %collective-permute-start.4 = (bf16[8,4,1024]{2,0,1:T(8,128)(2,1)S(1)}, bf16[8,4,1024]{2,0,1:T(8,128)(2,1)S(1)}, u32[]{:S(2)}, u32[]{:S(2)}) collective-permute-start(bf16[8,4,1024]{2,0,1:T(8,128)(2,1)S(1)} %get-tuple-element.70), channel_id=1, source_target_pairs={{0,64},{32,96},{64,0},{96,32},{1,65},{33,97},{65,1},{97,33},{2,66}... | collective-permute-start | bytes 196616 | tf_op jit(solution)/shard_map/ppermute | solution.py:188
  56.6 91.2 %collective-permute-start.3 = (bf16[8,4,1024]{2,0,1:T(8,128)(2,1)S(1)}, bf16[8,4,1024]{2,0,1:T(8,128)(2,1)S(1)}, u32[]{:S(2)}, u32[]{:S(2)}) collective-permute-start(bf16[8,4,1024]{2,0,1:T(8,128)(2,1)S(1)} %get-tuple-element.71), channel_id=1, source_target_pairs={{0,96},{32,0},{64,32},{96,64},{1,97},{33,1},{65,33},{97,65},{2,98}... | collective-permute-start | bytes 196616 | tf_op jit(solution)/shard_map/ppermute | solution.py:188
  179.4 1.9 collective-permute-start.6
  183.9 5.7 %collective-permute-start.7 = (f32[260,128]{1,0:T(8,128)S(1)}, f32[260,128]{1,0:T(8,128)S(1)}, u32[]{:S(2)}, u32[]{:S(2)}) collective-permute-start(f32[260,128]{1,0:T(8,128)S(1)} %pad_maximum_fusion.4), channel_id=1, source_target_pairs={{0,2},{1,3},{2,0},{3,1},{4,6},{5,7},{6,4},{7,5},{8,10},{9,11},{10,... | collective-permute-start | bytes 399368 | tf_op jit(solution)/shard_map/ppermute | solution.py:255
  190.4 6.6 %collective-permute-start.8 = (f32[260,128]{1,0:T(8,128)S(1)}, f32[260,128]{1,0:T(8,128)S(1)}, u32[]{:S(2)}, u32[]{:S(2)}) collective-permute-start(f32[260,128]{1,0:T(8,128)S(1)} %pad_maximum_fusion.5), channel_id=1, source_target_pairs={{0,4},{1,5},{2,6},{3,7},{4,0},{5,1},{6,2},{7,3},{8,12},{9,13},{10,... | collective-permute-start | bytes 399368 | tf_op jit(solution)/shard_map/ppermute | solution.py:255
  197.8 6.1 %collective-permute-start.9 = (f32[260,128]{1,0:T(8,128)S(1)}, f32[260,128]{1,0:T(8,128)S(1)}, u32[]{:S(2)}, u32[]{:S(2)}) collective-permute-start(f32[260,128]{1,0:T(8,128)S(1)} %pad_maximum_fusion.6), channel_id=1, source_target_pairs={{0,8},{1,9},{2,10},{3,11},{4,12},{5,13},{6,14},{7,15},{8,0},{9,1},... | collective-permute-start | bytes 399368 | tf_op jit(solution)/shard_map/ppermute | solution.py:255
  204.7 6.6 %collective-permute-start.10 = (f32[260,128]{1,0:T(8,128)S(1)}, f32[260,128]{1,0:T(8,128)S(1)}, u32[]{:S(2)}, u32[]{:S(2)}) collective-permute-start(f32[260,128]{1,0:T(8,128)S(1)} %pad_maximum_fusion.7), channel_id=1, source_target_pairs={{0,16},{1,17},{2,18},{3,19},{4,20},{5,21},{6,22},{7,23},{8,24},{9,... | collective-permute-start | bytes 399368 | tf_op jit(solution)/shard_map/ppermute | solution.py:255
  212.0 1.4 collective-permute-start.11
  215.9 16.6 %copy-start.1 = (bf16[8,4,2048]{2,1,0:T(4,128)(2,1)S(1)}, bf16[8,4,2048]{2,1,0:T(4,128)(2,1)}, u32[]{:S(2)}) copy-start(bf16[8,4,2048]{2,1,0:T(4,128)(2,1)} %param.11) | copy-start | bytes 393220
  216.2 4.0 %collective-permute-start.14 = (bf16[8,4,512]{2,0,1:T(8,128)(2,1)S(1)}, bf16[8,4,512]{2,0,1:T(8,128)(2,1)S(1)}, u32[]{:S(2)}, u32[]{:S(2)}) collective-permute-start(bf16[8,4,512]{2,0,1:T(8,128)(2,1)S(1)} %get-tuple-element.89), channel_id=1, source_target_pairs={{0,96},{32,0},{64,32},{96,64},{1,97},{33,1},{65,33},{97,65},{2,98}... | collective-permute-start | bytes 98312 | tf_op jit(solution)/shard_map/ppermute | solution.py:188
  216.3 5.6 %collective-permute-start.13 = (bf16[8,4,512]{2,0,1:T(8,128)(2,1)S(1)}, bf16[8,4,512]{2,0,1:T(8,128)(2,1)S(1)}, u32[]{:S(2)}, u32[]{:S(2)}) collective-permute-start(bf16[8,4,512]{2,0,1:T(8,128)(2,1)S(1)} %get-tuple-element.90), channel_id=1, source_target_pairs={{0,64},{32,96},{64,0},{96,32},{1,65},{33,97},{65,1},{97,33},{2,66}... | collective-permute-start | bytes 98312 | tf_op jit(solution)/shard_map/ppermute | solution.py:188
  216.3 6.5 %collective-permute-start.12 = (bf16[8,4,512]{2,0,1:T(8,128)(2,1)S(1)}, bf16[8,4,512]{2,0,1:T(8,128)(2,1)S(1)}, u32[]{:S(2)}, u32[]{:S(2)}) collective-permute-start(bf16[8,4,512]{2,0,1:T(8,128)(2,1)S(1)} %get-tuple-element.91), channel_id=1, source_target_pairs={{0,32},{32,64},{64,96},{96,0},{1,33},{33,65},{65,97},{97,1},{2,34}... | collective-permute-start | bytes 98312 | tf_op jit(solution)/shard_map/ppermute | solution.py:188
  223.3 8.6 %collective-permute-start.17 = (bf16[8,4,2048]{2,0,1:T(8,128)(2,1)S(1)}, bf16[8,4,2048]{2,0,1:T(8,128)(2,1)S(1)}, u32[]{:S(2)}, u32[]{:S(2)}) collective-permute-start(bf16[8,4,2048]{2,0,1:T(8,128)(2,1)S(1)} %get-tuple-element.58), channel_id=1, source_target_pairs={{0,32},{32,64},{64,96},{96,0},{1,33},{33,65},{65,97},{97,1},{2,34}... | collective-permute-start | bytes 393224 | tf_op jit(solution)/shard_map/ppermute | solution.py:188
  224.2 7.6 %collective-permute-start.16 = (bf16[8,4,2048]{2,0,1:T(8,128)(2,1)S(1)}, bf16[8,4,2048]{2,0,1:T(8,128)(2,1)S(1)}, u32[]{:S(2)}, u32[]{:S(2)}) collective-permute-start(bf16[8,4,2048]{2,0,1:T(8,128)(2,1)S(1)} %get-tuple-element.59), channel_id=1, source_target_pairs={{0,64},{32,96},{64,0},{96,32},{1,65},{33,97},{65,1},{97,33},{2,66}... | collective-permute-start | bytes 393224 | tf_op jit(solution)/shard_map/ppermute | solution.py:188
  226.9 5.6 %collective-permute-start.15 = (bf16[8,4,2048]{2,0,1:T(8,128)(2,1)S(1)}, bf16[8,4,2048]{2,0,1:T(8,128)(2,1)S(1)}, u32[]{:S(2)}, u32[]{:S(2)}) collective-permute-start(bf16[8,4,2048]{2,0,1:T(8,128)(2,1)S(1)} %get-tuple-element.57), channel_id=1, source_target_pairs={{0,96},{32,0},{64,32},{96,64},{1,97},{33,1},{65,33},{97,65},{2,98}... | collective-permute-start | bytes 393224 | tf_op jit(solution)/shard_map/ppermute | solution.py:188

commit v11 on v10

--- a/solution.py
+++ b/solution.py
@@ -37,27 +37,46 @@
 
 
 def _arrive_kernel(
-    lengths_ref, base_ref, arrived_ref, q_ref, fk_ref, fv_ref,
-    keys_out_ref, values_out_ref, acc_ref, peak_ref, mass_ref, *, scale
+    lengths_ref, base_ref, q_ref, fk_ref, fv_ref, keys_in_ref, values_in_ref,
+    keys_out_ref, values_out_ref, acc_ref, peak_ref, mass_ref,
+    buf, tiles, in_sem, tile_sem, *, scale
 ):
     r = pl.program_id(0)
-    pages = arrived_ref.shape[1]
-    page_len = arrived_ref.shape[3]
-    positions = pages * page_len
+    n = pl.num_programs(0)
+    slot = r % 2
+    positions = buf.shape[2]
+    page_len = tiles.shape[2]
+    pages = positions // page_len
     heads = q_ref.shape[1]
     head_dim = q_ref.shape[3]
     new_count = fk_ref.shape[1]
+    ins = (keys_in_ref, values_in_ref)
     outs = (keys_out_ref, values_out_ref)
-    keys_out_ref[0] = arrived_ref[0, :, 0]
-    values_out_ref[0] = arrived_ref[0, :, 1]
+
+    def block_copy(req, s, half):
+        return pltpu.make_async_copy(ins[half].at[req], buf.at[s, half], in_sem.at[s, half])
+
+    @pl.when(r == 0)
+    def _():
+        for half in range(2):
+            block_copy(0, 0, half).start()
+
+    for half in range(2):
+        block_copy(r, slot, half).wait()
+
+    @pl.when(r + 1 < n)
+    def _():
+        for half in range(2):
+            block_copy(r + 1, 1 - slot, half).start()
+
     length = lengths_ref[r]
     base = base_ref[0]
     spots = base + lax.broadcasted_iota(jnp.int32, (1, positions), 1)
     live = spots < length
     for kh in range(heads):
         cols = pl.ds(kh * head_dim, head_dim)
-        keys_h = arrived_ref[0, :, 0, :, cols].reshape(positions, head_dim)
-        values_h = arrived_ref[0, :, 1, :, cols].reshape(positions, head_dim)
+        keys_h = buf[slot, 0, :, cols]
+        values_h = buf[slot, 1, :, cols]
         query_h = q_ref[0, kh]
         scores = lax.dot_general(
             query_h, keys_h, (((1,), (1,)), ((), ())), preferred_element_type=jnp.float32
@@ -74,15 +93,24 @@
     page0 = first // page_len
     row_ids = lax.broadcasted_iota(jnp.int32, (page_len, 1), 0)
     fresh = (fk_ref[0], fv_ref[0])
-    for page in (page0, page0 + 1):
+    for j, page in enumerate((page0, page0 + 1)):
         @pl.when(jnp.logical_and(page >= 0, page < pages))
         def _():
+            rows = pl.ds(pl.multiple_of(page * page_len, page_len), page_len)
+            copies = []
             for half in range(2):
-                block = outs[half][0, page]
+                block = buf[slot, half, rows, :]
                 for t in range(new_count):
                     hit = row_ids == first + t - page * page_len
                     block = jnp.where(hit, fresh[half][t : t + 1, :], block)
-                outs[half][0, page] = block
+                tiles[j, half] = block
+                copy = pltpu.make_async_copy(
+                    tiles.at[j, half], outs[half].at[r, rows], tile_sem.at[j, half]
+                )
+                copy.start()
+                copies.append(copy)
+            for copy in copies:
+                copy.wait()
 
 
 def arrive_and_attend(arrival_src, lengths, base, incoming, queries, fresh_k, fresh_v, scale):
@@ -91,48 +119,52 @@
     page_len = incoming.shape[2]
     pages = arrival_src.shape[0] // local_reqs
     positions = pages * page_len
-    arrived = incoming[arrival_src].reshape(local_reqs, pages, 2, page_len, kv_width)
+    cache_k = incoming[arrival_src, 0].reshape(local_reqs, positions, kv_width)
+    cache_v = incoming[arrival_src, 1].reshape(local_reqs, positions, kv_width)
     grid_spec = pltpu.PrefetchScalarGridSpec(
         num_scalar_prefetch=2,
         grid=(local_reqs,),
         in_specs=[
-            pl.BlockSpec((1, pages, 2, page_len, kv_width), lambda r, *_: (r, 0, 0, 0, 0)),
             pl.BlockSpec((1, heads, rows, head_dim), lambda r, *_: (r, 0, 0, 0)),
             pl.BlockSpec((1, new_count, kv_width), lambda r, *_: (r, 0, 0)),
             pl.BlockSpec((1, new_count, kv_width), lambda r, *_: (r, 0, 0)),
+            pl.BlockSpec(memory_space=pl.ANY),
+            pl.BlockSpec(memory_space=pl.ANY),
         ],
         out_specs=[
-            pl.BlockSpec((1, pages, page_len, kv_width), lambda r, *_: (r, 0, 0, 0)),
-            pl.BlockSpec((1, pages, page_len, kv_width), lambda r, *_: (r, 0, 0, 0)),
+            pl.BlockSpec(memory_space=pl.ANY),
+            pl.BlockSpec(memory_space=pl.ANY),
             pl.BlockSpec((1, heads, rows, head_dim), lambda r, *_: (r, 0, 0, 0)),
             pl.BlockSpec((1, heads, rows, 1), lambda r, *_: (r, 0, 0, 0)),
             pl.BlockSpec((1, heads, rows, 1), lambda r, *_: (r, 0, 0, 0)),
         ],
+        scratch_shapes=[
+            pltpu.VMEM((2, 2, positions, kv_width), jnp.bfloat16),
+            pltpu.VMEM((2, 2, page_len, kv_width), jnp.bfloat16),
+            pltpu.SemaphoreType.DMA((2, 2)),
+            pltpu.SemaphoreType.DMA((2, 2)),
+        ],
     )
     cache_bytes = 2 * local_reqs * positions * kv_width * 2
-    keys_out, values_out, acc, peak, mass = pl.pallas_call(
+    return pl.pallas_call(
         functools.partial(_arrive_kernel, scale=scale),
         out_shape=[
-            jax.ShapeDtypeStruct((local_reqs, pages, page_len, kv_width), jnp.bfloat16),
-            jax.ShapeDtypeStruct((local_reqs, pages, page_len, kv_width), jnp.bfloat16),
+            jax.ShapeDtypeStruct((local_reqs, positions, kv_width), jnp.bfloat16),
+            jax.ShapeDtypeStruct((local_reqs, positions, kv_width), jnp.bfloat16),
             jax.ShapeDtypeStruct((local_reqs, heads, rows, head_dim), jnp.float32),
             jax.ShapeDtypeStruct((local_reqs, heads, rows, 1), jnp.float32),
             jax.ShapeDtypeStruct((local_reqs, heads, rows, 1), jnp.float32),
         ],
         grid_spec=grid_spec,
-        compiler_params=pltpu.CompilerParams(
-            dimension_semantics=("arbitrary",), vmem_limit_bytes=48 * 1024 * 1024
-        ),
+        input_output_aliases={5: 0, 6: 1},
+        compiler_params=pltpu.CompilerParams(dimension_semantics=("arbitrary",)),
         cost_estimate=pl.CostEstimate(
             flops=4 * local_reqs * heads * rows * positions * head_dim,
             transcendentals=local_reqs * heads * rows * positions,
-            bytes_accessed=2 * cache_bytes,
+            bytes_accessed=cache_bytes,
         ),
         name="arrive_and_attend",
-    )(lengths, base, arrived, queries, fresh_k, fresh_v)
-    keys_out = keys_out.reshape(local_reqs, positions, kv_width)
-    values_out = values_out.reshape(local_reqs, positions, kv_width)
-    return keys_out, values_out, acc, peak, mass
+    )(lengths, base, queries, fresh_k, fresh_v, cache_k, cache_v)
 
 
 def shards(

time: 234 us -> 242 us (1.034)
  local copies, waits for them, and re-layouts: 39.2 us -> 44.3 us
  other arithmetic: 16 us -> 19.1 us
    gather x1 -> x2, local copies, waits for them, and re-layouts: 9.96 us -> 12.5 us  [the longest x1 6.26 us: arrive_and_attend(): cache_k = incoming[arrival_src, 0].reshape(local_reqs, positions, kv_width)]
  transfers between devices with their start and end apart: 19 -> 19, of which waited for: 13 -> 12; matrix products, arithmetic and copies ran while one was open for 16% -> 17% of each run, Pallas kernels for 0% -> 0%
where the time goes in v11:
time: 242 us; the launch traced here: 241 us
  waiting for transfers between devices  120 us (50%)
  local copies, waits for them, and re-layouts  44.3 us (18%)
  starting transfers between devices  31.1 us (13%)
  Pallas kernels  19.4 us (8%)
  other arithmetic  19.1 us (8%)
  matrix products  5.53 us (2%)
    ppermute x12, waiting for transfers between devices, shift(): return lax.ppermute(value, 'req', pairs)  99.1 us
    ppermute x5, waiting for transfers between devices, merge(): other = lax.ppermute(pack(total, peak, mass), 'seq', pairs)  20.5 us
    pallas_call x1, Pallas kernels, arrive_and_attend(): pl.pallas_call(functools.partial(_arrive_kernel, scale=scale), out_shape=...  19.4 us
    ppermute x12, starting transfers between devices, shift(): return lax.ppermute(value, 'req', pairs)  16.2 us
    gather x2, local copies, waits for them, and re-layouts, shards(): outgoing = jnp.stack([pool_keys[send_pick], pool_values[send_pick]], axis=1)  10 us
    all_to_all x1, starting transfers between devices, shards(): lax.all_to_all(outgoing, ('req', 'seq'), split_axis=0, concat_axis=0, til...  10 us
    reshape x1, other arithmetic, shards(): outgoing = outgoing.reshape(devices, per_peer, 2, page_len, kv_width)  7.53 us
    gather x1, local copies, waits for them, and re-layouts, arrive_and_attend(): cache_k = incoming[arrival_src, 0].reshape(local_reqs, positions, kv_width)  6.26 us
  transfers between devices with their start and end apart: 19, of which 12 were waited for; matrix products, arithmetic and copies ran while one was open for 17% of the time, Pallas kernels for 0%

profile of v11, /device:TPU:32, one launch (start us, length us, event | category | flops | bytes accessed | tf_op | source)
XLA Modules:
  0.0 241.0 jit_solution(9054944317572600543)
XLA Ops:
  0.6 1.3 fusion.14
  1.9 1.0 fusion.16
  3.0 2.8 %collective-permute-start.2 = (bf16[8,4,2048]{2,0,1:T(8,128)(2,1)S(1)}, bf16[8,4,2048]{2,0,1:T(8,128)(2,1)S(1)}, u32[]{:S(2)}, u32[]{:S(2)}) collective-permute-start(bf16[8,4,2048]{2,0,1:T(8,128)(2,1)S(1)} %fusion.16), channel_id=1, source_target_pairs={{0,96},{32,0},{64,32},{96,64},{1,97},{33,1},{65,33},{97,65},{2,98}... | collective-permute-start | bytes 393224 | tf_op jit(solution)/shard_map/ppermute | solution.py:220
  5.8 0.8 collective-permute-start.1
  6.6 0.9 collective-permute-start
  7.5 0.8 select_reduce_fusion.1
  8.3 1.5 gather_fusion
  10.0 0.6 fusion.7
  10.7 5.0 %gather_fusion.2 = bf16[128,16,1024]{2,1,0:T(8,128)(2,1)} fusion(bf16[128,16,1024]{2,1,0:T(8,128)(2,1)} %param.18, s32[1024]{0:T(1024)S(1)} %pad_clamp_fusion.2), kind=kCustom, calls=%fused_computation.2 | custom fusion | bytes 8389120 | tf_op jit(solution)/shard_map/gather | solution.py:223
  15.7 5.0 %gather_fusion.1 = bf16[128,16,1024]{2,1,0:T(8,128)(2,1)} fusion(bf16[128,16,1024]{2,1,0:T(8,128)(2,1)} %param.17, s32[1024]{0:T(1024)S(1)} %pad_clamp_fusion.2), kind=kCustom, calls=%fused_computation.1 | custom fusion | bytes 8389120 | tf_op jit(solution)/shard_map/gather | solution.py:223
  20.7 7.5 %maximum_bitcast_fusion = bf16[128,1,2,16,1024]{4,3,2,1,0:T(8,128)(2,1)} fusion(bf16[128,1,16,1024]{3,2,1,0:T(8,128)(2,1)} %bitcast.164, bf16[128,1,16,1024]{3,2,1,0:T(8,128)(2,1)} %bitcast.165), kind=kLoop, calls=%fused_computation.7 | loop fusion | flops 4194304 | bytes 16777216 | tf_op jit(solution)/shard_map/reshape | solution.py:224
  28.3 0.9 pad_maximum_fusion
  29.2 10.0 %all-to-all-start = ((bf16[128,1,2,16,1024]{4,3,2,1,0:T(8,128)(2,1)}), bf16[128,1,2,16,1024]{4,3,2,1,0:T(8,128)(2,1)}, u32[]{:S(2)}, u32[]{:S(2)}) async-start(bf16[128,1,2,16,1024]{4,3,2,1,0:T(8,128)(2,1)} %maximum_bitcast_fusion), calls=%async_computation | async-start | bytes 16777216 | tf_op jit(solution)/shard_map/all_to_all | solution.py:226
  39.2 2.3 copy.188
  41.6 0.6 gather_fusion.3
  42.4 3.9 %copy.187 = bf16[512,2048]{1,0:T(8,128)(2,1)} copy(bf16[512,2048]{0,1:T(8,128)(2,1)} %bitcast.169) | data formatting | bytes 4194304 | tf_op jit(solution)/shard_map/dot_general | solution.py:232
  46.3 0.6 dynamic_slice.27.lengths_ref
  47.5 0.3 multiply_cosine_fusion
  47.8 1.7 fusion.8
  49.7 2.4 %fusion.10 = f32[32,4,4,128]{3,0,2,1:T(8,128)S(1)} fusion(bf16[4,128,2048,1]{2,1,0,3:T(8,128)(2,1)} %bitcast.166, bf16[32,4,2048]{2,0,1:T(8,128)(2,1)S(1)} %pad_maximum_fusion), kind=kOutput, calls=%fused_computation.27 | convolution fusion | flops 268435456 | bytes 2883584 | tf_op jit(solution)/shard_map/dot_general | solution.py:232
  52.4 0.3 convolution_convert_fusion.1
  52.8 1.5 collective-permute-start.5
  54.4 2.7 %collective-permute-start.4 = (bf16[8,4,1024]{2,0,1:T(8,128)(2,1)S(1)}, bf16[8,4,1024]{2,0,1:T(8,128)(2,1)S(1)}, u32[]{:S(2)}, u32[]{:S(2)}) collective-permute-start(bf16[8,4,1024]{2,0,1:T(8,128)(2,1)S(1)} %get-tuple-element.70), channel_id=1, source_target_pairs={{0,64},{32,96},{64,0},{96,32},{1,65},{33,97},{65,1},{97,33},{2,66}... | collective-permute-start | bytes 196616 | tf_op jit(solution)/shard_map/ppermute | solution.py:220
  57.1 1.4 collective-permute-start.3
  58.5 78.9 %collective-permute-done.5 = bf16[8,4,1024]{2,0,1:T(8,128)(2,1)S(1)} collective-permute-done((bf16[8,4,1024]{2,0,1:T(8,128)(2,1)S(1)}, bf16[8,4,1024]{2,0,1:T(8,128)(2,1)S(1)}, u32[]{:S(2)}, u32[]{:S(2)}) %collective-permute-start.5) | collective-permute-done | bytes 65568 | tf_op jit(solution)/shard_map/ppermute | solution.py:220
  137.4 10.4 %collective-permute-done.4 = bf16[8,4,1024]{2,0,1:T(8,128)(2,1)S(1)} collective-permute-done((bf16[8,4,1024]{2,0,1:T(8,128)(2,1)S(1)}, bf16[8,4,1024]{2,0,1:T(8,128)(2,1)S(1)}, u32[]{:S(2)}, u32[]{:S(2)}) %collective-permute-start.4) | collective-permute-done | bytes 65568 | tf_op jit(solution)/shard_map/ppermute | solution.py:220
  147.8 0.6 gather_fusion.4
  148.8 0.7 copy.155
  149.5 0.6 reshape_reshape.15.fk_ref
  150.2 0.6 reshape_reshape.16.fv_ref
  150.8 6.3 %gather_fusion.5 = bf16[128,16,1024]{2,1,0:T(8,128)(2,1)} fusion(bf16[128,2,16,1024]{3,2,1,0:T(8,128)(2,1)} %bitcast.27, s32[128]{0:T(128)S(1)} %get-tuple-element.102), kind=kCustom, calls=%fused_computation.5 | custom fusion | bytes 8389632 | tf_op jit(solution)/shard_map/gather | solution.py:122
  157.1 6.3 %gather_fusion.6 = bf16[128,16,1024]{2,1,0:T(8,128)(2,1)} fusion(bf16[128,2,16,1024]{3,2,1,0:T(8,128)(2,1)} %bitcast.27, s32[128]{0:T(128)S(1)} %get-tuple-element.101), kind=kCustom, calls=%fused_computation.6 | custom fusion | bytes 8389632 | tf_op jit(solution)/shard_map/gather | solution.py:123
  163.3 19.4 %arrive_and_attend.1 = (bf16[8,256,1024]{2,1,0:T(8,128)(2,1)}, bf16[8,256,1024]{2,1,0:T(8,128)(2,1)}, f32[8,8,8,128]{3,2,1,0:T(8,128)}, f32[8,8,8,1]{3,2,1,0:T(8,128)}, f32[8,8,8,1]{3,2,1,0:T(8,128)}) custom-call(s32[8]{0:T(128)} %dynamic_slice.27.lengths_ref, s32[1]{0:T(128)} %bitcast.base_ref, ...), custom_call_target="tpu_custom_call", output_to_operand_aliasing={{0}: (5, {}), {1}: (6, {})} | custom-call | flops 67108864 | bytes 8388608 | tf_op jit(solution)/shard_map/arrive_and_attend/pallas_call | solution.py:149
  182.8 1.1 reduce.3
  183.9 1.1 reduce.2
  185.1 1.0 pad_maximum_fusion.1
  186.1 0.9 collective-permute-start.6
  187.0 1.4 copy.159
  188.4 1.4 copy.162
  190.8 1.1 multiply_add_fusion.4
  192.0 0.3 collective-permute-start.7
  192.2 5.5 %collective-permute-done.7 = f32[260,128]{1,0:T(8,128)S(1)} collective-permute-done((f32[260,128]{1,0:T(8,128)S(1)}, f32[260,128]{1,0:T(8,128)S(1)}, u32[]{:S(2)}, u32[]{:S(2)}) %collective-permute-start.7) | collective-permute-done | bytes 133152 | tf_op jit(solution)/shard_map/ppermute | solution.py:287
  198.6 3.5 %collective-permute-start.8 = (f32[260,128]{1,0:T(8,128)S(1)}, f32[260,128]{1,0:T(8,128)S(1)}, u32[]{:S(2)}, u32[]{:S(2)}) collective-permute-start(f32[260,128]{1,0:T(8,128)S(1)} %pad_maximum_fusion.5), channel_id=1, source_target_pairs={{0,4},{1,5},{2,6},{3,7},{4,0},{5,1},{6,2},{7,3},{8,12},{9,13},{10,... | collective-permute-start | bytes 399368 | tf_op jit(solution)/shard_map/ppermute | solution.py:287
  202.0 3.4 %collective-permute-done.8 = f32[260,128]{1,0:T(8,128)S(1)} collective-permute-done((f32[260,128]{1,0:T(8,128)S(1)}, f32[260,128]{1,0:T(8,128)S(1)}, u32[]{:S(2)}, u32[]{:S(2)}) %collective-permute-start.8) | collective-permute-done | bytes 133152 | tf_op jit(solution)/shard_map/ppermute | solution.py:287
  206.3 5.2 %collective-permute-done.9 = f32[260,128]{1,0:T(8,128)S(1)} collective-permute-done((f32[260,128]{1,0:T(8,128)S(1)}, f32[260,128]{1,0:T(8,128)S(1)}, u32[]{:S(2)}, u32[]{:S(2)}) %collective-permute-start.9) | collective-permute-done | bytes 133152 | tf_op jit(solution)/shard_map/ppermute | solution.py:287
  212.1 0.2 multiply_add_fusion.1
  212.5 6.4 %collective-permute-done.10 = f32[260,128]{1,0:T(8,128)S(1)} collective-permute-done((f32[260,128]{1,0:T(8,128)S(1)}, f32[260,128]{1,0:T(8,128)S(1)}, u32[]{:S(2)}, u32[]{:S(2)}) %collective-permute-start.10) | collective-permute-done | bytes 133152 | tf_op jit(solution)/shard_map/ppermute | solution.py:287
  219.7 0.3 fusion.21
  220.1 0.5 copy.170
  220.6 0.4 collective-permute-done.11
  221.8 0.5 copy.173
  223.2 0.4 fusion.3
  223.9 1.4 collective-permute-start.13
  225.3 0.6 collective-permute-start.12
  225.9 1.9 collective-permute-done.14
  227.8 1.7 collective-permute-done.13
  229.5 1.0 collective-permute-done.12
  230.5 0.4 convolution_convert_fusion
  231.0 0.9 collective-permute-start.17
  231.9 2.6 %collective-permute-start.16 = (bf16[8,4,2048]{2,0,1:T(8,128)(2,1)S(1)}, bf16[8,4,2048]{2,0,1:T(8,128)(2,1)S(1)}, u32[]{:S(2)}, u32[]{:S(2)}) collective-permute-start(bf16[8,4,2048]{2,0,1:T(8,128)(2,1)S(1)} %get-tuple-element.59), channel_id=1, source_target_pairs={{0,64},{32,96},{64,0},{96,32},{1,65},{33,97},{65,1},{97,33},{2,66}... | collective-permute-start | bytes 393224 | tf_op jit(solution)/shard_map/ppermute | solution.py:220
  234.5 0.3 collective-permute-start.15
  234.8 4.7 %collective-permute-done.17 = bf16[8,4,2048]{2,0,1:T(8,128)(2,1)S(1)} collective-permute-done((bf16[8,4,2048]{2,0,1:T(8,128)(2,1)S(1)}, bf16[8,4,2048]{2,0,1:T(8,128)(2,1)S(1)}, u32[]{:S(2)}, u32[]{:S(2)}) %collective-permute-start.17) | collective-permute-done | bytes 131104 | tf_op jit(solution)/shard_map/ppermute | solution.py:220
  239.5 0.6 collective-permute-done.15
  240.3 0.8 copy.180
  (129 shorter events, 8.5 us)
Async XLA Ops:
  0.6 229.8 %copy-start = (bf16[512,2048]{1,0:T(8,128)(2,1)S(1)}, bf16[512,2048]{1,0:T(8,128)(2,1)}, u32[]{:S(2)}) copy-start(bf16[512,2048]{1,0:T(8,128)(2,1)} %param.16) | copy-start | bytes 6291460
  3.0 25.3 %collective-permute-start.2 = (bf16[8,4,2048]{2,0,1:T(8,128)(2,1)S(1)}, bf16[8,4,2048]{2,0,1:T(8,128)(2,1)S(1)}, u32[]{:S(2)}, u32[]{:S(2)}) collective-permute-start(bf16[8,4,2048]{2,0,1:T(8,128)(2,1)S(1)} %fusion.16), channel_id=1, source_target_pairs={{0,96},{32,0},{64,32},{96,64},{1,97},{33,1},{65,33},{97,65},{2,98}... | collective-permute-start | bytes 393224 | tf_op jit(solution)/shard_map/ppermute | solution.py:220
  5.8 22.5 %collective-permute-start.1 = (bf16[8,4,2048]{2,0,1:T(8,128)(2,1)S(1)}, bf16[8,4,2048]{2,0,1:T(8,128)(2,1)S(1)}, u32[]{:S(2)}, u32[]{:S(2)}) collective-permute-start(bf16[8,4,2048]{2,0,1:T(8,128)(2,1)S(1)} %fusion.16), channel_id=1, source_target_pairs={{0,64},{32,96},{64,0},{96,32},{1,65},{33,97},{65,1},{97,33},{2,66}... | collective-permute-start | bytes 393224 | tf_op jit(solution)/shard_map/ppermute | solution.py:220
  6.6 21.7 %collective-permute-start = (bf16[8,4,2048]{2,0,1:T(8,128)(2,1)S(1)}, bf16[8,4,2048]{2,0,1:T(8,128)(2,1)}, u32[]{:S(2)}, u32[]{:S(2)}) collective-permute-start(bf16[8,4,2048]{2,0,1:T(8,128)(2,1)S(1)} %fusion.16), channel_id=1, source_target_pairs={{0,32},{32,64},{64,96},{96,0},{1,33},{33,65},{65,97},{97,1},{2,34}... | collective-permute-start | bytes 393224 | tf_op jit(solution)/shard_map/ppermute | solution.py:220
  29.2 121.6 %all-to-all-start = ((bf16[128,1,2,16,1024]{4,3,2,1,0:T(8,128)(2,1)}), bf16[128,1,2,16,1024]{4,3,2,1,0:T(8,128)(2,1)}, u32[]{:S(2)}, u32[]{:S(2)}) async-start(bf16[128,1,2,16,1024]{4,3,2,1,0:T(8,128)(2,1)} %maximum_bitcast_fusion), calls=%async_computation | async-start | bytes 16777216 | tf_op jit(solution)/shard_map/all_to_all | solution.py:226
  47.2 5.2 %copy-start.2 = (bf16[2048,256]{1,0:T(8,128)(2,1)S(1)}, bf16[2048,256]{1,0:T(8,128)(2,1)}, u32[]{:S(2)}) copy-start(bf16[2048,256]{1,0:T(8,128)(2,1)} %param.15) | copy-start | bytes 3145732
  52.8 84.6 %collective-permute-start.5 = (bf16[8,4,1024]{2,0,1:T(8,128)(2,1)S(1)}, bf16[8,4,1024]{2,0,1:T(8,128)(2,1)S(1)}, u32[]{:S(2)}, u32[]{:S(2)}) collective-permute-start(bf16[8,4,1024]{2,0,1:T(8,128)(2,1)S(1)} %get-tuple-element.69), channel_id=1, source_target_pairs={{0,32},{32,64},{64,96},{96,0},{1,33},{33,65},{65,97},{97,1},{2,34}... | collective-permute-start | bytes 196616 | tf_op jit(solution)/shard_map/ppermute | solution.py:220
  54.4 93.4 %collective-permute-start.4 = (bf16[8,4,1024]{2,0,1:T(8,128)(2,1)S(1)}, bf16[8,4,1024]{2,0,1:T(8,128)(2,1)S(1)}, u32[]{:S(2)}, u32[]{:S(2)}) collective-permute-start(bf16[8,4,1024]{2,0,1:T(8,128)(2,1)S(1)} %get-tuple-element.70), channel_id=1, source_target_pairs={{0,64},{32,96},{64,0},{96,32},{1,65},{33,97},{65,1},{97,33},{2,66}... | collective-permute-start | bytes 196616 | tf_op jit(solution)/shard_map/ppermute | solution.py:220
  57.1 90.7 %collective-permute-start.3 = (bf16[8,4,1024]{2,0,1:T(8,128)(2,1)S(1)}, bf16[8,4,1024]{2,0,1:T(8,128)(2,1)S(1)}, u32[]{:S(2)}, u32[]{:S(2)}) collective-permute-start(bf16[8,4,1024]{2,0,1:T(8,128)(2,1)S(1)} %get-tuple-element.71), channel_id=1, source_target_pairs={{0,96},{32,0},{64,32},{96,64},{1,97},{33,1},{65,33},{97,65},{2,98}... | collective-permute-start | bytes 196616 | tf_op jit(solution)/shard_map/ppermute | solution.py:220
  186.1 4.0 %collective-permute-start.6 = (f32[520,128]{1,0:T(8,128)S(1)}, f32[520,128]{1,0:T(8,128)S(1)}, u32[]{:S(2)}, u32[]{:S(2)}) collective-permute-start(f32[520,128]{1,0:T(8,128)S(1)} %pad_maximum_fusion.1), channel_id=1, source_target_pairs={{0,1},{1,0},{2,3},{3,2},{4,5},{5,4},{6,7},{7,6},{8,9},{9,8},{10,11... | collective-permute-start | bytes 798728 | tf_op jit(solution)/shard_map/ppermute | solution.py:287
  192.0 5.8 %collective-permute-start.7 = (f32[260,128]{1,0:T(8,128)S(1)}, f32[260,128]{1,0:T(8,128)S(1)}, u32[]{:S(2)}, u32[]{:S(2)}) collective-permute-start(f32[260,128]{1,0:T(8,128)S(1)} %pad_maximum_fusion.4), channel_id=1, source_target_pairs={{0,2},{1,3},{2,0},{3,1},{4,6},{5,7},{6,4},{7,5},{8,10},{9,11},{10,... | collective-permute-start | bytes 399368 | tf_op jit(solution)/shard_map/ppermute | solution.py:287
  198.6 6.8 %collective-permute-start.8 = (f32[260,128]{1,0:T(8,128)S(1)}, f32[260,128]{1,0:T(8,128)S(1)}, u32[]{:S(2)}, u32[]{:S(2)}) collective-permute-start(f32[260,128]{1,0:T(8,128)S(1)} %pad_maximum_fusion.5), channel_id=1, source_target_pairs={{0,4},{1,5},{2,6},{3,7},{4,0},{5,1},{6,2},{7,3},{8,12},{9,13},{10,... | collective-permute-start | bytes 399368 | tf_op jit(solution)/shard_map/ppermute | solution.py:287
  206.2 5.3 %collective-permute-start.9 = (f32[260,128]{1,0:T(8,128)S(1)}, f32[260,128]{1,0:T(8,128)S(1)}, u32[]{:S(2)}, u32[]{:S(2)}) collective-permute-start(f32[260,128]{1,0:T(8,128)S(1)} %pad_maximum_fusion.6), channel_id=1, source_target_pairs={{0,8},{1,9},{2,10},{3,11},{4,12},{5,13},{6,14},{7,15},{8,0},{9,1},... | collective-permute-start | bytes 399368 | tf_op jit(solution)/shard_map/ppermute | solution.py:287
  212.3 6.6 %collective-permute-start.10 = (f32[260,128]{1,0:T(8,128)S(1)}, f32[260,128]{1,0:T(8,128)S(1)}, u32[]{:S(2)}, u32[]{:S(2)}) collective-permute-start(f32[260,128]{1,0:T(8,128)S(1)} %pad_maximum_fusion.7), channel_id=1, source_target_pairs={{0,16},{1,17},{2,18},{3,19},{4,20},{5,21},{6,22},{7,23},{8,24},{9,... | collective-permute-start | bytes 399368 | tf_op jit(solution)/shard_map/ppermute | solution.py:287
  219.7 1.4 collective-permute-start.11
  223.6 16.6 %copy-start.1 = (bf16[8,4,2048]{2,1,0:T(4,128)(2,1)S(1)}, bf16[8,4,2048]{2,1,0:T(4,128)(2,1)}, u32[]{:S(2)}) copy-start(bf16[8,4,2048]{2,1,0:T(4,128)(2,1)} %param.11) | copy-start | bytes 393220
  223.8 4.0 %collective-permute-start.14 = (bf16[8,4,512]{2,0,1:T(8,128)(2,1)S(1)}, bf16[8,4,512]{2,0,1:T(8,128)(2,1)S(1)}, u32[]{:S(2)}, u32[]{:S(2)}) collective-permute-start(bf16[8,4,512]{2,0,1:T(8,128)(2,1)S(1)} %get-tuple-element.89), channel_id=1, source_target_pairs={{0,96},{32,0},{64,32},{96,64},{1,97},{33,1},{65,33},{97,65},{2,98}... | collective-permute-start | bytes 98312 | tf_op jit(solution)/shard_map/ppermute | solution.py:220
  223.9 5.6 %collective-permute-start.13 = (bf16[8,4,512]{2,0,1:T(8,128)(2,1)S(1)}, bf16[8,4,512]{2,0,1:T(8,128)(2,1)S(1)}, u32[]{:S(2)}, u32[]{:S(2)}) collective-permute-start(bf16[8,4,512]{2,0,1:T(8,128)(2,1)S(1)} %get-tuple-element.90), channel_id=1, source_target_pairs={{0,64},{32,96},{64,0},{96,32},{1,65},{33,97},{65,1},{97,33},{2,66}... | collective-permute-start | bytes 98312 | tf_op jit(solution)/shard_map/ppermute | solution.py:220
  225.3 5.2 %collective-permute-start.12 = (bf16[8,4,512]{2,0,1:T(8,128)(2,1)S(1)}, bf16[8,4,512]{2,0,1:T(8,128)(2,1)S(1)}, u32[]{:S(2)}, u32[]{:S(2)}) collective-permute-start(bf16[8,4,512]{2,0,1:T(8,128)(2,1)S(1)} %get-tuple-element.91), channel_id=1, source_target_pairs={{0,32},{32,64},{64,96},{96,0},{1,33},{33,65},{65,97},{97,1},{2,34}... | collective-permute-start | bytes 98312 | tf_op jit(solution)/shard_map/ppermute | solution.py:220
  231.0 8.6 %collective-permute-start.17 = (bf16[8,4,2048]{2,0,1:T(8,128)(2,1)S(1)}, bf16[8,4,2048]{2,0,1:T(8,128)(2,1)S(1)}, u32[]{:S(2)}, u32[]{:S(2)}) collective-permute-start(bf16[8,4,2048]{2,0,1:T(8,128)(2,1)S(1)} %get-tuple-element.58), channel_id=1, source_target_pairs={{0,32},{32,64},{64,96},{96,0},{1,33},{33,65},{65,97},{97,1},{2,34}... | collective-permute-start | bytes 393224 | tf_op jit(solution)/shard_map/ppermute | solution.py:220
  231.9 7.6 %collective-permute-start.16 = (bf16[8,4,2048]{2,0,1:T(8,128)(2,1)S(1)}, bf16[8,4,2048]{2,0,1:T(8,128)(2,1)S(1)}, u32[]{:S(2)}, u32[]{:S(2)}) collective-permute-start(bf16[8,4,2048]{2,0,1:T(8,128)(2,1)S(1)} %get-tuple-element.59), channel_id=1, source_target_pairs={{0,64},{32,96},{64,0},{96,32},{1,65},{33,97},{65,1},{97,33},{2,66}... | collective-permute-start | bytes 393224 | tf_op jit(solution)/shard_map/ppermute | solution.py:220
  234.5 5.6 %collective-permute-start.15 = (bf16[8,4,2048]{2,0,1:T(8,128)(2,1)S(1)}, bf16[8,4,2048]{2,0,1:T(8,128)(2,1)S(1)}, u32[]{:S(2)}, u32[]{:S(2)}) collective-permute-start(bf16[8,4,2048]{2,0,1:T(8,128)(2,1)S(1)} %get-tuple-element.57), channel_id=1, source_target_pairs={{0,96},{32,0},{64,32},{96,64},{1,97},{33,1},{65,33},{97,65},{2,98}... | collective-permute-start | bytes 393224 | tf_op jit(solution)/shard_map/ppermute | solution.py:220

commit v12 on v10

--- a/solution.py
+++ b/solution.py
@@ -45,30 +45,29 @@
     page_len = arrived_ref.shape[3]
     positions = pages * page_len
     heads = q_ref.shape[1]
-    head_dim = q_ref.shape[3]
+    head_dim = q_ref.shape[2]
     new_count = fk_ref.shape[1]
     outs = (keys_out_ref, values_out_ref)
     keys_out_ref[0] = arrived_ref[0, :, 0]
     values_out_ref[0] = arrived_ref[0, :, 1]
     length = lengths_ref[r]
     base = base_ref[0]
-    spots = base + lax.broadcasted_iota(jnp.int32, (1, positions), 1)
+    spots = base + lax.broadcasted_iota(jnp.int32, (positions, 1), 0)
     live = spots < length
     for kh in range(heads):
         cols = pl.ds(kh * head_dim, head_dim)
         keys_h = arrived_ref[0, :, 0, :, cols].reshape(positions, head_dim)
         values_h = arrived_ref[0, :, 1, :, cols].reshape(positions, head_dim)
-        query_h = q_ref[0, kh]
-        scores = lax.dot_general(
-            query_h, keys_h, (((1,), (1,)), ((), ())), preferred_element_type=jnp.float32
-        ) * scale
+        query_t = q_ref[0, kh]
+        scores = jnp.dot(keys_h, query_t, preferred_element_type=jnp.float32) * scale
         scores = jnp.where(live, scores, MASKED)
-        peak = jnp.max(scores, axis=1, keepdims=True)
+        peak = jnp.max(scores, axis=0, keepdims=True)
         weights = jnp.where(live, jnp.exp(scores - peak), 0.0)
         peak_ref[0, kh] = peak
-        mass_ref[0, kh] = jnp.sum(weights, axis=1, keepdims=True)
-        acc_ref[0, kh] = jnp.dot(
-            weights.astype(jnp.bfloat16), values_h, preferred_element_type=jnp.float32
+        mass_ref[0, kh] = jnp.sum(weights, axis=0, keepdims=True)
+        acc_ref[0, kh] = lax.dot_general(
+            weights.astype(jnp.bfloat16), values_h, (((0,), (0,)), ((), ())),
+            preferred_element_type=jnp.float32,
         )
     first = length - base
     page0 = first // page_len
@@ -87,7 +86,7 @@
 
 def arrive_and_attend(arrival_src, lengths, base, incoming, queries, fresh_k, fresh_v, scale):
     local_reqs, new_count, kv_width = fresh_k.shape
-    _, heads, rows, head_dim = queries.shape
+    _, heads, head_dim, rows = queries.shape
     page_len = incoming.shape[2]
     pages = arrival_src.shape[0] // local_reqs
     positions = pages * page_len
@@ -97,7 +96,7 @@
         grid=(local_reqs,),
         in_specs=[
             pl.BlockSpec((1, pages, 2, page_len, kv_width), lambda r, *_: (r, 0, 0, 0, 0)),
-            pl.BlockSpec((1, heads, rows, head_dim), lambda r, *_: (r, 0, 0, 0)),
+            pl.BlockSpec((1, heads, head_dim, rows), lambda r, *_: (r, 0, 0, 0)),
             pl.BlockSpec((1, new_count, kv_width), lambda r, *_: (r, 0, 0)),
             pl.BlockSpec((1, new_count, kv_width), lambda r, *_: (r, 0, 0)),
         ],
@@ -105,8 +104,8 @@
             pl.BlockSpec((1, pages, page_len, kv_width), lambda r, *_: (r, 0, 0, 0)),
             pl.BlockSpec((1, pages, page_len, kv_width), lambda r, *_: (r, 0, 0, 0)),
             pl.BlockSpec((1, heads, rows, head_dim), lambda r, *_: (r, 0, 0, 0)),
-            pl.BlockSpec((1, heads, rows, 1), lambda r, *_: (r, 0, 0, 0)),
-            pl.BlockSpec((1, heads, rows, 1), lambda r, *_: (r, 0, 0, 0)),
+            pl.BlockSpec((1, heads, 1, rows), lambda r, *_: (r, 0, 0, 0)),
+            pl.BlockSpec((1, heads, 1, rows), lambda r, *_: (r, 0, 0, 0)),
         ],
     )
     cache_bytes = 2 * local_reqs * positions * kv_width * 2
@@ -116,8 +115,8 @@
             jax.ShapeDtypeStruct((local_reqs, pages, page_len, kv_width), jnp.bfloat16),
             jax.ShapeDtypeStruct((local_reqs, pages, page_len, kv_width), jnp.bfloat16),
             jax.ShapeDtypeStruct((local_reqs, heads, rows, head_dim), jnp.float32),
-            jax.ShapeDtypeStruct((local_reqs, heads, rows, 1), jnp.float32),
-            jax.ShapeDtypeStruct((local_reqs, heads, rows, 1), jnp.float32),
+            jax.ShapeDtypeStruct((local_reqs, heads, 1, rows), jnp.float32),
+            jax.ShapeDtypeStruct((local_reqs, heads, 1, rows), jnp.float32),
         ],
         grid_spec=grid_spec,
         compiler_params=pltpu.CompilerParams(
@@ -220,8 +219,8 @@
     )
     fresh_values = owned_rows[..., query_cols + key_cols :].reshape(local_reqs, new_count, KVH, HD)
     score_scale = 1.0 / math.sqrt(HD)
-    kernel_queries = jnp.transpose(queries, (0, 2, 3, 1, 4)).reshape(
-        local_reqs, KVH, groups * new_count, HD
+    kernel_queries = jnp.transpose(queries, (0, 2, 4, 3, 1)).reshape(
+        local_reqs, KVH, HD, groups * new_count
     )
     keys_out, values_out, gathered_sum, row_peak, row_mass = arrive_and_attend(
         arrival_src,

time: 234 us -> 237 us (1.013)
  no operation moved by 1% of the time
where the time goes in v12:
time: 237 us
  waiting for transfers between devices  122 us (51%)
  local copies, waits for them, and re-layouts  40.5 us (17%)
  starting transfers between devices  29.8 us (13%)
  Pallas kernels  20.2 us (9%)
  other arithmetic  16.5 us (7%)
  matrix products  5.59 us (2%)
    ppermute x12, waiting for transfers between devices, shift(): return lax.ppermute(value, 'req', pairs)  99.6 us
    ppermute x5, waiting for transfers between devices, merge(): other = lax.ppermute(pack(total, peak, mass), 'seq', pairs)  22.5 us
    pallas_call x1, Pallas kernels, arrive_and_attend(): pl.pallas_call(functools.partial(_arrive_kernel, scale=scale), out_shape=...  20.2 us
    ppermute x12, starting transfers between devices, shift(): return lax.ppermute(value, 'req', pairs)  16.2 us
    gather x2, local copies, waits for them, and re-layouts, shards(): outgoing = jnp.stack([pool_keys[send_pick], pool_values[send_pick]], axis=1)  10 us
    all_to_all x1, starting transfers between devices, shards(): lax.all_to_all(outgoing, ('req', 'seq'), split_axis=0, concat_axis=0, til...  10 us
    gather x1, local copies, waits for them, and re-layouts, arrive_and_attend(): incoming[arrival_src].reshape(local_reqs, pages, 2, page_len, kv_width)  9.96 us
    reshape x1, other arithmetic, shards(): outgoing = outgoing.reshape(devices, per_peer, 2, page_len, kv_width)  7.49 us
  transfers between devices with their start and end apart: 19, of which 13 were waited for; matrix products, arithmetic and copies ran while one was open for 16% of the time, Pallas kernels for 0%

profile of v12, /device:TPU:32, one launch (start us, length us, event | category | flops | bytes accessed | tf_op | source)
XLA Modules:
  0.0 236.6 jit_solution(12176178733319096547)
XLA Ops:
  0.6 1.3 fusion.14
  1.9 1.0 fusion.16
  3.0 2.8 %collective-permute-start.2 = (bf16[8,4,2048]{2,0,1:T(8,128)(2,1)S(1)}, bf16[8,4,2048]{2,0,1:T(8,128)(2,1)S(1)}, u32[]{:S(2)}, u32[]{:S(2)}) collective-permute-start(bf16[8,4,2048]{2,0,1:T(8,128)(2,1)S(1)} %fusion.16), channel_id=1, source_target_pairs={{0,96},{32,0},{64,32},{96,64},{1,97},{33,1},{65,33},{97,65},{2,98}... | collective-permute-start | bytes 393224 | tf_op jit(solution)/shard_map/ppermute | solution.py:187
  5.8 0.8 collective-permute-start.1
  6.6 0.9 collective-permute-start
  7.5 0.8 select_reduce_fusion.1
  8.3 1.5 gather_fusion
  9.8 0.2 reshape.606
  10.0 0.6 fusion.7
  10.7 5.0 %gather_fusion.2 = bf16[128,16,1024]{2,1,0:T(8,128)(2,1)} fusion(bf16[128,16,1024]{2,1,0:T(8,128)(2,1)} %param.18, s32[1024]{0:T(1024)S(1)} %pad_clamp_fusion.3), kind=kCustom, calls=%fused_computation.2 | custom fusion | bytes 8389120 | tf_op jit(solution)/shard_map/gather | solution.py:190
  15.7 5.0 %gather_fusion.1 = bf16[128,16,1024]{2,1,0:T(8,128)(2,1)} fusion(bf16[128,16,1024]{2,1,0:T(8,128)(2,1)} %param.17, s32[1024]{0:T(1024)S(1)} %pad_clamp_fusion.3), kind=kCustom, calls=%fused_computation.1 | custom fusion | bytes 8389120 | tf_op jit(solution)/shard_map/gather | solution.py:190
  20.7 7.5 %maximum_bitcast_fusion = bf16[128,1,2,16,1024]{4,3,2,1,0:T(8,128)(2,1)} fusion(bf16[128,1,16,1024]{3,2,1,0:T(8,128)(2,1)} %bitcast.160, bf16[128,1,16,1024]{3,2,1,0:T(8,128)(2,1)} %bitcast.161), kind=kLoop, calls=%fused_computation.6 | loop fusion | flops 4194304 | bytes 16777216 | tf_op jit(solution)/shard_map/reshape | solution.py:191
  28.2 0.9 pad_maximum_fusion
  29.2 10.0 %all-to-all-start = ((bf16[128,1,2,16,1024]{4,3,2,1,0:T(8,128)(2,1)}), bf16[128,1,2,16,1024]{4,3,2,1,0:T(8,128)(2,1)}, u32[]{:S(2)}, u32[]{:S(2)}) async-start(bf16[128,1,2,16,1024]{4,3,2,1,0:T(8,128)(2,1)} %maximum_bitcast_fusion), calls=%async_computation | async-start | bytes 16777216 | tf_op jit(solution)/shard_map/all_to_all | solution.py:193
  39.2 2.3 copy.193
  41.6 0.6 gather_fusion.4
  42.3 3.9 %copy.192 = bf16[512,2048]{1,0:T(8,128)(2,1)} copy(bf16[512,2048]{0,1:T(8,128)(2,1)} %bitcast.165) | data formatting | bytes 4194304 | tf_op jit(solution)/shard_map/dot_general | solution.py:199
  46.3 0.2 copy.154
  46.7 0.2 dynamic-slice_reduce_fusion
  47.0 0.3 multiply_cosine_fusion
  47.3 1.7 fusion.8
  49.2 2.4 %fusion.10 = f32[32,4,4,128]{3,0,2,1:T(8,128)S(1)} fusion(bf16[4,128,2048,1]{2,1,0,3:T(8,128)(2,1)} %bitcast.162, bf16[32,4,2048]{2,0,1:T(8,128)(2,1)S(1)} %pad_maximum_fusion), kind=kOutput, calls=%fused_computation.26 | convolution fusion | flops 268435456 | bytes 2883584 | tf_op jit(solution)/shard_map/dot_general | solution.py:199
  52.0 0.3 convolution_convert_fusion.1
  52.3 1.5 collective-permute-start.5
  53.9 2.7 %collective-permute-start.4 = (bf16[8,4,1024]{2,0,1:T(8,128)(2,1)S(1)}, bf16[8,4,1024]{2,0,1:T(8,128)(2,1)S(1)}, u32[]{:S(2)}, u32[]{:S(2)}) collective-permute-start(bf16[8,4,1024]{2,0,1:T(8,128)(2,1)S(1)} %get-tuple-element.70), channel_id=1, source_target_pairs={{0,64},{32,96},{64,0},{96,32},{1,65},{33,97},{65,1},{97,33},{2,66}... | collective-permute-start | bytes 196616 | tf_op jit(solution)/shard_map/ppermute | solution.py:187
  56.6 1.4 collective-permute-start.3
  58.0 79.3 %collective-permute-done.5 = bf16[8,4,1024]{2,0,1:T(8,128)(2,1)S(1)} collective-permute-done((bf16[8,4,1024]{2,0,1:T(8,128)(2,1)S(1)}, bf16[8,4,1024]{2,0,1:T(8,128)(2,1)S(1)}, u32[]{:S(2)}, u32[]{:S(2)}) %collective-permute-start.5) | collective-permute-done | bytes 65568 | tf_op jit(solution)/shard_map/ppermute | solution.py:187
  137.3 10.4 %collective-permute-done.4 = bf16[8,4,1024]{2,0,1:T(8,128)(2,1)S(1)} collective-permute-done((bf16[8,4,1024]{2,0,1:T(8,128)(2,1)S(1)}, bf16[8,4,1024]{2,0,1:T(8,128)(2,1)S(1)}, u32[]{:S(2)}, u32[]{:S(2)}) %collective-permute-start.4) | collective-permute-done | bytes 65568 | tf_op jit(solution)/shard_map/ppermute | solution.py:187
  147.8 0.6 gather_fusion.5
  148.8 1.7 copy.163.q_ref
  150.6 10.0 %gather_fusion.3 = bf16[128,2,16,1024]{3,2,1,0:T(8,128)(2,1)} fusion(bf16[128,2,16,1024]{3,2,1,0:T(8,128)(2,1)} %bitcast.8, s32[1024]{0:T(1024)S(1)} %pad_clamp_fusion.2), kind=kCustom, calls=%fused_computation.3 | custom fusion | bytes 16777728 | tf_op jit(solution)/shard_map/gather | solution.py:93
  160.6 1.6 copy-done.1
  162.2 20.2 %arrive_and_attend.1 = (bf16[8,16,16,1024]{3,2,1,0:T(8,128)(2,1)}, bf16[8,16,16,1024]{3,2,1,0:T(8,128)(2,1)}, f32[8,8,8,128]{3,2,1,0:T(8,128)S(1)}, f32[8,8,1,8]{3,2,1,0:T(1,128)S(1)}, f32[8,8,1,8]{3,2,1,0:T(1,128)S(1)}) custom-call(s32[8]{0:T(128)S(1)} %dynamic_slice.27.lengths_ref, s32[1]{0:T(128)} %bitcast.base_ref, ...), custom_call_target="tpu_custom_call" | custom-call | flops 67108864 | bytes 16777216 | tf_op jit(solution)/shard_map/arrive_and_attend/pallas_call | solution.py:112
  182.3 0.5 broadcast.453
  182.8 0.7 reduce.9
  183.7 0.7 reduce.10
  185.1 1.0 collective-permute-done.6
  186.8 0.2 multiply_add_fusion.4
  187.1 5.6 %collective-permute-done.7 = f32[260,128]{1,0:T(8,128)S(1)} collective-permute-done((f32[260,128]{1,0:T(8,128)S(1)}, f32[260,128]{1,0:T(8,128)S(1)}, u32[]{:S(2)}, u32[]{:S(2)}) %collective-permute-start.7) | collective-permute-done | bytes 133152 | tf_op jit(solution)/shard_map/ppermute | solution.py:254
  193.3 0.2 multiply_add_fusion.3
  193.6 3.2 %collective-permute-start.8 = (f32[260,128]{1,0:T(8,128)S(1)}, f32[260,128]{1,0:T(8,128)S(1)}, u32[]{:S(2)}, u32[]{:S(2)}) collective-permute-start(f32[260,128]{1,0:T(8,128)S(1)} %pad_maximum_fusion.5), channel_id=1, source_target_pairs={{0,4},{1,5},{2,6},{3,7},{4,0},{5,1},{6,2},{7,3},{8,12},{9,13},{10,... | collective-permute-start | bytes 399368 | tf_op jit(solution)/shard_map/ppermute | solution.py:254
  196.7 3.4 %collective-permute-done.8 = f32[260,128]{1,0:T(8,128)S(1)} collective-permute-done((f32[260,128]{1,0:T(8,128)S(1)}, f32[260,128]{1,0:T(8,128)S(1)}, u32[]{:S(2)}, u32[]{:S(2)}) %collective-permute-start.8) | collective-permute-done | bytes 133152 | tf_op jit(solution)/shard_map/ppermute | solution.py:254
  200.7 0.2 multiply_add_fusion.2
  201.0 6.0 %collective-permute-done.9 = f32[260,128]{1,0:T(8,128)S(1)} collective-permute-done((f32[260,128]{1,0:T(8,128)S(1)}, f32[260,128]{1,0:T(8,128)S(1)}, u32[]{:S(2)}, u32[]{:S(2)}) %collective-permute-start.9) | collective-permute-done | bytes 133152 | tf_op jit(solution)/shard_map/ppermute | solution.py:254
  207.6 0.2 multiply_add_fusion.1
  208.0 6.4 %collective-permute-done.10 = f32[260,128]{1,0:T(8,128)S(1)} collective-permute-done((f32[260,128]{1,0:T(8,128)S(1)}, f32[260,128]{1,0:T(8,128)S(1)}, u32[]{:S(2)}, u32[]{:S(2)}) %collective-permute-start.10) | collective-permute-done | bytes 133152 | tf_op jit(solution)/shard_map/ppermute | solution.py:254
  215.0 0.2 multiply_add_fusion
  215.3 0.3 fusion.21
  215.6 0.5 copy.175
  216.2 0.4 collective-permute-done.11
  217.4 0.5 copy.178
  218.4 0.2 copy.182
  218.8 0.4 fusion.3
  219.5 1.9 collective-permute-start.12
  221.5 1.9 collective-permute-done.14
  223.3 1.7 collective-permute-done.13
  225.0 1.0 collective-permute-done.12
  226.0 0.4 convolution_convert_fusion
  226.5 0.9 collective-permute-start.17
  227.4 2.6 %collective-permute-start.16 = (bf16[8,4,2048]{2,0,1:T(8,128)(2,1)S(1)}, bf16[8,4,2048]{2,0,1:T(8,128)(2,1)S(1)}, u32[]{:S(2)}, u32[]{:S(2)}) collective-permute-start(bf16[8,4,2048]{2,0,1:T(8,128)(2,1)S(1)} %get-tuple-element.59), channel_id=1, source_target_pairs={{0,64},{32,96},{64,0},{96,32},{1,65},{33,97},{65,1},{97,33},{2,66}... | collective-permute-start | bytes 393224 | tf_op jit(solution)/shard_map/ppermute | solution.py:187
  230.1 0.3 collective-permute-start.15
  230.4 4.7 %collective-permute-done.17 = bf16[8,4,2048]{2,0,1:T(8,128)(2,1)S(1)} collective-permute-done((bf16[8,4,2048]{2,0,1:T(8,128)(2,1)S(1)}, bf16[8,4,2048]{2,0,1:T(8,128)(2,1)S(1)}, u32[]{:S(2)}, u32[]{:S(2)}) %collective-permute-start.17) | collective-permute-done | bytes 131104 | tf_op jit(solution)/shard_map/ppermute | solution.py:187
  235.1 0.6 collective-permute-done.15
  235.8 0.8 copy.185
  (133 shorter events, 7.7 us)
Async XLA Ops:
  0.6 225.4 %copy-start = (bf16[512,2048]{1,0:T(8,128)(2,1)S(1)}, bf16[512,2048]{1,0:T(8,128)(2,1)}, u32[]{:S(2)}) copy-start(bf16[512,2048]{1,0:T(8,128)(2,1)} %param.16) | copy-start | bytes 6291460
  3.0 25.3 %collective-permute-start.2 = (bf16[8,4,2048]{2,0,1:T(8,128)(2,1)S(1)}, bf16[8,4,2048]{2,0,1:T(8,128)(2,1)S(1)}, u32[]{:S(2)}, u32[]{:S(2)}) collective-permute-start(bf16[8,4,2048]{2,0,1:T(8,128)(2,1)S(1)} %fusion.16), channel_id=1, source_target_pairs={{0,96},{32,0},{64,32},{96,64},{1,97},{33,1},{65,33},{97,65},{2,98}... | collective-permute-start | bytes 393224 | tf_op jit(solution)/shard_map/ppermute | solution.py:187
  5.8 22.4 %collective-permute-start.1 = (bf16[8,4,2048]{2,0,1:T(8,128)(2,1)S(1)}, bf16[8,4,2048]{2,0,1:T(8,128)(2,1)S(1)}, u32[]{:S(2)}, u32[]{:S(2)}) collective-permute-start(bf16[8,4,2048]{2,0,1:T(8,128)(2,1)S(1)} %fusion.16), channel_id=1, source_target_pairs={{0,64},{32,96},{64,0},{96,32},{1,65},{33,97},{65,1},{97,33},{2,66}... | collective-permute-start | bytes 393224 | tf_op jit(solution)/shard_map/ppermute | solution.py:187
  6.6 21.6 %collective-permute-start = (bf16[8,4,2048]{2,0,1:T(8,128)(2,1)S(1)}, bf16[8,4,2048]{2,0,1:T(8,128)(2,1)}, u32[]{:S(2)}, u32[]{:S(2)}) collective-permute-start(bf16[8,4,2048]{2,0,1:T(8,128)(2,1)S(1)} %fusion.16), channel_id=1, source_target_pairs={{0,32},{32,64},{64,96},{96,0},{1,33},{33,65},{65,97},{97,1},{2,34}... | collective-permute-start | bytes 393224 | tf_op jit(solution)/shard_map/ppermute | solution.py:187
  29.2 121.4 %all-to-all-start = ((bf16[128,1,2,16,1024]{4,3,2,1,0:T(8,128)(2,1)}), bf16[128,1,2,16,1024]{4,3,2,1,0:T(8,128)(2,1)}, u32[]{:S(2)}, u32[]{:S(2)}) async-start(bf16[128,1,2,16,1024]{4,3,2,1,0:T(8,128)(2,1)} %maximum_bitcast_fusion), calls=%async_computation | async-start | bytes 16777216 | tf_op jit(solution)/shard_map/all_to_all | solution.py:193
  46.7 5.3 %copy-start.3 = (bf16[2048,256]{1,0:T(8,128)(2,1)S(1)}, bf16[2048,256]{1,0:T(8,128)(2,1)}, u32[]{:S(2)}) copy-start(bf16[2048,256]{1,0:T(8,128)(2,1)} %param.15) | copy-start | bytes 3145732
  52.3 85.0 %collective-permute-start.5 = (bf16[8,4,1024]{2,0,1:T(8,128)(2,1)S(1)}, bf16[8,4,1024]{2,0,1:T(8,128)(2,1)S(1)}, u32[]{:S(2)}, u32[]{:S(2)}) collective-permute-start(bf16[8,4,1024]{2,0,1:T(8,128)(2,1)S(1)} %get-tuple-element.69), channel_id=1, source_target_pairs={{0,32},{32,64},{64,96},{96,0},{1,33},{33,65},{65,97},{97,1},{2,34}... | collective-permute-start | bytes 196616 | tf_op jit(solution)/shard_map/ppermute | solution.py:187
  53.9 93.9 %collective-permute-start.4 = (bf16[8,4,1024]{2,0,1:T(8,128)(2,1)S(1)}, bf16[8,4,1024]{2,0,1:T(8,128)(2,1)S(1)}, u32[]{:S(2)}, u32[]{:S(2)}) collective-permute-start(bf16[8,4,1024]{2,0,1:T(8,128)(2,1)S(1)} %get-tuple-element.70), channel_id=1, source_target_pairs={{0,64},{32,96},{64,0},{96,32},{1,65},{33,97},{65,1},{97,33},{2,66}... | collective-permute-start | bytes 196616 | tf_op jit(solution)/shard_map/ppermute | solution.py:187
  56.6 91.1 %collective-permute-start.3 = (bf16[8,4,1024]{2,0,1:T(8,128)(2,1)S(1)}, bf16[8,4,1024]{2,0,1:T(8,128)(2,1)S(1)}, u32[]{:S(2)}, u32[]{:S(2)}) collective-permute-start(bf16[8,4,1024]{2,0,1:T(8,128)(2,1)S(1)} %get-tuple-element.71), channel_id=1, source_target_pairs={{0,96},{32,0},{64,32},{96,64},{1,97},{33,1},{65,33},{97,65},{2,98}... | collective-permute-start | bytes 196616 | tf_op jit(solution)/shard_map/ppermute | solution.py:187
  160.6 1.6 copy-start.1
  184.5 1.6 collective-permute-start.6
  187.0 5.7 %collective-permute-start.7 = (f32[260,128]{1,0:T(8,128)S(1)}, f32[260,128]{1,0:T(8,128)S(1)}, u32[]{:S(2)}, u32[]{:S(2)}) collective-permute-start(f32[260,128]{1,0:T(8,128)S(1)} %pad_maximum_fusion.4), channel_id=1, source_target_pairs={{0,2},{1,3},{2,0},{3,1},{4,6},{5,7},{6,4},{7,5},{8,10},{9,11},{10,... | collective-permute-start | bytes 399368 | tf_op jit(solution)/shard_map/ppermute | solution.py:254
  193.6 6.6 %collective-permute-start.8 = (f32[260,128]{1,0:T(8,128)S(1)}, f32[260,128]{1,0:T(8,128)S(1)}, u32[]{:S(2)}, u32[]{:S(2)}) collective-permute-start(f32[260,128]{1,0:T(8,128)S(1)} %pad_maximum_fusion.5), channel_id=1, source_target_pairs={{0,4},{1,5},{2,6},{3,7},{4,0},{5,1},{6,2},{7,3},{8,12},{9,13},{10,... | collective-permute-start | bytes 399368 | tf_op jit(solution)/shard_map/ppermute | solution.py:254
  200.9 6.1 %collective-permute-start.9 = (f32[260,128]{1,0:T(8,128)S(1)}, f32[260,128]{1,0:T(8,128)S(1)}, u32[]{:S(2)}, u32[]{:S(2)}) collective-permute-start(f32[260,128]{1,0:T(8,128)S(1)} %pad_maximum_fusion.6), channel_id=1, source_target_pairs={{0,8},{1,9},{2,10},{3,11},{4,12},{5,13},{6,14},{7,15},{8,0},{9,1},... | collective-permute-start | bytes 399368 | tf_op jit(solution)/shard_map/ppermute | solution.py:254
  207.8 6.6 %collective-permute-start.10 = (f32[260,128]{1,0:T(8,128)S(1)}, f32[260,128]{1,0:T(8,128)S(1)}, u32[]{:S(2)}, u32[]{:S(2)}) collective-permute-start(f32[260,128]{1,0:T(8,128)S(1)} %pad_maximum_fusion.7), channel_id=1, source_target_pairs={{0,16},{1,17},{2,18},{3,19},{4,20},{5,21},{6,22},{7,23},{8,24},{9,... | collective-permute-start | bytes 399368 | tf_op jit(solution)/shard_map/ppermute | solution.py:254
  215.2 1.4 collective-permute-start.11
  219.1 16.6 %copy-start.2 = (bf16[8,4,2048]{2,1,0:T(4,128)(2,1)S(1)}, bf16[8,4,2048]{2,1,0:T(4,128)(2,1)}, u32[]{:S(2)}) copy-start(bf16[8,4,2048]{2,1,0:T(4,128)(2,1)} %param.11) | copy-start | bytes 393220
  219.4 4.0 %collective-permute-start.14 = (bf16[8,4,512]{2,0,1:T(8,128)(2,1)S(1)}, bf16[8,4,512]{2,0,1:T(8,128)(2,1)S(1)}, u32[]{:S(2)}, u32[]{:S(2)}) collective-permute-start(bf16[8,4,512]{2,0,1:T(8,128)(2,1)S(1)} %get-tuple-element.89), channel_id=1, source_target_pairs={{0,96},{32,0},{64,32},{96,64},{1,97},{33,1},{65,33},{97,65},{2,98}... | collective-permute-start | bytes 98312 | tf_op jit(solution)/shard_map/ppermute | solution.py:187
  219.4 5.6 %collective-permute-start.13 = (bf16[8,4,512]{2,0,1:T(8,128)(2,1)S(1)}, bf16[8,4,512]{2,0,1:T(8,128)(2,1)S(1)}, u32[]{:S(2)}, u32[]{:S(2)}) collective-permute-start(bf16[8,4,512]{2,0,1:T(8,128)(2,1)S(1)} %get-tuple-element.90), channel_id=1, source_target_pairs={{0,64},{32,96},{64,0},{96,32},{1,65},{33,97},{65,1},{97,33},{2,66}... | collective-permute-start | bytes 98312 | tf_op jit(solution)/shard_map/ppermute | solution.py:187
  219.5 6.5 %collective-permute-start.12 = (bf16[8,4,512]{2,0,1:T(8,128)(2,1)S(1)}, bf16[8,4,512]{2,0,1:T(8,128)(2,1)S(1)}, u32[]{:S(2)}, u32[]{:S(2)}) collective-permute-start(bf16[8,4,512]{2,0,1:T(8,128)(2,1)S(1)} %get-tuple-element.91), channel_id=1, source_target_pairs={{0,32},{32,64},{64,96},{96,0},{1,33},{33,65},{65,97},{97,1},{2,34}... | collective-permute-start | bytes 98312 | tf_op jit(solution)/shard_map/ppermute | solution.py:187
  226.5 8.6 %collective-permute-start.17 = (bf16[8,4,2048]{2,0,1:T(8,128)(2,1)S(1)}, bf16[8,4,2048]{2,0,1:T(8,128)(2,1)S(1)}, u32[]{:S(2)}, u32[]{:S(2)}) collective-permute-start(bf16[8,4,2048]{2,0,1:T(8,128)(2,1)S(1)} %get-tuple-element.58), channel_id=1, source_target_pairs={{0,32},{32,64},{64,96},{96,0},{1,33},{33,65},{65,97},{97,1},{2,34}... | collective-permute-start | bytes 393224 | tf_op jit(solution)/shard_map/ppermute | solution.py:187
  227.4 7.6 %collective-permute-start.16 = (bf16[8,4,2048]{2,0,1:T(8,128)(2,1)S(1)}, bf16[8,4,2048]{2,0,1:T(8,128)(2,1)S(1)}, u32[]{:S(2)}, u32[]{:S(2)}) collective-permute-start(bf16[8,4,2048]{2,0,1:T(8,128)(2,1)S(1)} %get-tuple-element.59), channel_id=1, source_target_pairs={{0,64},{32,96},{64,0},{96,32},{1,65},{33,97},{65,1},{97,33},{2,66}... | collective-permute-start | bytes 393224 | tf_op jit(solution)/shard_map/ppermute | solution.py:187
  230.1 5.6 %collective-permute-start.15 = (bf16[8,4,2048]{2,0,1:T(8,128)(2,1)S(1)}, bf16[8,4,2048]{2,0,1:T(8,128)(2,1)S(1)}, u32[]{:S(2)}, u32[]{:S(2)}) collective-permute-start(bf16[8,4,2048]{2,0,1:T(8,128)(2,1)S(1)} %get-tuple-element.57), channel_id=1, source_target_pairs={{0,96},{32,0},{64,32},{96,64},{1,97},{33,1},{65,33},{97,65},{2,98}... | collective-permute-start | bytes 393224 | tf_op jit(solution)/shard_map/ppermute | solution.py:187

commit v13 on v10

--- a/solution.py
+++ b/solution.py
@@ -44,8 +44,8 @@
     pages = arrived_ref.shape[1]
     page_len = arrived_ref.shape[3]
     positions = pages * page_len
-    heads = q_ref.shape[1]
-    head_dim = q_ref.shape[3]
+    heads = acc_ref.shape[1]
+    head_dim = acc_ref.shape[3]
     new_count = fk_ref.shape[1]
     outs = (keys_out_ref, values_out_ref)
     keys_out_ref[0] = arrived_ref[0, :, 0]
@@ -54,22 +54,21 @@
     base = base_ref[0]
     spots = base + lax.broadcasted_iota(jnp.int32, (1, positions), 1)
     live = spots < length
+    rows = q_ref.shape[1] // heads
+    keys_all = arrived_ref[0, :, 0].reshape(positions, heads * head_dim)
+    values_all = arrived_ref[0, :, 1].reshape(positions, heads * head_dim)
+    scores = lax.dot_general(
+        q_ref[0], keys_all, (((1,), (1,)), ((), ())), preferred_element_type=jnp.float32
+    ) * scale
+    scores = jnp.where(live, scores, MASKED)
+    peak = jnp.max(scores, axis=1, keepdims=True)
+    weights = jnp.where(live, jnp.exp(scores - peak), 0.0)
+    mass = jnp.sum(weights, axis=1, keepdims=True)
+    acc_all = jnp.dot(weights.astype(jnp.bfloat16), values_all, preferred_element_type=jnp.float32)
     for kh in range(heads):
-        cols = pl.ds(kh * head_dim, head_dim)
-        keys_h = arrived_ref[0, :, 0, :, cols].reshape(positions, head_dim)
-        values_h = arrived_ref[0, :, 1, :, cols].reshape(positions, head_dim)
-        query_h = q_ref[0, kh]
-        scores = lax.dot_general(
-            query_h, keys_h, (((1,), (1,)), ((), ())), preferred_element_type=jnp.float32
-        ) * scale
-        scores = jnp.where(live, scores, MASKED)
-        peak = jnp.max(scores, axis=1, keepdims=True)
-        weights = jnp.where(live, jnp.exp(scores - peak), 0.0)
-        peak_ref[0, kh] = peak
-        mass_ref[0, kh] = jnp.sum(weights, axis=1, keepdims=True)
-        acc_ref[0, kh] = jnp.dot(
-            weights.astype(jnp.bfloat16), values_h, preferred_element_type=jnp.float32
-        )
+        peak_ref[0, kh] = peak[kh * rows : (kh + 1) * rows]
+        mass_ref[0, kh] = mass[kh * rows : (kh + 1) * rows]
+        acc_ref[0, kh] = acc_all[kh * rows : (kh + 1) * rows, kh * head_dim : (kh + 1) * head_dim]
     first = length - base
     page0 = first // page_len
     row_ids = lax.broadcasted_iota(jnp.int32, (page_len, 1), 0)
@@ -88,6 +87,9 @@
 def arrive_and_attend(arrival_src, lengths, base, incoming, queries, fresh_k, fresh_v, scale):
     local_reqs, new_count, kv_width = fresh_k.shape
     _, heads, rows, head_dim = queries.shape
+    eye = jnp.arange(heads)[:, None] == jnp.arange(heads)[None, :]
+    block_q = jnp.where(eye[None, :, None, :, None], queries[:, :, :, None, :], jnp.zeros((), queries.dtype))
+    block_q = block_q.reshape(local_reqs, heads * rows, heads * head_dim)
     page_len = incoming.shape[2]
     pages = arrival_src.shape[0] // local_reqs
     positions = pages * page_len
@@ -97,7 +99,7 @@
         grid=(local_reqs,),
         in_specs=[
             pl.BlockSpec((1, pages, 2, page_len, kv_width), lambda r, *_: (r, 0, 0, 0, 0)),
-            pl.BlockSpec((1, heads, rows, head_dim), lambda r, *_: (r, 0, 0, 0)),
+            pl.BlockSpec((1, heads * rows, heads * head_dim), lambda r, *_: (r, 0, 0)),
             pl.BlockSpec((1, new_count, kv_width), lambda r, *_: (r, 0, 0)),
             pl.BlockSpec((1, new_count, kv_width), lambda r, *_: (r, 0, 0)),
         ],
@@ -129,7 +131,7 @@
             bytes_accessed=2 * cache_bytes,
         ),
         name="arrive_and_attend",
-    )(lengths, base, arrived, queries, fresh_k, fresh_v)
+    )(lengths, base, arrived, block_q, fresh_k, fresh_v)
     keys_out = keys_out.reshape(local_reqs, positions, kv_width)
     values_out = values_out.reshape(local_reqs, positions, kv_width)
     return keys_out, values_out, acc, peak, mass

time: 234 us -> 230 us (0.983)
  Pallas kernels: 19.3 us -> 11.2 us
  other arithmetic: 16 us -> 19.1 us
    pallas_call x1, Pallas kernels: 19.3 us -> 11.2 us  [arrive_and_attend(): pl.pallas_call(functools.partial(_arrive_kernel, scale=scale), out_shape=...]
  transfers between devices with their start and end apart: 19 -> 19, of which waited for: 13 -> 12; matrix products, arithmetic and copies ran while one was open for 16% -> 17% of each run, Pallas kernels for 0% -> 0%
where the time goes in v13:
time: 230 us; the launch traced here: 229 us
  waiting for transfers between devices  120 us (52%)
  local copies, waits for them, and re-layouts  41.2 us (18%)
  starting transfers between devices  29.9 us (13%)
  other arithmetic  19.1 us (8%)
  Pallas kernels  11.2 us (5%)
  matrix products  5.58 us (2%)
    ppermute x12, waiting for transfers between devices, shift(): return lax.ppermute(value, 'req', pairs)  98.8 us
    ppermute x5, waiting for transfers between devices, merge(): other = lax.ppermute(pack(total, peak, mass), 'seq', pairs)  21.2 us
    ppermute x12, starting transfers between devices, shift(): return lax.ppermute(value, 'req', pairs)  16.2 us
    pallas_call x1, Pallas kernels, arrive_and_attend(): pl.pallas_call(functools.partial(_arrive_kernel, scale=scale), out_shape=...  11.2 us
    gather x2, local copies, waits for them, and re-layouts, shards(): outgoing = jnp.stack([pool_keys[send_pick], pool_values[send_pick]], axis=1)  10 us
    all_to_all x1, starting transfers between devices, shards(): lax.all_to_all(outgoing, ('req', 'seq'), split_axis=0, concat_axis=0, til...  10 us
    gather x1, local copies, waits for them, and re-layouts, arrive_and_attend(): incoming[arrival_src].reshape(local_reqs, pages, 2, page_len, kv_width)  9.96 us
    reshape x1, other arithmetic, shards(): outgoing = outgoing.reshape(devices, per_peer, 2, page_len, kv_width)  7.49 us
  transfers between devices with their start and end apart: 19, of which 12 were waited for; matrix products, arithmetic and copies ran while one was open for 17% of the time, Pallas kernels for 0%

profile of v13, /device:TPU:32, one launch (start us, length us, event | category | flops | bytes accessed | tf_op | source)
XLA Modules:
  0.0 229.0 jit_solution(18404716357144177863)
XLA Ops:
  0.6 1.3 fusion.14
  1.9 1.0 fusion.16
  3.0 2.8 %collective-permute-start.2 = (bf16[8,4,2048]{2,0,1:T(8,128)(2,1)S(1)}, bf16[8,4,2048]{2,0,1:T(8,128)(2,1)S(1)}, u32[]{:S(2)}, u32[]{:S(2)}) collective-permute-start(bf16[8,4,2048]{2,0,1:T(8,128)(2,1)S(1)} %fusion.16), channel_id=1, source_target_pairs={{0,96},{32,0},{64,32},{96,64},{1,97},{33,1},{65,33},{97,65},{2,98}... | collective-permute-start | bytes 393224 | tf_op jit(solution)/shard_map/ppermute | solution.py:190
  5.8 0.8 collective-permute-start.1
  6.6 0.9 collective-permute-start
  7.5 0.8 select_reduce_fusion.1
  8.3 1.5 gather_fusion
  10.0 0.6 fusion.7
  10.7 5.0 %gather_fusion.2 = bf16[128,16,1024]{2,1,0:T(8,128)(2,1)} fusion(bf16[128,16,1024]{2,1,0:T(8,128)(2,1)} %param.18, s32[1024]{0:T(1024)S(1)} %pad_clamp_fusion.3), kind=kCustom, calls=%fused_computation.2 | custom fusion | bytes 8389120 | tf_op jit(solution)/shard_map/gather | solution.py:193
  15.7 5.0 %gather_fusion.1 = bf16[128,16,1024]{2,1,0:T(8,128)(2,1)} fusion(bf16[128,16,1024]{2,1,0:T(8,128)(2,1)} %param.17, s32[1024]{0:T(1024)S(1)} %pad_clamp_fusion.3), kind=kCustom, calls=%fused_computation.1 | custom fusion | bytes 8389120 | tf_op jit(solution)/shard_map/gather | solution.py:193
  20.7 7.5 %maximum_bitcast_fusion = bf16[128,1,2,16,1024]{4,3,2,1,0:T(8,128)(2,1)} fusion(bf16[128,1,16,1024]{3,2,1,0:T(8,128)(2,1)} %bitcast.164, bf16[128,1,16,1024]{3,2,1,0:T(8,128)(2,1)} %bitcast.165), kind=kLoop, calls=%fused_computation.6 | loop fusion | flops 4194304 | bytes 16777216 | tf_op jit(solution)/shard_map/reshape | solution.py:194
  28.2 0.9 pad_maximum_fusion
  29.2 10.0 %all-to-all-start = ((bf16[128,1,2,16,1024]{4,3,2,1,0:T(8,128)(2,1)}), bf16[128,1,2,16,1024]{4,3,2,1,0:T(8,128)(2,1)}, u32[]{:S(2)}, u32[]{:S(2)}) async-start(bf16[128,1,2,16,1024]{4,3,2,1,0:T(8,128)(2,1)} %maximum_bitcast_fusion), calls=%async_computation | async-start | bytes 16777216 | tf_op jit(solution)/shard_map/all_to_all | solution.py:196
  39.2 2.3 copy.190
  41.6 0.6 gather_fusion.4
  42.3 3.9 %copy.189 = bf16[512,2048]{1,0:T(8,128)(2,1)} copy(bf16[512,2048]{0,1:T(8,128)(2,1)} %bitcast.169) | data formatting | bytes 4194304 | tf_op jit(solution)/shard_map/dot_general | solution.py:202
  46.3 0.2 copy.151
  47.0 0.8 broadcast_bitcast_fusion
  47.7 0.3 multiply_cosine_fusion
  48.0 1.7 fusion.8
  50.0 2.4 %fusion.10 = f32[32,4,4,128]{3,0,2,1:T(8,128)S(1)} fusion(bf16[4,128,2048,1]{2,1,0,3:T(8,128)(2,1)} %bitcast.166, bf16[32,4,2048]{2,0,1:T(8,128)(2,1)S(1)} %pad_maximum_fusion), kind=kOutput, calls=%fused_computation.27 | convolution fusion | flops 268435456 | bytes 2883584 | tf_op jit(solution)/shard_map/dot_general | solution.py:202
  52.7 0.3 convolution_convert_fusion.1
  53.1 1.5 collective-permute-start.5
  54.7 2.7 %collective-permute-start.4 = (bf16[8,4,1024]{2,0,1:T(8,128)(2,1)S(1)}, bf16[8,4,1024]{2,0,1:T(8,128)(2,1)S(1)}, u32[]{:S(2)}, u32[]{:S(2)}) collective-permute-start(bf16[8,4,1024]{2,0,1:T(8,128)(2,1)S(1)} %get-tuple-element.70), channel_id=1, source_target_pairs={{0,64},{32,96},{64,0},{96,32},{1,65},{33,97},{65,1},{97,33},{2,66}... | collective-permute-start | bytes 196616 | tf_op jit(solution)/shard_map/ppermute | solution.py:190
  57.4 1.4 collective-permute-start.3
  58.8 78.5 %collective-permute-done.5 = bf16[8,4,1024]{2,0,1:T(8,128)(2,1)S(1)} collective-permute-done((bf16[8,4,1024]{2,0,1:T(8,128)(2,1)S(1)}, bf16[8,4,1024]{2,0,1:T(8,128)(2,1)S(1)}, u32[]{:S(2)}, u32[]{:S(2)}) %collective-permute-start.5) | collective-permute-done | bytes 65568 | tf_op jit(solution)/shard_map/ppermute | solution.py:190
  137.3 10.4 %collective-permute-done.4 = bf16[8,4,1024]{2,0,1:T(8,128)(2,1)S(1)} collective-permute-done((bf16[8,4,1024]{2,0,1:T(8,128)(2,1)S(1)}, bf16[8,4,1024]{2,0,1:T(8,128)(2,1)S(1)}, u32[]{:S(2)}, u32[]{:S(2)}) %collective-permute-start.4) | collective-permute-done | bytes 65568 | tf_op jit(solution)/shard_map/ppermute | solution.py:190
  147.8 0.6 gather_fusion.5
  148.8 0.5 copy-done.9
  149.5 0.9 bitcast_select_fusion.q_ref
  150.4 10.0 %gather_fusion.3 = bf16[128,2,16,1024]{3,2,1,0:T(8,128)(2,1)} fusion(bf16[128,2,16,1024]{3,2,1,0:T(8,128)(2,1)} %bitcast.8, s32[1024]{0:T(1024)S(1)} %pad_clamp_fusion.2), kind=kCustom, calls=%fused_computation.3 | custom fusion | bytes 16777728 | tf_op jit(solution)/shard_map/gather | solution.py:96
  160.4 11.2 %arrive_and_attend.1 = (bf16[8,16,16,1024]{3,2,1,0:T(8,128)(2,1)}, bf16[8,16,16,1024]{3,2,1,0:T(8,128)(2,1)}, f32[8,8,8,128]{3,2,1,0:T(8,128)S(1)}, f32[8,8,8,1]{3,2,1,0:T(8,128)S(1)}, f32[8,8,8,1]{3,2,1,0:T(8,128)S(1)}) custom-call(s32[8]{0:T(128)S(1)} %dynamic_slice.27.lengths_ref, s32[1]{0:T(128)} %bitcast.base_ref, ...), custom_call_target="tpu_custom_call" | custom-call | flops 67108864 | bytes 16777216 | tf_op jit(solution)/shard_map/arrive_and_attend/pallas_call | solution.py:115
  171.5 0.7 copy-done.1
  172.3 0.7 copy-done.2
  173.2 1.1 reduce.2
  174.4 1.0 pad_maximum_fusion.1
  175.4 0.3 collective-permute-start.6
  175.7 1.4 copy.161
  177.0 0.5 copy.164
  178.5 1.1 multiply_add_fusion.4
  179.8 5.9 %collective-permute-done.7 = f32[260,128]{1,0:T(8,128)S(1)} collective-permute-done((f32[260,128]{1,0:T(8,128)S(1)}, f32[260,128]{1,0:T(8,128)S(1)}, u32[]{:S(2)}, u32[]{:S(2)}) %collective-permute-start.7) | collective-permute-done | bytes 133152 | tf_op jit(solution)/shard_map/ppermute | solution.py:257
  186.3 0.2 multiply_add_fusion.3
  186.5 3.2 %collective-permute-start.8 = (f32[260,128]{1,0:T(8,128)S(1)}, f32[260,128]{1,0:T(8,128)S(1)}, u32[]{:S(2)}, u32[]{:S(2)}) collective-permute-start(f32[260,128]{1,0:T(8,128)S(1)} %pad_maximum_fusion.5), channel_id=1, source_target_pairs={{0,4},{1,5},{2,6},{3,7},{4,0},{5,1},{6,2},{7,3},{8,12},{9,13},{10,... | collective-permute-start | bytes 399368 | tf_op jit(solution)/shard_map/ppermute | solution.py:257
  189.7 3.5 %collective-permute-done.8 = f32[260,128]{1,0:T(8,128)S(1)} collective-permute-done((f32[260,128]{1,0:T(8,128)S(1)}, f32[260,128]{1,0:T(8,128)S(1)}, u32[]{:S(2)}, u32[]{:S(2)}) %collective-permute-start.8) | collective-permute-done | bytes 133152 | tf_op jit(solution)/shard_map/ppermute | solution.py:257
  193.8 0.2 multiply_add_fusion.2
  194.1 5.4 %collective-permute-done.9 = f32[260,128]{1,0:T(8,128)S(1)} collective-permute-done((f32[260,128]{1,0:T(8,128)S(1)}, f32[260,128]{1,0:T(8,128)S(1)}, u32[]{:S(2)}, u32[]{:S(2)}) %collective-permute-start.9) | collective-permute-done | bytes 133152 | tf_op jit(solution)/shard_map/ppermute | solution.py:257
  200.5 6.4 %collective-permute-done.10 = f32[260,128]{1,0:T(8,128)S(1)} collective-permute-done((f32[260,128]{1,0:T(8,128)S(1)}, f32[260,128]{1,0:T(8,128)S(1)}, u32[]{:S(2)}, u32[]{:S(2)}) %collective-permute-start.10) | collective-permute-done | bytes 133152 | tf_op jit(solution)/shard_map/ppermute | solution.py:257
  207.7 0.3 fusion.21
  208.1 0.5 copy.172
  208.6 0.4 collective-permute-done.11
  209.8 0.5 copy.175
  211.2 0.4 fusion.3
  211.9 0.3 collective-permute-start.13
  212.2 1.7 collective-permute-start.12
  213.9 1.9 collective-permute-done.14
  215.8 1.7 collective-permute-done.13
  217.5 1.0 collective-permute-done.12
  218.4 0.4 convolution_convert_fusion
  218.9 0.9 collective-permute-start.17
  219.9 2.6 %collective-permute-start.16 = (bf16[8,4,2048]{2,0,1:T(8,128)(2,1)S(1)}, bf16[8,4,2048]{2,0,1:T(8,128)(2,1)S(1)}, u32[]{:S(2)}, u32[]{:S(2)}) collective-permute-start(bf16[8,4,2048]{2,0,1:T(8,128)(2,1)S(1)} %get-tuple-element.59), channel_id=1, source_target_pairs={{0,64},{32,96},{64,0},{96,32},{1,65},{33,97},{65,1},{97,33},{2,66}... | collective-permute-start | bytes 393224 | tf_op jit(solution)/shard_map/ppermute | solution.py:190
  222.5 0.3 collective-permute-start.15
  222.8 4.7 %collective-permute-done.17 = bf16[8,4,2048]{2,0,1:T(8,128)(2,1)S(1)} collective-permute-done((bf16[8,4,2048]{2,0,1:T(8,128)(2,1)S(1)}, bf16[8,4,2048]{2,0,1:T(8,128)(2,1)S(1)}, u32[]{:S(2)}, u32[]{:S(2)}) %collective-permute-start.17) | collective-permute-done | bytes 131104 | tf_op jit(solution)/shard_map/ppermute | solution.py:190
  227.5 0.6 collective-permute-done.15
  228.3 0.8 copy.182
  (149 shorter events, 8.5 us)
Async XLA Ops:
  0.6 217.8 %copy-start = (bf16[512,2048]{1,0:T(8,128)(2,1)S(1)}, bf16[512,2048]{1,0:T(8,128)(2,1)}, u32[]{:S(2)}) copy-start(bf16[512,2048]{1,0:T(8,128)(2,1)} %param.16) | copy-start | bytes 6291460
  3.0 25.3 %collective-permute-start.2 = (bf16[8,4,2048]{2,0,1:T(8,128)(2,1)S(1)}, bf16[8,4,2048]{2,0,1:T(8,128)(2,1)S(1)}, u32[]{:S(2)}, u32[]{:S(2)}) collective-permute-start(bf16[8,4,2048]{2,0,1:T(8,128)(2,1)S(1)} %fusion.16), channel_id=1, source_target_pairs={{0,96},{32,0},{64,32},{96,64},{1,97},{33,1},{65,33},{97,65},{2,98}... | collective-permute-start | bytes 393224 | tf_op jit(solution)/shard_map/ppermute | solution.py:190
  5.8 22.4 %collective-permute-start.1 = (bf16[8,4,2048]{2,0,1:T(8,128)(2,1)S(1)}, bf16[8,4,2048]{2,0,1:T(8,128)(2,1)S(1)}, u32[]{:S(2)}, u32[]{:S(2)}) collective-permute-start(bf16[8,4,2048]{2,0,1:T(8,128)(2,1)S(1)} %fusion.16), channel_id=1, source_target_pairs={{0,64},{32,96},{64,0},{96,32},{1,65},{33,97},{65,1},{97,33},{2,66}... | collective-permute-start | bytes 393224 | tf_op jit(solution)/shard_map/ppermute | solution.py:190
  6.6 21.6 %collective-permute-start = (bf16[8,4,2048]{2,0,1:T(8,128)(2,1)S(1)}, bf16[8,4,2048]{2,0,1:T(8,128)(2,1)}, u32[]{:S(2)}, u32[]{:S(2)}) collective-permute-start(bf16[8,4,2048]{2,0,1:T(8,128)(2,1)S(1)} %fusion.16), channel_id=1, source_target_pairs={{0,32},{32,64},{64,96},{96,0},{1,33},{33,65},{65,97},{97,1},{2,34}... | collective-permute-start | bytes 393224 | tf_op jit(solution)/shard_map/ppermute | solution.py:190
  29.2 121.2 %all-to-all-start = ((bf16[128,1,2,16,1024]{4,3,2,1,0:T(8,128)(2,1)}), bf16[128,1,2,16,1024]{4,3,2,1,0:T(8,128)(2,1)}, u32[]{:S(2)}, u32[]{:S(2)}) async-start(bf16[128,1,2,16,1024]{4,3,2,1,0:T(8,128)(2,1)} %maximum_bitcast_fusion), calls=%async_computation | async-start | bytes 16777216 | tf_op jit(solution)/shard_map/all_to_all | solution.py:196
  46.7 6.0 %copy-start.4 = (bf16[2048,256]{1,0:T(8,128)(2,1)S(1)}, bf16[2048,256]{1,0:T(8,128)(2,1)}, u32[]{:S(2)}) copy-start(bf16[2048,256]{1,0:T(8,128)(2,1)} %param.15) | copy-start | bytes 3145732
  53.1 84.2 %collective-permute-start.5 = (bf16[8,4,1024]{2,0,1:T(8,128)(2,1)S(1)}, bf16[8,4,1024]{2,0,1:T(8,128)(2,1)S(1)}, u32[]{:S(2)}, u32[]{:S(2)}) collective-permute-start(bf16[8,4,1024]{2,0,1:T(8,128)(2,1)S(1)} %get-tuple-element.69), channel_id=1, source_target_pairs={{0,32},{32,64},{64,96},{96,0},{1,33},{33,65},{65,97},{97,1},{2,34}... | collective-permute-start | bytes 196616 | tf_op jit(solution)/shard_map/ppermute | solution.py:190
  54.7 93.1 %collective-permute-start.4 = (bf16[8,4,1024]{2,0,1:T(8,128)(2,1)S(1)}, bf16[8,4,1024]{2,0,1:T(8,128)(2,1)S(1)}, u32[]{:S(2)}, u32[]{:S(2)}) collective-permute-start(bf16[8,4,1024]{2,0,1:T(8,128)(2,1)S(1)} %get-tuple-element.70), channel_id=1, source_target_pairs={{0,64},{32,96},{64,0},{96,32},{1,65},{33,97},{65,1},{97,33},{2,66}... | collective-permute-start | bytes 196616 | tf_op jit(solution)/shard_map/ppermute | solution.py:190
  57.4 90.4 %collective-permute-start.3 = (bf16[8,4,1024]{2,0,1:T(8,128)(2,1)S(1)}, bf16[8,4,1024]{2,0,1:T(8,128)(2,1)S(1)}, u32[]{:S(2)}, u32[]{:S(2)}) collective-permute-start(bf16[8,4,1024]{2,0,1:T(8,128)(2,1)S(1)} %get-tuple-element.71), channel_id=1, source_target_pairs={{0,96},{32,0},{64,32},{96,64},{1,97},{33,1},{65,33},{97,65},{2,98}... | collective-permute-start | bytes 196616 | tf_op jit(solution)/shard_map/ppermute | solution.py:190
  148.6 0.7 copy-start.9
  148.7 0.6 copy-start.7
  149.4 10.9 %copy-start.5 = (bf16[8,4,4,256]{3,2,1,0:T(4,128)(2,1)}, bf16[8,4,4,256]{3,2,1,0:T(4,128)(2,1)S(1)}, u32[]{:S(2)}) copy-start(bf16[8,4,4,256]{3,2,1,0:T(4,128)(2,1)S(1)} %copy.160) | copy-start | bytes 196612
  171.5 0.7 copy-start.1
  172.2 0.7 copy-start.2
  173.0 27.5 %copy-start.8 = (bf16[8,4,4,256]{3,2,1,0:T(4,128)(2,1)S(1)}, bf16[8,4,4,256]{3,2,1,0:T(4,128)(2,1)}, u32[]{:S(2)}) copy-start(bf16[8,4,4,256]{3,2,1,0:T(4,128)(2,1)} %copy-done.7) | copy-start | bytes 196612
  175.4 2.5 %collective-permute-start.6 = (f32[520,128]{1,0:T(8,128)S(1)}, f32[520,128]{1,0:T(8,128)S(1)}, u32[]{:S(2)}, u32[]{:S(2)}) collective-permute-start(f32[520,128]{1,0:T(8,128)S(1)} %pad_maximum_fusion.1), channel_id=1, source_target_pairs={{0,1},{1,0},{2,3},{3,2},{4,5},{5,4},{6,7},{7,6},{8,9},{9,8},{10,11... | collective-permute-start | bytes 798728 | tf_op jit(solution)/shard_map/ppermute | solution.py:257
  177.5 30.2 %copy-start.10 = (bf16[8,4,8,2,128]{4,3,2,1,0:T(2,128)(2,1)S(1)}, bf16[8,4,8,2,128]{4,3,2,1,0:T(2,128)(2,1)}, u32[]{:S(2)}) copy-start(bf16[8,4,8,2,128]{4,3,2,1,0:T(2,128)(2,1)} %copy-done.9) | copy-start | bytes 393220
  178.2 29.8 %copy-start.6 = (bf16[8,4,4,256]{3,2,1,0:T(4,128)(2,1)S(1)}, bf16[8,4,4,256]{3,2,1,0:T(4,128)(2,1)}, u32[]{:S(2)}) copy-start(bf16[8,4,4,256]{3,2,1,0:T(4,128)(2,1)} %copy-done.5) | copy-start | bytes 196612
  179.7 6.0 %collective-permute-start.7 = (f32[260,128]{1,0:T(8,128)S(1)}, f32[260,128]{1,0:T(8,128)S(1)}, u32[]{:S(2)}, u32[]{:S(2)}) collective-permute-start(f32[260,128]{1,0:T(8,128)S(1)} %pad_maximum_fusion.4), channel_id=1, source_target_pairs={{0,2},{1,3},{2,0},{3,1},{4,6},{5,7},{6,4},{7,5},{8,10},{9,11},{10,... | collective-permute-start | bytes 399368 | tf_op jit(solution)/shard_map/ppermute | solution.py:257
  186.5 6.7 %collective-permute-start.8 = (f32[260,128]{1,0:T(8,128)S(1)}, f32[260,128]{1,0:T(8,128)S(1)}, u32[]{:S(2)}, u32[]{:S(2)}) collective-permute-start(f32[260,128]{1,0:T(8,128)S(1)} %pad_maximum_fusion.5), channel_id=1, source_target_pairs={{0,4},{1,5},{2,6},{3,7},{4,0},{5,1},{6,2},{7,3},{8,12},{9,13},{10,... | collective-permute-start | bytes 399368 | tf_op jit(solution)/shard_map/ppermute | solution.py:257
  194.0 5.5 %collective-permute-start.9 = (f32[260,128]{1,0:T(8,128)S(1)}, f32[260,128]{1,0:T(8,128)S(1)}, u32[]{:S(2)}, u32[]{:S(2)}) collective-permute-start(f32[260,128]{1,0:T(8,128)S(1)} %pad_maximum_fusion.6), channel_id=1, source_target_pairs={{0,8},{1,9},{2,10},{3,11},{4,12},{5,13},{6,14},{7,15},{8,0},{9,1},... | collective-permute-start | bytes 399368 | tf_op jit(solution)/shard_map/ppermute | solution.py:257
  200.3 6.6 %collective-permute-start.10 = (f32[260,128]{1,0:T(8,128)S(1)}, f32[260,128]{1,0:T(8,128)S(1)}, u32[]{:S(2)}, u32[]{:S(2)}) collective-permute-start(f32[260,128]{1,0:T(8,128)S(1)} %pad_maximum_fusion.7), channel_id=1, source_target_pairs={{0,16},{1,17},{2,18},{3,19},{4,20},{5,21},{6,22},{7,23},{8,24},{9,... | collective-permute-start | bytes 399368 | tf_op jit(solution)/shard_map/ppermute | solution.py:257
  207.6 1.4 collective-permute-start.11
  211.5 16.6 %copy-start.3 = (bf16[8,4,2048]{2,1,0:T(4,128)(2,1)S(1)}, bf16[8,4,2048]{2,1,0:T(4,128)(2,1)}, u32[]{:S(2)}) copy-start(bf16[8,4,2048]{2,1,0:T(4,128)(2,1)} %param.11) | copy-start | bytes 393220
  211.8 4.0 %collective-permute-start.14 = (bf16[8,4,512]{2,0,1:T(8,128)(2,1)S(1)}, bf16[8,4,512]{2,0,1:T(8,128)(2,1)S(1)}, u32[]{:S(2)}, u32[]{:S(2)}) collective-permute-start(bf16[8,4,512]{2,0,1:T(8,128)(2,1)S(1)} %get-tuple-element.89), channel_id=1, source_target_pairs={{0,96},{32,0},{64,32},{96,64},{1,97},{33,1},{65,33},{97,65},{2,98}... | collective-permute-start | bytes 98312 | tf_op jit(solution)/shard_map/ppermute | solution.py:190
  211.9 5.6 %collective-permute-start.13 = (bf16[8,4,512]{2,0,1:T(8,128)(2,1)S(1)}, bf16[8,4,512]{2,0,1:T(8,128)(2,1)S(1)}, u32[]{:S(2)}, u32[]{:S(2)}) collective-permute-start(bf16[8,4,512]{2,0,1:T(8,128)(2,1)S(1)} %get-tuple-element.90), channel_id=1, source_target_pairs={{0,64},{32,96},{64,0},{96,32},{1,65},{33,97},{65,1},{97,33},{2,66}... | collective-permute-start | bytes 98312 | tf_op jit(solution)/shard_map/ppermute | solution.py:190
  212.2 6.3 %collective-permute-start.12 = (bf16[8,4,512]{2,0,1:T(8,128)(2,1)S(1)}, bf16[8,4,512]{2,0,1:T(8,128)(2,1)S(1)}, u32[]{:S(2)}, u32[]{:S(2)}) collective-permute-start(bf16[8,4,512]{2,0,1:T(8,128)(2,1)S(1)} %get-tuple-element.91), channel_id=1, source_target_pairs={{0,32},{32,64},{64,96},{96,0},{1,33},{33,65},{65,97},{97,1},{2,34}... | collective-permute-start | bytes 98312 | tf_op jit(solution)/shard_map/ppermute | solution.py:190
  218.9 8.6 %collective-permute-start.17 = (bf16[8,4,2048]{2,0,1:T(8,128)(2,1)S(1)}, bf16[8,4,2048]{2,0,1:T(8,128)(2,1)S(1)}, u32[]{:S(2)}, u32[]{:S(2)}) collective-permute-start(bf16[8,4,2048]{2,0,1:T(8,128)(2,1)S(1)} %get-tuple-element.58), channel_id=1, source_target_pairs={{0,32},{32,64},{64,96},{96,0},{1,33},{33,65},{65,97},{97,1},{2,34}... | collective-permute-start | bytes 393224 | tf_op jit(solution)/shard_map/ppermute | solution.py:190
  219.9 7.6 %collective-permute-start.16 = (bf16[8,4,2048]{2,0,1:T(8,128)(2,1)S(1)}, bf16[8,4,2048]{2,0,1:T(8,128)(2,1)S(1)}, u32[]{:S(2)}, u32[]{:S(2)}) collective-permute-start(bf16[8,4,2048]{2,0,1:T(8,128)(2,1)S(1)} %get-tuple-element.59), channel_id=1, source_target_pairs={{0,64},{32,96},{64,0},{96,32},{1,65},{33,97},{65,1},{97,33},{2,66}... | collective-permute-start | bytes 393224 | tf_op jit(solution)/shard_map/ppermute | solution.py:190
  222.5 5.6 %collective-permute-start.15 = (bf16[8,4,2048]{2,0,1:T(8,128)(2,1)S(1)}, bf16[8,4,2048]{2,0,1:T(8,128)(2,1)S(1)}, u32[]{:S(2)}, u32[]{:S(2)}) collective-permute-start(bf16[8,4,2048]{2,0,1:T(8,128)(2,1)S(1)} %get-tuple-element.57), channel_id=1, source_target_pairs={{0,96},{32,0},{64,32},{96,64},{1,97},{33,1},{65,33},{97,65},{2,98}... | collective-permute-start | bytes 393224 | tf_op jit(solution)/shard_map/ppermute | solution.py:190

commit v14 on v13

--- a/solution.py
+++ b/solution.py
@@ -48,40 +48,42 @@
     head_dim = acc_ref.shape[3]
     new_count = fk_ref.shape[1]
     outs = (keys_out_ref, values_out_ref)
-    keys_out_ref[0] = arrived_ref[0, :, 0]
-    values_out_ref[0] = arrived_ref[0, :, 1]
-    length = lengths_ref[r]
-    base = base_ref[0]
-    spots = base + lax.broadcasted_iota(jnp.int32, (1, positions), 1)
-    live = spots < length
-    rows = q_ref.shape[1] // heads
-    keys_all = arrived_ref[0, :, 0].reshape(positions, heads * head_dim)
-    values_all = arrived_ref[0, :, 1].reshape(positions, heads * head_dim)
-    scores = lax.dot_general(
-        q_ref[0], keys_all, (((1,), (1,)), ((), ())), preferred_element_type=jnp.float32
-    ) * scale
-    scores = jnp.where(live, scores, MASKED)
-    peak = jnp.max(scores, axis=1, keepdims=True)
-    weights = jnp.where(live, jnp.exp(scores - peak), 0.0)
-    mass = jnp.sum(weights, axis=1, keepdims=True)
-    acc_all = jnp.dot(weights.astype(jnp.bfloat16), values_all, preferred_element_type=jnp.float32)
-    for kh in range(heads):
-        peak_ref[0, kh] = peak[kh * rows : (kh + 1) * rows]
-        mass_ref[0, kh] = mass[kh * rows : (kh + 1) * rows]
-        acc_ref[0, kh] = acc_all[kh * rows : (kh + 1) * rows, kh * head_dim : (kh + 1) * head_dim]
-    first = length - base
-    page0 = first // page_len
-    row_ids = lax.broadcasted_iota(jnp.int32, (page_len, 1), 0)
-    fresh = (fk_ref[0], fv_ref[0])
-    for page in (page0, page0 + 1):
-        @pl.when(jnp.logical_and(page >= 0, page < pages))
-        def _():
-            for half in range(2):
-                block = outs[half][0, page]
-                for t in range(new_count):
-                    hit = row_ids == first + t - page * page_len
-                    block = jnp.where(hit, fresh[half][t : t + 1, :], block)
-                outs[half][0, page] = block
+    per_step = arrived_ref.shape[0]
+    for j in range(per_step):
+        keys_out_ref[j] = arrived_ref[j, :, 0]
+        values_out_ref[j] = arrived_ref[j, :, 1]
+        length = lengths_ref[r * per_step + j]
+        base = base_ref[0]
+        spots = base + lax.broadcasted_iota(jnp.int32, (1, positions), 1)
+        live = spots < length
+        rows = q_ref.shape[1] // heads
+        keys_all = arrived_ref[j, :, 0].reshape(positions, heads * head_dim)
+        values_all = arrived_ref[j, :, 1].reshape(positions, heads * head_dim)
+        scores = lax.dot_general(
+            q_ref[j], keys_all, (((1,), (1,)), ((), ())), preferred_element_type=jnp.float32
+        ) * scale
+        scores = jnp.where(live, scores, MASKED)
+        peak = jnp.max(scores, axis=1, keepdims=True)
+        weights = jnp.where(live, jnp.exp(scores - peak), 0.0)
+        mass = jnp.sum(weights, axis=1, keepdims=True)
+        acc_all = jnp.dot(weights.astype(jnp.bfloat16), values_all, preferred_element_type=jnp.float32)
+        for kh in range(heads):
+            peak_ref[j, kh] = peak[kh * rows : (kh + 1) * rows]
+            mass_ref[j, kh] = mass[kh * rows : (kh + 1) * rows]
+            acc_ref[j, kh] = acc_all[kh * rows : (kh + 1) * rows, kh * head_dim : (kh + 1) * head_dim]
+        first = length - base
+        page0 = first // page_len
+        row_ids = lax.broadcasted_iota(jnp.int32, (page_len, 1), 0)
+        fresh = (fk_ref[j], fv_ref[j])
+        for page in (page0, page0 + 1):
+            @pl.when(jnp.logical_and(page >= 0, page < pages))
+            def _():
+                for half in range(2):
+                    block = outs[half][j, page]
+                    for t in range(new_count):
+                        hit = row_ids == first + t - page * page_len
+                        block = jnp.where(hit, fresh[half][t : t + 1, :], block)
+                    outs[half][j, page] = block
 
 
 def arrive_and_attend(arrival_src, lengths, base, incoming, queries, fresh_k, fresh_v, scale):
@@ -96,19 +98,19 @@
     arrived = incoming[arrival_src].reshape(local_reqs, pages, 2, page_len, kv_width)
     grid_spec = pltpu.PrefetchScalarGridSpec(
         num_scalar_prefetch=2,
-        grid=(local_reqs,),
+        grid=(local_reqs // 2,),
         in_specs=[
-            pl.BlockSpec((1, pages, 2, page_len, kv_width), lambda r, *_: (r, 0, 0, 0, 0)),
-            pl.BlockSpec((1, heads * rows, heads * head_dim), lambda r, *_: (r, 0, 0)),
-            pl.BlockSpec((1, new_count, kv_width), lambda r, *_: (r, 0, 0)),
-            pl.BlockSpec((1, new_count, kv_width), lambda r, *_: (r, 0, 0)),
+            pl.BlockSpec((2, pages, 2, page_len, kv_width), lambda r, *_: (r, 0, 0, 0, 0)),
+            pl.BlockSpec((2, heads * rows, heads * head_dim), lambda r, *_: (r, 0, 0)),
+            pl.BlockSpec((2, new_count, kv_width), lambda r, *_: (r, 0, 0)),
+            pl.BlockSpec((2, new_count, kv_width), lambda r, *_: (r, 0, 0)),
         ],
         out_specs=[
-            pl.BlockSpec((1, pages, page_len, kv_width), lambda r, *_: (r, 0, 0, 0)),
-            pl.BlockSpec((1, pages, page_len, kv_width), lambda r, *_: (r, 0, 0, 0)),
-            pl.BlockSpec((1, heads, rows, head_dim), lambda r, *_: (r, 0, 0, 0)),
-            pl.BlockSpec((1, heads, rows, 1), lambda r, *_: (r, 0, 0, 0)),
-            pl.BlockSpec((1, heads, rows, 1), lambda r, *_: (r, 0, 0, 0)),
+            pl.BlockSpec((2, pages, page_len, kv_width), lambda r, *_: (r, 0, 0, 0)),
+            pl.BlockSpec((2, pages, page_len, kv_width), lambda r, *_: (r, 0, 0, 0)),
+            pl.BlockSpec((2, heads, rows, head_dim), lambda r, *_: (r, 0, 0, 0)),
+            pl.BlockSpec((2, heads, rows, 1), lambda r, *_: (r, 0, 0, 0)),
+            pl.BlockSpec((2, heads, rows, 1), lambda r, *_: (r, 0, 0, 0)),
         ],
     )
     cache_bytes = 2 * local_reqs * positions * kv_width * 2

time: 230 us -> 229 us (level)
  no operation moved by 1% of the time
where the time goes in v14:
time: 229 us; the launch traced here: 228 us
  waiting for transfers between devices  120 us (52%)
  local copies, waits for them, and re-layouts  41.2 us (18%)
  starting transfers between devices  30 us (13%)
  other arithmetic  19.1 us (8%)
  Pallas kernels  10.4 us (5%)
  matrix products  5.59 us (2%)
    ppermute x12, waiting for transfers between devices, shift(): return lax.ppermute(value, 'req', pairs)  98.8 us
    ppermute x5, waiting for transfers between devices, merge(): other = lax.ppermute(pack(total, peak, mass), 'seq', pairs)  21.2 us
    ppermute x12, starting transfers between devices, shift(): return lax.ppermute(value, 'req', pairs)  16.2 us
    pallas_call x1, Pallas kernels, arrive_and_attend(): pl.pallas_call(functools.partial(_arrive_kernel, scale=scale), out_shape=...  10.4 us
    gather x2, local copies, waits for them, and re-layouts, shards(): outgoing = jnp.stack([pool_keys[send_pick], pool_values[send_pick]], axis=1)  10 us
    all_to_all x1, starting transfers between devices, shards(): lax.all_to_all(outgoing, ('req', 'seq'), split_axis=0, concat_axis=0, til...  10 us
    gather x1, local copies, waits for them, and re-layouts, arrive_and_attend(): incoming[arrival_src].reshape(local_reqs, pages, 2, page_len, kv_width)  9.96 us
    reshape x1, other arithmetic, shards(): outgoing = outgoing.reshape(devices, per_peer, 2, page_len, kv_width)  7.49 us
  transfers between devices with their start and end apart: 19, of which 12 were waited for; matrix products, arithmetic and copies ran while one was open for 17% of the time, Pallas kernels for 0%

profile of v14, /device:TPU:32, one launch (start us, length us, event | category | flops | bytes accessed | tf_op | source)
XLA Modules:
  0.0 228.2 jit_solution(14800111196362138590)
XLA Ops:
  0.6 1.3 fusion.14
  1.9 1.0 fusion.16
  3.0 2.8 %collective-permute-start.2 = (bf16[8,4,2048]{2,0,1:T(8,128)(2,1)S(1)}, bf16[8,4,2048]{2,0,1:T(8,128)(2,1)S(1)}, u32[]{:S(2)}, u32[]{:S(2)}) collective-permute-start(bf16[8,4,2048]{2,0,1:T(8,128)(2,1)S(1)} %fusion.16), channel_id=1, source_target_pairs={{0,96},{32,0},{64,32},{96,64},{1,97},{33,1},{65,33},{97,65},{2,98}... | collective-permute-start | bytes 393224 | tf_op jit(solution)/shard_map/ppermute | solution.py:192
  5.8 0.8 collective-permute-start.1
  6.6 0.9 collective-permute-start
  7.5 0.8 select_reduce_fusion.1
  8.3 1.5 gather_fusion
  10.0 0.6 fusion.7
  10.7 5.0 %gather_fusion.2 = bf16[128,16,1024]{2,1,0:T(8,128)(2,1)} fusion(bf16[128,16,1024]{2,1,0:T(8,128)(2,1)} %param.18, s32[1024]{0:T(1024)S(1)} %pad_clamp_fusion.3), kind=kCustom, calls=%fused_computation.2 | custom fusion | bytes 8389120 | tf_op jit(solution)/shard_map/gather | solution.py:195
  15.7 5.0 %gather_fusion.1 = bf16[128,16,1024]{2,1,0:T(8,128)(2,1)} fusion(bf16[128,16,1024]{2,1,0:T(8,128)(2,1)} %param.17, s32[1024]{0:T(1024)S(1)} %pad_clamp_fusion.3), kind=kCustom, calls=%fused_computation.1 | custom fusion | bytes 8389120 | tf_op jit(solution)/shard_map/gather | solution.py:195
  20.7 7.5 %maximum_bitcast_fusion = bf16[128,1,2,16,1024]{4,3,2,1,0:T(8,128)(2,1)} fusion(bf16[128,1,16,1024]{3,2,1,0:T(8,128)(2,1)} %bitcast.164, bf16[128,1,16,1024]{3,2,1,0:T(8,128)(2,1)} %bitcast.165), kind=kLoop, calls=%fused_computation.6 | loop fusion | flops 4194304 | bytes 16777216 | tf_op jit(solution)/shard_map/reshape | solution.py:196
  28.2 0.9 pad_maximum_fusion
  29.2 10.0 %all-to-all-start = ((bf16[128,1,2,16,1024]{4,3,2,1,0:T(8,128)(2,1)}), bf16[128,1,2,16,1024]{4,3,2,1,0:T(8,128)(2,1)}, u32[]{:S(2)}, u32[]{:S(2)}) async-start(bf16[128,1,2,16,1024]{4,3,2,1,0:T(8,128)(2,1)} %maximum_bitcast_fusion), calls=%async_computation | async-start | bytes 16777216 | tf_op jit(solution)/shard_map/all_to_all | solution.py:198
  39.2 2.3 copy.190
  41.6 0.6 gather_fusion.4
  42.3 3.9 %copy.189 = bf16[512,2048]{1,0:T(8,128)(2,1)} copy(bf16[512,2048]{0,1:T(8,128)(2,1)} %bitcast.169) | data formatting | bytes 4194304 | tf_op jit(solution)/shard_map/dot_general | solution.py:204
  46.3 0.2 copy.151
  47.0 0.8 broadcast_bitcast_fusion
  47.7 0.3 multiply_cosine_fusion
  48.0 1.7 fusion.8
  50.0 2.4 %fusion.10 = f32[32,4,4,128]{3,0,2,1:T(8,128)S(1)} fusion(bf16[4,128,2048,1]{2,1,0,3:T(8,128)(2,1)} %bitcast.166, bf16[32,4,2048]{2,0,1:T(8,128)(2,1)S(1)} %pad_maximum_fusion), kind=kOutput, calls=%fused_computation.27 | convolution fusion | flops 268435456 | bytes 2883584 | tf_op jit(solution)/shard_map/dot_general | solution.py:204
  52.7 0.3 convolution_convert_fusion.1
  53.1 1.5 collective-permute-start.5
  54.7 2.7 %collective-permute-start.4 = (bf16[8,4,1024]{2,0,1:T(8,128)(2,1)S(1)}, bf16[8,4,1024]{2,0,1:T(8,128)(2,1)S(1)}, u32[]{:S(2)}, u32[]{:S(2)}) collective-permute-start(bf16[8,4,1024]{2,0,1:T(8,128)(2,1)S(1)} %get-tuple-element.70), channel_id=1, source_target_pairs={{0,64},{32,96},{64,0},{96,32},{1,65},{33,97},{65,1},{97,33},{2,66}... | collective-permute-start | bytes 196616 | tf_op jit(solution)/shard_map/ppermute | solution.py:192
  57.4 1.4 collective-permute-start.3
  58.8 78.5 %collective-permute-done.5 = bf16[8,4,1024]{2,0,1:T(8,128)(2,1)S(1)} collective-permute-done((bf16[8,4,1024]{2,0,1:T(8,128)(2,1)S(1)}, bf16[8,4,1024]{2,0,1:T(8,128)(2,1)S(1)}, u32[]{:S(2)}, u32[]{:S(2)}) %collective-permute-start.5) | collective-permute-done | bytes 65568 | tf_op jit(solution)/shard_map/ppermute | solution.py:192
  137.3 10.4 %collective-permute-done.4 = bf16[8,4,1024]{2,0,1:T(8,128)(2,1)S(1)} collective-permute-done((bf16[8,4,1024]{2,0,1:T(8,128)(2,1)S(1)}, bf16[8,4,1024]{2,0,1:T(8,128)(2,1)S(1)}, u32[]{:S(2)}, u32[]{:S(2)}) %collective-permute-start.4) | collective-permute-done | bytes 65568 | tf_op jit(solution)/shard_map/ppermute | solution.py:192
  147.8 0.6 gather_fusion.5
  148.8 0.5 copy-done.9
  149.5 0.9 bitcast_select_fusion.q_ref
  150.4 10.0 %gather_fusion.3 = bf16[128,2,16,1024]{3,2,1,0:T(8,128)(2,1)} fusion(bf16[128,2,16,1024]{3,2,1,0:T(8,128)(2,1)} %bitcast.8, s32[1024]{0:T(1024)S(1)} %pad_clamp_fusion.2), kind=kCustom, calls=%fused_computation.3 | custom fusion | bytes 16777728 | tf_op jit(solution)/shard_map/gather | solution.py:98
  160.4 10.4 %arrive_and_attend.1 = (bf16[8,16,16,1024]{3,2,1,0:T(8,128)(2,1)}, bf16[8,16,16,1024]{3,2,1,0:T(8,128)(2,1)}, f32[8,8,8,128]{3,2,1,0:T(8,128)S(1)}, f32[8,8,8,1]{3,2,1,0:T(8,128)S(1)}, f32[8,8,8,1]{3,2,1,0:T(8,128)S(1)}) custom-call(s32[8]{0:T(128)S(1)} %dynamic_slice.27.lengths_ref, s32[1]{0:T(128)} %bitcast.base_ref, ...), custom_call_target="tpu_custom_call" | custom-call | flops 67108864 | bytes 16777216 | tf_op jit(solution)/shard_map/arrive_and_attend/pallas_call | solution.py:117
  170.8 0.7 copy-done.1
  171.5 0.7 copy-done.2
  172.4 1.1 reduce.2
  173.6 1.0 pad_maximum_fusion.1
  174.6 0.3 collective-permute-start.6
  174.9 1.4 copy.161
  176.3 0.5 copy.164
  177.7 1.1 multiply_add_fusion.4
  179.0 5.9 %collective-permute-done.7 = f32[260,128]{1,0:T(8,128)S(1)} collective-permute-done((f32[260,128]{1,0:T(8,128)S(1)}, f32[260,128]{1,0:T(8,128)S(1)}, u32[]{:S(2)}, u32[]{:S(2)}) %collective-permute-start.7) | collective-permute-done | bytes 133152 | tf_op jit(solution)/shard_map/ppermute | solution.py:259
  185.5 0.2 multiply_add_fusion.3
  185.8 3.2 %collective-permute-start.8 = (f32[260,128]{1,0:T(8,128)S(1)}, f32[260,128]{1,0:T(8,128)S(1)}, u32[]{:S(2)}, u32[]{:S(2)}) collective-permute-start(f32[260,128]{1,0:T(8,128)S(1)} %pad_maximum_fusion.5), channel_id=1, source_target_pairs={{0,4},{1,5},{2,6},{3,7},{4,0},{5,1},{6,2},{7,3},{8,12},{9,13},{10,... | collective-permute-start | bytes 399368 | tf_op jit(solution)/shard_map/ppermute | solution.py:259
  189.0 3.5 %collective-permute-done.8 = f32[260,128]{1,0:T(8,128)S(1)} collective-permute-done((f32[260,128]{1,0:T(8,128)S(1)}, f32[260,128]{1,0:T(8,128)S(1)}, u32[]{:S(2)}, u32[]{:S(2)}) %collective-permute-start.8) | collective-permute-done | bytes 133152 | tf_op jit(solution)/shard_map/ppermute | solution.py:259
  193.0 0.2 multiply_add_fusion.2
  193.3 5.4 %collective-permute-done.9 = f32[260,128]{1,0:T(8,128)S(1)} collective-permute-done((f32[260,128]{1,0:T(8,128)S(1)}, f32[260,128]{1,0:T(8,128)S(1)}, u32[]{:S(2)}, u32[]{:S(2)}) %collective-permute-start.9) | collective-permute-done | bytes 133152 | tf_op jit(solution)/shard_map/ppermute | solution.py:259
  199.7 6.4 %collective-permute-done.10 = f32[260,128]{1,0:T(8,128)S(1)} collective-permute-done((f32[260,128]{1,0:T(8,128)S(1)}, f32[260,128]{1,0:T(8,128)S(1)}, u32[]{:S(2)}, u32[]{:S(2)}) %collective-permute-start.10) | collective-permute-done | bytes 133152 | tf_op jit(solution)/shard_map/ppermute | solution.py:259
  206.9 0.3 fusion.21
  207.3 0.5 copy.172
  207.8 0.4 collective-permute-done.11
  209.0 0.5 copy.175
  210.4 0.4 fusion.3
  211.1 0.3 collective-permute-start.13
  211.4 1.7 collective-permute-start.12
  213.1 1.9 collective-permute-done.14
  215.0 1.7 collective-permute-done.13
  216.7 1.0 collective-permute-done.12
  217.7 0.4 convolution_convert_fusion
  218.1 0.9 collective-permute-start.17
  219.1 2.6 %collective-permute-start.16 = (bf16[8,4,2048]{2,0,1:T(8,128)(2,1)S(1)}, bf16[8,4,2048]{2,0,1:T(8,128)(2,1)S(1)}, u32[]{:S(2)}, u32[]{:S(2)}) collective-permute-start(bf16[8,4,2048]{2,0,1:T(8,128)(2,1)S(1)} %get-tuple-element.59), channel_id=1, source_target_pairs={{0,64},{32,96},{64,0},{96,32},{1,65},{33,97},{65,1},{97,33},{2,66}... | collective-permute-start | bytes 393224 | tf_op jit(solution)/shard_map/ppermute | solution.py:192
  221.7 0.3 collective-permute-start.15
  222.0 4.7 %collective-permute-done.17 = bf16[8,4,2048]{2,0,1:T(8,128)(2,1)S(1)} collective-permute-done((bf16[8,4,2048]{2,0,1:T(8,128)(2,1)S(1)}, bf16[8,4,2048]{2,0,1:T(8,128)(2,1)S(1)}, u32[]{:S(2)}, u32[]{:S(2)}) %collective-permute-start.17) | collective-permute-done | bytes 131104 | tf_op jit(solution)/shard_map/ppermute | solution.py:192
  226.7 0.6 collective-permute-done.15
  227.5 0.8 copy.182
  (149 shorter events, 8.5 us)
Async XLA Ops:
  0.6 217.0 %copy-start = (bf16[512,2048]{1,0:T(8,128)(2,1)S(1)}, bf16[512,2048]{1,0:T(8,128)(2,1)}, u32[]{:S(2)}) copy-start(bf16[512,2048]{1,0:T(8,128)(2,1)} %param.16) | copy-start | bytes 6291460
  3.0 25.3 %collective-permute-start.2 = (bf16[8,4,2048]{2,0,1:T(8,128)(2,1)S(1)}, bf16[8,4,2048]{2,0,1:T(8,128)(2,1)S(1)}, u32[]{:S(2)}, u32[]{:S(2)}) collective-permute-start(bf16[8,4,2048]{2,0,1:T(8,128)(2,1)S(1)} %fusion.16), channel_id=1, source_target_pairs={{0,96},{32,0},{64,32},{96,64},{1,97},{33,1},{65,33},{97,65},{2,98}... | collective-permute-start | bytes 393224 | tf_op jit(solution)/shard_map/ppermute | solution.py:192
  5.8 22.4 %collective-permute-start.1 = (bf16[8,4,2048]{2,0,1:T(8,128)(2,1)S(1)}, bf16[8,4,2048]{2,0,1:T(8,128)(2,1)S(1)}, u32[]{:S(2)}, u32[]{:S(2)}) collective-permute-start(bf16[8,4,2048]{2,0,1:T(8,128)(2,1)S(1)} %fusion.16), channel_id=1, source_target_pairs={{0,64},{32,96},{64,0},{96,32},{1,65},{33,97},{65,1},{97,33},{2,66}... | collective-permute-start | bytes 393224 | tf_op jit(solution)/shard_map/ppermute | solution.py:192
  6.6 21.6 %collective-permute-start = (bf16[8,4,2048]{2,0,1:T(8,128)(2,1)S(1)}, bf16[8,4,2048]{2,0,1:T(8,128)(2,1)}, u32[]{:S(2)}, u32[]{:S(2)}) collective-permute-start(bf16[8,4,2048]{2,0,1:T(8,128)(2,1)S(1)} %fusion.16), channel_id=1, source_target_pairs={{0,32},{32,64},{64,96},{96,0},{1,33},{33,65},{65,97},{97,1},{2,34}... | collective-permute-start | bytes 393224 | tf_op jit(solution)/shard_map/ppermute | solution.py:192
  29.2 121.2 %all-to-all-start = ((bf16[128,1,2,16,1024]{4,3,2,1,0:T(8,128)(2,1)}), bf16[128,1,2,16,1024]{4,3,2,1,0:T(8,128)(2,1)}, u32[]{:S(2)}, u32[]{:S(2)}) async-start(bf16[128,1,2,16,1024]{4,3,2,1,0:T(8,128)(2,1)} %maximum_bitcast_fusion), calls=%async_computation | async-start | bytes 16777216 | tf_op jit(solution)/shard_map/all_to_all | solution.py:198
  46.7 6.0 %copy-start.4 = (bf16[2048,256]{1,0:T(8,128)(2,1)S(1)}, bf16[2048,256]{1,0:T(8,128)(2,1)}, u32[]{:S(2)}) copy-start(bf16[2048,256]{1,0:T(8,128)(2,1)} %param.15) | copy-start | bytes 3145732
  53.1 84.2 %collective-permute-start.5 = (bf16[8,4,1024]{2,0,1:T(8,128)(2,1)S(1)}, bf16[8,4,1024]{2,0,1:T(8,128)(2,1)S(1)}, u32[]{:S(2)}, u32[]{:S(2)}) collective-permute-start(bf16[8,4,1024]{2,0,1:T(8,128)(2,1)S(1)} %get-tuple-element.69), channel_id=1, source_target_pairs={{0,32},{32,64},{64,96},{96,0},{1,33},{33,65},{65,97},{97,1},{2,34}... | collective-permute-start | bytes 196616 | tf_op jit(solution)/shard_map/ppermute | solution.py:192
  54.7 93.1 %collective-permute-start.4 = (bf16[8,4,1024]{2,0,1:T(8,128)(2,1)S(1)}, bf16[8,4,1024]{2,0,1:T(8,128)(2,1)S(1)}, u32[]{:S(2)}, u32[]{:S(2)}) collective-permute-start(bf16[8,4,1024]{2,0,1:T(8,128)(2,1)S(1)} %get-tuple-element.70), channel_id=1, source_target_pairs={{0,64},{32,96},{64,0},{96,32},{1,65},{33,97},{65,1},{97,33},{2,66}... | collective-permute-start | bytes 196616 | tf_op jit(solution)/shard_map/ppermute | solution.py:192
  57.4 90.4 %collective-permute-start.3 = (bf16[8,4,1024]{2,0,1:T(8,128)(2,1)S(1)}, bf16[8,4,1024]{2,0,1:T(8,128)(2,1)S(1)}, u32[]{:S(2)}, u32[]{:S(2)}) collective-permute-start(bf16[8,4,1024]{2,0,1:T(8,128)(2,1)S(1)} %get-tuple-element.71), channel_id=1, source_target_pairs={{0,96},{32,0},{64,32},{96,64},{1,97},{33,1},{65,33},{97,65},{2,98}... | collective-permute-start | bytes 196616 | tf_op jit(solution)/shard_map/ppermute | solution.py:192
  148.6 0.7 copy-start.9
  148.7 0.6 copy-start.7
  149.4 10.9 %copy-start.5 = (bf16[8,4,4,256]{3,2,1,0:T(4,128)(2,1)}, bf16[8,4,4,256]{3,2,1,0:T(4,128)(2,1)S(1)}, u32[]{:S(2)}) copy-start(bf16[8,4,4,256]{3,2,1,0:T(4,128)(2,1)S(1)} %copy.160) | copy-start | bytes 196612
  170.8 0.7 copy-start.1
  171.5 0.7 copy-start.2
  172.2 27.5 %copy-start.8 = (bf16[8,4,4,256]{3,2,1,0:T(4,128)(2,1)S(1)}, bf16[8,4,4,256]{3,2,1,0:T(4,128)(2,1)}, u32[]{:S(2)}) copy-start(bf16[8,4,4,256]{3,2,1,0:T(4,128)(2,1)} %copy-done.7) | copy-start | bytes 196612
  174.6 2.5 %collective-permute-start.6 = (f32[520,128]{1,0:T(8,128)S(1)}, f32[520,128]{1,0:T(8,128)S(1)}, u32[]{:S(2)}, u32[]{:S(2)}) collective-permute-start(f32[520,128]{1,0:T(8,128)S(1)} %pad_maximum_fusion.1), channel_id=1, source_target_pairs={{0,1},{1,0},{2,3},{3,2},{4,5},{5,4},{6,7},{7,6},{8,9},{9,8},{10,11... | collective-permute-start | bytes 798728 | tf_op jit(solution)/shard_map/ppermute | solution.py:259
  176.7 30.2 %copy-start.10 = (bf16[8,4,8,2,128]{4,3,2,1,0:T(2,128)(2,1)S(1)}, bf16[8,4,8,2,128]{4,3,2,1,0:T(2,128)(2,1)}, u32[]{:S(2)}) copy-start(bf16[8,4,8,2,128]{4,3,2,1,0:T(2,128)(2,1)} %copy-done.9) | copy-start | bytes 393220
  177.4 29.8 %copy-start.6 = (bf16[8,4,4,256]{3,2,1,0:T(4,128)(2,1)S(1)}, bf16[8,4,4,256]{3,2,1,0:T(4,128)(2,1)}, u32[]{:S(2)}) copy-start(bf16[8,4,4,256]{3,2,1,0:T(4,128)(2,1)} %copy-done.5) | copy-start | bytes 196612
  178.9 6.0 %collective-permute-start.7 = (f32[260,128]{1,0:T(8,128)S(1)}, f32[260,128]{1,0:T(8,128)S(1)}, u32[]{:S(2)}, u32[]{:S(2)}) collective-permute-start(f32[260,128]{1,0:T(8,128)S(1)} %pad_maximum_fusion.4), channel_id=1, source_target_pairs={{0,2},{1,3},{2,0},{3,1},{4,6},{5,7},{6,4},{7,5},{8,10},{9,11},{10,... | collective-permute-start | bytes 399368 | tf_op jit(solution)/shard_map/ppermute | solution.py:259
  185.8 6.7 %collective-permute-start.8 = (f32[260,128]{1,0:T(8,128)S(1)}, f32[260,128]{1,0:T(8,128)S(1)}, u32[]{:S(2)}, u32[]{:S(2)}) collective-permute-start(f32[260,128]{1,0:T(8,128)S(1)} %pad_maximum_fusion.5), channel_id=1, source_target_pairs={{0,4},{1,5},{2,6},{3,7},{4,0},{5,1},{6,2},{7,3},{8,12},{9,13},{10,... | collective-permute-start | bytes 399368 | tf_op jit(solution)/shard_map/ppermute | solution.py:259
  193.2 5.5 %collective-permute-start.9 = (f32[260,128]{1,0:T(8,128)S(1)}, f32[260,128]{1,0:T(8,128)S(1)}, u32[]{:S(2)}, u32[]{:S(2)}) collective-permute-start(f32[260,128]{1,0:T(8,128)S(1)} %pad_maximum_fusion.6), channel_id=1, source_target_pairs={{0,8},{1,9},{2,10},{3,11},{4,12},{5,13},{6,14},{7,15},{8,0},{9,1},... | collective-permute-start | bytes 399368 | tf_op jit(solution)/shard_map/ppermute | solution.py:259
  199.5 6.6 %collective-permute-start.10 = (f32[260,128]{1,0:T(8,128)S(1)}, f32[260,128]{1,0:T(8,128)S(1)}, u32[]{:S(2)}, u32[]{:S(2)}) collective-permute-start(f32[260,128]{1,0:T(8,128)S(1)} %pad_maximum_fusion.7), channel_id=1, source_target_pairs={{0,16},{1,17},{2,18},{3,19},{4,20},{5,21},{6,22},{7,23},{8,24},{9,... | collective-permute-start | bytes 399368 | tf_op jit(solution)/shard_map/ppermute | solution.py:259
  206.8 1.4 collective-permute-start.11
  210.8 16.6 %copy-start.3 = (bf16[8,4,2048]{2,1,0:T(4,128)(2,1)S(1)}, bf16[8,4,2048]{2,1,0:T(4,128)(2,1)}, u32[]{:S(2)}) copy-start(bf16[8,4,2048]{2,1,0:T(4,128)(2,1)} %param.11) | copy-start | bytes 393220
  211.0 4.0 %collective-permute-start.14 = (bf16[8,4,512]{2,0,1:T(8,128)(2,1)S(1)}, bf16[8,4,512]{2,0,1:T(8,128)(2,1)S(1)}, u32[]{:S(2)}, u32[]{:S(2)}) collective-permute-start(bf16[8,4,512]{2,0,1:T(8,128)(2,1)S(1)} %get-tuple-element.89), channel_id=1, source_target_pairs={{0,96},{32,0},{64,32},{96,64},{1,97},{33,1},{65,33},{97,65},{2,98}... | collective-permute-start | bytes 98312 | tf_op jit(solution)/shard_map/ppermute | solution.py:192
  211.1 5.6 %collective-permute-start.13 = (bf16[8,4,512]{2,0,1:T(8,128)(2,1)S(1)}, bf16[8,4,512]{2,0,1:T(8,128)(2,1)S(1)}, u32[]{:S(2)}, u32[]{:S(2)}) collective-permute-start(bf16[8,4,512]{2,0,1:T(8,128)(2,1)S(1)} %get-tuple-element.90), channel_id=1, source_target_pairs={{0,64},{32,96},{64,0},{96,32},{1,65},{33,97},{65,1},{97,33},{2,66}... | collective-permute-start | bytes 98312 | tf_op jit(solution)/shard_map/ppermute | solution.py:192
  211.4 6.3 %collective-permute-start.12 = (bf16[8,4,512]{2,0,1:T(8,128)(2,1)S(1)}, bf16[8,4,512]{2,0,1:T(8,128)(2,1)S(1)}, u32[]{:S(2)}, u32[]{:S(2)}) collective-permute-start(bf16[8,4,512]{2,0,1:T(8,128)(2,1)S(1)} %get-tuple-element.91), channel_id=1, source_target_pairs={{0,32},{32,64},{64,96},{96,0},{1,33},{33,65},{65,97},{97,1},{2,34}... | collective-permute-start | bytes 98312 | tf_op jit(solution)/shard_map/ppermute | solution.py:192
  218.1 8.6 %collective-permute-start.17 = (bf16[8,4,2048]{2,0,1:T(8,128)(2,1)S(1)}, bf16[8,4,2048]{2,0,1:T(8,128)(2,1)S(1)}, u32[]{:S(2)}, u32[]{:S(2)}) collective-permute-start(bf16[8,4,2048]{2,0,1:T(8,128)(2,1)S(1)} %get-tuple-element.58), channel_id=1, source_target_pairs={{0,32},{32,64},{64,96},{96,0},{1,33},{33,65},{65,97},{97,1},{2,34}... | collective-permute-start | bytes 393224 | tf_op jit(solution)/shard_map/ppermute | solution.py:192
  219.1 7.6 %collective-permute-start.16 = (bf16[8,4,2048]{2,0,1:T(8,128)(2,1)S(1)}, bf16[8,4,2048]{2,0,1:T(8,128)(2,1)S(1)}, u32[]{:S(2)}, u32[]{:S(2)}) collective-permute-start(bf16[8,4,2048]{2,0,1:T(8,128)(2,1)S(1)} %get-tuple-element.59), channel_id=1, source_target_pairs={{0,64},{32,96},{64,0},{96,32},{1,65},{33,97},{65,1},{97,33},{2,66}... | collective-permute-start | bytes 393224 | tf_op jit(solution)/shard_map/ppermute | solution.py:192
  221.7 5.6 %collective-permute-start.15 = (bf16[8,4,2048]{2,0,1:T(8,128)(2,1)S(1)}, bf16[8,4,2048]{2,0,1:T(8,128)(2,1)S(1)}, u32[]{:S(2)}, u32[]{:S(2)}) collective-permute-start(bf16[8,4,2048]{2,0,1:T(8,128)(2,1)S(1)} %get-tuple-element.57), channel_id=1, source_target_pairs={{0,96},{32,0},{64,32},{96,64},{1,97},{33,1},{65,33},{97,65},{2,98}... | collective-permute-start | bytes 393224 | tf_op jit(solution)/shard_map/ppermute | solution.py:192

commit v15 on v14

--- a/solution.py
+++ b/solution.py
@@ -38,7 +38,7 @@
 
 def _arrive_kernel(
     lengths_ref, base_ref, arrived_ref, q_ref, fk_ref, fv_ref,
-    keys_out_ref, values_out_ref, acc_ref, peak_ref, mass_ref, *, scale
+    keys_out_ref, values_out_ref, acc_ref, peak_ref, mass_ref, block_q, *, scale
 ):
     r = pl.program_id(0)
     pages = arrived_ref.shape[1]
@@ -49,18 +49,25 @@
     new_count = fk_ref.shape[1]
     outs = (keys_out_ref, values_out_ref)
     per_step = arrived_ref.shape[0]
+    rows = q_ref.shape[2]
+
+    @pl.when(r == 0)
+    def _():
+        block_q[...] = jnp.zeros_like(block_q)
+
     for j in range(per_step):
+        for kh in range(heads):
+            block_q[kh * rows : (kh + 1) * rows, kh * head_dim : (kh + 1) * head_dim] = q_ref[j, kh]
         keys_out_ref[j] = arrived_ref[j, :, 0]
         values_out_ref[j] = arrived_ref[j, :, 1]
         length = lengths_ref[r * per_step + j]
         base = base_ref[0]
         spots = base + lax.broadcasted_iota(jnp.int32, (1, positions), 1)
         live = spots < length
-        rows = q_ref.shape[1] // heads
         keys_all = arrived_ref[j, :, 0].reshape(positions, heads * head_dim)
         values_all = arrived_ref[j, :, 1].reshape(positions, heads * head_dim)
         scores = lax.dot_general(
-            q_ref[j], keys_all, (((1,), (1,)), ((), ())), preferred_element_type=jnp.float32
+            block_q[...], keys_all, (((1,), (1,)), ((), ())), preferred_element_type=jnp.float32
         ) * scale
         scores = jnp.where(live, scores, MASKED)
         peak = jnp.max(scores, axis=1, keepdims=True)
@@ -89,9 +96,6 @@
 def arrive_and_attend(arrival_src, lengths, base, incoming, queries, fresh_k, fresh_v, scale):
     local_reqs, new_count, kv_width = fresh_k.shape
     _, heads, rows, head_dim = queries.shape
-    eye = jnp.arange(heads)[:, None] == jnp.arange(heads)[None, :]
-    block_q = jnp.where(eye[None, :, None, :, None], queries[:, :, :, None, :], jnp.zeros((), queries.dtype))
-    block_q = block_q.reshape(local_reqs, heads * rows, heads * head_dim)
     page_len = incoming.shape[2]
     pages = arrival_src.shape[0] // local_reqs
     positions = pages * page_len
@@ -101,7 +105,7 @@
         grid=(local_reqs // 2,),
         in_specs=[
             pl.BlockSpec((2, pages, 2, page_len, kv_width), lambda r, *_: (r, 0, 0, 0, 0)),
-            pl.BlockSpec((2, heads * rows, heads * head_dim), lambda r, *_: (r, 0, 0)),
+            pl.BlockSpec((2, heads, rows, head_dim), lambda r, *_: (r, 0, 0, 0)),
             pl.BlockSpec((2, new_count, kv_width), lambda r, *_: (r, 0, 0)),
             pl.BlockSpec((2, new_count, kv_width), lambda r, *_: (r, 0, 0)),
         ],
@@ -112,6 +116,7 @@
             pl.BlockSpec((2, heads, rows, 1), lambda r, *_: (r, 0, 0, 0)),
             pl.BlockSpec((2, heads, rows, 1), lambda r, *_: (r, 0, 0, 0)),
         ],
+        scratch_shapes=[pltpu.VMEM((heads * rows, heads * head_dim), jnp.bfloat16)],
     )
     cache_bytes = 2 * local_reqs * positions * kv_width * 2
     keys_out, values_out, acc, peak, mass = pl.pallas_call(
@@ -133,7 +138,7 @@
             bytes_accessed=2 * cache_bytes,
         ),
         name="arrive_and_attend",
-    )(lengths, base, arrived, block_q, fresh_k, fresh_v)
+    )(lengths, base, arrived, queries, fresh_k, fresh_v)
     keys_out = keys_out.reshape(local_reqs, positions, kv_width)
     values_out = values_out.reshape(local_reqs, positions, kv_width)
     return keys_out, values_out, acc, peak, mass

time: 229 us -> 225 us (0.983)
  other arithmetic: 19.1 us -> 16 us
  transfers between devices with their start and end apart: 19 -> 19, of which waited for: 12 -> 13; matrix products, arithmetic and copies ran while one was open for 17% -> 16% of each run, Pallas kernels for 0% -> 0%
where the time goes in v15:
time: 225 us
  waiting for transfers between devices  122 us (54%)
  local copies, waits for them, and re-layouts  39.2 us (17%)
  starting transfers between devices  29.7 us (13%)
  other arithmetic  16 us (7%)
  Pallas kernels  10.4 us (5%)
  matrix products  5.57 us (2%)
    ppermute x12, waiting for transfers between devices, shift(): return lax.ppermute(value, 'req', pairs)  99.6 us
    ppermute x5, waiting for transfers between devices, merge(): other = lax.ppermute(pack(total, peak, mass), 'seq', pairs)  22.1 us
    ppermute x12, starting transfers between devices, shift(): return lax.ppermute(value, 'req', pairs)  16.2 us
    pallas_call x1, Pallas kernels, arrive_and_attend(): pl.pallas_call(functools.partial(_arrive_kernel, scale=scale), out_shape=...  10.4 us
    gather x2, local copies, waits for them, and re-layouts, shards(): outgoing = jnp.stack([pool_keys[send_pick], pool_values[send_pick]], axis=1)  10 us
    all_to_all x1, starting transfers between devices, shards(): lax.all_to_all(outgoing, ('req', 'seq'), split_axis=0, concat_axis=0, til...  10 us
    gather x1, local copies, waits for them, and re-layouts, arrive_and_attend(): incoming[arrival_src].reshape(local_reqs, pages, 2, page_len, kv_width)  9.96 us
    reshape x1, other arithmetic, shards(): outgoing = outgoing.reshape(devices, per_peer, 2, page_len, kv_width)  7.5 us
  transfers between devices with their start and end apart: 19, of which 13 were waited for; matrix products, arithmetic and copies ran while one was open for 16% of the time, Pallas kernels for 0%

profile of v15, /device:TPU:32, one launch (start us, length us, event | category | flops | bytes accessed | tf_op | source)
XLA Modules:
  0.0 224.5 jit_solution(7559453596578518343)
XLA Ops:
  0.6 1.3 fusion.14
  1.9 1.0 fusion.16
  3.0 2.8 %collective-permute-start.2 = (bf16[8,4,2048]{2,0,1:T(8,128)(2,1)S(1)}, bf16[8,4,2048]{2,0,1:T(8,128)(2,1)S(1)}, u32[]{:S(2)}, u32[]{:S(2)}) collective-permute-start(bf16[8,4,2048]{2,0,1:T(8,128)(2,1)S(1)} %fusion.16), channel_id=1, source_target_pairs={{0,96},{32,0},{64,32},{96,64},{1,97},{33,1},{65,33},{97,65},{2,98}... | collective-permute-start | bytes 393224 | tf_op jit(solution)/shard_map/ppermute | solution.py:197
  5.8 0.8 collective-permute-start.1
  6.6 0.9 collective-permute-start
  7.5 0.8 select_reduce_fusion.1
  8.3 1.5 gather_fusion
  9.8 0.2 reshape.606
  10.0 0.6 fusion.7
  10.7 5.0 %gather_fusion.2 = bf16[128,16,1024]{2,1,0:T(8,128)(2,1)} fusion(bf16[128,16,1024]{2,1,0:T(8,128)(2,1)} %param.18, s32[1024]{0:T(1024)S(1)} %pad_clamp_fusion.3), kind=kCustom, calls=%fused_computation.2 | custom fusion | bytes 8389120 | tf_op jit(solution)/shard_map/gather | solution.py:200
  15.7 5.0 %gather_fusion.1 = bf16[128,16,1024]{2,1,0:T(8,128)(2,1)} fusion(bf16[128,16,1024]{2,1,0:T(8,128)(2,1)} %param.17, s32[1024]{0:T(1024)S(1)} %pad_clamp_fusion.3), kind=kCustom, calls=%fused_computation.1 | custom fusion | bytes 8389120 | tf_op jit(solution)/shard_map/gather | solution.py:200
  20.7 7.5 %maximum_bitcast_fusion = bf16[128,1,2,16,1024]{4,3,2,1,0:T(8,128)(2,1)} fusion(bf16[128,1,16,1024]{3,2,1,0:T(8,128)(2,1)} %bitcast.161, bf16[128,1,16,1024]{3,2,1,0:T(8,128)(2,1)} %bitcast.162), kind=kLoop, calls=%fused_computation.6 | loop fusion | flops 4194304 | bytes 16777216 | tf_op jit(solution)/shard_map/reshape | solution.py:201
  28.2 0.9 pad_maximum_fusion
  29.2 10.0 %all-to-all-start = ((bf16[128,1,2,16,1024]{4,3,2,1,0:T(8,128)(2,1)}), bf16[128,1,2,16,1024]{4,3,2,1,0:T(8,128)(2,1)}, u32[]{:S(2)}, u32[]{:S(2)}) async-start(bf16[128,1,2,16,1024]{4,3,2,1,0:T(8,128)(2,1)} %maximum_bitcast_fusion), calls=%async_computation | async-start | bytes 16777216 | tf_op jit(solution)/shard_map/all_to_all | solution.py:203
  39.2 2.3 %copy.186 = bf16[256,2048]{1,0:T(8,128)(2,1)} copy(bf16[256,2048]{0,1:T(8,128)(2,1)} %bitcast.173) | data formatting | bytes 2097152 | tf_op jit(solution)/shard_map/dot_general | solution.py:212
  41.6 0.6 gather_fusion.4
  42.3 3.9 %copy.185 = bf16[512,2048]{1,0:T(8,128)(2,1)} copy(bf16[512,2048]{0,1:T(8,128)(2,1)} %bitcast.166) | data formatting | bytes 4194304 | tf_op jit(solution)/shard_map/dot_general | solution.py:209
  46.3 0.2 copy.148
  46.7 0.2 dynamic-slice_reduce_fusion
  47.0 0.3 multiply_cosine_fusion
  47.3 1.7 fusion.8
  49.2 2.4 %fusion.10 = f32[32,4,4,128]{3,0,2,1:T(8,128)S(1)} fusion(bf16[4,128,2048,1]{2,1,0,3:T(8,128)(2,1)} %bitcast.163, bf16[32,4,2048]{2,0,1:T(8,128)(2,1)S(1)} %pad_maximum_fusion), kind=kOutput, calls=%fused_computation.26 | convolution fusion | flops 268435456 | bytes 2883584 | tf_op jit(solution)/shard_map/dot_general | solution.py:209
  52.0 0.3 convolution_convert_fusion.1
  52.3 1.5 collective-permute-start.5
  53.9 2.7 %collective-permute-start.4 = (bf16[8,4,1024]{2,0,1:T(8,128)(2,1)S(1)}, bf16[8,4,1024]{2,0,1:T(8,128)(2,1)S(1)}, u32[]{:S(2)}, u32[]{:S(2)}) collective-permute-start(bf16[8,4,1024]{2,0,1:T(8,128)(2,1)S(1)} %get-tuple-element.70), channel_id=1, source_target_pairs={{0,64},{32,96},{64,0},{96,32},{1,65},{33,97},{65,1},{97,33},{2,66}... | collective-permute-start | bytes 196616 | tf_op jit(solution)/shard_map/ppermute | solution.py:197
  56.6 1.4 collective-permute-start.3
  58.0 79.3 %collective-permute-done.5 = bf16[8,4,1024]{2,0,1:T(8,128)(2,1)S(1)} collective-permute-done((bf16[8,4,1024]{2,0,1:T(8,128)(2,1)S(1)}, bf16[8,4,1024]{2,0,1:T(8,128)(2,1)S(1)}, u32[]{:S(2)}, u32[]{:S(2)}) %collective-permute-start.5) | collective-permute-done | bytes 65568 | tf_op jit(solution)/shard_map/ppermute | solution.py:197
  137.4 10.4 %collective-permute-done.4 = bf16[8,4,1024]{2,0,1:T(8,128)(2,1)S(1)} collective-permute-done((bf16[8,4,1024]{2,0,1:T(8,128)(2,1)S(1)}, bf16[8,4,1024]{2,0,1:T(8,128)(2,1)S(1)}, u32[]{:S(2)}, u32[]{:S(2)}) %collective-permute-start.4) | collective-permute-done | bytes 65568 | tf_op jit(solution)/shard_map/ppermute | solution.py:197
  147.8 0.6 gather_fusion.5
  148.9 10.0 %gather_fusion.3 = bf16[128,2,16,1024]{3,2,1,0:T(8,128)(2,1)} fusion(bf16[128,2,16,1024]{3,2,1,0:T(8,128)(2,1)} %bitcast.8, s32[1024]{0:T(1024)S(1)} %pad_clamp_fusion.2), kind=kCustom, calls=%fused_computation.3 | custom fusion | bytes 16777728 | tf_op jit(solution)/shard_map/gather | solution.py:102
  158.9 10.4 %arrive_and_attend.1 = (bf16[8,16,16,1024]{3,2,1,0:T(8,128)(2,1)}, bf16[8,16,16,1024]{3,2,1,0:T(8,128)(2,1)}, f32[8,8,8,128]{3,2,1,0:T(8,128)S(1)}, f32[8,8,8,1]{3,2,1,0:T(8,128)S(1)}, f32[8,8,8,1]{3,2,1,0:T(8,128)S(1)}) custom-call(s32[8]{0:T(128)S(1)} %dynamic_slice.27.lengths_ref, s32[1]{0:T(128)} %bitcast.base_ref, ...), custom_call_target="tpu_custom_call" | custom-call | flops 67108864 | bytes 16777216 | tf_op jit(solution)/shard_map/arrive_and_attend/pallas_call | solution.py:122
  169.8 0.7 pad_maximum_fusion.1
  170.5 0.5 copy.157
  170.9 0.5 copy.160
  171.7 0.7 collective-permute-done.6
  172.4 0.7 fusion.47
  173.8 1.0 slice.174
  174.7 0.2 multiply_add_fusion.4
  175.1 5.6 %collective-permute-done.7 = f32[260,128]{1,0:T(8,128)S(1)} collective-permute-done((f32[260,128]{1,0:T(8,128)S(1)}, f32[260,128]{1,0:T(8,128)S(1)}, u32[]{:S(2)}, u32[]{:S(2)}) %collective-permute-start.7) | collective-permute-done | bytes 133152 | tf_op jit(solution)/shard_map/ppermute | solution.py:264
  181.3 0.2 multiply_add_fusion.3
  181.5 3.1 %collective-permute-start.8 = (f32[260,128]{1,0:T(8,128)S(1)}, f32[260,128]{1,0:T(8,128)S(1)}, u32[]{:S(2)}, u32[]{:S(2)}) collective-permute-start(f32[260,128]{1,0:T(8,128)S(1)} %pad_maximum_fusion.5), channel_id=1, source_target_pairs={{0,4},{1,5},{2,6},{3,7},{4,0},{5,1},{6,2},{7,3},{8,12},{9,13},{10,... | collective-permute-start | bytes 399368 | tf_op jit(solution)/shard_map/ppermute | solution.py:264
  184.7 3.4 %collective-permute-done.8 = f32[260,128]{1,0:T(8,128)S(1)} collective-permute-done((f32[260,128]{1,0:T(8,128)S(1)}, f32[260,128]{1,0:T(8,128)S(1)}, u32[]{:S(2)}, u32[]{:S(2)}) %collective-permute-start.8) | collective-permute-done | bytes 133152 | tf_op jit(solution)/shard_map/ppermute | solution.py:264
  188.6 0.2 multiply_add_fusion.2
  189.0 6.0 %collective-permute-done.9 = f32[260,128]{1,0:T(8,128)S(1)} collective-permute-done((f32[260,128]{1,0:T(8,128)S(1)}, f32[260,128]{1,0:T(8,128)S(1)}, u32[]{:S(2)}, u32[]{:S(2)}) %collective-permute-start.9) | collective-permute-done | bytes 133152 | tf_op jit(solution)/shard_map/ppermute | solution.py:264
  195.5 0.2 multiply_add_fusion.1
  196.0 6.4 %collective-permute-done.10 = f32[260,128]{1,0:T(8,128)S(1)} collective-permute-done((f32[260,128]{1,0:T(8,128)S(1)}, f32[260,128]{1,0:T(8,128)S(1)}, u32[]{:S(2)}, u32[]{:S(2)}) %collective-permute-start.10) | collective-permute-done | bytes 133152 | tf_op jit(solution)/shard_map/ppermute | solution.py:264
  202.9 0.2 multiply_add_fusion
  203.2 0.3 fusion.21
  203.5 0.5 copy.168
  204.1 0.4 collective-permute-done.11
  205.3 0.5 copy.171
  206.3 0.2 copy.175
  206.7 0.4 fusion.3
  207.5 1.9 collective-permute-start.12
  209.4 1.9 collective-permute-done.14
  211.3 1.7 collective-permute-done.13
  213.0 1.0 collective-permute-done.12
  213.9 0.4 convolution_convert_fusion
  214.4 0.9 collective-permute-start.17
  215.4 2.6 %collective-permute-start.16 = (bf16[8,4,2048]{2,0,1:T(8,128)(2,1)S(1)}, bf16[8,4,2048]{2,0,1:T(8,128)(2,1)S(1)}, u32[]{:S(2)}, u32[]{:S(2)}) collective-permute-start(bf16[8,4,2048]{2,0,1:T(8,128)(2,1)S(1)} %get-tuple-element.59), channel_id=1, source_target_pairs={{0,64},{32,96},{64,0},{96,32},{1,65},{33,97},{65,1},{97,33},{2,66}... | collective-permute-start | bytes 393224 | tf_op jit(solution)/shard_map/ppermute | solution.py:197
  218.0 0.3 collective-permute-start.15
  218.3 4.7 %collective-permute-done.17 = bf16[8,4,2048]{2,0,1:T(8,128)(2,1)S(1)} collective-permute-done((bf16[8,4,2048]{2,0,1:T(8,128)(2,1)S(1)}, bf16[8,4,2048]{2,0,1:T(8,128)(2,1)S(1)}, u32[]{:S(2)}, u32[]{:S(2)}) %collective-permute-start.17) | collective-permute-done | bytes 131104 | tf_op jit(solution)/shard_map/ppermute | solution.py:197
  223.0 0.6 collective-permute-done.15
  223.7 0.8 copy.178
  (129 shorter events, 7.7 us)
Async XLA Ops:
  0.6 213.3 %copy-start = (bf16[512,2048]{1,0:T(8,128)(2,1)S(1)}, bf16[512,2048]{1,0:T(8,128)(2,1)}, u32[]{:S(2)}) copy-start(bf16[512,2048]{1,0:T(8,128)(2,1)} %param.16) | copy-start | bytes 6291460
  3.0 25.3 %collective-permute-start.2 = (bf16[8,4,2048]{2,0,1:T(8,128)(2,1)S(1)}, bf16[8,4,2048]{2,0,1:T(8,128)(2,1)S(1)}, u32[]{:S(2)}, u32[]{:S(2)}) collective-permute-start(bf16[8,4,2048]{2,0,1:T(8,128)(2,1)S(1)} %fusion.16), channel_id=1, source_target_pairs={{0,96},{32,0},{64,32},{96,64},{1,97},{33,1},{65,33},{97,65},{2,98}... | collective-permute-start | bytes 393224 | tf_op jit(solution)/shard_map/ppermute | solution.py:197
  5.8 22.4 %collective-permute-start.1 = (bf16[8,4,2048]{2,0,1:T(8,128)(2,1)S(1)}, bf16[8,4,2048]{2,0,1:T(8,128)(2,1)S(1)}, u32[]{:S(2)}, u32[]{:S(2)}) collective-permute-start(bf16[8,4,2048]{2,0,1:T(8,128)(2,1)S(1)} %fusion.16), channel_id=1, source_target_pairs={{0,64},{32,96},{64,0},{96,32},{1,65},{33,97},{65,1},{97,33},{2,66}... | collective-permute-start | bytes 393224 | tf_op jit(solution)/shard_map/ppermute | solution.py:197
  6.6 21.6 %collective-permute-start = (bf16[8,4,2048]{2,0,1:T(8,128)(2,1)S(1)}, bf16[8,4,2048]{2,0,1:T(8,128)(2,1)}, u32[]{:S(2)}, u32[]{:S(2)}) collective-permute-start(bf16[8,4,2048]{2,0,1:T(8,128)(2,1)S(1)} %fusion.16), channel_id=1, source_target_pairs={{0,32},{32,64},{64,96},{96,0},{1,33},{33,65},{65,97},{97,1},{2,34}... | collective-permute-start | bytes 393224 | tf_op jit(solution)/shard_map/ppermute | solution.py:197
  29.2 119.7 %all-to-all-start = ((bf16[128,1,2,16,1024]{4,3,2,1,0:T(8,128)(2,1)}), bf16[128,1,2,16,1024]{4,3,2,1,0:T(8,128)(2,1)}, u32[]{:S(2)}, u32[]{:S(2)}) async-start(bf16[128,1,2,16,1024]{4,3,2,1,0:T(8,128)(2,1)} %maximum_bitcast_fusion), calls=%async_computation | async-start | bytes 16777216 | tf_op jit(solution)/shard_map/all_to_all | solution.py:203
  46.7 5.3 %copy-start.2 = (bf16[2048,256]{1,0:T(8,128)(2,1)S(1)}, bf16[2048,256]{1,0:T(8,128)(2,1)}, u32[]{:S(2)}) copy-start(bf16[2048,256]{1,0:T(8,128)(2,1)} %param.15) | copy-start | bytes 3145732
  52.3 85.0 %collective-permute-start.5 = (bf16[8,4,1024]{2,0,1:T(8,128)(2,1)S(1)}, bf16[8,4,1024]{2,0,1:T(8,128)(2,1)S(1)}, u32[]{:S(2)}, u32[]{:S(2)}) collective-permute-start(bf16[8,4,1024]{2,0,1:T(8,128)(2,1)S(1)} %get-tuple-element.69), channel_id=1, source_target_pairs={{0,32},{32,64},{64,96},{96,0},{1,33},{33,65},{65,97},{97,1},{2,34}... | collective-permute-start | bytes 196616 | tf_op jit(solution)/shard_map/ppermute | solution.py:197
  53.9 93.9 %collective-permute-start.4 = (bf16[8,4,1024]{2,0,1:T(8,128)(2,1)S(1)}, bf16[8,4,1024]{2,0,1:T(8,128)(2,1)S(1)}, u32[]{:S(2)}, u32[]{:S(2)}) collective-permute-start(bf16[8,4,1024]{2,0,1:T(8,128)(2,1)S(1)} %get-tuple-element.70), channel_id=1, source_target_pairs={{0,64},{32,96},{64,0},{96,32},{1,65},{33,97},{65,1},{97,33},{2,66}... | collective-permute-start | bytes 196616 | tf_op jit(solution)/shard_map/ppermute | solution.py:197
  56.6 91.2 %collective-permute-start.3 = (bf16[8,4,1024]{2,0,1:T(8,128)(2,1)S(1)}, bf16[8,4,1024]{2,0,1:T(8,128)(2,1)S(1)}, u32[]{:S(2)}, u32[]{:S(2)}) collective-permute-start(bf16[8,4,1024]{2,0,1:T(8,128)(2,1)S(1)} %get-tuple-element.71), channel_id=1, source_target_pairs={{0,96},{32,0},{64,32},{96,64},{1,97},{33,1},{65,33},{97,65},{2,98}... | collective-permute-start | bytes 196616 | tf_op jit(solution)/shard_map/ppermute | solution.py:197
  170.5 1.9 collective-permute-start.6
  175.0 5.7 %collective-permute-start.7 = (f32[260,128]{1,0:T(8,128)S(1)}, f32[260,128]{1,0:T(8,128)S(1)}, u32[]{:S(2)}, u32[]{:S(2)}) collective-permute-start(f32[260,128]{1,0:T(8,128)S(1)} %pad_maximum_fusion.4), channel_id=1, source_target_pairs={{0,2},{1,3},{2,0},{3,1},{4,6},{5,7},{6,4},{7,5},{8,10},{9,11},{10,... | collective-permute-start | bytes 399368 | tf_op jit(solution)/shard_map/ppermute | solution.py:264
  181.5 6.6 %collective-permute-start.8 = (f32[260,128]{1,0:T(8,128)S(1)}, f32[260,128]{1,0:T(8,128)S(1)}, u32[]{:S(2)}, u32[]{:S(2)}) collective-permute-start(f32[260,128]{1,0:T(8,128)S(1)} %pad_maximum_fusion.5), channel_id=1, source_target_pairs={{0,4},{1,5},{2,6},{3,7},{4,0},{5,1},{6,2},{7,3},{8,12},{9,13},{10,... | collective-permute-start | bytes 399368 | tf_op jit(solution)/shard_map/ppermute | solution.py:264
  188.9 6.1 %collective-permute-start.9 = (f32[260,128]{1,0:T(8,128)S(1)}, f32[260,128]{1,0:T(8,128)S(1)}, u32[]{:S(2)}, u32[]{:S(2)}) collective-permute-start(f32[260,128]{1,0:T(8,128)S(1)} %pad_maximum_fusion.6), channel_id=1, source_target_pairs={{0,8},{1,9},{2,10},{3,11},{4,12},{5,13},{6,14},{7,15},{8,0},{9,1},... | collective-permute-start | bytes 399368 | tf_op jit(solution)/shard_map/ppermute | solution.py:264
  195.8 6.6 %collective-permute-start.10 = (f32[260,128]{1,0:T(8,128)S(1)}, f32[260,128]{1,0:T(8,128)S(1)}, u32[]{:S(2)}, u32[]{:S(2)}) collective-permute-start(f32[260,128]{1,0:T(8,128)S(1)} %pad_maximum_fusion.7), channel_id=1, source_target_pairs={{0,16},{1,17},{2,18},{3,19},{4,20},{5,21},{6,22},{7,23},{8,24},{9,... | collective-permute-start | bytes 399368 | tf_op jit(solution)/shard_map/ppermute | solution.py:264
  203.1 1.4 collective-permute-start.11
  207.0 16.6 %copy-start.1 = (bf16[8,4,2048]{2,1,0:T(4,128)(2,1)S(1)}, bf16[8,4,2048]{2,1,0:T(4,128)(2,1)}, u32[]{:S(2)}) copy-start(bf16[8,4,2048]{2,1,0:T(4,128)(2,1)} %param.11) | copy-start | bytes 393220
  207.3 4.0 %collective-permute-start.14 = (bf16[8,4,512]{2,0,1:T(8,128)(2,1)S(1)}, bf16[8,4,512]{2,0,1:T(8,128)(2,1)S(1)}, u32[]{:S(2)}, u32[]{:S(2)}) collective-permute-start(bf16[8,4,512]{2,0,1:T(8,128)(2,1)S(1)} %get-tuple-element.89), channel_id=1, source_target_pairs={{0,96},{32,0},{64,32},{96,64},{1,97},{33,1},{65,33},{97,65},{2,98}... | collective-permute-start | bytes 98312 | tf_op jit(solution)/shard_map/ppermute | solution.py:197
  207.4 5.6 %collective-permute-start.13 = (bf16[8,4,512]{2,0,1:T(8,128)(2,1)S(1)}, bf16[8,4,512]{2,0,1:T(8,128)(2,1)S(1)}, u32[]{:S(2)}, u32[]{:S(2)}) collective-permute-start(bf16[8,4,512]{2,0,1:T(8,128)(2,1)S(1)} %get-tuple-element.90), channel_id=1, source_target_pairs={{0,64},{32,96},{64,0},{96,32},{1,65},{33,97},{65,1},{97,33},{2,66}... | collective-permute-start | bytes 98312 | tf_op jit(solution)/shard_map/ppermute | solution.py:197
  207.5 6.5 %collective-permute-start.12 = (bf16[8,4,512]{2,0,1:T(8,128)(2,1)S(1)}, bf16[8,4,512]{2,0,1:T(8,128)(2,1)S(1)}, u32[]{:S(2)}, u32[]{:S(2)}) collective-permute-start(bf16[8,4,512]{2,0,1:T(8,128)(2,1)S(1)} %get-tuple-element.91), channel_id=1, source_target_pairs={{0,32},{32,64},{64,96},{96,0},{1,33},{33,65},{65,97},{97,1},{2,34}... | collective-permute-start | bytes 98312 | tf_op jit(solution)/shard_map/ppermute | solution.py:197
  214.4 8.6 %collective-permute-start.17 = (bf16[8,4,2048]{2,0,1:T(8,128)(2,1)S(1)}, bf16[8,4,2048]{2,0,1:T(8,128)(2,1)S(1)}, u32[]{:S(2)}, u32[]{:S(2)}) collective-permute-start(bf16[8,4,2048]{2,0,1:T(8,128)(2,1)S(1)} %get-tuple-element.58), channel_id=1, source_target_pairs={{0,32},{32,64},{64,96},{96,0},{1,33},{33,65},{65,97},{97,1},{2,34}... | collective-permute-start | bytes 393224 | tf_op jit(solution)/shard_map/ppermute | solution.py:197
  215.4 7.6 %collective-permute-start.16 = (bf16[8,4,2048]{2,0,1:T(8,128)(2,1)S(1)}, bf16[8,4,2048]{2,0,1:T(8,128)(2,1)S(1)}, u32[]{:S(2)}, u32[]{:S(2)}) collective-permute-start(bf16[8,4,2048]{2,0,1:T(8,128)(2,1)S(1)} %get-tuple-element.59), channel_id=1, source_target_pairs={{0,64},{32,96},{64,0},{96,32},{1,65},{33,97},{65,1},{97,33},{2,66}... | collective-permute-start | bytes 393224 | tf_op jit(solution)/shard_map/ppermute | solution.py:197
  218.0 5.6 %collective-permute-start.15 = (bf16[8,4,2048]{2,0,1:T(8,128)(2,1)S(1)}, bf16[8,4,2048]{2,0,1:T(8,128)(2,1)S(1)}, u32[]{:S(2)}, u32[]{:S(2)}) collective-permute-start(bf16[8,4,2048]{2,0,1:T(8,128)(2,1)S(1)} %get-tuple-element.57), channel_id=1, source_target_pairs={{0,96},{32,0},{64,32},{96,64},{1,97},{33,1},{65,33},{97,65},{2,98}... | collective-permute-start | bytes 393224 | tf_op jit(solution)/shard_map/ppermute | solution.py:197
